TPU v7x, 32 devices: a whole 2x2x4 slice. The times are simulated.
32 devices in a mesh: group: 2 (over y), dp: 4 (over x, core), tensor: 4 (over z).
Axes of the slice: x: 2, y: 2, z: 4, core: 2. Of those that a mesh axis runs over, the one named last changes fastest.
Arguments:
- tokens: bfloat16 [8192, 1024], P(('group', 'dp')), parts along dimension 0, may hold values from -6 to 6
- past_states: float32 [256, 8, 128, 128], P(('group', 'dp'), 'tensor'), parts along dimension 0, may hold values from -3 to 3
- attn_weights: bfloat16 [5, 1024, 1024], P(None, 'dp', 'tensor'), may hold values from -0.1875 to 0.1875
- ffn_weights: bfloat16 [2, 1024, 4096], P(None, 'dp', 'tensor'), may hold values from -0.1875 to 0.1875
- norm_gains: float32 [2, 1024], replicated, may hold values from 0.1 to 1.9
- head_rates: float32 [8], replicated, may hold values from 0.004 to 0.15
- end_lengths: int32 [256], P(('group', 'dp')), parts along dimension 0, may hold values from 1 to 64, as said below
- new_slot: int32 [256], P(('group', 'dp')), parts along dimension 0, may hold values from 0 to 127, as said below
Outputs:
- next_tokens: bfloat16 [8192, 1024], P(('group', 'dp'), 'tensor'), parts along dimension 0
- moved_states: float32 [256, 8, 128, 128], P(('group', 'dp'), 'tensor'), parts along dimension 0
There are 2 independent parts, one for each index of `group`. A program takes and returns all parts, laid end to end along the dimension named above; an argument that names none is the same for every part. Nothing has to cross between parts.
Inputs may be any that keep to these rules, and one draw needn't show every extreme that they name: `end_lengths`: of the sessions in one aligned block of 32 sessions whose end lengths exceed 32, at most 16 have new slots in one aligned block of 32 slots, and some pair of blocks has exactly 16. `new_slot`: A permutation of the 128 slots.
All inputs are finite; a program needn't handle non-finite values.
Results may differ from a plain program's by a relative error of at most 0.018.
Values may be sent and summed in bfloat16 or wider, within the bound.
No kernel may reach another device: no remote copies, remote signals or barrier semaphores. Data moves between devices by JAX's collectives and lax.ppermute only.
A program may use at most 64 MiB of HBM per device.

v0:
```python
import functools
import jax
import jax.numpy as jnp
from jax import lax
from jax.experimental import pallas as pl
from jax.experimental.pallas import tpu as pltpu
from jax.sharding import PartitionSpec as P

CHUNKS = 2
BLOCK_ROWS = 256
VMEM_LIMIT = 56 * 1024 * 1024


NT = (((1,), (1,)), ((), ()))


def dot_nt(a, b):
    return lax.dot_general(a, b, NT, preferred_element_type=jnp.float32)


def dot_nn(a, b):
    return jnp.dot(a, b, preferred_element_type=jnp.float32)


def rms_scale(values, gain_row):
    meansq = jnp.mean(values * values, axis=-1, keepdims=True)
    return (values * lax.rsqrt(meansq + 1e-05) * gain_row).astype(jnp.bfloat16)


def piece_copies(pieces, dest, sems, me, pick):
    copies = []
    rows = dest.shape[-2] // len(pieces)
    for k, piece in enumerate(pieces):
        start = pl.multiple_of(jnp.bitwise_xor(me, k) * rows, rows)
        copies.append(
            pltpu.make_async_copy(pick(piece), dest.at[..., pl.ds(start, rows), :], sems.at[k])
        )
    return copies


def project_kernel(n_dp, heads, event_count, *refs):
    ids_ref, rates_ref, tok_ref, gain_ref, past_ref = refs[:5]
    pieces = refs[5 : 5 + n_dp]
    gated_ref, key_ref, value_ref, w_ref, decay_ref, sems = refs[-6:]
    rows = tok_ref.shape[0]
    head_dim = past_ref.shape[3]
    sessions = rows // event_count
    key_scale = head_dim ** (-0.5)
    first = pl.program_id(0) == 0
    depth = w_ref.shape[1] // n_dp
    copies = []
    for m in range(4):
        span = pl.ds(m * depth, depth)
        copies += piece_copies(
            pieces, w_ref.at[m], sems.at[m], ids_ref[0], lambda piece: piece.at[span]
        )

    @pl.when(first)
    def _():
        for copy in copies:
            copy.start()
        at = lax.broadcasted_iota(jnp.int32, (rows, rows), 0)
        to = lax.broadcasted_iota(jnp.int32, (rows, rows), 1)
        allowed = (at // event_count == to // event_count) & (at >= to)
        distance = jnp.maximum(at - to, 0).astype(jnp.float32)
        for h in range(heads):
            rate = rates_ref[ids_ref[1] * heads + h]
            decay_ref[h] = jnp.where(allowed, jnp.exp(-rate * distance), 0.0) * key_scale

    normed = rms_scale(tok_ref[...].astype(jnp.float32), gain_ref[0:1, :])

    @pl.when(first)
    def _():
        for copy in copies:
            copy.wait()

    query = dot_nn(normed, w_ref[0]).astype(jnp.bfloat16)
    keys = dot_nn(normed, w_ref[1]).astype(jnp.bfloat16)
    key_ref[...] = keys
    values = dot_nn(normed, w_ref[2]).astype(jnp.bfloat16)
    value_ref[...] = values
    gate = dot_nn(normed, w_ref[3])
    place = lax.broadcasted_iota(jnp.int32, (rows, head_dim), 0) % event_count
    for h in range(heads):
        cols = slice(h * head_dim, (h + 1) * head_dim)
        qh, kh, vh = query[:, cols], keys[:, cols], values[:, cols]
        mix = (dot_nt(qh, kh) * decay_ref[h]).astype(jnp.bfloat16)
        intra = dot_nn(mix, vh)
        parts = []
        for s in range(sessions):
            parts.append(
                dot_nn(
                    qh[s * event_count : (s + 1) * event_count],
                    past_ref[s, h].astype(jnp.bfloat16),
                )
            )
        rate = rates_ref[ids_ref[1] * heads + h]
        factor = jnp.exp(-rate * (place + 1).astype(jnp.float32))
        retained = intra + jnp.concatenate(parts, axis=0) * factor
        centred = retained - jnp.mean(retained, axis=-1, keepdims=True)
        row_var = jnp.mean(centred * centred, axis=-1, keepdims=True)
        normalised = centred * lax.rsqrt(row_var + 1e-05)
        gated_ref[:, cols] = (jax.nn.silu(gate[:, cols]) * normalised).astype(jnp.bfloat16)


def state_kernel(heads, event_count, *refs):
    ids_ref, rates_ref, pos_ref, key_ref, value_ref, past_ref = refs[:6]
    out_ref = refs[6]
    buf_ref, sems = refs[7:]
    sessions, _, head_dim, _ = past_ref.shape
    step = pl.program_id(0)
    steps = pl.num_programs(0)
    slot = lax.rem(step, 2)
    key_scale = head_dim ** (-0.5)

    def copy_of(which_slot, session, target):
        return pltpu.make_async_copy(
            buf_ref.at[which_slot, session], out_ref.at[target], sems.at[which_slot, session]
        )

    def drain(which_slot, which_step):
        for s in range(sessions):
            pos = pos_ref[which_step * sessions + s]

            @pl.when(pos >= 0)
            def _():
                copy_of(which_slot, s, pos).wait()

    @pl.when(step >= 2)
    def _():
        drain(slot, step - 2)

    place = lax.broadcasted_iota(jnp.int32, (key_ref.shape[0], head_dim), 0) % event_count
    left = (event_count - 1 - place).astype(jnp.float32)
    for h in range(heads):
        rate = rates_ref[ids_ref[1] * heads + h]
        cols = slice(h * head_dim, (h + 1) * head_dim)
        factor = jnp.exp(-rate * left) * key_scale
        weighted = (key_ref[:, cols].astype(jnp.float32) * factor).astype(jnp.bfloat16)
        carry = jnp.exp(jnp.full((head_dim, head_dim), -rate * event_count, jnp.float32))
        for s in range(sessions):
            span = slice(s * event_count, (s + 1) * event_count)
            grown = lax.dot_general(
                weighted[span],
                value_ref[span, cols],
                (((0,), (0,)), ((), ())),
                preferred_element_type=jnp.float32,
            )
            buf_ref[slot, s, h] = (carry * past_ref[s, h] + grown).astype(jnp.bfloat16)
    for s in range(sessions):
        pos = pos_ref[step * sessions + s]

        @pl.when(pos >= 0)
        def _():
            copy_of(slot, s, pos).start()

    @pl.when(step == steps - 1)
    def _():
        @pl.when(step >= 1)
        def _():
            drain(1 - slot, step - 1)

        drain(slot, step)


def unpack_kernel(src_ref, recv_ref, out_ref, buf_ref, sems):
    per_step = out_ref.shape[0]
    step = pl.program_id(0)

    def copy_of(slot):
        return pltpu.make_async_copy(
            recv_ref.at[jnp.maximum(src_ref[slot], 0)], buf_ref.at[slot], sems.at[slot]
        )

    @pl.when(step == 0)
    def _():
        for slot in range(buf_ref.shape[0]):

            @pl.when(src_ref[slot] >= 0)
            def _():
                copy_of(slot).start()

    for i in range(per_step):
        slot = step * per_step + i

        @pl.when(src_ref[slot] >= 0)
        def _():
            copy_of(slot).wait()
            out_ref[i] = buf_ref[slot].astype(jnp.float32)

        @pl.when(src_ref[slot] < 0)
        def _():
            out_ref[i] = jnp.zeros(out_ref.shape[1:], jnp.float32)


def feed_kernel(n_dp, n_tensor, *refs):
    ids_ref, tok_ref, gain_ref = refs[:3]
    gated = refs[3 : 3 + n_tensor]
    at = 3 + n_tensor
    out_pieces = refs[at : at + n_dp]
    ffn_pieces = refs[at + n_dp : at + 2 * n_dp]
    at += 2 * n_dp
    own_ref = refs[at]
    part_refs = refs[at + 1 : at + n_tensor]
    wo_ref, wf_ref, res_ref, sem_out, sem_up, sem_down = refs[at + n_tensor :]
    first = pl.program_id(0) == 0
    me = ids_ref[0]
    out_copies = piece_copies(out_pieces, wo_ref, sem_out, me, lambda piece: piece)
    up_copies = piece_copies(ffn_pieces, wf_ref.at[0], sem_up, me, lambda piece: piece.at[0])
    down_copies = piece_copies(ffn_pieces, wf_ref.at[1], sem_down, me, lambda piece: piece.at[1])

    @pl.when(first)
    def _():
        for copy in out_copies + up_copies + down_copies:
            copy.start()
        for copy in out_copies:
            copy.wait()

    attended = dot_nt(gated[0][...], wo_ref[ids_ref[2]])
    for k in range(1, n_tensor):
        attended += dot_nt(gated[k][...], wo_ref[ids_ref[2 + k]])
    residual = tok_ref[...].astype(jnp.float32) + attended
    res_ref[...] = residual
    width = own_ref.shape[1]
    hidden = rms_scale(residual, gain_ref[1:2, :])

    @pl.when(first)
    def _():
        for copy in up_copies:
            copy.wait()

    activated = jax.nn.gelu(dot_nn(hidden, wf_ref[0]), approximate=True).astype(jnp.bfloat16)

    @pl.when(first)
    def _():
        for copy in down_copies:
            copy.wait()

    def term(k):
        owner = lax.rem(ids_ref[1] + k, n_tensor)
        span = pl.ds(pl.multiple_of(owner * width, width), width)
        return dot_nt(activated, wf_ref[1, span, :])

    for k in range(1, n_tensor):
        part_refs[k - 1][...] = term(k).astype(jnp.bfloat16)
    mine = pl.ds(pl.multiple_of(ids_ref[1] * width, width), width)
    own_ref[...] = res_ref[:, mine] + term(0)


def xor_gather(value, axis):
    pieces = [value]
    size = lax.axis_size(axis)
    bit = size // 2
    order = [0]
    while bit:
        pairs = [(i, i ^ bit) for i in range(size)]
        arrived = []
        for piece in pieces:
            arrived.append(lax.ppermute(piece, axis, pairs))
        pieces = pieces + arrived
        order = order + [k ^ bit for k in order]
        bit //= 2
    return [pieces[order.index(k)] for k in range(size)]


def ring_order(size):
    return list(range(0, size, 2)) + list(range(1, size, 2))[::-1]


def ring_pairs(size):
    order = ring_order(size)
    return [(order[i], order[(i + 1) % size]) for i in range(size)]


def ring_sources(size):
    order = ring_order(size)
    return [[order[(order.index(at) - k) % size] for k in range(size)] for at in range(size)]


def any_spec():
    return pl.BlockSpec(memory_space=pl.ANY)


def smem_spec():
    return pl.BlockSpec(memory_space=pltpu.SMEM)


def per_device(
    tokens, past_states, attn_weights, ffn_weights, norm_gains, head_rates, end_lengths, new_slot
):
    sessions_here = end_lengths.shape[0]
    row_count, width = tokens.shape
    event_count = row_count // sessions_here
    heads_here, head_dim = past_states.shape[1], past_states.shape[3]
    cols_here = heads_here * head_dim
    units_here = ffn_weights.shape[2]
    n_dp, n_tensor = lax.axis_size("dp"), lax.axis_size("tensor")
    dp_at, tensor_at = lax.axis_index("dp"), lax.axis_index("tensor")
    share = width // n_tensor
    pair_cap = max(2, 2 * sessions_here // n_dp)
    slot_count = n_dp * pair_cap
    chunk_rows = row_count // CHUNKS
    block = min(BLOCK_ROWS, chunk_rows)
    block_sessions = block // event_count
    steps = chunk_rows // block
    ring = ring_pairs(n_tensor)
    sources = jnp.array(ring_sources(n_tensor), jnp.int32)[tensor_at]
    ids = jnp.concatenate([jnp.stack([dp_at, tensor_at]).astype(jnp.int32), sources])

    survive = end_lengths > event_count
    target_dev = new_slot // sessions_here
    session_ids = jnp.arange(sessions_here, dtype=jnp.int32)
    proj_rows = attn_weights.shape[1]
    notes = jnp.stack([jnp.where(survive, target_dev, -1), new_slot % sessions_here])
    notes = jnp.pad(notes.astype(jnp.bfloat16), ((0, 6), (0, cols_here - sessions_here)))
    proj_own = jnp.concatenate([attn_weights[:4].reshape(4 * proj_rows, cols_here), notes])
    proj_pieces = xor_gather(proj_own, "dp")
    out_own = lax.all_to_all(
        jnp.broadcast_to(attn_weights[4:], (n_tensor, proj_rows, cols_here)),
        "tensor",
        split_axis=0,
        concat_axis=0,
        tiled=True,
    )

    meta = jnp.stack([piece[4 * proj_rows :, :sessions_here] for piece in proj_pieces])
    meta = meta.astype(jnp.int32)
    from_dev = jnp.bitwise_xor(dp_at, jnp.arange(n_dp, dtype=jnp.int32))
    earlier = (
        (target_dev[None, :] == target_dev[:, None])
        & survive[None, :]
        & (session_ids[None, :] < session_ids[:, None])
    )
    pair_rank = jnp.sum(earlier.astype(jnp.int32), axis=1)
    send_pos = jnp.where(survive, target_dev * pair_cap + pair_rank, -1)
    coming = meta[:, 0] == dp_at
    ahead = coming[:, None, :] & (session_ids[None, None, :] < session_ids[None, :, None])
    rank_all = jnp.sum(ahead.astype(jnp.int32), axis=2)
    from_pos = from_dev[:, None] * pair_cap + rank_all + 1
    lands = meta[:, 1][None] == session_ids[:, None, None]
    recv_src = jnp.sum(jnp.where(lands & coming[None], from_pos[None], 0), axis=(1, 2)) - 1

    live_len = jnp.minimum(end_lengths, event_count)
    keep = jnp.arange(event_count, dtype=jnp.int32)[None, :] < live_len[:, None]
    keep = jnp.broadcast_to(keep.reshape(-1)[:, None], (row_count, share)).astype(jnp.bfloat16)
    send_pos, recv_src, keep = lax.optimization_barrier((send_pos, recv_src, keep))

    def project(c, so_far):
        base = c * steps
        rows_spec = pl.BlockSpec((block, cols_here), lambda i: (base + i, 0))
        rows_shape = jax.ShapeDtypeStruct((row_count, cols_here), jnp.bfloat16)
        return pl.pallas_call(
            functools.partial(project_kernel, n_dp, heads_here, event_count),
            grid=(steps,),
            in_specs=[
                smem_spec(),
                smem_spec(),
                pl.BlockSpec((block, width), lambda i: (base + i, 0)),
                pl.BlockSpec(norm_gains.shape, lambda i: (0, 0)),
                pl.BlockSpec(
                    (block_sessions, heads_here, head_dim, head_dim),
                    lambda i: (base + i, 0, 0, 0),
                ),
            ]
            + [any_spec()] * (n_dp + len(so_far)),
            out_specs=[pl.BlockSpec((block, cols_here), lambda i: (i, 0)), rows_spec, rows_spec],
            out_shape=[
                jax.ShapeDtypeStruct((chunk_rows, cols_here), jnp.bfloat16),
                rows_shape,
                rows_shape,
            ],
            input_output_aliases={5 + n_dp + k: 1 + k for k in range(len(so_far))},
            scratch_shapes=[
                pltpu.VMEM((4, width, cols_here), jnp.bfloat16),
                pltpu.VMEM((heads_here, block, block), jnp.float32),
                pltpu.SemaphoreType.DMA((4, n_dp)),
            ],
            compiler_params=pltpu.CompilerParams(vmem_limit_bytes=VMEM_LIMIT),
            cost_estimate=pl.CostEstimate(
                flops=2 * chunk_rows * width * cols_here * 4,
                bytes_accessed=chunk_rows * width * 4,
                transcendentals=0,
            ),
            name="project",
        )(ids, head_rates, tokens, norm_gains, past_states, *proj_pieces, *so_far)

    gated, kept = [], []
    for c in range(CHUNKS):
        g, *kept = project(c, kept)
        gated.append([g])
    for _ in range(n_tensor - 1):
        for c in range(CHUNKS):
            gated[c].append(lax.ppermute(gated[c][-1], "tensor", ring))

    out_pieces = xor_gather(out_own, "dp")
    ffn_pieces = xor_gather(ffn_weights, "dp")

    packed = pl.pallas_call(
        functools.partial(state_kernel, heads_here, event_count),
        grid=(row_count // block,),
        in_specs=[smem_spec(), smem_spec(), smem_spec()]
        + [pl.BlockSpec((block, cols_here), lambda i: (i, 0))] * 2
        + [pl.BlockSpec((block_sessions, heads_here, head_dim, head_dim), lambda i: (i, 0, 0, 0))],
        out_specs=any_spec(),
        out_shape=jax.ShapeDtypeStruct((slot_count, heads_here, head_dim, head_dim), jnp.bfloat16),
        scratch_shapes=[
            pltpu.VMEM((2, block_sessions, heads_here, head_dim, head_dim), jnp.bfloat16),
            pltpu.SemaphoreType.DMA((2, block_sessions)),
        ],
        compiler_params=pltpu.CompilerParams(vmem_limit_bytes=VMEM_LIMIT),
        cost_estimate=pl.CostEstimate(
            flops=2 * row_count * head_dim * cols_here,
            bytes_accessed=past_states.size * 6,
            transcendentals=0,
        ),
        name="states",
    )(ids, head_rates, send_pos, *kept, past_states)
    received = lax.all_to_all(packed, "dp", split_axis=0, concat_axis=0, tiled=True)

    def feed(c):
        base = c * steps
        row_spec = pl.BlockSpec((block, cols_here), lambda i: (i, 0))
        return pl.pallas_call(
            functools.partial(feed_kernel, n_dp, n_tensor),
            grid=(steps,),
            in_specs=[
                smem_spec(),
                pl.BlockSpec((block, width), lambda i: (base + i, 0)),
                pl.BlockSpec(norm_gains.shape, lambda i: (0, 0)),
            ]
            + [row_spec] * n_tensor
            + [any_spec()] * (2 * n_dp),
            out_specs=[pl.BlockSpec((block, share), lambda i: (i, 0))] * n_tensor,
            out_shape=[jax.ShapeDtypeStruct((chunk_rows, share), jnp.float32)]
            + [jax.ShapeDtypeStruct((chunk_rows, share), jnp.bfloat16)] * (n_tensor - 1),
            scratch_shapes=[
                pltpu.VMEM((n_tensor, width, cols_here), jnp.bfloat16),
                pltpu.VMEM((2, width, units_here), jnp.bfloat16),
                pltpu.VMEM((block, width), jnp.float32),
                pltpu.SemaphoreType.DMA((n_dp,)),
                pltpu.SemaphoreType.DMA((n_dp,)),
                pltpu.SemaphoreType.DMA((n_dp,)),
            ],
            compiler_params=pltpu.CompilerParams(vmem_limit_bytes=VMEM_LIMIT),
            cost_estimate=pl.CostEstimate(
                flops=2 * chunk_rows * width * (width + 2 * units_here),
                bytes_accessed=chunk_rows * width * 8,
                transcendentals=0,
            ),
            name="feed",
        )(ids, tokens, norm_gains, *gated[c], *out_pieces, *ffn_pieces)

    rows_out = []
    for c in range(CHUNKS):
        own, *parts = feed(c)
        terms = []
        for k, part in enumerate(parts):
            pairs = [(i, (i + k + 1) % n_tensor) for i in range(n_tensor)]
            terms.append(lax.ppermute(part, "tensor", pairs))
        total = own
        for term in terms:
            total = total + term.astype(jnp.float32)
        keep_here = keep[c * chunk_rows : (c + 1) * chunk_rows] > 0
        rows_out.append(jnp.where(keep_here, total, 0.0).astype(jnp.bfloat16))
    next_tokens = jnp.concatenate(rows_out)

    per_step = min(8, sessions_here)
    moved_states = pl.pallas_call(
        unpack_kernel,
        grid=(sessions_here // per_step,),
        in_specs=[smem_spec(), any_spec()],
        out_specs=pl.BlockSpec((per_step, heads_here, head_dim, head_dim), lambda i: (i, 0, 0, 0)),
        out_shape=jax.ShapeDtypeStruct(past_states.shape, jnp.float32),
        scratch_shapes=[
            pltpu.VMEM((sessions_here, heads_here, head_dim, head_dim), jnp.bfloat16),
            pltpu.SemaphoreType.DMA((sessions_here,)),
        ],
        compiler_params=pltpu.CompilerParams(vmem_limit_bytes=VMEM_LIMIT),
        cost_estimate=pl.CostEstimate(
            flops=0, bytes_accessed=past_states.size * 6, transcendentals=0
        ),
        name="unpack",
    )(recv_src, received)
    return (next_tokens, moved_states)


def solution(mesh):
    placed = (
        P(("group", "dp"), None),
        P(("group", "dp"), "tensor", None, None),
        P(None, "dp", "tensor"),
        P(None, "dp", "tensor"),
        P(),
        P(),
        P(("group", "dp")),
        P(("group", "dp")),
    )

    return jax.shard_map(
        per_device,
        mesh=mesh,
        in_specs=placed,
        out_specs=(P(("group", "dp"), "tensor"), P(("group", "dp"), "tensor", None, None)),
        check_vma=False,
    )
```

profile of v0, /device:TPU:9, one launch (start us, length us, event | category | flops | bytes accessed | tf_op | source)
XLA Modules:
  0.0 191.0 jit_solution(17231389651998462920)
XLA Ops:
  6.5 4.8 %all-to-all-start = ((bf16[4,256,256]{2,1,0:T(8,128)(2,1)}), bf16[4,256,256]{2,1,0:T(8,128)(2,1)S(1)}, u32[]{:S(2)}, u32[]{:S(2)}) async-start(bf16[4,256,256]{2,1,0:T(8,128)(2,1)} %broadcast_in_dim.29), calls=%async_computation | async-start | bytes 1048576 | tf_op jit(solution)/shard_map/all_to_all | solution.py:318
  13.0 2.4 %collective-permute-done.1.refs_7_ = bf16[1032,256]{1,0:T(8,128)(2,1)S(1)} collective-permute-done((bf16[1032,256]{1,0:T(8,128)(2,1)S(1)}, bf16[1032,256]{1,0:T(8,128)(2,1)S(1)}, u32[]{:S(2)}, u32[]{:S(2)}) %collective-permute-start.1) | collective-permute-done | bytes 528416 | tf_op jit(solution)/shard_map/ppermute | solution.py:259
  15.4 2.7 %collective-permute-start.2 = (bf16[1032,256]{1,0:T(8,128)(2,1)S(1)}, bf16[1032,256]{1,0:T(8,128)(2,1)S(1)}, u32[]{:S(2)}, u32[]{:S(2)}) collective-permute-start(bf16[1032,256]{1,0:T(8,128)(2,1)S(1)} %collective-permute-done.1.refs_7_), channel_id=1, source_target_pairs={{0,4},{4,0},{8,12},{12,8},{1,5},{5,1},{9,13},{13,9},{2,6},{6,2},{1... | collective-permute-start | bytes 1585160 | tf_op jit(solution)/shard_map/ppermute | solution.py:259
  21.6 6.5 %project.2 = (bf16[512,256]{1,0:T(8,128)(2,1)}, bf16[1024,256]{1,0:T(8,128)(2,1)}, bf16[1024,256]{1,0:T(8,128)(2,1)}) custom-call(s32[6]{0:T(128)} %pad_add_fusion.refs_0_, f32[8]{0:T(128)} %refs_1_.9, bf16[1024,1024]{1,0:T(8,128)(2,1)} %refs_1_.8, f32[2,1024]{1,0:T(2,128)} %refs_2_.7, f32[32,2,128,128]{3,2,1,0:T(8,128)} %refs_5_.1, ...), custom_call_target="tpu_custom_call" | custom-call | flops 1073741824 | bytes 2097152 | tf_op jit(solution)/shard_map/project/pallas_call | solution.py:352
  28.1 6.5 %project.3 = (bf16[512,256]{1,0:T(8,128)(2,1)}, bf16[1024,256]{1,0:T(8,128)(2,1)}, bf16[1024,256]{1,0:T(8,128)(2,1)}) custom-call(s32[6]{0:T(128)} %pad_add_fusion.refs_0_, f32[8]{0:T(128)} %refs_1_.9, bf16[1024,1024]{1,0:T(8,128)(2,1)} %refs_1_.8, f32[2,1024]{1,0:T(2,128)} %refs_2_.7, ...), custom_call_target="tpu_custom_call", output_to_operand_aliasing={{1}: (9, {}), {2}: (10, {})} | custom-call | flops 1073741824 | bytes 2097152 | tf_op jit(solution)/shard_map/project/pallas_call | solution.py:352
  34.6 5.3 %states.1 = bf16[64,2,128,128]{3,2,1,0:T(8,128)(2,1)} custom-call(s32[6]{0:T(128)} %pad_add_fusion.refs_0_, f32[8]{0:T(128)} %refs_1_.9, s32[32]{0:T(128)} %get-tuple-element.33.refs_2_, bf16[1024,256]{1,0:T(8,128)(2,1)} %get-tuple-element.34.refs_3_, bf16[1024,256]{1,0:T(8,128)(2,1)} %get-tuple-element.35.refs_4_, f32[32,2,128,128]{3,2,1,0:T(8,128)} %refs_5_.1), custom_call_target="tpu_custom_call" | custom-call | flops 67108864 | bytes 6291456 | tf_op jit(solution)/shard_map/states/pallas_call | solution.py:398
  40.0 5.2 %all-to-all-start.1 = ((bf16[64,2,128,128]{3,2,1,0:T(8,128)(2,1)}), bf16[64,2,128,128]{3,2,1,0:T(8,128)(2,1)}, u32[]{:S(2)}, u32[]{:S(2)}) async-start(bf16[64,2,128,128]{3,2,1,0:T(8,128)(2,1)} %states.1), calls=%async_computation.1 | async-start | bytes 8388608 | tf_op jit(solution)/shard_map/all_to_all | solution.py:418
  45.3 1.6 collective-permute-start.7
  47.6 1.5 collective-permute-done.9.refs_12_
  50.3 53.3 %collective-permute-done.7.refs_9_ = bf16[4,256,256]{2,1,0:T(8,128)(2,1)S(1)} collective-permute-done((bf16[4,256,256]{2,1,0:T(8,128)(2,1)S(1)}, bf16[4,256,256]{2,1,0:T(8,128)(2,1)S(1)}, u32[]{:S(2)}, u32[]{:S(2)}) %collective-permute-start.7) | collective-permute-done | bytes 524320 | tf_op jit(solution)/shard_map/ppermute | solution.py:259
  104.6 2.5 %collective-permute-start.4 = (bf16[512,256]{1,0:T(8,128)(2,1)S(1)}, bf16[512,256]{1,0:T(8,128)(2,1)S(1)}, u32[]{:S(2)}, u32[]{:S(2)}) collective-permute-start(bf16[512,256]{1,0:T(8,128)(2,1)S(1)} %collective-permute-done.3.refs_4_), channel_id=1, source_target_pairs={{0,2},{2,3},{3,1},{1,0},{4,6},{6,7},{7,5},{5,4},{8,10},{10,11},{11... | collective-permute-start | bytes 786440 | tf_op jit(solution)/shard_map/ppermute | solution.py:393
  107.1 6.2 %collective-permute-done.16.refs_5_ = bf16[512,256]{1,0:T(8,128)(2,1)S(1)} collective-permute-done((bf16[512,256]{1,0:T(8,128)(2,1)S(1)}, bf16[512,256]{1,0:T(8,128)(2,1)S(1)}, u32[]{:S(2)}, u32[]{:S(2)}) %collective-permute-start.16) | collective-permute-done | bytes 262176 | tf_op jit(solution)/shard_map/ppermute | solution.py:393
  113.3 5.6 %collective-permute-done.4.refs_5_ = bf16[512,256]{1,0:T(8,128)(2,1)S(1)} collective-permute-done((bf16[512,256]{1,0:T(8,128)(2,1)S(1)}, bf16[512,256]{1,0:T(8,128)(2,1)S(1)}, u32[]{:S(2)}, u32[]{:S(2)}) %collective-permute-start.4) | collective-permute-done | bytes 262176 | tf_op jit(solution)/shard_map/ppermute | solution.py:393
  118.9 5.6 %collective-permute-done.17.refs_6_ = bf16[512,256]{1,0:T(8,128)(2,1)S(1)} collective-permute-done((bf16[512,256]{1,0:T(8,128)(2,1)S(1)}, bf16[512,256]{1,0:T(8,128)(2,1)S(1)}, u32[]{:S(2)}, u32[]{:S(2)}) %collective-permute-start.17) | collective-permute-done | bytes 262176 | tf_op jit(solution)/shard_map/ppermute | solution.py:393
  126.2 10.2 %feed.3 = (f32[512,256]{1,0:T(8,128)}, bf16[512,256]{1,0:T(8,128)(2,1)}, bf16[512,256]{1,0:T(8,128)(2,1)}, bf16[512,256]{1,0:T(8,128)(2,1)}) custom-call(s32[6]{0:T(128)} %pad_add_fusion.refs_0_, bf16[1024,1024]{1,0:T(8,128)(2,1)} %refs_1_.8, f32[2,1024]{1,0:T(2,128)} %refs_2_.7, bf16[512,256]{1,0:T(8,128)(2,1)} %get-tuple-element.27.refs_3_, ...), custom_call_target="tpu_custom_call" | custom-call | flops 3221225472 | bytes 4194304 | tf_op jit(solution)/shard_map/feed/pallas_call | solution.py:423
  140.0 10.1 %feed.2 = (f32[512,256]{1,0:T(8,128)}, bf16[512,256]{1,0:T(8,128)(2,1)}, bf16[512,256]{1,0:T(8,128)(2,1)}, bf16[512,256]{1,0:T(8,128)(2,1)}) custom-call(s32[6]{0:T(128)} %pad_add_fusion.refs_0_, bf16[1024,1024]{1,0:T(8,128)(2,1)} %refs_1_.8, f32[2,1024]{1,0:T(2,128)} %refs_2_.7, bf16[512,256]{1,0:T(8,128)(2,1)} %get-tuple-element.20.refs_3_, ...), custom_call_target="tpu_custom_call" | custom-call | flops 3221225472 | bytes 4194304 | tf_op jit(solution)/shard_map/feed/pallas_call | solution.py:423
  150.3 4.0 %collective-permute-start.13 = (bf16[512,256]{1,0:T(8,128)(2,1)}, bf16[512,256]{1,0:T(8,128)(2,1)S(1)}, u32[]{:S(2)}, u32[]{:S(2)}) collective-permute-start(bf16[512,256]{1,0:T(8,128)(2,1)} %get-tuple-element.23), channel_id=1, source_target_pairs={{0,2},{1,3},{2,0},{3,1},{4,6},{5,7},{6,4},{7,5},{8,10},{9,11},{10,... | collective-permute-start | bytes 786440 | tf_op jit(solution)/shard_map/ppermute | solution.py:459
  154.3 4.9 %collective-permute-done.19 = bf16[512,256]{1,0:T(8,128)(2,1)S(1)} collective-permute-done((bf16[512,256]{1,0:T(8,128)(2,1)}, bf16[512,256]{1,0:T(8,128)(2,1)S(1)}, u32[]{:S(2)}, u32[]{:S(2)}) %collective-permute-start.19) | collective-permute-done | bytes 262176 | tf_op jit(solution)/shard_map/ppermute | solution.py:459
  159.2 13.8 %collective-permute-done.20 = bf16[512,256]{1,0:T(8,128)(2,1)S(1)} collective-permute-done((bf16[512,256]{1,0:T(8,128)(2,1)}, bf16[512,256]{1,0:T(8,128)(2,1)S(1)}, u32[]{:S(2)}, u32[]{:S(2)}) %collective-permute-start.20) | collective-permute-done | bytes 262176 | tf_op jit(solution)/shard_map/ppermute | solution.py:459
  173.0 3.0 %collective-permute-done.12 = bf16[512,256]{1,0:T(8,128)(2,1)S(1)} collective-permute-done((bf16[512,256]{1,0:T(8,128)(2,1)}, bf16[512,256]{1,0:T(8,128)(2,1)S(1)}, u32[]{:S(2)}, u32[]{:S(2)}) %collective-permute-start.12) | collective-permute-done | bytes 262176 | tf_op jit(solution)/shard_map/ppermute | solution.py:459
  176.0 5.6 %collective-permute-done.13 = bf16[512,256]{1,0:T(8,128)(2,1)S(1)} collective-permute-done((bf16[512,256]{1,0:T(8,128)(2,1)}, bf16[512,256]{1,0:T(8,128)(2,1)S(1)}, u32[]{:S(2)}, u32[]{:S(2)}) %collective-permute-start.13) | collective-permute-done | bytes 262176 | tf_op jit(solution)/shard_map/ppermute | solution.py:459
  181.6 2.6 %collective-permute-done.14 = bf16[512,256]{1,0:T(8,128)(2,1)S(1)} collective-permute-done((bf16[512,256]{1,0:T(8,128)(2,1)}, bf16[512,256]{1,0:T(8,128)(2,1)S(1)}, u32[]{:S(2)}, u32[]{:S(2)}) %collective-permute-start.14) | collective-permute-done | bytes 262176 | tf_op jit(solution)/shard_map/ppermute | solution.py:459
  184.2 1.4 select_convert_fusion.1
  186.5 4.5 %unpack.1 = f32[32,2,128,128]{3,2,1,0:T(8,128)} custom-call(s32[32]{0:T(128)} %get-tuple-element.32.src_ref, bf16[64,2,128,128]{3,2,1,0:T(8,128)(2,1)} %all-to-all-done.1.recv_ref), custom_call_target="tpu_custom_call" | custom-call | bytes 6291456 | tf_op jit(solution)/shard_map/unpack/pallas_call | solution.py:468
  (96 shorter events, 20.3 us)
Async XLA Ops:
  2.5 13.0 %collective-permute-start.1 = (bf16[1032,256]{1,0:T(8,128)(2,1)S(1)}, bf16[1032,256]{1,0:T(8,128)(2,1)S(1)}, u32[]{:S(2)}, u32[]{:S(2)}) collective-permute-start(bf16[1032,256]{1,0:T(8,128)(2,1)S(1)} %pad_maximum_fusion.refs_5_), channel_id=1, source_target_pairs={{0,8},{4,12},{8,0},{12,4},{1,9},{5,13},{9,1},{13,5},{2,10},{6,14},... | collective-permute-start | bytes 1585160 | tf_op jit(solution)/shard_map/ppermute | solution.py:259
  3.8 14.9 %collective-permute-start = (bf16[1032,256]{1,0:T(8,128)(2,1)S(1)}, bf16[1032,256]{1,0:T(8,128)(2,1)S(1)}, u32[]{:S(2)}, u32[]{:S(2)}) collective-permute-start(bf16[1032,256]{1,0:T(8,128)(2,1)S(1)} %pad_maximum_fusion.refs_5_), channel_id=1, source_target_pairs={{0,4},{4,0},{8,12},{12,8},{1,5},{5,1},{9,13},{13,9},{2,6},{6,2},{1... | collective-permute-start | bytes 1585160 | tf_op jit(solution)/shard_map/ppermute | solution.py:259
  6.5 33.6 %all-to-all-start = ((bf16[4,256,256]{2,1,0:T(8,128)(2,1)}), bf16[4,256,256]{2,1,0:T(8,128)(2,1)S(1)}, u32[]{:S(2)}, u32[]{:S(2)}) async-start(bf16[4,256,256]{2,1,0:T(8,128)(2,1)} %broadcast_in_dim.29), calls=%async_computation | async-start | bytes 1048576 | tf_op jit(solution)/shard_map/all_to_all | solution.py:318
  11.2 35.7 %collective-permute-start.10 = (bf16[2,256,1024]{2,1,0:T(8,128)(2,1)}, bf16[2,256,1024]{2,1,0:T(8,128)(2,1)}, u32[]{:S(2)}, u32[]{:S(2)}) collective-permute-start(bf16[2,256,1024]{2,1,0:T(8,128)(2,1)} %refs_11_.3), channel_id=1, source_target_pairs={{0,8},{4,12},{8,0},{12,4},{1,9},{5,13},{9,1},{13,5},{2,10},{6,14},... | collective-permute-start | bytes 3145736 | tf_op jit(solution)/shard_map/ppermute | solution.py:259
  15.4 4.2 %collective-permute-start.2 = (bf16[1032,256]{1,0:T(8,128)(2,1)S(1)}, bf16[1032,256]{1,0:T(8,128)(2,1)S(1)}, u32[]{:S(2)}, u32[]{:S(2)}) collective-permute-start(bf16[1032,256]{1,0:T(8,128)(2,1)S(1)} %collective-permute-done.1.refs_7_), channel_id=1, source_target_pairs={{0,4},{4,0},{8,12},{12,8},{1,5},{5,1},{9,13},{13,9},{2,6},{6,2},{1... | collective-permute-start | bytes 1585160 | tf_op jit(solution)/shard_map/ppermute | solution.py:259
  40.0 146.4 %all-to-all-start.1 = ((bf16[64,2,128,128]{3,2,1,0:T(8,128)(2,1)}), bf16[64,2,128,128]{3,2,1,0:T(8,128)(2,1)}, u32[]{:S(2)}, u32[]{:S(2)}) async-start(bf16[64,2,128,128]{3,2,1,0:T(8,128)(2,1)} %states.1), calls=%async_computation.1 | async-start | bytes 8388608 | tf_op jit(solution)/shard_map/all_to_all | solution.py:418
  45.2 4.0 %collective-permute-start.9 = (bf16[2,256,1024]{2,1,0:T(8,128)(2,1)S(1)}, bf16[2,256,1024]{2,1,0:T(8,128)(2,1)S(1)}, u32[]{:S(2)}, u32[]{:S(2)}) collective-permute-start(bf16[2,256,1024]{2,1,0:T(8,128)(2,1)S(1)} %copy-done.6), channel_id=1, source_target_pairs={{0,4},{4,0},{8,12},{12,8},{1,5},{5,1},{9,13},{13,9},{2,6},{6,2},{1... | collective-permute-start | bytes 3145736 | tf_op jit(solution)/shard_map/ppermute | solution.py:259
  45.3 58.3 %collective-permute-start.7 = (bf16[4,256,256]{2,1,0:T(8,128)(2,1)S(1)}, bf16[4,256,256]{2,1,0:T(8,128)(2,1)S(1)}, u32[]{:S(2)}, u32[]{:S(2)}) collective-permute-start(bf16[4,256,256]{2,1,0:T(8,128)(2,1)S(1)} %all-to-all-done.refs_7_), channel_id=1, source_target_pairs={{0,8},{4,12},{8,0},{12,4},{1,9},{5,13},{9,1},{13,5},{2,10},{6,14},... | collective-permute-start | bytes 1572872 | tf_op jit(solution)/shard_map/ppermute | solution.py:259
  46.9 77.6 %collective-permute-start.11 = (bf16[2,256,1024]{2,1,0:T(8,128)(2,1)}, bf16[2,256,1024]{2,1,0:T(8,128)(2,1)S(1)}, u32[]{:S(2)}, u32[]{:S(2)}) collective-permute-start(bf16[2,256,1024]{2,1,0:T(8,128)(2,1)} %collective-permute-done.10.refs_13_), channel_id=1, source_target_pairs={{0,4},{4,0},{8,12},{12,8},{1,5},{5,1},{9,13},{13,9},{2,6},{6,2},{1... | collective-permute-start | bytes 3145736 | tf_op jit(solution)/shard_map/ppermute | solution.py:259
  47.3 57.2 %collective-permute-start.15 = (bf16[512,256]{1,0:T(8,128)(2,1)S(1)}, bf16[512,256]{1,0:T(8,128)(2,1)S(1)}, u32[]{:S(2)}, u32[]{:S(2)}) collective-permute-start(bf16[512,256]{1,0:T(8,128)(2,1)S(1)} %copy-done.13), channel_id=1, source_target_pairs={{0,2},{2,3},{3,1},{1,0},{4,6},{6,7},{7,5},{5,4},{8,10},{10,11},{11... | collective-permute-start | bytes 786440 | tf_op jit(solution)/shard_map/ppermute | solution.py:393
  47.4 71.5 %collective-permute-start.6 = (bf16[4,256,256]{2,1,0:T(8,128)(2,1)S(1)}, bf16[4,256,256]{2,1,0:T(8,128)(2,1)S(1)}, u32[]{:S(2)}, u32[]{:S(2)}) collective-permute-start(bf16[4,256,256]{2,1,0:T(8,128)(2,1)S(1)} %all-to-all-done.refs_7_), channel_id=1, source_target_pairs={{0,4},{4,0},{8,12},{12,8},{1,5},{5,1},{9,13},{13,9},{2,6},{6,2},{1... | collective-permute-start | bytes 1572872 | tf_op jit(solution)/shard_map/ppermute | solution.py:259
  49.2 75.3 %copy-start.7 = (bf16[2,256,1024]{2,1,0:T(8,128)(2,1)}, bf16[2,256,1024]{2,1,0:T(8,128)(2,1)S(1)}, u32[]{:S(2)}) copy-start(bf16[2,256,1024]{2,1,0:T(8,128)(2,1)S(1)} %collective-permute-done.9.refs_12_) | copy-start | bytes 3145732
  49.2 55.4 %collective-permute-start.3 = (bf16[512,256]{1,0:T(8,128)(2,1)S(1)}, bf16[512,256]{1,0:T(8,128)(2,1)S(1)}, u32[]{:S(2)}, u32[]{:S(2)}) collective-permute-start(bf16[512,256]{1,0:T(8,128)(2,1)S(1)} %copy-done.12), channel_id=1, source_target_pairs={{0,2},{2,3},{3,1},{1,0},{4,6},{6,7},{7,5},{5,4},{8,10},{10,11},{11... | collective-permute-start | bytes 786440 | tf_op jit(solution)/shard_map/ppermute | solution.py:393
  103.6 15.3 %collective-permute-start.8 = (bf16[4,256,256]{2,1,0:T(8,128)(2,1)S(1)}, bf16[4,256,256]{2,1,0:T(8,128)(2,1)S(1)}, u32[]{:S(2)}, u32[]{:S(2)}) collective-permute-start(bf16[4,256,256]{2,1,0:T(8,128)(2,1)S(1)} %collective-permute-done.7.refs_9_), channel_id=1, source_target_pairs={{0,4},{4,0},{8,12},{12,8},{1,5},{5,1},{9,13},{13,9},{2,6},{6,2},{1... | collective-permute-start | bytes 1572872 | tf_op jit(solution)/shard_map/ppermute | solution.py:259
  104.6 8.7 %collective-permute-start.16 = (bf16[512,256]{1,0:T(8,128)(2,1)S(1)}, bf16[512,256]{1,0:T(8,128)(2,1)S(1)}, u32[]{:S(2)}, u32[]{:S(2)}) collective-permute-start(bf16[512,256]{1,0:T(8,128)(2,1)S(1)} %collective-permute-done.15.refs_4_), channel_id=1, source_target_pairs={{0,2},{2,3},{3,1},{1,0},{4,6},{6,7},{7,5},{5,4},{8,10},{10,11},{11... | collective-permute-start | bytes 786440 | tf_op jit(solution)/shard_map/ppermute | solution.py:393
  104.6 14.3 %collective-permute-start.4 = (bf16[512,256]{1,0:T(8,128)(2,1)S(1)}, bf16[512,256]{1,0:T(8,128)(2,1)S(1)}, u32[]{:S(2)}, u32[]{:S(2)}) collective-permute-start(bf16[512,256]{1,0:T(8,128)(2,1)S(1)} %collective-permute-done.3.refs_4_), channel_id=1, source_target_pairs={{0,2},{2,3},{3,1},{1,0},{4,6},{6,7},{7,5},{5,4},{8,10},{10,11},{11... | collective-permute-start | bytes 786440 | tf_op jit(solution)/shard_map/ppermute | solution.py:393
  113.3 11.2 %collective-permute-start.17 = (bf16[512,256]{1,0:T(8,128)(2,1)S(1)}, bf16[512,256]{1,0:T(8,128)(2,1)S(1)}, u32[]{:S(2)}, u32[]{:S(2)}) collective-permute-start(bf16[512,256]{1,0:T(8,128)(2,1)S(1)} %collective-permute-done.16.refs_5_), channel_id=1, source_target_pairs={{0,2},{2,3},{3,1},{1,0},{4,6},{6,7},{7,5},{5,4},{8,10},{10,11},{11... | collective-permute-start | bytes 786440 | tf_op jit(solution)/shard_map/ppermute | solution.py:393
  118.9 20.4 %collective-permute-start.5 = (bf16[512,256]{1,0:T(8,128)(2,1)S(1)}, bf16[512,256]{1,0:T(8,128)(2,1)S(1)}, u32[]{:S(2)}, u32[]{:S(2)}) collective-permute-start(bf16[512,256]{1,0:T(8,128)(2,1)S(1)} %collective-permute-done.4.refs_5_), channel_id=1, source_target_pairs={{0,2},{2,3},{3,1},{1,0},{4,6},{6,7},{7,5},{5,4},{8,10},{10,11},{11... | collective-permute-start | bytes 786440 | tf_op jit(solution)/shard_map/ppermute | solution.py:393
  136.4 17.9 %collective-permute-start.18 = (bf16[512,256]{1,0:T(8,128)(2,1)}, bf16[512,256]{1,0:T(8,128)(2,1)S(1)}, u32[]{:S(2)}, u32[]{:S(2)}) collective-permute-start(bf16[512,256]{1,0:T(8,128)(2,1)} %get-tuple-element.29), channel_id=1, source_target_pairs={{0,1},{1,2},{2,3},{3,0},{4,5},{5,6},{6,7},{7,4},{8,9},{9,10},{10,1... | collective-permute-start | bytes 786440 | tf_op jit(solution)/shard_map/ppermute | solution.py:459
  137.7 21.4 %collective-permute-start.19 = (bf16[512,256]{1,0:T(8,128)(2,1)}, bf16[512,256]{1,0:T(8,128)(2,1)S(1)}, u32[]{:S(2)}, u32[]{:S(2)}) collective-permute-start(bf16[512,256]{1,0:T(8,128)(2,1)} %get-tuple-element.30), channel_id=1, source_target_pairs={{0,2},{1,3},{2,0},{3,1},{4,6},{5,7},{6,4},{7,5},{8,10},{9,11},{10,... | collective-permute-start | bytes 786440 | tf_op jit(solution)/shard_map/ppermute | solution.py:459
  137.9 35.1 %collective-permute-start.20 = (bf16[512,256]{1,0:T(8,128)(2,1)}, bf16[512,256]{1,0:T(8,128)(2,1)S(1)}, u32[]{:S(2)}, u32[]{:S(2)}) collective-permute-start(bf16[512,256]{1,0:T(8,128)(2,1)} %get-tuple-element.31), channel_id=1, source_target_pairs={{0,3},{1,0},{2,1},{3,2},{4,7},{5,4},{6,5},{7,6},{8,11},{9,8},{10,9... | collective-permute-start | bytes 786440 | tf_op jit(solution)/shard_map/ppermute | solution.py:459
  150.1 25.9 %collective-permute-start.12 = (bf16[512,256]{1,0:T(8,128)(2,1)}, bf16[512,256]{1,0:T(8,128)(2,1)S(1)}, u32[]{:S(2)}, u32[]{:S(2)}) collective-permute-start(bf16[512,256]{1,0:T(8,128)(2,1)} %get-tuple-element.22), channel_id=1, source_target_pairs={{0,1},{1,2},{2,3},{3,0},{4,5},{5,6},{6,7},{7,4},{8,9},{9,10},{10,1... | collective-permute-start | bytes 786440 | tf_op jit(solution)/shard_map/ppermute | solution.py:459
  150.3 31.4 %collective-permute-start.13 = (bf16[512,256]{1,0:T(8,128)(2,1)}, bf16[512,256]{1,0:T(8,128)(2,1)S(1)}, u32[]{:S(2)}, u32[]{:S(2)}) collective-permute-start(bf16[512,256]{1,0:T(8,128)(2,1)} %get-tuple-element.23), channel_id=1, source_target_pairs={{0,2},{1,3},{2,0},{3,1},{4,6},{5,7},{6,4},{7,5},{8,10},{9,11},{10,... | collective-permute-start | bytes 786440 | tf_op jit(solution)/shard_map/ppermute | solution.py:459
  154.3 30.0 %collective-permute-start.14 = (bf16[512,256]{1,0:T(8,128)(2,1)}, bf16[512,256]{1,0:T(8,128)(2,1)S(1)}, u32[]{:S(2)}, u32[]{:S(2)}) collective-permute-start(bf16[512,256]{1,0:T(8,128)(2,1)} %get-tuple-element.24), channel_id=1, source_target_pairs={{0,3},{1,0},{2,1},{3,2},{4,7},{5,4},{6,5},{7,6},{8,11},{9,8},{10,9... | collective-permute-start | bytes 786440 | tf_op jit(solution)/shard_map/ppermute | solution.py:459
  (19 other events, 226.6 us)
where the time goes:
time: 192 us; the launch traced here: 191 us
  waiting for transfers between devices  106 us (55%)
  Pallas kernels  43.1 us (22%)
  starting transfers between devices  29.1 us (15%)
  local copies, waits for them, and re-layouts  6.23 us (3%)
  other arithmetic  6.06 us (3%)
    ppermute x9, waiting for transfers between devices, xor_gather(): arrived.append(lax.ppermute(piece, axis, pairs))  58.2 us
    ppermute x6, waiting for transfers between devices, per_device(): terms.append(lax.ppermute(part, 'tensor', pairs))  30 us
    pallas_call x2, Pallas kernels, feed(): pl.pallas_call(functools.partial(feed_kernel, n_dp, n_tensor), grid=(step...  20.3 us
    ppermute x6, waiting for transfers between devices, per_device(): gated[c].append(lax.ppermute(gated[c][-1], 'tensor', ring))  17.4 us
    pallas_call x2, Pallas kernels, project(): pl.pallas_call(functools.partial(project_kernel, n_dp, heads_here, event_...  13 us
    ppermute x9, starting transfers between devices, xor_gather(): arrived.append(lax.ppermute(piece, axis, pairs))  8.55 us
    ppermute x6, starting transfers between devices, per_device(): terms.append(lax.ppermute(part, 'tensor', pairs))  7.04 us
    pallas_call x1, Pallas kernels, per_device(): pl.pallas_call(functools.partial(state_kernel, heads_here, event_count),...  5.35 us
  transfers between devices with their start and end apart: 23, of which 12 were waited for; matrix products, arithmetic and copies ran while one was open for 4% of the time, Pallas kernels for 20%

commit v1 on v0

v1 whole, which is shorter than its diff:
```python
import functools
import jax
import jax.numpy as jnp
from jax import lax
from jax.experimental import pallas as pl
from jax.experimental.pallas import tpu as pltpu
from jax.sharding import PartitionSpec as P

CHUNKS = 2
BLOCK_ROWS = 256


NT = (((1,), (1,)), ((), ()))


def dot_nt(a, b):
    return lax.dot_general(a, b, NT, preferred_element_type=jnp.float32)


def dot_nn(a, b):
    return jnp.dot(a, b, preferred_element_type=jnp.float32)


def rms_scale(values, gain_row):
    meansq = jnp.mean(values * values, axis=-1, keepdims=True)
    return (values * lax.rsqrt(meansq + 1e-05) * gain_row).astype(jnp.bfloat16)


def piece_copies(pieces, dest, sems, me, pick):
    copies = []
    rows = dest.shape[-2] // len(pieces)
    for k, piece in enumerate(pieces):
        start = pl.multiple_of(jnp.bitwise_xor(me, k) * rows, rows)
        copies.append(
            pltpu.make_async_copy(pick(piece), dest.at[..., pl.ds(start, rows), :], sems.at[k])
        )
    return copies


def project_kernel(n_dp, heads, event_count, block, base, *refs):
    ids_ref, rates_ref, tok_ref, gain_ref, past_hbm = refs[:5]
    pieces = refs[5 : 5 + n_dp]
    gated_ref, key_hbm, value_hbm = refs[5 + n_dp : 8 + n_dp]
    w_ref, past_ref, decay_ref, key_ref, value_ref, sems, own_sems = refs[8 + n_dp :]
    depth = w_ref.shape[1] // n_dp
    copies = []
    for m in range(4):
        span = pl.ds(m * depth, depth)
        copies += piece_copies(
            pieces, w_ref.at[m], sems.at[m], ids_ref[0], lambda piece: piece.at[span]
        )
    for copy in copies:
        copy.start()
    past_copy = pltpu.make_async_copy(
        past_hbm.at[pl.ds(base // event_count, past_ref.shape[0])], past_ref, own_sems.at[0]
    )
    past_copy.start()
    out_copies = [
        pltpu.make_async_copy(key_ref, key_hbm, own_sems.at[1]),
        pltpu.make_async_copy(value_ref, value_hbm, own_sems.at[2]),
    ]
    rows = gated_ref.shape[0]
    head_dim = past_ref.shape[3]
    sessions = block // event_count
    key_scale = head_dim ** (-0.5)
    at = lax.broadcasted_iota(jnp.int32, (block, block), 0)
    to = lax.broadcasted_iota(jnp.int32, (block, block), 1)
    allowed = (at // event_count == to // event_count) & (at >= to)
    distance = jnp.maximum(at - to, 0).astype(jnp.float32)
    place = lax.broadcasted_iota(jnp.int32, (block, head_dim), 0) % event_count
    since = (place + 1).astype(jnp.float32)
    factors = []
    for h in range(heads):
        rate = rates_ref[ids_ref[1] * heads + h]
        decay_ref[h] = jnp.where(allowed, jnp.exp(-rate * distance), 0.0) * key_scale
        factors.append(jnp.exp(-rate * since))
    spans = [slice(r, r + block) for r in range(0, rows, block)]
    normed = [
        rms_scale(
            tok_ref[base + span.start : base + span.stop].astype(jnp.float32), gain_ref[0:1, :]
        )
        for span in spans
    ]
    for copy in copies:
        copy.wait()
    past_copy.wait()
    for span, rows_in in zip(spans, normed):
        query = dot_nn(rows_in, w_ref[0]).astype(jnp.bfloat16)
        keys = dot_nn(rows_in, w_ref[1]).astype(jnp.bfloat16)
        key_ref[span] = keys
        values = dot_nn(rows_in, w_ref[2]).astype(jnp.bfloat16)
        value_ref[span] = values
        gate = dot_nn(rows_in, w_ref[3])
        first_session = span.start // event_count
        for h in range(heads):
            cols = slice(h * head_dim, (h + 1) * head_dim)
            qh, kh, vh = query[:, cols], keys[:, cols], values[:, cols]
            mix = (dot_nt(qh, kh) * decay_ref[h]).astype(jnp.bfloat16)
            intra = dot_nn(mix, vh)
            parts = []
            for s in range(sessions):
                parts.append(
                    dot_nn(
                        qh[s * event_count : (s + 1) * event_count],
                        past_ref[first_session + s, h].astype(jnp.bfloat16),
                    )
                )
            retained = intra + jnp.concatenate(parts, axis=0) * factors[h]
            centred = retained - jnp.mean(retained, axis=-1, keepdims=True)
            row_var = jnp.mean(centred * centred, axis=-1, keepdims=True)
            normalised = centred * lax.rsqrt(row_var + 1e-05)
            gated_ref[span, cols] = (jax.nn.silu(gate[:, cols]) * normalised).astype(jnp.bfloat16)
    for copy in out_copies:
        copy.start()
    for copy in out_copies:
        copy.wait()


def state_kernel(chunks, heads, event_count, *refs):
    ids_ref, rates_ref, pos_ref, past_hbm = refs[:4]
    sources = refs[4 : 4 + 2 * chunks]
    out_ref, buf_ref, past_ref, kv_ref, sems, past_sems, kv_sems = refs[4 + 2 * chunks :]
    kv_copies = [
        pltpu.make_async_copy(source, kv_ref.at[k], kv_sems.at[k])
        for k, source in enumerate(sources)
    ]
    for copy in kv_copies:
        copy.start()
    sessions, _, head_dim, _ = past_ref.shape
    groups = past_sems.shape[0]
    group = sessions // groups
    past_copies = [
        pltpu.make_async_copy(
            past_hbm.at[pl.ds(k * group, group)],
            past_ref.at[pl.ds(k * group, group)],
            past_sems.at[k],
        )
        for k in range(groups)
    ]
    for copy in past_copies:
        copy.start()
    rows = kv_ref.shape[1]
    key_scale = head_dim ** (-0.5)

    def copy_of(session):
        return pltpu.make_async_copy(
            buf_ref.at[session], out_ref.at[pos_ref[session]], sems.at[session]
        )

    place = lax.broadcasted_iota(jnp.int32, (rows, head_dim), 0) % event_count
    left = (event_count - 1 - place).astype(jnp.float32)
    factors, carries = [], []
    for h in range(heads):
        rate = rates_ref[ids_ref[1] * heads + h]
        factors.append(jnp.exp(-rate * left) * key_scale)
        carries.append(jnp.exp(jnp.full((head_dim, head_dim), -rate * event_count, jnp.float32)))
    for c in range(chunks):
        kv_copies[c].wait()
        kv_copies[chunks + c].wait()
        weighted = []
        for h in range(heads):
            cols = slice(h * head_dim, (h + 1) * head_dim)
            weighted.append(
                (kv_ref[c, :, cols].astype(jnp.float32) * factors[h]).astype(jnp.bfloat16)
            )
        for s in range(rows // event_count):
            session = c * (rows // event_count) + s
            if session % group == 0:
                past_copies[session // group].wait()
            span = slice(s * event_count, (s + 1) * event_count)
            for h in range(heads):
                cols = slice(h * head_dim, (h + 1) * head_dim)
                grown = lax.dot_general(
                    weighted[h][span],
                    kv_ref[chunks + c, span, cols],
                    (((0,), (0,)), ((), ())),
                    preferred_element_type=jnp.float32,
                )
                buf_ref[session, h] = (carries[h] * past_ref[session, h] + grown).astype(
                    jnp.bfloat16
                )

            @pl.when(pos_ref[session] >= 0)
            def _():
                copy_of(session).start()

    for session in range(sessions):

        @pl.when(pos_ref[session] >= 0)
        def _():
            copy_of(session).wait()


def unpack_kernel(src_ref, recv_ref, out_ref, buf_ref, sems):
    per_step = out_ref.shape[0]
    step = pl.program_id(0)

    def copy_of(slot):
        return pltpu.make_async_copy(
            recv_ref.at[jnp.maximum(src_ref[slot], 0)], buf_ref.at[slot], sems.at[slot]
        )

    @pl.when(step == 0)
    def _():
        for slot in range(buf_ref.shape[0]):

            @pl.when(src_ref[slot] >= 0)
            def _():
                copy_of(slot).start()

    for i in range(per_step):
        slot = step * per_step + i

        @pl.when(src_ref[slot] >= 0)
        def _():
            copy_of(slot).wait()
            out_ref[i] = buf_ref[slot].astype(jnp.float32)

        @pl.when(src_ref[slot] < 0)
        def _():
            out_ref[i] = jnp.zeros(out_ref.shape[1:], jnp.float32)


def feed_kernel(n_dp, n_tensor, block, base, *refs):
    ids_ref, tok_ref, gain_ref = refs[:3]
    gated = refs[3 : 3 + n_tensor]
    at = 3 + n_tensor
    out_pieces = refs[at : at + n_dp]
    ffn_pieces = refs[at + n_dp : at + 2 * n_dp]
    at += 2 * n_dp
    own_ref = refs[at]
    part_refs = refs[at + 1 : at + n_tensor]
    wo_ref, up_ref, down_ref, res_ref, sems = refs[at + n_tensor :]
    me = ids_ref[0]
    out_copies = piece_copies(out_pieces, wo_ref, sems.at[0], me, lambda piece: piece)
    up_copies = piece_copies(ffn_pieces, up_ref, sems.at[1], me, lambda piece: piece.at[0])
    down_copies = piece_copies(ffn_pieces, down_ref, sems.at[2], me, lambda piece: piece.at[1])
    for copy in out_copies + up_copies + down_copies:
        copy.start()
    for copy in out_copies:
        copy.wait()
    rows, width = own_ref.shape
    for r in range(0, rows, block):
        span = slice(r, r + block)
        attended = dot_nt(gated[0][span], wo_ref[ids_ref[2]])
        for k in range(1, n_tensor):
            attended += dot_nt(gated[k][span], wo_ref[ids_ref[2 + k]])
        residual = tok_ref[base + r : base + r + block].astype(jnp.float32) + attended
        res_ref[span] = residual
        hidden = rms_scale(residual, gain_ref[1:2, :])
        if r == 0:
            for copy in up_copies:
                copy.wait()
        activated = jax.nn.gelu(dot_nn(hidden, up_ref[...]), approximate=True)
        activated = activated.astype(jnp.bfloat16)
        if r == 0:
            for copy in down_copies:
                copy.wait()

        def term(k):
            start = pl.multiple_of(ids_ref[2 + k] * width, width)
            return dot_nt(activated, down_ref[pl.ds(start, width), :])

        for k in range(1, n_tensor):
            part_refs[k - 1][span] = term(k).astype(jnp.bfloat16)
        mine = pl.ds(pl.multiple_of(ids_ref[1] * width, width), width)
        own_ref[span] = res_ref[span, mine] + term(0)


def add_kernel(a_ref, b_ref, out_ref):
    total = a_ref[...].astype(jnp.float32) + b_ref[...].astype(jnp.float32)
    out_ref[...] = total.astype(jnp.bfloat16)


def last_kernel(chunks, event_count, *refs):
    lengths_ref = refs[0]
    owns = refs[1 : 1 + chunks]
    terms = refs[1 + chunks : 1 + 2 * chunks]
    out_ref = refs[-1]
    rows, width = owns[0].shape
    place = lax.broadcasted_iota(jnp.int32, (event_count, width), 0)
    for c in range(chunks):
        for s in range(rows // event_count):
            span = slice(s * event_count, (s + 1) * event_count)
            total = owns[c][span] + terms[c][span].astype(jnp.float32)
            session = c * (rows // event_count) + s
            keep = place < lengths_ref[session]
            out_ref[session * event_count : (session + 1) * event_count] = jnp.where(
                keep, total, 0.0
            ).astype(jnp.bfloat16)


def xor_gather(value, axis):
    pieces = [value]
    size = lax.axis_size(axis)
    bit = size // 2
    order = [0]
    while bit:
        pairs = [(i, i ^ bit) for i in range(size)]
        arrived = []
        for piece in pieces:
            arrived.append(lax.ppermute(piece, axis, pairs))
        pieces = pieces + arrived
        order = order + [k ^ bit for k in order]
        bit //= 2
    return [pieces[order.index(k)] for k in range(size)]


def ring_order(size):
    return list(range(0, size, 2)) + list(range(1, size, 2))[::-1]


def ring_pairs(size):
    order = ring_order(size)
    return [(order[i], order[(i + 1) % size]) for i in range(size)]


def ring_sources(size):
    order = ring_order(size)
    return [[order[(order.index(at) - k) % size] for k in range(size)] for at in range(size)]


def any_spec():
    return pl.BlockSpec(memory_space=pl.ANY)


def smem_spec():
    return pl.BlockSpec(memory_space=pltpu.SMEM)


def hbm_spec():
    return pl.BlockSpec(memory_space=pltpu.HBM)


def in_hbm(arrays):
    return [pltpu.with_memory_space_constraint(array, pltpu.HBM) for array in arrays]


def vmem_spec():
    return pl.BlockSpec(memory_space=pltpu.VMEM)


def kernel_call(kernel, in_specs, out_specs, out_shape, scratch, flops, limit_mib=24):
    return pl.pallas_call(
        kernel,
        in_specs=in_specs,
        out_specs=out_specs,
        out_shape=out_shape,
        scratch_shapes=scratch,
        compiler_params=pltpu.CompilerParams(vmem_limit_bytes=limit_mib * 1024 * 1024),
        cost_estimate=pl.CostEstimate(
            flops=flops, bytes_accessed=4 * 1024 * 1024, transcendentals=0
        ),
    )


def per_device(
    tokens, past_states, attn_weights, ffn_weights, norm_gains, head_rates, end_lengths, new_slot
):
    sessions_here = end_lengths.shape[0]
    row_count, width = tokens.shape
    event_count = row_count // sessions_here
    heads_here, head_dim = past_states.shape[1], past_states.shape[3]
    cols_here = heads_here * head_dim
    units_here = ffn_weights.shape[2]
    n_dp, n_tensor = lax.axis_size("dp"), lax.axis_size("tensor")
    dp_at, tensor_at = lax.axis_index("dp"), lax.axis_index("tensor")
    share = width // n_tensor
    pair_cap = max(2, 2 * sessions_here // n_dp)
    slot_count = n_dp * pair_cap
    chunk_rows = row_count // CHUNKS
    block = min(BLOCK_ROWS, chunk_rows)
    ring = ring_pairs(n_tensor)
    bf16, f32 = jnp.bfloat16, jnp.float32
    shape_of = jax.ShapeDtypeStruct

    survive = end_lengths > event_count
    target_dev = new_slot // sessions_here
    session_ids = jnp.arange(sessions_here, dtype=jnp.int32)
    proj_rows = attn_weights.shape[1]
    notes = jnp.stack([jnp.where(survive, target_dev, -1), new_slot % sessions_here])
    notes = jnp.pad(notes.astype(bf16), ((0, 6), (0, cols_here - sessions_here)))
    proj_own = jnp.concatenate([attn_weights[:4].reshape(4 * proj_rows, cols_here), notes])
    proj_pieces = xor_gather(proj_own, "dp")
    out_own = lax.all_to_all(
        jnp.broadcast_to(attn_weights[4:], (n_tensor, proj_rows, cols_here)),
        "tensor",
        split_axis=0,
        concat_axis=0,
        tiled=True,
    )
    sources = jnp.array(ring_sources(n_tensor), jnp.int32)[tensor_at]
    ids = jnp.concatenate([jnp.stack([dp_at, tensor_at]).astype(jnp.int32), sources])

    meta = jnp.stack([piece[4 * proj_rows :, :sessions_here] for piece in proj_pieces])
    meta = meta.astype(jnp.int32)
    from_dev = jnp.bitwise_xor(dp_at, jnp.arange(n_dp, dtype=jnp.int32))
    earlier = (
        (target_dev[None, :] == target_dev[:, None])
        & survive[None, :]
        & (session_ids[None, :] < session_ids[:, None])
    )
    pair_rank = jnp.sum(earlier.astype(jnp.int32), axis=1)
    send_pos = jnp.where(survive, target_dev * pair_cap + pair_rank, -1)
    coming = meta[:, 0] == dp_at
    ahead = coming[:, None, :] & (session_ids[None, None, :] < session_ids[None, :, None])
    rank_all = jnp.sum(ahead.astype(jnp.int32), axis=2)
    from_pos = from_dev[:, None] * pair_cap + rank_all + 1
    lands = meta[:, 1][None] == session_ids[:, None, None]
    recv_src = jnp.sum(jnp.where(lands & coming[None], from_pos[None], 0), axis=(1, 2)) - 1
    send_pos, recv_src = lax.optimization_barrier((send_pos, recv_src))

    rows_shape = shape_of((chunk_rows, cols_here), bf16)
    decay_shape = pltpu.VMEM((heads_here, block, block), f32)
    chunk_sessions = chunk_rows // event_count
    gated, keys, values = [], [], []
    for c in range(CHUNKS):
        g, k, v = kernel_call(
            functools.partial(project_kernel, n_dp, heads_here, event_count, block, c * chunk_rows),
            [smem_spec()] * 2 + [vmem_spec()] * 2 + [hbm_spec()] + [any_spec()] * n_dp,
            [vmem_spec()] + [hbm_spec()] * 2,
            [rows_shape] + [pltpu.HBM((chunk_rows, cols_here), bf16)] * 2,
            [
                pltpu.VMEM((4, width, cols_here), bf16),
                pltpu.VMEM((chunk_sessions, heads_here, head_dim, head_dim), f32),
                decay_shape,
                pltpu.VMEM((chunk_rows, cols_here), bf16),
                pltpu.VMEM((chunk_rows, cols_here), bf16),
                pltpu.SemaphoreType.DMA((4, n_dp)),
                pltpu.SemaphoreType.DMA((3,)),
            ],
            2 * chunk_rows * width * cols_here * 4,
        )(ids, head_rates, tokens, norm_gains, *in_hbm([past_states]), *proj_pieces)
        gated.append([g])
        keys.append(k)
        values.append(v)
    for _ in range(n_tensor - 1):
        for c in range(CHUNKS):
            gated[c].append(lax.ppermute(gated[c][-1], "tensor", ring))

    out_pieces = xor_gather(out_own, "dp")
    ffn_pieces = xor_gather(ffn_weights, "dp")
    packed = kernel_call(
        functools.partial(state_kernel, CHUNKS, heads_here, event_count),
        [smem_spec()] * 3 + [hbm_spec()] * (1 + 2 * CHUNKS),
        hbm_spec(),
        pltpu.HBM((slot_count, heads_here, head_dim, head_dim), bf16),
        [
            pltpu.VMEM((sessions_here, heads_here, head_dim, head_dim), bf16),
            pltpu.VMEM((sessions_here, heads_here, head_dim, head_dim), f32),
            pltpu.VMEM((2 * CHUNKS, chunk_rows, cols_here), bf16),
            pltpu.SemaphoreType.DMA((sessions_here,)),
            pltpu.SemaphoreType.DMA((4,)),
            pltpu.SemaphoreType.DMA((2 * CHUNKS,)),
        ],
        2 * row_count * head_dim * cols_here,
    )(ids, head_rates, send_pos, *in_hbm([past_states, *keys, *values]))
    received = lax.all_to_all(packed, "dp", split_axis=0, concat_axis=0, tiled=True)

    owns, parts, sums = [], [], []
    for c in range(CHUNKS):
        own, *part = kernel_call(
            functools.partial(feed_kernel, n_dp, n_tensor, block, c * chunk_rows),
            [smem_spec()] + [vmem_spec()] * (2 + n_tensor) + [hbm_spec()] * (2 * n_dp),
            [vmem_spec()] * n_tensor,
            [shape_of((chunk_rows, share), f32)]
            + [shape_of((chunk_rows, share), bf16)] * (n_tensor - 1),
            [
                pltpu.VMEM((n_tensor, width, cols_here), bf16),
                pltpu.VMEM((width, units_here), bf16),
                pltpu.VMEM((width, units_here), bf16),
                pltpu.VMEM((chunk_rows, width), f32),
                pltpu.SemaphoreType.DMA((3, n_dp)),
            ],
            2 * chunk_rows * width * (width + 2 * units_here),
        )(ids, tokens, norm_gains, *gated[c], *in_hbm(out_pieces + ffn_pieces))
        owns.append(own)
        parts.append(part)
        sums.append(None)
    for hop in range(n_tensor - 1):
        for c in range(CHUNKS):
            mine = parts[c][hop]
            if hop:
                mine = kernel_call(
                    add_kernel,
                    [vmem_spec()] * 2,
                    vmem_spec(),
                    shape_of((chunk_rows, share), bf16),
                    [],
                    0,
                    limit_mib=4,
                )(sums[c], mine)
            sums[c] = lax.ppermute(mine, "tensor", ring)

    next_tokens = kernel_call(
        functools.partial(last_kernel, CHUNKS, event_count),
        [smem_spec()] + [vmem_spec()] * (2 * CHUNKS),
        vmem_spec(),
        shape_of((row_count, share), bf16),
        [],
        0,
        limit_mib=8,
    )(end_lengths, *owns, *sums)

    per_step = min(8, sessions_here)
    moved_states = pl.pallas_call(
        unpack_kernel,
        grid=(sessions_here // per_step,),
        in_specs=[smem_spec(), any_spec()],
        out_specs=pl.BlockSpec((per_step, heads_here, head_dim, head_dim), lambda i: (i, 0, 0, 0)),
        out_shape=shape_of(past_states.shape, f32),
        scratch_shapes=[
            pltpu.VMEM((sessions_here, heads_here, head_dim, head_dim), bf16),
            pltpu.SemaphoreType.DMA((sessions_here,)),
        ],
        compiler_params=pltpu.CompilerParams(vmem_limit_bytes=16 * 1024 * 1024),
        cost_estimate=pl.CostEstimate(
            flops=0, bytes_accessed=past_states.size * 6, transcendentals=0
        ),
        name="unpack",
    )(recv_src, received)
    return (next_tokens, moved_states)


def solution(mesh):
    placed = (
        P(("group", "dp"), None),
        P(("group", "dp"), "tensor", None, None),
        P(None, "dp", "tensor"),
        P(None, "dp", "tensor"),
        P(),
        P(),
        P(("group", "dp")),
        P(("group", "dp")),
    )

    return jax.shard_map(
        per_device,
        mesh=mesh,
        in_specs=placed,
        out_specs=(P(("group", "dp"), "tensor"), P(("group", "dp"), "tensor", None, None)),
        check_vma=False,
    )
```

time: 192 us -> 181 us (0.943)
  the two profiles are of different devices: /device:TPU:9 before, /device:TPU:0 now
where the time goes in v1:
time: 181 us; the launch traced here: 180 us
  waiting for transfers between devices  89.2 us (49%)
  starting transfers between devices  42.7 us (24%)
  Pallas kernels  37.7 us (21%)
  local copies, waits for them, and re-layouts  6.68 us (4%)
  other arithmetic  2.7 us (1%)
    ppermute x9, waiting for transfers between devices, xor_gather(): arrived.append(lax.ppermute(piece, axis, pairs))  57.2 us
    ppermute x6, waiting for transfers between devices, per_device(): sums[c] = lax.ppermute(mine, 'tensor', ring)  22.4 us
    ppermute x6, starting transfers between devices, per_device(): gated[c].append(lax.ppermute(gated[c][-1], 'tensor', ring))  16.5 us
    pallas_call x2, Pallas kernels, per_device(): kernel_call(functools.partial(feed_kernel, n_dp, n_tensor, block, c * chu...  13.5 us
    pallas_call x2, Pallas kernels, per_device(): kernel_call(functools.partial(project_kernel, n_dp, heads_here, event_cou...  13.4 us
    ppermute x6, starting transfers between devices, per_device(): sums[c] = lax.ppermute(mine, 'tensor', ring)  10.3 us
    ppermute x6, waiting for transfers between devices, per_device(): gated[c].append(lax.ppermute(gated[c][-1], 'tensor', ring))  9.57 us
    ppermute x9, starting transfers between devices, xor_gather(): arrived.append(lax.ppermute(piece, axis, pairs))  6 us
  transfers between devices with their start and end apart: 23, of which 11 were waited for; matrix products, arithmetic and copies ran while one was open for 3% of the time, Pallas kernels for 19%

profile of v1, /device:TPU:0, one launch (start us, length us, event | category | flops | bytes accessed | tf_op | source)
XLA Modules:
  0.0 180.0 jit_solution(17969826617079497450)
XLA Ops:
  2.6 3.0 %collective-permute-start.1 = (bf16[1032,256]{1,0:T(8,128)(2,1)S(1)}, bf16[1032,256]{1,0:T(8,128)(2,1)S(1)}, u32[]{:S(2)}, u32[]{:S(2)}) collective-permute-start(bf16[1032,256]{1,0:T(8,128)(2,1)S(1)} %pad_maximum_fusion.refs_5_), channel_id=1, source_target_pairs={{0,8},{4,12},{8,0},{12,4},{1,9},{5,13},{9,1},{13,5},{2,10},{6,14},... | collective-permute-start | bytes 1585160 | tf_op jit(solution)/shard_map/ppermute | solution.py:302
  7.4 4.9 %all-to-all-start = ((bf16[4,256,256]{2,1,0:T(8,128)(2,1)}), bf16[4,256,256]{2,1,0:T(8,128)(2,1)}, u32[]{:S(2)}, u32[]{:S(2)}) async-start(bf16[4,256,256]{2,1,0:T(8,128)(2,1)} %broadcast_in_dim.16), calls=%async_computation | async-start | bytes 1048576 | tf_op jit(solution)/shard_map/all_to_all | solution.py:385
  14.4 4.2 %collective-permute-done.1.refs_7_ = bf16[1032,256]{1,0:T(8,128)(2,1)S(1)} collective-permute-done((bf16[1032,256]{1,0:T(8,128)(2,1)S(1)}, bf16[1032,256]{1,0:T(8,128)(2,1)S(1)}, u32[]{:S(2)}, u32[]{:S(2)}) %collective-permute-start.1) | collective-permute-done | bytes 528416 | tf_op jit(solution)/shard_map/ppermute | solution.py:302
  22.8 6.7 %shard_map.106 = (bf16[512,256]{1,0:T(8,128)(2,1)S(1)}, bf16[512,256]{1,0:T(8,128)(2,1)}, bf16[512,256]{1,0:T(8,128)(2,1)}) custom-call(s32[6]{0:T(128)S(1)} %pad_add_fusion.refs_0_, f32[8]{0:T(128)S(1)} %copy-done.3, bf16[1024,1024]{1,0:T(8,128)(2,1)S(1)} %copy-done, f32[2,1024]{1,0:T(2,128)S(1)} %copy-done.1, f32[32,2,128,128]{3,2,1,0:T(8,128)} %refs_3_.5, ...), custom_call_target="tpu_custom_call" | custom-call | flops 1073741824 | bytes 4194304 | tf_op jit(solution)/shard_map/pallas_call | solution.py:418
  29.6 6.7 %shard_map.104 = (bf16[512,256]{1,0:T(8,128)(2,1)S(1)}, bf16[512,256]{1,0:T(8,128)(2,1)}, bf16[512,256]{1,0:T(8,128)(2,1)}) custom-call(s32[6]{0:T(128)S(1)} %pad_add_fusion.refs_0_, f32[8]{0:T(128)S(1)} %copy-done.3, bf16[1024,1024]{1,0:T(8,128)(2,1)S(1)} %copy-done, f32[2,1024]{1,0:T(2,128)S(1)} %copy-done.1, f32[32,2,128,128]{3,2,1,0:T(8,128)} %refs_3_.5, ...), custom_call_target="tpu_custom_call" | custom-call | flops 1073741824 | bytes 4194304 | tf_op jit(solution)/shard_map/pallas_call | solution.py:418
  36.3 4.7 %shard_map.113 = bf16[64,2,128,128]{3,2,1,0:T(8,128)(2,1)} custom-call(s32[6]{0:T(128)S(1)} %pad_add_fusion.refs_0_, f32[8]{0:T(128)S(1)} %copy-done.3, s32[32]{0:T(128)S(1)} %get-tuple-element.29.refs_2_, f32[32,2,128,128]{3,2,1,0:T(8,128)} %refs_3_.5, bf16[512,256]{1,0:T(8,128)(2,1)} %get-tuple-element.30.refs_4_, ...), custom_call_target="tpu_custom_call" | custom-call | flops 67108864 | bytes 4194304 | tf_op jit(solution)/shard_map/pallas_call | solution.py:443
  41.1 5.0 %all-to-all-start.1 = ((bf16[64,2,128,128]{3,2,1,0:T(8,128)(2,1)}), bf16[64,2,128,128]{3,2,1,0:T(8,128)(2,1)}, u32[]{:S(2)}, u32[]{:S(2)}) async-start(bf16[64,2,128,128]{3,2,1,0:T(8,128)(2,1)} %shard_map.113), calls=%async_computation.1 | async-start | bytes 8388608 | tf_op jit(solution)/shard_map/all_to_all | solution.py:458
  48.4 3.0 %collective-permute-start.12 = (bf16[512,256]{1,0:T(8,128)(2,1)S(1)}, bf16[512,256]{1,0:T(8,128)(2,1)S(1)}, u32[]{:S(2)}, u32[]{:S(2)}) collective-permute-start(bf16[512,256]{1,0:T(8,128)(2,1)S(1)} %copy-done.6), channel_id=1, source_target_pairs={{0,2},{2,3},{3,1},{1,0},{4,6},{6,7},{7,5},{5,4},{8,10},{10,11},{11... | collective-permute-start | bytes 786440 | tf_op jit(solution)/shard_map/ppermute | solution.py:439
  53.5 51.9 %collective-permute-done.7.refs_9_ = bf16[4,256,256]{2,1,0:T(8,128)(2,1)S(1)} collective-permute-done((bf16[4,256,256]{2,1,0:T(8,128)(2,1)}, bf16[4,256,256]{2,1,0:T(8,128)(2,1)S(1)}, u32[]{:S(2)}, u32[]{:S(2)}) %collective-permute-start.7) | collective-permute-done | bytes 524320 | tf_op jit(solution)/shard_map/ppermute | solution.py:302
  105.4 3.1 %collective-permute-start.13 = (bf16[512,256]{1,0:T(8,128)(2,1)S(1)}, bf16[512,256]{1,0:T(8,128)(2,1)S(1)}, u32[]{:S(2)}, u32[]{:S(2)}) collective-permute-start(bf16[512,256]{1,0:T(8,128)(2,1)S(1)} %collective-permute-done.12.refs_4_), channel_id=1, source_target_pairs={{0,2},{2,3},{3,1},{1,0},{4,6},{6,7},{7,5},{5,4},{8,10},{10,11},{11... | collective-permute-start | bytes 786440 | tf_op jit(solution)/shard_map/ppermute | solution.py:439
  110.2 5.1 %collective-permute-done.13.refs_5_ = bf16[512,256]{1,0:T(8,128)(2,1)S(1)} collective-permute-done((bf16[512,256]{1,0:T(8,128)(2,1)S(1)}, bf16[512,256]{1,0:T(8,128)(2,1)S(1)}, u32[]{:S(2)}, u32[]{:S(2)}) %collective-permute-start.13) | collective-permute-done | bytes 262176 | tf_op jit(solution)/shard_map/ppermute | solution.py:439
  115.3 3.4 %collective-permute-start.14 = (bf16[512,256]{1,0:T(8,128)(2,1)S(1)}, bf16[512,256]{1,0:T(8,128)(2,1)S(1)}, u32[]{:S(2)}, u32[]{:S(2)}) collective-permute-start(bf16[512,256]{1,0:T(8,128)(2,1)S(1)} %collective-permute-done.13.refs_5_), channel_id=1, source_target_pairs={{0,2},{2,3},{3,1},{1,0},{4,6},{6,7},{7,5},{5,4},{8,10},{10,11},{11... | collective-permute-start | bytes 786440 | tf_op jit(solution)/shard_map/ppermute | solution.py:439
  118.7 2.2 %collective-permute-done.4.refs_5_ = bf16[512,256]{1,0:T(8,128)(2,1)S(1)} collective-permute-done((bf16[512,256]{1,0:T(8,128)(2,1)S(1)}, bf16[512,256]{1,0:T(8,128)(2,1)S(1)}, u32[]{:S(2)}, u32[]{:S(2)}) %collective-permute-start.4) | collective-permute-done | bytes 262176 | tf_op jit(solution)/shard_map/ppermute | solution.py:439
  120.9 3.4 %collective-permute-start.5 = (bf16[512,256]{1,0:T(8,128)(2,1)S(1)}, bf16[512,256]{1,0:T(8,128)(2,1)S(1)}, u32[]{:S(2)}, u32[]{:S(2)}) collective-permute-start(bf16[512,256]{1,0:T(8,128)(2,1)S(1)} %collective-permute-done.4.refs_5_), channel_id=1, source_target_pairs={{0,2},{2,3},{3,1},{1,0},{4,6},{6,7},{7,5},{5,4},{8,10},{10,11},{11... | collective-permute-start | bytes 786440 | tf_op jit(solution)/shard_map/ppermute | solution.py:439
  124.3 2.2 %collective-permute-done.14.refs_6_ = bf16[512,256]{1,0:T(8,128)(2,1)S(1)} collective-permute-done((bf16[512,256]{1,0:T(8,128)(2,1)S(1)}, bf16[512,256]{1,0:T(8,128)(2,1)S(1)}, u32[]{:S(2)}, u32[]{:S(2)}) %collective-permute-start.14) | collective-permute-done | bytes 262176 | tf_op jit(solution)/shard_map/ppermute | solution.py:439
  127.5 6.8 %shard_map.107 = (f32[512,256]{1,0:T(8,128)S(1)}, bf16[512,256]{1,0:T(8,128)(2,1)S(1)}, bf16[512,256]{1,0:T(8,128)(2,1)S(1)}, bf16[512,256]{1,0:T(8,128)(2,1)S(1)}) custom-call(s32[6]{0:T(128)S(1)} %pad_add_fusion.refs_0_, bf16[1024,1024]{1,0:T(8,128)(2,1)S(1)} %copy-done, f32[2,1024]{1,0:T(2,128)S(1)} %copy-done.2, bf16[512,256]{1,0:T(8,128)(2,1)S(1)} %copy-done.6, ...), custom_call_target="tpu_custom_call" | custom-call | flops 3221225472 | bytes 4194304 | tf_op jit(solution)/shard_map/pallas_call | solution.py:462
  134.3 3.4 %collective-permute-start.18 = (bf16[512,256]{1,0:T(8,128)(2,1)S(1)}, bf16[512,256]{1,0:T(8,128)(2,1)S(1)}, u32[]{:S(2)}, u32[]{:S(2)}) collective-permute-start(bf16[512,256]{1,0:T(8,128)(2,1)S(1)} %get-tuple-element.25), channel_id=1, source_target_pairs={{0,2},{2,3},{3,1},{1,0},{4,6},{6,7},{7,5},{5,4},{8,10},{10,11},{11... | collective-permute-start | bytes 786440 | tf_op jit(solution)/shard_map/ppermute | solution.py:493
  137.7 6.8 %shard_map.105 = (f32[512,256]{1,0:T(8,128)S(1)}, bf16[512,256]{1,0:T(8,128)(2,1)S(1)}, bf16[512,256]{1,0:T(8,128)(2,1)S(1)}, bf16[512,256]{1,0:T(8,128)(2,1)S(1)}) custom-call(s32[6]{0:T(128)S(1)} %pad_add_fusion.refs_0_, bf16[1024,1024]{1,0:T(8,128)(2,1)S(1)} %copy-done, f32[2,1024]{1,0:T(2,128)S(1)} %copy-done.2, ...), custom_call_target="tpu_custom_call" | custom-call | flops 3221225472 | bytes 4194304 | tf_op jit(solution)/shard_map/pallas_call | solution.py:462
  146.6 7.1 %collective-permute-done.15.a_ref = bf16[512,256]{1,0:T(8,128)(2,1)S(1)} collective-permute-done((bf16[512,256]{1,0:T(8,128)(2,1)S(1)}, bf16[512,256]{1,0:T(8,128)(2,1)S(1)}, u32[]{:S(2)}, u32[]{:S(2)}) %collective-permute-start.15) | collective-permute-done | bytes 262176 | tf_op jit(solution)/shard_map/ppermute | solution.py:493
  155.4 3.9 %collective-permute-done.19.a_ref = bf16[512,256]{1,0:T(8,128)(2,1)S(1)} collective-permute-done((bf16[512,256]{1,0:T(8,128)(2,1)S(1)}, bf16[512,256]{1,0:T(8,128)(2,1)S(1)}, u32[]{:S(2)}, u32[]{:S(2)}) %collective-permute-start.19) | collective-permute-done | bytes 262176 | tf_op jit(solution)/shard_map/ppermute | solution.py:493
  161.0 3.9 %collective-permute-done.16.a_ref = bf16[512,256]{1,0:T(8,128)(2,1)S(1)} collective-permute-done((bf16[512,256]{1,0:T(8,128)(2,1)S(1)}, bf16[512,256]{1,0:T(8,128)(2,1)S(1)}, u32[]{:S(2)}, u32[]{:S(2)}) %collective-permute-start.16) | collective-permute-done | bytes 262176 | tf_op jit(solution)/shard_map/ppermute | solution.py:493
  166.6 3.9 %collective-permute-done.20.refs_4_ = bf16[512,256]{1,0:T(8,128)(2,1)S(1)} collective-permute-done((bf16[512,256]{1,0:T(8,128)(2,1)S(1)}, bf16[512,256]{1,0:T(8,128)(2,1)S(1)}, u32[]{:S(2)}, u32[]{:S(2)}) %collective-permute-start.20) | collective-permute-done | bytes 262176 | tf_op jit(solution)/shard_map/ppermute | solution.py:493
  170.6 3.5 %collective-permute-done.17.refs_3_ = bf16[512,256]{1,0:T(8,128)(2,1)S(1)} collective-permute-done((bf16[512,256]{1,0:T(8,128)(2,1)S(1)}, bf16[512,256]{1,0:T(8,128)(2,1)S(1)}, u32[]{:S(2)}, u32[]{:S(2)}) %collective-permute-start.17) | collective-permute-done | bytes 262176 | tf_op jit(solution)/shard_map/ppermute | solution.py:493
  175.5 4.3 %unpack.1 = f32[32,2,128,128]{3,2,1,0:T(8,128)} custom-call(s32[32]{0:T(128)S(1)} %get-tuple-element.28.src_ref, bf16[64,2,128,128]{3,2,1,0:T(8,128)(2,1)} %all-to-all-done.1.recv_ref), custom_call_target="tpu_custom_call" | custom-call | bytes 6291456 | tf_op jit(solution)/shard_map/unpack/pallas_call | solution.py:506
  (80 shorter events, 25.7 us)
Async XLA Ops:
  2.6 15.9 %collective-permute-start.1 = (bf16[1032,256]{1,0:T(8,128)(2,1)S(1)}, bf16[1032,256]{1,0:T(8,128)(2,1)S(1)}, u32[]{:S(2)}, u32[]{:S(2)}) collective-permute-start(bf16[1032,256]{1,0:T(8,128)(2,1)S(1)} %pad_maximum_fusion.refs_5_), channel_id=1, source_target_pairs={{0,8},{4,12},{8,0},{12,4},{1,9},{5,13},{9,1},{13,5},{2,10},{6,14},... | collective-permute-start | bytes 1585160 | tf_op jit(solution)/shard_map/ppermute | solution.py:302
  5.7 12.9 %collective-permute-start = (bf16[1032,256]{1,0:T(8,128)(2,1)S(1)}, bf16[1032,256]{1,0:T(8,128)(2,1)}, u32[]{:S(2)}, u32[]{:S(2)}) collective-permute-start(bf16[1032,256]{1,0:T(8,128)(2,1)S(1)} %pad_maximum_fusion.refs_5_), channel_id=1, source_target_pairs={{0,4},{4,0},{8,12},{12,8},{1,5},{5,1},{9,13},{13,9},{2,6},{6,2},{1... | collective-permute-start | bytes 1585160 | tf_op jit(solution)/shard_map/ppermute | solution.py:302
  7.4 33.7 %all-to-all-start = ((bf16[4,256,256]{2,1,0:T(8,128)(2,1)}), bf16[4,256,256]{2,1,0:T(8,128)(2,1)}, u32[]{:S(2)}, u32[]{:S(2)}) async-start(bf16[4,256,256]{2,1,0:T(8,128)(2,1)} %broadcast_in_dim.16), calls=%async_computation | async-start | bytes 1048576 | tf_op jit(solution)/shard_map/all_to_all | solution.py:385
  12.3 36.0 %collective-permute-start.10 = (bf16[2,256,1024]{2,1,0:T(8,128)(2,1)}, bf16[2,256,1024]{2,1,0:T(8,128)(2,1)}, u32[]{:S(2)}, u32[]{:S(2)}) collective-permute-start(bf16[2,256,1024]{2,1,0:T(8,128)(2,1)} %refs_11_.3), channel_id=1, source_target_pairs={{0,8},{4,12},{8,0},{12,4},{1,9},{5,13},{9,1},{13,5},{2,10},{6,14},... | collective-permute-start | bytes 3145736 | tf_op jit(solution)/shard_map/ppermute | solution.py:302
  18.5 1.9 %collective-permute-start.2 = (bf16[1032,256]{1,0:T(8,128)(2,1)S(1)}, bf16[1032,256]{1,0:T(8,128)(2,1)S(1)}, u32[]{:S(2)}, u32[]{:S(2)}) collective-permute-start(bf16[1032,256]{1,0:T(8,128)(2,1)S(1)} %collective-permute-done.1.refs_7_), channel_id=1, source_target_pairs={{0,4},{4,0},{8,12},{12,8},{1,5},{5,1},{9,13},{13,9},{2,6},{6,2},{1... | collective-permute-start | bytes 1585160 | tf_op jit(solution)/shard_map/ppermute | solution.py:302
  41.0 86.5 %copy-start.2 = (f32[2,1024]{1,0:T(2,128)S(1)}, f32[2,1024]{1,0:T(2,128)}, u32[]{:S(2)}) copy-start(f32[2,1024]{1,0:T(2,128)} %refs_2_.7) | copy-start | bytes 24580
  41.1 134.4 %all-to-all-start.1 = ((bf16[64,2,128,128]{3,2,1,0:T(8,128)(2,1)}), bf16[64,2,128,128]{3,2,1,0:T(8,128)(2,1)}, u32[]{:S(2)}, u32[]{:S(2)}) async-start(bf16[64,2,128,128]{3,2,1,0:T(8,128)(2,1)} %shard_map.113), calls=%async_computation.1 | async-start | bytes 8388608 | tf_op jit(solution)/shard_map/all_to_all | solution.py:458
  46.1 5.5 %collective-permute-start.9 = (bf16[2,256,1024]{2,1,0:T(8,128)(2,1)}, bf16[2,256,1024]{2,1,0:T(8,128)(2,1)S(1)}, u32[]{:S(2)}, u32[]{:S(2)}) collective-permute-start(bf16[2,256,1024]{2,1,0:T(8,128)(2,1)} %refs_11_.3), channel_id=1, source_target_pairs={{0,4},{4,0},{8,12},{12,8},{1,5},{5,1},{9,13},{13,9},{2,6},{6,2},{1... | collective-permute-start | bytes 3145736 | tf_op jit(solution)/shard_map/ppermute | solution.py:302
  46.5 58.9 %collective-permute-start.7 = (bf16[4,256,256]{2,1,0:T(8,128)(2,1)}, bf16[4,256,256]{2,1,0:T(8,128)(2,1)S(1)}, u32[]{:S(2)}, u32[]{:S(2)}) collective-permute-start(bf16[4,256,256]{2,1,0:T(8,128)(2,1)} %all-to-all-done.refs_7_), channel_id=1, source_target_pairs={{0,8},{4,12},{8,0},{12,4},{1,9},{5,13},{9,1},{13,5},{2,10},{6,14},... | collective-permute-start | bytes 1572872 | tf_op jit(solution)/shard_map/ppermute | solution.py:302
  48.3 78.2 %collective-permute-start.11 = (bf16[2,256,1024]{2,1,0:T(8,128)(2,1)}, bf16[2,256,1024]{2,1,0:T(8,128)(2,1)S(1)}, u32[]{:S(2)}, u32[]{:S(2)}) collective-permute-start(bf16[2,256,1024]{2,1,0:T(8,128)(2,1)} %collective-permute-done.10.refs_13_), channel_id=1, source_target_pairs={{0,4},{4,0},{8,12},{12,8},{1,5},{5,1},{9,13},{13,9},{2,6},{6,2},{1... | collective-permute-start | bytes 3145736 | tf_op jit(solution)/shard_map/ppermute | solution.py:302
  48.4 57.0 %collective-permute-start.12 = (bf16[512,256]{1,0:T(8,128)(2,1)S(1)}, bf16[512,256]{1,0:T(8,128)(2,1)S(1)}, u32[]{:S(2)}, u32[]{:S(2)}) collective-permute-start(bf16[512,256]{1,0:T(8,128)(2,1)S(1)} %copy-done.6), channel_id=1, source_target_pairs={{0,2},{2,3},{3,1},{1,0},{4,6},{6,7},{7,5},{5,4},{8,10},{10,11},{11... | collective-permute-start | bytes 786440 | tf_op jit(solution)/shard_map/ppermute | solution.py:439
  51.4 72.9 %collective-permute-start.6 = (bf16[4,256,256]{2,1,0:T(8,128)(2,1)}, bf16[4,256,256]{2,1,0:T(8,128)(2,1)S(1)}, u32[]{:S(2)}, u32[]{:S(2)}) collective-permute-start(bf16[4,256,256]{2,1,0:T(8,128)(2,1)} %all-to-all-done.refs_7_), channel_id=1, source_target_pairs={{0,4},{4,0},{8,12},{12,8},{1,5},{5,1},{9,13},{13,9},{2,6},{6,2},{1... | collective-permute-start | bytes 1572872 | tf_op jit(solution)/shard_map/ppermute | solution.py:302
  51.5 57.1 %collective-permute-start.3 = (bf16[512,256]{1,0:T(8,128)(2,1)S(1)}, bf16[512,256]{1,0:T(8,128)(2,1)S(1)}, u32[]{:S(2)}, u32[]{:S(2)}) collective-permute-start(bf16[512,256]{1,0:T(8,128)(2,1)S(1)} %get-tuple-element.18.refs_3_), channel_id=1, source_target_pairs={{0,2},{2,3},{3,1},{1,0},{4,6},{6,7},{7,5},{5,4},{8,10},{10,11},{11... | collective-permute-start | bytes 786440 | tf_op jit(solution)/shard_map/ppermute | solution.py:439
  105.4 18.9 %collective-permute-start.8 = (bf16[4,256,256]{2,1,0:T(8,128)(2,1)S(1)}, bf16[4,256,256]{2,1,0:T(8,128)(2,1)S(1)}, u32[]{:S(2)}, u32[]{:S(2)}) collective-permute-start(bf16[4,256,256]{2,1,0:T(8,128)(2,1)S(1)} %collective-permute-done.7.refs_9_), channel_id=1, source_target_pairs={{0,4},{4,0},{8,12},{12,8},{1,5},{5,1},{9,13},{13,9},{2,6},{6,2},{1... | collective-permute-start | bytes 1572872 | tf_op jit(solution)/shard_map/ppermute | solution.py:302
  105.4 9.8 %collective-permute-start.13 = (bf16[512,256]{1,0:T(8,128)(2,1)S(1)}, bf16[512,256]{1,0:T(8,128)(2,1)S(1)}, u32[]{:S(2)}, u32[]{:S(2)}) collective-permute-start(bf16[512,256]{1,0:T(8,128)(2,1)S(1)} %collective-permute-done.12.refs_4_), channel_id=1, source_target_pairs={{0,2},{2,3},{3,1},{1,0},{4,6},{6,7},{7,5},{5,4},{8,10},{10,11},{11... | collective-permute-start | bytes 786440 | tf_op jit(solution)/shard_map/ppermute | solution.py:439
  108.6 12.3 %collective-permute-start.4 = (bf16[512,256]{1,0:T(8,128)(2,1)S(1)}, bf16[512,256]{1,0:T(8,128)(2,1)S(1)}, u32[]{:S(2)}, u32[]{:S(2)}) collective-permute-start(bf16[512,256]{1,0:T(8,128)(2,1)S(1)} %collective-permute-done.3.refs_4_), channel_id=1, source_target_pairs={{0,2},{2,3},{3,1},{1,0},{4,6},{6,7},{7,5},{5,4},{8,10},{10,11},{11... | collective-permute-start | bytes 786440 | tf_op jit(solution)/shard_map/ppermute | solution.py:439
  115.3 11.2 %collective-permute-start.14 = (bf16[512,256]{1,0:T(8,128)(2,1)S(1)}, bf16[512,256]{1,0:T(8,128)(2,1)S(1)}, u32[]{:S(2)}, u32[]{:S(2)}) collective-permute-start(bf16[512,256]{1,0:T(8,128)(2,1)S(1)} %collective-permute-done.13.refs_5_), channel_id=1, source_target_pairs={{0,2},{2,3},{3,1},{1,0},{4,6},{6,7},{7,5},{5,4},{8,10},{10,11},{11... | collective-permute-start | bytes 786440 | tf_op jit(solution)/shard_map/ppermute | solution.py:439
  120.9 16.8 %collective-permute-start.5 = (bf16[512,256]{1,0:T(8,128)(2,1)S(1)}, bf16[512,256]{1,0:T(8,128)(2,1)S(1)}, u32[]{:S(2)}, u32[]{:S(2)}) collective-permute-start(bf16[512,256]{1,0:T(8,128)(2,1)S(1)} %collective-permute-done.4.refs_5_), channel_id=1, source_target_pairs={{0,2},{2,3},{3,1},{1,0},{4,6},{6,7},{7,5},{5,4},{8,10},{10,11},{11... | collective-permute-start | bytes 786440 | tf_op jit(solution)/shard_map/ppermute | solution.py:439
  134.3 10.9 %collective-permute-start.18 = (bf16[512,256]{1,0:T(8,128)(2,1)S(1)}, bf16[512,256]{1,0:T(8,128)(2,1)S(1)}, u32[]{:S(2)}, u32[]{:S(2)}) collective-permute-start(bf16[512,256]{1,0:T(8,128)(2,1)S(1)} %get-tuple-element.25), channel_id=1, source_target_pairs={{0,2},{2,3},{3,1},{1,0},{4,6},{6,7},{7,5},{5,4},{8,10},{10,11},{11... | collective-permute-start | bytes 786440 | tf_op jit(solution)/shard_map/ppermute | solution.py:493
  144.5 9.2 %collective-permute-start.15 = (bf16[512,256]{1,0:T(8,128)(2,1)S(1)}, bf16[512,256]{1,0:T(8,128)(2,1)S(1)}, u32[]{:S(2)}, u32[]{:S(2)}) collective-permute-start(bf16[512,256]{1,0:T(8,128)(2,1)S(1)} %get-tuple-element.22), channel_id=1, source_target_pairs={{0,2},{2,3},{3,1},{1,0},{4,6},{6,7},{7,5},{5,4},{8,10},{10,11},{11... | collective-permute-start | bytes 786440 | tf_op jit(solution)/shard_map/ppermute | solution.py:493
  145.3 14.1 %collective-permute-start.19 = (bf16[512,256]{1,0:T(8,128)(2,1)S(1)}, bf16[512,256]{1,0:T(8,128)(2,1)S(1)}, u32[]{:S(2)}, u32[]{:S(2)}) collective-permute-start(bf16[512,256]{1,0:T(8,128)(2,1)S(1)} %shard_map.110), channel_id=1, source_target_pairs={{0,2},{2,3},{3,1},{1,0},{4,6},{6,7},{7,5},{5,4},{8,10},{10,11},{11... | collective-permute-start | bytes 786440 | tf_op jit(solution)/shard_map/ppermute | solution.py:493
  153.8 11.2 %collective-permute-start.16 = (bf16[512,256]{1,0:T(8,128)(2,1)S(1)}, bf16[512,256]{1,0:T(8,128)(2,1)S(1)}, u32[]{:S(2)}, u32[]{:S(2)}) collective-permute-start(bf16[512,256]{1,0:T(8,128)(2,1)S(1)} %shard_map.108), channel_id=1, source_target_pairs={{0,2},{2,3},{3,1},{1,0},{4,6},{6,7},{7,5},{5,4},{8,10},{10,11},{11... | collective-permute-start | bytes 786440 | tf_op jit(solution)/shard_map/ppermute | solution.py:493
  159.4 11.2 %collective-permute-start.20 = (bf16[512,256]{1,0:T(8,128)(2,1)S(1)}, bf16[512,256]{1,0:T(8,128)(2,1)S(1)}, u32[]{:S(2)}, u32[]{:S(2)}) collective-permute-start(bf16[512,256]{1,0:T(8,128)(2,1)S(1)} %shard_map.111), channel_id=1, source_target_pairs={{0,2},{2,3},{3,1},{1,0},{4,6},{6,7},{7,5},{5,4},{8,10},{10,11},{11... | collective-permute-start | bytes 786440 | tf_op jit(solution)/shard_map/ppermute | solution.py:493
  165.0 9.0 %collective-permute-start.17 = (bf16[512,256]{1,0:T(8,128)(2,1)S(1)}, bf16[512,256]{1,0:T(8,128)(2,1)S(1)}, u32[]{:S(2)}, u32[]{:S(2)}) collective-permute-start(bf16[512,256]{1,0:T(8,128)(2,1)S(1)} %shard_map.109), channel_id=1, source_target_pairs={{0,2},{2,3},{3,1},{1,0},{4,6},{6,7},{7,5},{5,4},{8,10},{10,11},{11... | collective-permute-start | bytes 786440 | tf_op jit(solution)/shard_map/ppermute | solution.py:493
  (11 other events, 177.6 us)

commit v2 on v1

--- a/solution.py
+++ b/solution.py
@@ -38,31 +38,29 @@
 
 
 def project_kernel(n_dp, heads, event_count, block, base, *refs):
-    ids_ref, rates_ref, tok_ref, gain_ref, past_hbm = refs[:5]
-    pieces = refs[5 : 5 + n_dp]
-    gated_ref, key_hbm, value_hbm = refs[5 + n_dp : 8 + n_dp]
-    w_ref, past_ref, decay_ref, key_ref, value_ref, sems, own_sems = refs[8 + n_dp :]
-    depth = w_ref.shape[1] // n_dp
-    copies = []
-    for m in range(4):
-        span = pl.ds(m * depth, depth)
-        copies += piece_copies(
-            pieces, w_ref.at[m], sems.at[m], ids_ref[0], lambda piece: piece.at[span]
-        )
-    for copy in copies:
-        copy.start()
+    ids_ref, small_ref, tok_ref, past_hbm = refs[:4]
+    pieces = refs[4 : 4 + n_dp]
+    gated_ref, key_hbm, value_hbm = refs[4 + n_dp : 7 + n_dp]
+    normed_ref, past_ref, decay_ref, key_ref, value_ref, w_ref, sems = refs[7 + n_dp :]
     past_copy = pltpu.make_async_copy(
-        past_hbm.at[pl.ds(base // event_count, past_ref.shape[0])], past_ref, own_sems.at[0]
+        past_hbm.at[pl.ds(base // event_count, past_ref.shape[0])], past_ref, sems.at[0]
     )
     past_copy.start()
     out_copies = [
-        pltpu.make_async_copy(key_ref, key_hbm, own_sems.at[1]),
-        pltpu.make_async_copy(value_ref, value_hbm, own_sems.at[2]),
+        pltpu.make_async_copy(key_ref, key_hbm, sems.at[1]),
+        pltpu.make_async_copy(value_ref, value_hbm, sems.at[2]),
     ]
-    rows = gated_ref.shape[0]
+    rows, _ = gated_ref.shape
     head_dim = past_ref.shape[3]
     sessions = block // event_count
     key_scale = head_dim ** (-0.5)
+    depth = tok_ref.shape[1] // n_dp
+    starts = [pl.multiple_of(jnp.bitwise_xor(ids_ref[0], k) * depth, depth) for k in range(n_dp)]
+    split = depth % 128 == 0
+    if not split:
+        for m in range(4):
+            for k in range(n_dp):
+                w_ref[m, pl.ds(starts[k], depth), :] = pieces[k][m * depth : (m + 1) * depth]
     at = lax.broadcasted_iota(jnp.int32, (block, block), 0)
     to = lax.broadcasted_iota(jnp.int32, (block, block), 1)
     allowed = (at // event_count == to // event_count) & (at >= to)
@@ -71,27 +69,38 @@
     since = (place + 1).astype(jnp.float32)
     factors = []
     for h in range(heads):
-        rate = rates_ref[ids_ref[1] * heads + h]
-        decay_ref[h] = jnp.where(allowed, jnp.exp(-rate * distance), 0.0) * key_scale
-        factors.append(jnp.exp(-rate * since))
-    spans = [slice(r, r + block) for r in range(0, rows, block)]
-    normed = [
-        rms_scale(
-            tok_ref[base + span.start : base + span.stop].astype(jnp.float32), gain_ref[0:1, :]
+        rate = small_ref[2 + h : 3 + h, :]
+        decay_ref[h] = jnp.where(allowed, jnp.exp(-rate[:, :block] * distance), 0.0) * key_scale
+        factors.append(jnp.exp(-rate[:, :head_dim] * since))
+
+    def product(span, m):
+        if not split:
+            return dot_nn(normed_ref[span], w_ref[m])
+        total = None
+        for k in range(n_dp):
+            term = dot_nn(
+                normed_ref[span, pl.ds(starts[k], depth)], pieces[k][m * depth : (m + 1) * depth]
+            )
+            total = term if total is None else total + term
+        return total
+
+    for r in range(0, rows, block):
+        span = slice(r, r + block)
+        normed_ref[span] = rms_scale(
+            tok_ref[base + r : base + r + block].astype(jnp.float32), small_ref[0:1, :]
         )
-        for span in spans
-    ]
-    for copy in copies:
-        copy.wait()
-    past_copy.wait()
-    for span, rows_in in zip(spans, normed):
-        query = dot_nn(rows_in, w_ref[0]).astype(jnp.bfloat16)
-        keys = dot_nn(rows_in, w_ref[1]).astype(jnp.bfloat16)
+        query = product(span, 0).astype(jnp.bfloat16)
+        keys = product(span, 1).astype(jnp.bfloat16)
         key_ref[span] = keys
-        values = dot_nn(rows_in, w_ref[2]).astype(jnp.bfloat16)
+        values = product(span, 2).astype(jnp.bfloat16)
         value_ref[span] = values
-        gate = dot_nn(rows_in, w_ref[3])
-        first_session = span.start // event_count
+        gate = product(span, 3)
+        if r == 0:
+            past_copy.wait()
+        if r + block == rows:
+            for copy in out_copies:
+                copy.start()
+        first_session = r // event_count
         for h in range(heads):
             cols = slice(h * head_dim, (h + 1) * head_dim)
             qh, kh, vh = query[:, cols], keys[:, cols], values[:, cols]
@@ -111,15 +120,13 @@
             normalised = centred * lax.rsqrt(row_var + 1e-05)
             gated_ref[span, cols] = (jax.nn.silu(gate[:, cols]) * normalised).astype(jnp.bfloat16)
     for copy in out_copies:
-        copy.start()
-    for copy in out_copies:
         copy.wait()
 
 
 def state_kernel(chunks, heads, event_count, *refs):
-    ids_ref, rates_ref, pos_ref, past_hbm = refs[:4]
-    sources = refs[4 : 4 + 2 * chunks]
-    out_ref, buf_ref, past_ref, kv_ref, sems, past_sems, kv_sems = refs[4 + 2 * chunks :]
+    small_ref, pos_ref, past_hbm = refs[:3]
+    sources = refs[3 : 3 + 2 * chunks]
+    out_ref, buf_ref, past_ref, kv_ref, sems, past_sems, kv_sems = refs[3 + 2 * chunks :]
     kv_copies = [
         pltpu.make_async_copy(source, kv_ref.at[k], kv_sems.at[k])
         for k, source in enumerate(sources)
@@ -151,9 +158,9 @@
     left = (event_count - 1 - place).astype(jnp.float32)
     factors, carries = [], []
     for h in range(heads):
-        rate = rates_ref[ids_ref[1] * heads + h]
+        rate = small_ref[2 + h : 3 + h, :head_dim]
         factors.append(jnp.exp(-rate * left) * key_scale)
-        carries.append(jnp.exp(jnp.full((head_dim, head_dim), -rate * event_count, jnp.float32)))
+        carries.append(jnp.exp(-rate * event_count))
     for c in range(chunks):
         kv_copies[c].wait()
         kv_copies[chunks + c].wait()
@@ -222,32 +229,41 @@
 
 
 def feed_kernel(n_dp, n_tensor, block, base, *refs):
-    ids_ref, tok_ref, gain_ref = refs[:3]
-    gated = refs[3 : 3 + n_tensor]
+    ids_ref, small_ref, tok_ref = refs[:3]
+    gated_hbm = refs[3 : 3 + n_tensor]
     at = 3 + n_tensor
     out_pieces = refs[at : at + n_dp]
     ffn_pieces = refs[at + n_dp : at + 2 * n_dp]
     at += 2 * n_dp
-    own_ref = refs[at]
-    part_refs = refs[at + 1 : at + n_tensor]
-    wo_ref, up_ref, down_ref, res_ref, sems = refs[at + n_tensor :]
+    own_hbm, *part_hbm = refs[at : at + n_tensor]
+    wo_ref, up_ref, down_ref, res_ref, gated, own_ref, part_ref = refs[at + n_tensor : -3]
+    sems, gated_sems, done_sems = refs[-3:]
+    rows, width = own_ref.shape
     me = ids_ref[0]
     out_copies = piece_copies(out_pieces, wo_ref, sems.at[0], me, lambda piece: piece)
     up_copies = piece_copies(ffn_pieces, up_ref, sems.at[1], me, lambda piece: piece.at[0])
     down_copies = piece_copies(ffn_pieces, down_ref, sems.at[2], me, lambda piece: piece.at[1])
-    for copy in out_copies + up_copies + down_copies:
+    gated_copies = [
+        pltpu.make_async_copy(source, gated.at[k], gated_sems.at[k])
+        for k, source in enumerate(gated_hbm)
+    ]
+    for copy in gated_copies + out_copies + up_copies + down_copies:
         copy.start()
-    for copy in out_copies:
+    for copy in gated_copies + out_copies:
         copy.wait()
-    rows, width = own_ref.shape
+    done_copies = [pltpu.make_async_copy(own_ref, own_hbm, done_sems.at[0])]
+    for k in range(1, n_tensor):
+        done_copies.append(
+            pltpu.make_async_copy(part_ref.at[k - 1], part_hbm[k - 1], done_sems.at[k])
+        )
     for r in range(0, rows, block):
         span = slice(r, r + block)
-        attended = dot_nt(gated[0][span], wo_ref[ids_ref[2]])
+        attended = dot_nt(gated[0, span], wo_ref[ids_ref[2]])
         for k in range(1, n_tensor):
-            attended += dot_nt(gated[k][span], wo_ref[ids_ref[2 + k]])
+            attended += dot_nt(gated[k, span], wo_ref[ids_ref[2 + k]])
         residual = tok_ref[base + r : base + r + block].astype(jnp.float32) + attended
         res_ref[span] = residual
-        hidden = rms_scale(residual, gain_ref[1:2, :])
+        hidden = rms_scale(residual, small_ref[1:2, :])
         if r == 0:
             for copy in up_copies:
                 copy.wait()
@@ -256,15 +272,22 @@
         if r == 0:
             for copy in down_copies:
                 copy.wait()
+        final = r + block == rows
 
         def term(k):
             start = pl.multiple_of(ids_ref[2 + k] * width, width)
             return dot_nt(activated, down_ref[pl.ds(start, width), :])
 
         for k in range(1, n_tensor):
-            part_refs[k - 1][span] = term(k).astype(jnp.bfloat16)
+            part_ref[k - 1, span] = term(k).astype(jnp.bfloat16)
+            if final:
+                done_copies[k].start()
         mine = pl.ds(pl.multiple_of(ids_ref[1] * width, width), width)
         own_ref[span] = res_ref[span, mine] + term(0)
+        if final:
+            done_copies[0].start()
+    for copy in done_copies:
+        copy.wait()
 
 
 def add_kernel(a_ref, b_ref, out_ref):
@@ -272,22 +295,19 @@
     out_ref[...] = total.astype(jnp.bfloat16)
 
 
-def last_kernel(chunks, event_count, *refs):
-    lengths_ref = refs[0]
-    owns = refs[1 : 1 + chunks]
-    terms = refs[1 + chunks : 1 + 2 * chunks]
-    out_ref = refs[-1]
-    rows, width = owns[0].shape
+def last_kernel(event_count, base, *refs):
+    lengths_ref, own_ref, term_ref = refs[:3]
+    out_hbm, out_ref, sem = refs[-3:]
+    rows, width = own_ref.shape
     place = lax.broadcasted_iota(jnp.int32, (event_count, width), 0)
-    for c in range(chunks):
-        for s in range(rows // event_count):
-            span = slice(s * event_count, (s + 1) * event_count)
-            total = owns[c][span] + terms[c][span].astype(jnp.float32)
-            session = c * (rows // event_count) + s
-            keep = place < lengths_ref[session]
-            out_ref[session * event_count : (session + 1) * event_count] = jnp.where(
-                keep, total, 0.0
-            ).astype(jnp.bfloat16)
+    for s in range(rows // event_count):
+        span = slice(s * event_count, (s + 1) * event_count)
+        total = own_ref[span] + term_ref[span].astype(jnp.float32)
+        keep = place < lengths_ref[base // event_count + s]
+        out_ref[span] = jnp.where(keep, total, 0.0).astype(jnp.bfloat16)
+    copy = pltpu.make_async_copy(out_ref, out_hbm.at[pl.ds(base, rows)], sem)
+    copy.start()
+    copy.wait()
 
 
 def xor_gather(value, axis):
@@ -412,25 +432,29 @@
 
     rows_shape = shape_of((chunk_rows, cols_here), bf16)
     decay_shape = pltpu.VMEM((heads_here, block, block), f32)
+    head_decay = lax.dynamic_slice_in_dim(head_rates, tensor_at * heads_here, heads_here)
+    small = jnp.concatenate(
+        [norm_gains, jnp.broadcast_to(head_decay[:, None], (heads_here, width))]
+    )
     chunk_sessions = chunk_rows // event_count
     gated, keys, values = [], [], []
     for c in range(CHUNKS):
         g, k, v = kernel_call(
             functools.partial(project_kernel, n_dp, heads_here, event_count, block, c * chunk_rows),
-            [smem_spec()] * 2 + [vmem_spec()] * 2 + [hbm_spec()] + [any_spec()] * n_dp,
+            [smem_spec()] + [vmem_spec()] * 2 + [hbm_spec()] + [vmem_spec()] * n_dp,
             [vmem_spec()] + [hbm_spec()] * 2,
             [rows_shape] + [pltpu.HBM((chunk_rows, cols_here), bf16)] * 2,
             [
-                pltpu.VMEM((4, width, cols_here), bf16),
+                pltpu.VMEM((chunk_rows, width), bf16),
                 pltpu.VMEM((chunk_sessions, heads_here, head_dim, head_dim), f32),
                 decay_shape,
                 pltpu.VMEM((chunk_rows, cols_here), bf16),
                 pltpu.VMEM((chunk_rows, cols_here), bf16),
-                pltpu.SemaphoreType.DMA((4, n_dp)),
+                pltpu.VMEM((4, width, cols_here), bf16),
                 pltpu.SemaphoreType.DMA((3,)),
             ],
             2 * chunk_rows * width * cols_here * 4,
-        )(ids, head_rates, tokens, norm_gains, *in_hbm([past_states]), *proj_pieces)
+        )(ids, small, tokens, *in_hbm([past_states]), *proj_pieces)
         gated.append([g])
         keys.append(k)
         values.append(v)
@@ -442,7 +466,7 @@
     ffn_pieces = xor_gather(ffn_weights, "dp")
     packed = kernel_call(
         functools.partial(state_kernel, CHUNKS, heads_here, event_count),
-        [smem_spec()] * 3 + [hbm_spec()] * (1 + 2 * CHUNKS),
+        [vmem_spec(), smem_spec()] + [hbm_spec()] * (1 + 2 * CHUNKS),
         hbm_spec(),
         pltpu.HBM((slot_count, heads_here, head_dim, head_dim), bf16),
         [
@@ -454,26 +478,31 @@
             pltpu.SemaphoreType.DMA((2 * CHUNKS,)),
         ],
         2 * row_count * head_dim * cols_here,
-    )(ids, head_rates, send_pos, *in_hbm([past_states, *keys, *values]))
+    )(small, send_pos, *in_hbm([past_states, *keys, *values]))
     received = lax.all_to_all(packed, "dp", split_axis=0, concat_axis=0, tiled=True)
 
     owns, parts, sums = [], [], []
     for c in range(CHUNKS):
         own, *part = kernel_call(
             functools.partial(feed_kernel, n_dp, n_tensor, block, c * chunk_rows),
-            [smem_spec()] + [vmem_spec()] * (2 + n_tensor) + [hbm_spec()] * (2 * n_dp),
-            [vmem_spec()] * n_tensor,
-            [shape_of((chunk_rows, share), f32)]
-            + [shape_of((chunk_rows, share), bf16)] * (n_tensor - 1),
+            [smem_spec()] + [vmem_spec()] * 2 + [hbm_spec()] * (n_tensor + 2 * n_dp),
+            [hbm_spec()] * n_tensor,
+            [pltpu.HBM((chunk_rows, share), f32)]
+            + [pltpu.HBM((chunk_rows, share), bf16)] * (n_tensor - 1),
             [
                 pltpu.VMEM((n_tensor, width, cols_here), bf16),
                 pltpu.VMEM((width, units_here), bf16),
                 pltpu.VMEM((width, units_here), bf16),
                 pltpu.VMEM((chunk_rows, width), f32),
+                pltpu.VMEM((n_tensor, chunk_rows, cols_here), bf16),
+                pltpu.VMEM((chunk_rows, share), f32),
+                pltpu.VMEM((n_tensor - 1, chunk_rows, share), bf16),
                 pltpu.SemaphoreType.DMA((3, n_dp)),
+                pltpu.SemaphoreType.DMA((n_tensor,)),
+                pltpu.SemaphoreType.DMA((n_tensor,)),
             ],
             2 * chunk_rows * width * (width + 2 * units_here),
-        )(ids, tokens, norm_gains, *gated[c], *in_hbm(out_pieces + ffn_pieces))
+        )(ids, small, tokens, *in_hbm(gated[c] + out_pieces + ffn_pieces))
         owns.append(own)
         parts.append(part)
         sums.append(None)
@@ -492,15 +521,27 @@
                 )(sums[c], mine)
             sums[c] = lax.ppermute(mine, "tensor", ring)
 
-    next_tokens = kernel_call(
-        functools.partial(last_kernel, CHUNKS, event_count),
-        [smem_spec()] + [vmem_spec()] * (2 * CHUNKS),
-        vmem_spec(),
-        shape_of((row_count, share), bf16),
-        [],
-        0,
-        limit_mib=8,
-    )(end_lengths, *owns, *sums)
+    so_far = []
+    for c in range(CHUNKS):
+        so_far = [
+            pl.pallas_call(
+                functools.partial(last_kernel, event_count, c * chunk_rows),
+                in_specs=[smem_spec()] + [vmem_spec()] * 2 + [hbm_spec()] * len(so_far),
+                out_specs=hbm_spec(),
+                out_shape=shape_of((row_count, share), bf16),
+                scratch_shapes=[
+                    pltpu.VMEM((chunk_rows, share), bf16),
+                    pltpu.SemaphoreType.DMA,
+                ],
+                input_output_aliases={3: 0} if so_far else {},
+                compiler_params=pltpu.CompilerParams(vmem_limit_bytes=8 * 1024 * 1024),
+                cost_estimate=pl.CostEstimate(
+                    flops=0, bytes_accessed=chunk_rows * share * 8, transcendentals=0
+                ),
+                name="last",
+            )(end_lengths, owns[c], sums[c], *so_far)
+        ]
+    (next_tokens,) = so_far
 
     per_step = min(8, sessions_here)
     moved_states = pl.pallas_call(

time: 181 us -> 181 us (level)
  waiting for transfers between devices: 89.2 us -> 84.5 us
  local copies, waits for them, and re-layouts: 6.68 us -> 9.46 us
  Pallas kernels: 37.7 us -> 39.8 us
    pallas_call x2, Pallas kernels: 13.5 us -> 18.5 us  [per_device(): kernel_call(functools.partial(feed_kernel, n_dp, n_tensor, block, c * chu...]
    pallas_call x2, Pallas kernels: 13.4 us -> 9.33 us  [per_device(): kernel_call(functools.partial(project_kernel, n_dp, heads_here, event_cou...]
    ppermute x6, waiting for transfers between devices: 22.4 us -> 19.3 us  [per_device(): sums[c] = lax.ppermute(mine, 'tensor', ring)]
    unnamed x25 -> x45, local copies, waits for them, and re-layouts: 2.34 us -> 4.31 us
  transfers between devices with their start and end apart: 23 -> 23, of which waited for: 11 -> 11; matrix products, arithmetic and copies ran while one was open for 3% -> 3% of each run, Pallas kernels for 19% -> 20%
where the time goes in v2:
time: 181 us; the launch traced here: 180 us
  waiting for transfers between devices  84.5 us (47%)
  starting transfers between devices  42.7 us (24%)
  Pallas kernels  39.8 us (22%)
  local copies, waits for them, and re-layouts  9.46 us (5%)
  other arithmetic  2.81 us (2%)
    ppermute x9, waiting for transfers between devices, xor_gather(): arrived.append(lax.ppermute(piece, axis, pairs))  55.7 us
    ppermute x6, waiting for transfers between devices, per_device(): sums[c] = lax.ppermute(mine, 'tensor', ring)  19.3 us
    pallas_call x2, Pallas kernels, per_device(): kernel_call(functools.partial(feed_kernel, n_dp, n_tensor, block, c * chu...  18.5 us
    ppermute x6, starting transfers between devices, per_device(): gated[c].append(lax.ppermute(gated[c][-1], 'tensor', ring))  16.5 us
    ppermute x6, starting transfers between devices, per_device(): sums[c] = lax.ppermute(mine, 'tensor', ring)  10.4 us
    ppermute x6, waiting for transfers between devices, per_device(): gated[c].append(lax.ppermute(gated[c][-1], 'tensor', ring))  9.57 us
    pallas_call x2, Pallas kernels, per_device(): kernel_call(functools.partial(project_kernel, n_dp, heads_here, event_cou...  9.33 us
    ppermute x9, starting transfers between devices, xor_gather(): arrived.append(lax.ppermute(piece, axis, pairs))  6 us
  transfers between devices with their start and end apart: 23, of which 11 were waited for; matrix products, arithmetic and copies ran while one was open for 3% of the time, Pallas kernels for 20%

profile of v2, /device:TPU:0, one launch (start us, length us, event | category | flops | bytes accessed | tf_op | source)
XLA Modules:
  0.0 180.4 jit_solution(10434363880369959281)
XLA Ops:
  2.6 3.0 %collective-permute-start.1 = (bf16[1032,256]{1,0:T(8,128)(2,1)S(1)}, bf16[1032,256]{1,0:T(8,128)(2,1)S(1)}, u32[]{:S(2)}, u32[]{:S(2)}) collective-permute-start(bf16[1032,256]{1,0:T(8,128)(2,1)S(1)} %pad_maximum_fusion.refs_4_), channel_id=1, source_target_pairs={{0,8},{4,12},{8,0},{12,4},{1,9},{5,13},{9,1},{13,5},{2,10},{6,14},... | collective-permute-start | bytes 1585160 | tf_op jit(solution)/shard_map/ppermute | solution.py:322
  7.4 4.9 %all-to-all-start = ((bf16[4,256,256]{2,1,0:T(8,128)(2,1)}), bf16[4,256,256]{2,1,0:T(8,128)(2,1)}, u32[]{:S(2)}, u32[]{:S(2)}) async-start(bf16[4,256,256]{2,1,0:T(8,128)(2,1)} %broadcast_in_dim.19), calls=%async_computation | async-start | bytes 1048576 | tf_op jit(solution)/shard_map/all_to_all | solution.py:405
  16.0 2.6 %collective-permute-done.1.refs_6_ = bf16[1032,256]{1,0:T(8,128)(2,1)S(1)} collective-permute-done((bf16[1032,256]{1,0:T(8,128)(2,1)S(1)}, bf16[1032,256]{1,0:T(8,128)(2,1)S(1)}, u32[]{:S(2)}, u32[]{:S(2)}) %collective-permute-start.1) | collective-permute-done | bytes 528416 | tf_op jit(solution)/shard_map/ppermute | solution.py:322
  20.9 4.6 %shard_map.108 = (bf16[512,256]{1,0:T(8,128)(2,1)S(1)}, bf16[512,256]{1,0:T(8,128)(2,1)}, bf16[512,256]{1,0:T(8,128)(2,1)}) custom-call(s32[6]{0:T(128)S(1)} %pad_add_fusion.refs_0_, f32[4,1024]{1,0:T(4,128)S(1)} %pad_maximum_fusion.1.refs_1_.refs_0_, bf16[1024,1024]{1,0:T(8,128)(2,1)S(1)} %copy-done, f32[32,2,128,128]{3,2,1,0:T(8,128)} %refs_2_.9, ...), custom_call_target="tpu_custom_call" | custom-call | flops 1073741824 | bytes 4194304 | tf_op jit(solution)/shard_map/pallas_call | solution.py:442
  25.5 4.7 %shard_map.104 = (bf16[512,256]{1,0:T(8,128)(2,1)S(1)}, bf16[512,256]{1,0:T(8,128)(2,1)}, bf16[512,256]{1,0:T(8,128)(2,1)}) custom-call(s32[6]{0:T(128)S(1)} %pad_add_fusion.refs_0_, f32[4,1024]{1,0:T(4,128)S(1)} %pad_maximum_fusion.1.refs_1_.refs_0_, bf16[1024,1024]{1,0:T(8,128)(2,1)S(1)} %copy-done, f32[32,2,128,128]{3,2,1,0:T(8,128)} %refs_2_.9, ...), custom_call_target="tpu_custom_call" | custom-call | flops 1073741824 | bytes 4194304 | tf_op jit(solution)/shard_map/pallas_call | solution.py:442
  30.2 4.7 %shard_map.112 = bf16[64,2,128,128]{3,2,1,0:T(8,128)(2,1)} custom-call(f32[4,1024]{1,0:T(4,128)S(1)} %pad_maximum_fusion.1.refs_1_.refs_0_, s32[32]{0:T(128)S(1)} %get-tuple-element.29.refs_1_, f32[32,2,128,128]{3,2,1,0:T(8,128)} %refs_2_.9, bf16[512,256]{1,0:T(8,128)(2,1)} %get-tuple-element.30.refs_3_, bf16[512,256]{1,0:T(8,128)(2,1)} %get-tuple-element.31.refs_4_, ...), custom_call_target="tpu_custom_call" | custom-call | flops 67108864 | bytes 4194304 | tf_op jit(solution)/shard_map/pallas_call | solution.py:467
  35.0 5.0 %all-to-all-start.1 = ((bf16[64,2,128,128]{3,2,1,0:T(8,128)(2,1)}), bf16[64,2,128,128]{3,2,1,0:T(8,128)(2,1)}, u32[]{:S(2)}, u32[]{:S(2)}) async-start(bf16[64,2,128,128]{3,2,1,0:T(8,128)(2,1)} %shard_map.112), calls=%async_computation.1 | async-start | bytes 8388608 | tf_op jit(solution)/shard_map/all_to_all | solution.py:482
  42.3 3.0 %collective-permute-start.15 = (bf16[512,256]{1,0:T(8,128)(2,1)S(1)}, bf16[512,256]{1,0:T(8,128)(2,1)S(1)}, u32[]{:S(2)}, u32[]{:S(2)}) collective-permute-start(bf16[512,256]{1,0:T(8,128)(2,1)S(1)} %copy-done.10), channel_id=1, source_target_pairs={{0,2},{2,3},{3,1},{1,0},{4,6},{6,7},{7,5},{5,4},{8,10},{10,11},{11... | collective-permute-start | bytes 786440 | tf_op jit(solution)/shard_map/ppermute | solution.py:463
  47.5 51.9 %collective-permute-done.7.refs_9_ = bf16[4,256,256]{2,1,0:T(8,128)(2,1)S(1)} collective-permute-done((bf16[4,256,256]{2,1,0:T(8,128)(2,1)}, bf16[4,256,256]{2,1,0:T(8,128)(2,1)S(1)}, u32[]{:S(2)}, u32[]{:S(2)}) %collective-permute-start.7) | collective-permute-done | bytes 524320 | tf_op jit(solution)/shard_map/ppermute | solution.py:322
  99.4 3.1 %collective-permute-start.16 = (bf16[512,256]{1,0:T(8,128)(2,1)S(1)}, bf16[512,256]{1,0:T(8,128)(2,1)S(1)}, u32[]{:S(2)}, u32[]{:S(2)}) collective-permute-start(bf16[512,256]{1,0:T(8,128)(2,1)S(1)} %collective-permute-done.15.refs_4_), channel_id=1, source_target_pairs={{0,2},{2,3},{3,1},{1,0},{4,6},{6,7},{7,5},{5,4},{8,10},{10,11},{11... | collective-permute-start | bytes 786440 | tf_op jit(solution)/shard_map/ppermute | solution.py:463
  104.1 5.1 %collective-permute-done.16.refs_5_ = bf16[512,256]{1,0:T(8,128)(2,1)S(1)} collective-permute-done((bf16[512,256]{1,0:T(8,128)(2,1)S(1)}, bf16[512,256]{1,0:T(8,128)(2,1)S(1)}, u32[]{:S(2)}, u32[]{:S(2)}) %collective-permute-start.16) | collective-permute-done | bytes 262176 | tf_op jit(solution)/shard_map/ppermute | solution.py:463
  109.2 3.4 %collective-permute-start.17 = (bf16[512,256]{1,0:T(8,128)(2,1)S(1)}, bf16[512,256]{1,0:T(8,128)(2,1)S(1)}, u32[]{:S(2)}, u32[]{:S(2)}) collective-permute-start(bf16[512,256]{1,0:T(8,128)(2,1)S(1)} %collective-permute-done.16.refs_5_), channel_id=1, source_target_pairs={{0,2},{2,3},{3,1},{1,0},{4,6},{6,7},{7,5},{5,4},{8,10},{10,11},{11... | collective-permute-start | bytes 786440 | tf_op jit(solution)/shard_map/ppermute | solution.py:463
  112.6 2.2 %collective-permute-done.4.refs_5_ = bf16[512,256]{1,0:T(8,128)(2,1)S(1)} collective-permute-done((bf16[512,256]{1,0:T(8,128)(2,1)S(1)}, bf16[512,256]{1,0:T(8,128)(2,1)S(1)}, u32[]{:S(2)}, u32[]{:S(2)}) %collective-permute-start.4) | collective-permute-done | bytes 262176 | tf_op jit(solution)/shard_map/ppermute | solution.py:463
  114.8 3.4 %collective-permute-start.5 = (bf16[512,256]{1,0:T(8,128)(2,1)S(1)}, bf16[512,256]{1,0:T(8,128)(2,1)S(1)}, u32[]{:S(2)}, u32[]{:S(2)}) collective-permute-start(bf16[512,256]{1,0:T(8,128)(2,1)S(1)} %collective-permute-done.4.refs_5_), channel_id=1, source_target_pairs={{0,2},{2,3},{3,1},{1,0},{4,6},{6,7},{7,5},{5,4},{8,10},{10,11},{11... | collective-permute-start | bytes 786440 | tf_op jit(solution)/shard_map/ppermute | solution.py:463
  118.3 2.2 %collective-permute-done.17.refs_6_ = bf16[512,256]{1,0:T(8,128)(2,1)S(1)} collective-permute-done((bf16[512,256]{1,0:T(8,128)(2,1)S(1)}, bf16[512,256]{1,0:T(8,128)(2,1)S(1)}, u32[]{:S(2)}, u32[]{:S(2)}) %collective-permute-start.17) | collective-permute-done | bytes 262176 | tf_op jit(solution)/shard_map/ppermute | solution.py:463
  122.2 9.3 %shard_map.109 = (f32[512,256]{1,0:T(8,128)}, bf16[512,256]{1,0:T(8,128)(2,1)}, bf16[512,256]{1,0:T(8,128)(2,1)}, bf16[512,256]{1,0:T(8,128)(2,1)}) custom-call(s32[6]{0:T(128)S(1)} %pad_add_fusion.refs_0_, f32[4,1024]{1,0:T(4,128)S(1)} %pad_maximum_fusion.1.refs_1_.refs_0_, bf16[1024,1024]{1,0:T(8,128)(2,1)S(1)} %copy-done, bf16[512,256]{1,0:T(8,128)(2,1)} %copy-done.9, ...), custom_call_target="tpu_custom_call" | custom-call | flops 3221225472 | bytes 4194304 | tf_op jit(solution)/shard_map/pallas_call | solution.py:486
  131.5 3.4 %collective-permute-start.18 = (bf16[512,256]{1,0:T(8,128)(2,1)}, bf16[512,256]{1,0:T(8,128)(2,1)S(1)}, u32[]{:S(2)}, u32[]{:S(2)}) collective-permute-start(bf16[512,256]{1,0:T(8,128)(2,1)} %get-tuple-element.25), channel_id=1, source_target_pairs={{0,2},{2,3},{3,1},{1,0},{4,6},{6,7},{7,5},{5,4},{8,10},{10,11},{11... | collective-permute-start | bytes 786440 | tf_op jit(solution)/shard_map/ppermute | solution.py:522
  135.7 9.2 %shard_map.105 = (f32[512,256]{1,0:T(8,128)}, bf16[512,256]{1,0:T(8,128)(2,1)}, bf16[512,256]{1,0:T(8,128)(2,1)}, bf16[512,256]{1,0:T(8,128)(2,1)}) custom-call(s32[6]{0:T(128)S(1)} %pad_add_fusion.refs_0_, f32[4,1024]{1,0:T(4,128)S(1)} %pad_maximum_fusion.1.refs_1_.refs_0_, bf16[1024,1024]{1,0:T(8,128)(2,1)S(1)} %copy-done, bf16[512,256]{1,0:T(8,128)(2,1)} %copy-done.8, ...), custom_call_target="tpu_custom_call" | custom-call | flops 3221225472 | bytes 4194304 | tf_op jit(solution)/shard_map/pallas_call | solution.py:486
  146.9 7.3 %collective-permute-done.12.a_ref = bf16[512,256]{1,0:T(8,128)(2,1)S(1)} collective-permute-done((bf16[512,256]{1,0:T(8,128)(2,1)}, bf16[512,256]{1,0:T(8,128)(2,1)S(1)}, u32[]{:S(2)}, u32[]{:S(2)}) %collective-permute-start.12) | collective-permute-done | bytes 262176 | tf_op jit(solution)/shard_map/ppermute | solution.py:522
  156.9 3.0 %collective-permute-done.19.a_ref = bf16[512,256]{1,0:T(8,128)(2,1)S(1)} collective-permute-done((bf16[512,256]{1,0:T(8,128)(2,1)S(1)}, bf16[512,256]{1,0:T(8,128)(2,1)S(1)}, u32[]{:S(2)}, u32[]{:S(2)}) %collective-permute-start.19) | collective-permute-done | bytes 262176 | tf_op jit(solution)/shard_map/ppermute | solution.py:522
  161.6 3.9 %collective-permute-done.13.a_ref = bf16[512,256]{1,0:T(8,128)(2,1)S(1)} collective-permute-done((bf16[512,256]{1,0:T(8,128)(2,1)S(1)}, bf16[512,256]{1,0:T(8,128)(2,1)S(1)}, u32[]{:S(2)}, u32[]{:S(2)}) %collective-permute-start.13) | collective-permute-done | bytes 262176 | tf_op jit(solution)/shard_map/ppermute | solution.py:522
  168.2 3.0 %collective-permute-done.20.refs_2_ = bf16[512,256]{1,0:T(8,128)(2,1)S(1)} collective-permute-done((bf16[512,256]{1,0:T(8,128)(2,1)S(1)}, bf16[512,256]{1,0:T(8,128)(2,1)S(1)}, u32[]{:S(2)}, u32[]{:S(2)}) %collective-permute-start.20) | collective-permute-done | bytes 262176 | tf_op jit(solution)/shard_map/ppermute | solution.py:522
  172.5 2.1 %collective-permute-done.14.refs_2_ = bf16[512,256]{1,0:T(8,128)(2,1)S(1)} collective-permute-done((bf16[512,256]{1,0:T(8,128)(2,1)S(1)}, bf16[512,256]{1,0:T(8,128)(2,1)S(1)}, u32[]{:S(2)}, u32[]{:S(2)}) %collective-permute-start.14) | collective-permute-done | bytes 262176 | tf_op jit(solution)/shard_map/ppermute | solution.py:522
  175.9 4.3 %unpack.1 = f32[32,2,128,128]{3,2,1,0:T(8,128)} custom-call(s32[32]{0:T(128)S(1)} %get-tuple-element.28.src_ref, bf16[64,2,128,128]{3,2,1,0:T(8,128)(2,1)} %all-to-all-done.1.recv_ref), custom_call_target="tpu_custom_call" | custom-call | bytes 6291456 | tf_op jit(solution)/shard_map/unpack/pallas_call | solution.py:547
  (104 shorter events, 29.8 us)
Async XLA Ops:
  2.6 15.9 %collective-permute-start.1 = (bf16[1032,256]{1,0:T(8,128)(2,1)S(1)}, bf16[1032,256]{1,0:T(8,128)(2,1)S(1)}, u32[]{:S(2)}, u32[]{:S(2)}) collective-permute-start(bf16[1032,256]{1,0:T(8,128)(2,1)S(1)} %pad_maximum_fusion.refs_4_), channel_id=1, source_target_pairs={{0,8},{4,12},{8,0},{12,4},{1,9},{5,13},{9,1},{13,5},{2,10},{6,14},... | collective-permute-start | bytes 1585160 | tf_op jit(solution)/shard_map/ppermute | solution.py:322
  5.7 12.9 %collective-permute-start = (bf16[1032,256]{1,0:T(8,128)(2,1)S(1)}, bf16[1032,256]{1,0:T(8,128)(2,1)}, u32[]{:S(2)}, u32[]{:S(2)}) collective-permute-start(bf16[1032,256]{1,0:T(8,128)(2,1)S(1)} %pad_maximum_fusion.refs_4_), channel_id=1, source_target_pairs={{0,4},{4,0},{8,12},{12,8},{1,5},{5,1},{9,13},{13,9},{2,6},{6,2},{1... | collective-permute-start | bytes 1585160 | tf_op jit(solution)/shard_map/ppermute | solution.py:322
  7.4 27.6 %all-to-all-start = ((bf16[4,256,256]{2,1,0:T(8,128)(2,1)}), bf16[4,256,256]{2,1,0:T(8,128)(2,1)}, u32[]{:S(2)}, u32[]{:S(2)}) async-start(bf16[4,256,256]{2,1,0:T(8,128)(2,1)} %broadcast_in_dim.19), calls=%async_computation | async-start | bytes 1048576 | tf_op jit(solution)/shard_map/all_to_all | solution.py:405
  12.3 30.0 %collective-permute-start.10 = (bf16[2,256,1024]{2,1,0:T(8,128)(2,1)}, bf16[2,256,1024]{2,1,0:T(8,128)(2,1)}, u32[]{:S(2)}, u32[]{:S(2)}) collective-permute-start(bf16[2,256,1024]{2,1,0:T(8,128)(2,1)} %refs_11_.3), channel_id=1, source_target_pairs={{0,8},{4,12},{8,0},{12,4},{1,9},{5,13},{9,1},{13,5},{2,10},{6,14},... | collective-permute-start | bytes 3145736 | tf_op jit(solution)/shard_map/ppermute | solution.py:322
  18.5 1.9 %collective-permute-start.2 = (bf16[1032,256]{1,0:T(8,128)(2,1)S(1)}, bf16[1032,256]{1,0:T(8,128)(2,1)S(1)}, u32[]{:S(2)}, u32[]{:S(2)}) collective-permute-start(bf16[1032,256]{1,0:T(8,128)(2,1)S(1)} %collective-permute-done.1.refs_6_), channel_id=1, source_target_pairs={{0,4},{4,0},{8,12},{12,8},{1,5},{5,1},{9,13},{13,9},{2,6},{6,2},{1... | collective-permute-start | bytes 1585160 | tf_op jit(solution)/shard_map/ppermute | solution.py:322
  35.0 140.9 %all-to-all-start.1 = ((bf16[64,2,128,128]{3,2,1,0:T(8,128)(2,1)}), bf16[64,2,128,128]{3,2,1,0:T(8,128)(2,1)}, u32[]{:S(2)}, u32[]{:S(2)}) async-start(bf16[64,2,128,128]{3,2,1,0:T(8,128)(2,1)} %shard_map.112), calls=%async_computation.1 | async-start | bytes 8388608 | tf_op jit(solution)/shard_map/all_to_all | solution.py:482
  40.0 5.5 %collective-permute-start.9 = (bf16[2,256,1024]{2,1,0:T(8,128)(2,1)}, bf16[2,256,1024]{2,1,0:T(8,128)(2,1)S(1)}, u32[]{:S(2)}, u32[]{:S(2)}) collective-permute-start(bf16[2,256,1024]{2,1,0:T(8,128)(2,1)} %refs_11_.3), channel_id=1, source_target_pairs={{0,4},{4,0},{8,12},{12,8},{1,5},{5,1},{9,13},{13,9},{2,6},{6,2},{1... | collective-permute-start | bytes 3145736 | tf_op jit(solution)/shard_map/ppermute | solution.py:322
  40.5 58.9 %collective-permute-start.7 = (bf16[4,256,256]{2,1,0:T(8,128)(2,1)}, bf16[4,256,256]{2,1,0:T(8,128)(2,1)S(1)}, u32[]{:S(2)}, u32[]{:S(2)}) collective-permute-start(bf16[4,256,256]{2,1,0:T(8,128)(2,1)} %all-to-all-done.refs_7_), channel_id=1, source_target_pairs={{0,8},{4,12},{8,0},{12,4},{1,9},{5,13},{9,1},{13,5},{2,10},{6,14},... | collective-permute-start | bytes 1572872 | tf_op jit(solution)/shard_map/ppermute | solution.py:322
  42.2 78.2 %collective-permute-start.11 = (bf16[2,256,1024]{2,1,0:T(8,128)(2,1)}, bf16[2,256,1024]{2,1,0:T(8,128)(2,1)S(1)}, u32[]{:S(2)}, u32[]{:S(2)}) collective-permute-start(bf16[2,256,1024]{2,1,0:T(8,128)(2,1)} %collective-permute-done.10.refs_13_), channel_id=1, source_target_pairs={{0,4},{4,0},{8,12},{12,8},{1,5},{5,1},{9,13},{13,9},{2,6},{6,2},{1... | collective-permute-start | bytes 3145736 | tf_op jit(solution)/shard_map/ppermute | solution.py:322
  42.3 57.1 %collective-permute-start.15 = (bf16[512,256]{1,0:T(8,128)(2,1)S(1)}, bf16[512,256]{1,0:T(8,128)(2,1)S(1)}, u32[]{:S(2)}, u32[]{:S(2)}) collective-permute-start(bf16[512,256]{1,0:T(8,128)(2,1)S(1)} %copy-done.10), channel_id=1, source_target_pairs={{0,2},{2,3},{3,1},{1,0},{4,6},{6,7},{7,5},{5,4},{8,10},{10,11},{11... | collective-permute-start | bytes 786440 | tf_op jit(solution)/shard_map/ppermute | solution.py:463
  45.3 72.9 %collective-permute-start.6 = (bf16[4,256,256]{2,1,0:T(8,128)(2,1)}, bf16[4,256,256]{2,1,0:T(8,128)(2,1)S(1)}, u32[]{:S(2)}, u32[]{:S(2)}) collective-permute-start(bf16[4,256,256]{2,1,0:T(8,128)(2,1)} %all-to-all-done.refs_7_), channel_id=1, source_target_pairs={{0,4},{4,0},{8,12},{12,8},{1,5},{5,1},{9,13},{13,9},{2,6},{6,2},{1... | collective-permute-start | bytes 1572872 | tf_op jit(solution)/shard_map/ppermute | solution.py:322
  45.5 75.0 %copy-start.11 = (bf16[2,256,1024]{2,1,0:T(8,128)(2,1)}, bf16[2,256,1024]{2,1,0:T(8,128)(2,1)S(1)}, u32[]{:S(2)}) copy-start(bf16[2,256,1024]{2,1,0:T(8,128)(2,1)S(1)} %collective-permute-done.9.refs_12_) | copy-start | bytes 3145732
  45.5 57.1 %collective-permute-start.3 = (bf16[512,256]{1,0:T(8,128)(2,1)S(1)}, bf16[512,256]{1,0:T(8,128)(2,1)S(1)}, u32[]{:S(2)}, u32[]{:S(2)}) collective-permute-start(bf16[512,256]{1,0:T(8,128)(2,1)S(1)} %get-tuple-element.18.refs_3_), channel_id=1, source_target_pairs={{0,2},{2,3},{3,1},{1,0},{4,6},{6,7},{7,5},{5,4},{8,10},{10,11},{11... | collective-permute-start | bytes 786440 | tf_op jit(solution)/shard_map/ppermute | solution.py:463
  99.4 18.9 %collective-permute-start.8 = (bf16[4,256,256]{2,1,0:T(8,128)(2,1)S(1)}, bf16[4,256,256]{2,1,0:T(8,128)(2,1)S(1)}, u32[]{:S(2)}, u32[]{:S(2)}) collective-permute-start(bf16[4,256,256]{2,1,0:T(8,128)(2,1)S(1)} %collective-permute-done.7.refs_9_), channel_id=1, source_target_pairs={{0,4},{4,0},{8,12},{12,8},{1,5},{5,1},{9,13},{13,9},{2,6},{6,2},{1... | collective-permute-start | bytes 1572872 | tf_op jit(solution)/shard_map/ppermute | solution.py:322
  99.4 9.8 %collective-permute-start.16 = (bf16[512,256]{1,0:T(8,128)(2,1)S(1)}, bf16[512,256]{1,0:T(8,128)(2,1)S(1)}, u32[]{:S(2)}, u32[]{:S(2)}) collective-permute-start(bf16[512,256]{1,0:T(8,128)(2,1)S(1)} %collective-permute-done.15.refs_4_), channel_id=1, source_target_pairs={{0,2},{2,3},{3,1},{1,0},{4,6},{6,7},{7,5},{5,4},{8,10},{10,11},{11... | collective-permute-start | bytes 786440 | tf_op jit(solution)/shard_map/ppermute | solution.py:463
  102.5 12.3 %collective-permute-start.4 = (bf16[512,256]{1,0:T(8,128)(2,1)S(1)}, bf16[512,256]{1,0:T(8,128)(2,1)S(1)}, u32[]{:S(2)}, u32[]{:S(2)}) collective-permute-start(bf16[512,256]{1,0:T(8,128)(2,1)S(1)} %collective-permute-done.3.refs_4_), channel_id=1, source_target_pairs={{0,2},{2,3},{3,1},{1,0},{4,6},{6,7},{7,5},{5,4},{8,10},{10,11},{11... | collective-permute-start | bytes 786440 | tf_op jit(solution)/shard_map/ppermute | solution.py:463
  109.2 11.2 %collective-permute-start.17 = (bf16[512,256]{1,0:T(8,128)(2,1)S(1)}, bf16[512,256]{1,0:T(8,128)(2,1)S(1)}, u32[]{:S(2)}, u32[]{:S(2)}) collective-permute-start(bf16[512,256]{1,0:T(8,128)(2,1)S(1)} %collective-permute-done.16.refs_5_), channel_id=1, source_target_pairs={{0,2},{2,3},{3,1},{1,0},{4,6},{6,7},{7,5},{5,4},{8,10},{10,11},{11... | collective-permute-start | bytes 786440 | tf_op jit(solution)/shard_map/ppermute | solution.py:463
  114.8 20.1 %collective-permute-start.5 = (bf16[512,256]{1,0:T(8,128)(2,1)S(1)}, bf16[512,256]{1,0:T(8,128)(2,1)S(1)}, u32[]{:S(2)}, u32[]{:S(2)}) collective-permute-start(bf16[512,256]{1,0:T(8,128)(2,1)S(1)} %collective-permute-done.4.refs_5_), channel_id=1, source_target_pairs={{0,2},{2,3},{3,1},{1,0},{4,6},{6,7},{7,5},{5,4},{8,10},{10,11},{11... | collective-permute-start | bytes 786440 | tf_op jit(solution)/shard_map/ppermute | solution.py:463
  131.5 14.1 %collective-permute-start.18 = (bf16[512,256]{1,0:T(8,128)(2,1)}, bf16[512,256]{1,0:T(8,128)(2,1)S(1)}, u32[]{:S(2)}, u32[]{:S(2)}) collective-permute-start(bf16[512,256]{1,0:T(8,128)(2,1)} %get-tuple-element.25), channel_id=1, source_target_pairs={{0,2},{2,3},{3,1},{1,0},{4,6},{6,7},{7,5},{5,4},{8,10},{10,11},{11... | collective-permute-start | bytes 786440 | tf_op jit(solution)/shard_map/ppermute | solution.py:522
  144.9 9.4 %collective-permute-start.12 = (bf16[512,256]{1,0:T(8,128)(2,1)}, bf16[512,256]{1,0:T(8,128)(2,1)S(1)}, u32[]{:S(2)}, u32[]{:S(2)}) collective-permute-start(bf16[512,256]{1,0:T(8,128)(2,1)} %get-tuple-element.20), channel_id=1, source_target_pairs={{0,2},{2,3},{3,1},{1,0},{4,6},{6,7},{7,5},{5,4},{8,10},{10,11},{11... | collective-permute-start | bytes 786440 | tf_op jit(solution)/shard_map/ppermute | solution.py:522
  145.7 14.2 %collective-permute-start.19 = (bf16[512,256]{1,0:T(8,128)(2,1)S(1)}, bf16[512,256]{1,0:T(8,128)(2,1)S(1)}, u32[]{:S(2)}, u32[]{:S(2)}) collective-permute-start(bf16[512,256]{1,0:T(8,128)(2,1)S(1)} %shard_map.110), channel_id=1, source_target_pairs={{0,2},{2,3},{3,1},{1,0},{4,6},{6,7},{7,5},{5,4},{8,10},{10,11},{11... | collective-permute-start | bytes 786440 | tf_op jit(solution)/shard_map/ppermute | solution.py:522
  155.3 10.2 %collective-permute-start.13 = (bf16[512,256]{1,0:T(8,128)(2,1)S(1)}, bf16[512,256]{1,0:T(8,128)(2,1)S(1)}, u32[]{:S(2)}, u32[]{:S(2)}) collective-permute-start(bf16[512,256]{1,0:T(8,128)(2,1)S(1)} %shard_map.106), channel_id=1, source_target_pairs={{0,2},{2,3},{3,1},{1,0},{4,6},{6,7},{7,5},{5,4},{8,10},{10,11},{11... | collective-permute-start | bytes 786440 | tf_op jit(solution)/shard_map/ppermute | solution.py:522
  160.0 11.2 %collective-permute-start.20 = (bf16[512,256]{1,0:T(8,128)(2,1)S(1)}, bf16[512,256]{1,0:T(8,128)(2,1)S(1)}, u32[]{:S(2)}, u32[]{:S(2)}) collective-permute-start(bf16[512,256]{1,0:T(8,128)(2,1)S(1)} %shard_map.111), channel_id=1, source_target_pairs={{0,2},{2,3},{3,1},{1,0},{4,6},{6,7},{7,5},{5,4},{8,10},{10,11},{11... | collective-permute-start | bytes 786440 | tf_op jit(solution)/shard_map/ppermute | solution.py:522
  166.5 8.0 %collective-permute-start.14 = (bf16[512,256]{1,0:T(8,128)(2,1)S(1)}, bf16[512,256]{1,0:T(8,128)(2,1)S(1)}, u32[]{:S(2)}, u32[]{:S(2)}) collective-permute-start(bf16[512,256]{1,0:T(8,128)(2,1)S(1)} %shard_map.107), channel_id=1, source_target_pairs={{0,2},{2,3},{3,1},{1,0},{4,6},{6,7},{7,5},{5,4},{8,10},{10,11},{11... | collective-permute-start | bytes 786440 | tf_op jit(solution)/shard_map/ppermute | solution.py:522
  (21 other events, 294.5 us)

commit v3 on v2

--- a/solution.py
+++ b/solution.py
@@ -233,29 +233,54 @@
     gated_hbm = refs[3 : 3 + n_tensor]
     at = 3 + n_tensor
     out_pieces = refs[at : at + n_dp]
-    ffn_pieces = refs[at + n_dp : at + 2 * n_dp]
-    at += 2 * n_dp
+    at += n_dp
+    pairs = refs[at : at + 2]
+    near = refs[at + 2 : at + n_dp]
+    far = refs[at + n_dp : at + 2 * n_dp - 2]
+    at += 2 * n_dp - 2
     own_hbm, *part_hbm = refs[at : at + n_tensor]
-    wo_ref, up_ref, down_ref, res_ref, gated, own_ref, part_ref = refs[at + n_tensor : -3]
+    wo_ref, ffn_ref, res_ref, gated, own_ref, part_ref, hid_ref, act_ref = refs[
+        at + n_tensor : -3
+    ]
     sems, gated_sems, done_sems = refs[-3:]
     rows, width = own_ref.shape
-    me = ids_ref[0]
-    out_copies = piece_copies(out_pieces, wo_ref, sems.at[0], me, lambda piece: piece)
-    up_copies = piece_copies(ffn_pieces, up_ref, sems.at[1], me, lambda piece: piece.at[0])
-    down_copies = piece_copies(ffn_pieces, down_ref, sems.at[2], me, lambda piece: piece.at[1])
+    me, group = ids_ref[0], ids_ref[2 + n_tensor]
+    out_copies = piece_copies(
+        out_pieces, wo_ref, sems.at[0], me, lambda piece: piece.at[:, pl.ds(0, wo_ref.shape[1] // n_dp)]
+    )
+    depth = ffn_ref.shape[1] // n_dp
+
+    def ffn_copy(source, half, k):
+        start = pl.multiple_of(jnp.bitwise_xor(me, k) * depth, depth)
+        return pltpu.make_async_copy(
+            source, ffn_ref.at[half, pl.ds(start, depth)], sems.at[1 + half, k]
+        )
+
+    up_copies = [ffn_copy(pairs[k].at[0], 0, k) for k in range(2)]
+    down_copies = [ffn_copy(pairs[k].at[1], 1, k) for k in range(2)]
+    rest = []
+    for k in range(2, n_dp):
+        rest.append(ffn_copy(near[k - 2], group, k))
+        rest.append(ffn_copy(far[k - 2], 1 - group, k))
+        up_copies.append(ffn_copy(near[k - 2], 0, k))
+        down_copies.append(ffn_copy(near[k - 2], 1, k))
     gated_copies = [
         pltpu.make_async_copy(source, gated.at[k], gated_sems.at[k])
         for k, source in enumerate(gated_hbm)
     ]
-    for copy in gated_copies + out_copies + up_copies + down_copies:
-        copy.start()
-    for copy in gated_copies + out_copies:
-        copy.wait()
     done_copies = [pltpu.make_async_copy(own_ref, own_hbm, done_sems.at[0])]
     for k in range(1, n_tensor):
         done_copies.append(
             pltpu.make_async_copy(part_ref.at[k - 1], part_hbm[k - 1], done_sems.at[k])
         )
+    for copy in out_copies + gated_copies:
+        copy.start()
+    for copy in up_copies[:2] + rest:
+        copy.start()
+    for copy in out_copies + gated_copies:
+        copy.wait()
+    for copy in down_copies[:2]:
+        copy.start()
     for r in range(0, rows, block):
         span = slice(r, r + block)
         attended = dot_nt(gated[0, span], wo_ref[ids_ref[2]])
@@ -263,29 +288,26 @@
             attended += dot_nt(gated[k, span], wo_ref[ids_ref[2 + k]])
         residual = tok_ref[base + r : base + r + block].astype(jnp.float32) + attended
         res_ref[span] = residual
-        hidden = rms_scale(residual, small_ref[1:2, :])
-        if r == 0:
-            for copy in up_copies:
-                copy.wait()
-        activated = jax.nn.gelu(dot_nn(hidden, up_ref[...]), approximate=True)
-        activated = activated.astype(jnp.bfloat16)
-        if r == 0:
-            for copy in down_copies:
-                copy.wait()
-        final = r + block == rows
-
-        def term(k):
-            start = pl.multiple_of(ids_ref[2 + k] * width, width)
-            return dot_nt(activated, down_ref[pl.ds(start, width), :])
-
-        for k in range(1, n_tensor):
-            part_ref[k - 1, span] = term(k).astype(jnp.bfloat16)
-            if final:
-                done_copies[k].start()
-        mine = pl.ds(pl.multiple_of(ids_ref[1] * width, width), width)
-        own_ref[span] = res_ref[span, mine] + term(0)
-        if final:
-            done_copies[0].start()
+        hid_ref[span] = rms_scale(residual, small_ref[1:2, :])
+    for copy in up_copies:
+        copy.wait()
+    for r in range(0, rows, block):
+        span = slice(r, r + block)
+        activated = jax.nn.gelu(dot_nn(hid_ref[span], ffn_ref[0]), approximate=True)
+        act_ref[span] = activated.astype(jnp.bfloat16)
+    for copy in down_copies:
+        copy.wait()
+
+    def term(k):
+        start = pl.multiple_of(ids_ref[2 + k] * width, width)
+        return dot_nt(act_ref[...], ffn_ref[1, pl.ds(start, width), :])
+
+    mine = pl.ds(pl.multiple_of(ids_ref[1] * width, width), width)
+    own_ref[...] = res_ref[:, mine] + term(0)
+    done_copies[0].start()
+    for k in list(range(2, n_tensor)) + [1]:
+        part_ref[k - 1] = term(k).astype(jnp.bfloat16)
+        done_copies[k].start()
     for copy in done_copies:
         copy.wait()
 
@@ -310,12 +332,12 @@
     copy.wait()
 
 
-def xor_gather(value, axis):
+def xor_gather(value, axis, last_bit=1):
     pieces = [value]
     size = lax.axis_size(axis)
     bit = size // 2
     order = [0]
-    while bit:
+    while bit >= last_bit:
         pairs = [(i, i ^ bit) for i in range(size)]
         arrived = []
         for piece in pieces:
@@ -323,7 +345,7 @@
         pieces = pieces + arrived
         order = order + [k ^ bit for k in order]
         bit //= 2
-    return [pieces[order.index(k)] for k in range(size)]
+    return [pieces[order.index(k)] for k in range(0, size, last_bit)]
 
 
 def ring_order(size):
@@ -398,23 +420,28 @@
     target_dev = new_slot // sessions_here
     session_ids = jnp.arange(sessions_here, dtype=jnp.int32)
     proj_rows = attn_weights.shape[1]
+    proj_pieces = xor_gather(attn_weights[:4].reshape(-1, cols_here), "dp")
     notes = jnp.stack([jnp.where(survive, target_dev, -1), new_slot % sessions_here])
-    notes = jnp.pad(notes.astype(bf16), ((0, 6), (0, cols_here - sessions_here)))
-    proj_own = jnp.concatenate([attn_weights[:4].reshape(4 * proj_rows, cols_here), notes])
-    proj_pieces = xor_gather(proj_own, "dp")
+    note_rows = 16
+    notes = jnp.pad(
+        notes.astype(bf16), ((0, note_rows - 2), (0, cols_here - sessions_here))
+    )
     out_own = lax.all_to_all(
-        jnp.broadcast_to(attn_weights[4:], (n_tensor, proj_rows, cols_here)),
+        jnp.broadcast_to(
+            jnp.concatenate([attn_weights[4], notes])[None],
+            (n_tensor, proj_rows + note_rows, cols_here),
+        ),
         "tensor",
         split_axis=0,
         concat_axis=0,
         tiled=True,
     )
+    half_own = lax.dynamic_index_in_dim(ffn_weights, lax.axis_index("group"), 0, keepdims=False)
     sources = jnp.array(ring_sources(n_tensor), jnp.int32)[tensor_at]
-    ids = jnp.concatenate([jnp.stack([dp_at, tensor_at]).astype(jnp.int32), sources])
-
-    meta = jnp.stack([piece[4 * proj_rows :, :sessions_here] for piece in proj_pieces])
-    meta = meta.astype(jnp.int32)
-    from_dev = jnp.bitwise_xor(dp_at, jnp.arange(n_dp, dtype=jnp.int32))
+    places = jnp.stack([dp_at, tensor_at]).astype(jnp.int32)
+    ids = jnp.concatenate([places, sources, lax.axis_index("group").astype(jnp.int32)[None]])
+    out_pieces = xor_gather(out_own, "dp")
+
     earlier = (
         (target_dev[None, :] == target_dev[:, None])
         & survive[None, :]
@@ -422,13 +449,15 @@
     )
     pair_rank = jnp.sum(earlier.astype(jnp.int32), axis=1)
     send_pos = jnp.where(survive, target_dev * pair_cap + pair_rank, -1)
+    meta = jnp.stack([piece[0, proj_rows:, :sessions_here] for piece in out_pieces])
+    meta = meta.astype(jnp.int32)
+    from_dev = jnp.bitwise_xor(dp_at, jnp.arange(n_dp, dtype=jnp.int32))
     coming = meta[:, 0] == dp_at
     ahead = coming[:, None, :] & (session_ids[None, None, :] < session_ids[None, :, None])
     rank_all = jnp.sum(ahead.astype(jnp.int32), axis=2)
     from_pos = from_dev[:, None] * pair_cap + rank_all + 1
     lands = meta[:, 1][None] == session_ids[:, None, None]
     recv_src = jnp.sum(jnp.where(lands & coming[None], from_pos[None], 0), axis=(1, 2)) - 1
-    send_pos, recv_src = lax.optimization_barrier((send_pos, recv_src))
 
     rows_shape = shape_of((chunk_rows, cols_here), bf16)
     decay_shape = pltpu.VMEM((heads_here, block, block), f32)
@@ -437,6 +466,7 @@
         [norm_gains, jnp.broadcast_to(head_decay[:, None], (heads_here, width))]
     )
     chunk_sessions = chunk_rows // event_count
+    split = (width // n_dp) % 128 == 0
     gated, keys, values = [], [], []
     for c in range(CHUNKS):
         g, k, v = kernel_call(
@@ -450,7 +480,7 @@
                 decay_shape,
                 pltpu.VMEM((chunk_rows, cols_here), bf16),
                 pltpu.VMEM((chunk_rows, cols_here), bf16),
-                pltpu.VMEM((4, width, cols_here), bf16),
+                pltpu.VMEM((4, 16 if split else width, cols_here), bf16),
                 pltpu.SemaphoreType.DMA((3,)),
             ],
             2 * chunk_rows * width * cols_here * 4,
@@ -462,8 +492,20 @@
         for c in range(CHUNKS):
             gated[c].append(lax.ppermute(gated[c][-1], "tensor", ring))
 
-    out_pieces = xor_gather(out_own, "dp")
-    ffn_pieces = xor_gather(ffn_weights, "dp")
+    near = xor_gather(half_own, "dp", last_bit=2)[1:]
+    swap = [(0, 1), (1, 0)]
+    far = []
+    for k, piece in enumerate(near):
+        far.append(lax.ppermute(piece, "group", swap))
+    beside = [(i, i ^ 1) for i in range(n_dp)]
+
+    def to_beside(value):
+        return lax.ppermute(value, "dp", beside)
+
+    ffn_pieces = [ffn_weights, to_beside(ffn_weights)]
+    for side in (near, far):
+        for k, piece in enumerate(side):
+            ffn_pieces += [piece, to_beside(piece)]
     packed = kernel_call(
         functools.partial(state_kernel, CHUNKS, heads_here, event_count),
         [vmem_spec(), smem_spec()] + [hbm_spec()] * (1 + 2 * CHUNKS),
@@ -485,18 +527,19 @@
     for c in range(CHUNKS):
         own, *part = kernel_call(
             functools.partial(feed_kernel, n_dp, n_tensor, block, c * chunk_rows),
-            [smem_spec()] + [vmem_spec()] * 2 + [hbm_spec()] * (n_tensor + 2 * n_dp),
+            [smem_spec()] + [vmem_spec()] * 2 + [hbm_spec()] * (n_tensor + n_dp + 2 * n_dp - 2),
             [hbm_spec()] * n_tensor,
             [pltpu.HBM((chunk_rows, share), f32)]
             + [pltpu.HBM((chunk_rows, share), bf16)] * (n_tensor - 1),
             [
                 pltpu.VMEM((n_tensor, width, cols_here), bf16),
-                pltpu.VMEM((width, units_here), bf16),
-                pltpu.VMEM((width, units_here), bf16),
+                pltpu.VMEM((2, width, units_here), bf16),
                 pltpu.VMEM((chunk_rows, width), f32),
                 pltpu.VMEM((n_tensor, chunk_rows, cols_here), bf16),
                 pltpu.VMEM((chunk_rows, share), f32),
                 pltpu.VMEM((n_tensor - 1, chunk_rows, share), bf16),
+                pltpu.VMEM((chunk_rows, width), bf16),
+                pltpu.VMEM((chunk_rows, units_here), bf16),
                 pltpu.SemaphoreType.DMA((3, n_dp)),
                 pltpu.SemaphoreType.DMA((n_tensor,)),
                 pltpu.SemaphoreType.DMA((n_tensor,)),

time: 181 us -> 184 us (1.017)
  local copies, waits for them, and re-layouts: 9.46 us -> 12.6 us
    ppermute x0 -> x4, waiting for transfers between devices: none -> 9.98 us  [the longest x1 9.97 us: per_device(): far.append(lax.ppermute(piece, 'group', swap))]
    ppermute x9 -> x7, waiting for transfers between devices: 55.7 us -> 46.7 us  [xor_gather(): arrived.append(lax.ppermute(piece, axis, pairs))]
    squeeze x0 -> x2, local copies, waits for them, and re-layouts: none -> 2.78 us  [the longest x1 1.87 us: per_device(): lax.dynamic_index_in_dim(ffn_weights, lax.axis_index('group'), 0, keepdim...]
    slice x1 -> x5, local copies, waits for them, and re-layouts: 1.23 us -> 3.95 us  [the longest x4 2.72 us: per_device(): piece[0, proj_rows:, :sessions_here]]
    ppermute x6, waiting for transfers between devices: 19.3 us -> 17.1 us  [per_device(): sums[c] = lax.ppermute(mine, 'tensor', ring)]
    ppermute x6, waiting for transfers between devices: 9.57 us -> 11.6 us  [per_device(): gated[c].append(lax.ppermute(gated[c][-1], 'tensor', ring))]
    ppermute x0 -> x4, starting transfers between devices: none -> 1.95 us  [the longest x1 1.52 us: per_device(): far.append(lax.ppermute(piece, 'group', swap))]
    unnamed x45 -> x51, local copies, waits for them, and re-layouts: 4.31 us -> 4.15 us
  transfers between devices with their start and end apart: 23 -> 25, of which waited for: 11 -> 13; matrix products, arithmetic and copies ran while one was open for 3% -> 5% of each run, Pallas kernels for 20% -> 19%
where the time goes in v3:
time: 184 us; the launch traced here: 183 us
  waiting for transfers between devices  85.4 us (46%)
  starting transfers between devices  43.9 us (24%)
  Pallas kernels  38.4 us (21%)
  local copies, waits for them, and re-layouts  12.6 us (7%)
    ppermute x7, waiting for transfers between devices, xor_gather(): arrived.append(lax.ppermute(piece, axis, pairs))  46.7 us
    pallas_call x2, Pallas kernels, per_device(): kernel_call(functools.partial(feed_kernel, n_dp, n_tensor, block, c * chu...  17.2 us
    ppermute x6, waiting for transfers between devices, per_device(): sums[c] = lax.ppermute(mine, 'tensor', ring)  17.1 us
    ppermute x6, starting transfers between devices, per_device(): gated[c].append(lax.ppermute(gated[c][-1], 'tensor', ring))  16.7 us
    ppermute x6, waiting for transfers between devices, per_device(): gated[c].append(lax.ppermute(gated[c][-1], 'tensor', ring))  11.6 us
    ppermute x1, waiting for transfers between devices, per_device(): far.append(lax.ppermute(piece, 'group', swap))  9.97 us
    ppermute x6, starting transfers between devices, per_device(): sums[c] = lax.ppermute(mine, 'tensor', ring)  9.46 us
    pallas_call x2, Pallas kernels, per_device(): kernel_call(functools.partial(project_kernel, n_dp, heads_here, event_cou...  9.27 us
  transfers between devices with their start and end apart: 25, of which 13 were waited for; matrix products, arithmetic and copies ran while one was open for 5% of the time, Pallas kernels for 19%

profile of v3, /device:TPU:0, one launch (start us, length us, event | category | flops | bytes accessed | tf_op | source)
XLA Modules:
  0.0 182.9 jit_solution(14974658589968868950)
XLA Ops:
  1.9 3.0 %collective-permute-start.1 = (bf16[1024,256]{1,0:T(8,128)(2,1)S(1)}, bf16[1024,256]{1,0:T(8,128)(2,1)S(1)}, u32[]{:S(2)}, u32[]{:S(2)}) collective-permute-start(bf16[1024,256]{1,0:T(8,128)(2,1)S(1)} %bitcast.18), channel_id=1, source_target_pairs={{0,8},{4,12},{8,0},{12,4},{1,9},{5,13},{9,1},{13,5},{2,10},{6,14},... | collective-permute-start | bytes 1572872 | tf_op jit(solution)/shard_map/ppermute | solution.py:344
  7.4 4.9 %all-to-all-start = ((bf16[4,272,256]{2,1,0:T(8,128)(2,1)}), bf16[4,272,256]{2,1,0:T(8,128)(2,1)}, u32[]{:S(2)}, u32[]{:S(2)}) async-start(bf16[4,272,256]{2,1,0:T(8,128)(2,1)} %broadcast_in_dim.19), calls=%async_computation | async-start | bytes 1114112 | tf_op jit(solution)/shard_map/all_to_all | solution.py:429
  18.8 4.6 %shard_map.108 = (bf16[512,256]{1,0:T(8,128)(2,1)S(1)}, bf16[512,256]{1,0:T(8,128)(2,1)}, bf16[512,256]{1,0:T(8,128)(2,1)}) custom-call(s32[7]{0:T(128)S(1)} %pad_add_fusion.refs_0_, f32[4,1024]{1,0:T(4,128)S(1)} %pad_maximum_fusion.1.refs_1_.refs_0_, bf16[1024,1024]{1,0:T(8,128)(2,1)S(1)} %copy-done, f32[32,2,128,128]{3,2,1,0:T(8,128)} %refs_2_.9, ...), custom_call_target="tpu_custom_call" | custom-call | flops 1073741824 | bytes 4194304 | tf_op jit(solution)/shard_map/pallas_call | solution.py:472
  23.4 4.7 %shard_map.104 = (bf16[512,256]{1,0:T(8,128)(2,1)S(1)}, bf16[512,256]{1,0:T(8,128)(2,1)}, bf16[512,256]{1,0:T(8,128)(2,1)}) custom-call(s32[7]{0:T(128)S(1)} %pad_add_fusion.refs_0_, f32[4,1024]{1,0:T(4,128)S(1)} %pad_maximum_fusion.1.refs_1_.refs_0_, bf16[1024,1024]{1,0:T(8,128)(2,1)S(1)} %copy-done, f32[32,2,128,128]{3,2,1,0:T(8,128)} %refs_2_.9, ...), custom_call_target="tpu_custom_call" | custom-call | flops 1073741824 | bytes 4194304 | tf_op jit(solution)/shard_map/pallas_call | solution.py:472
  28.1 4.7 %shard_map.112 = bf16[64,2,128,128]{3,2,1,0:T(8,128)(2,1)} custom-call(f32[4,1024]{1,0:T(4,128)S(1)} %pad_maximum_fusion.1.refs_1_.refs_0_, s32[32]{0:T(128)S(1)} %add_select_fusion.refs_1_, f32[32,2,128,128]{3,2,1,0:T(8,128)} %refs_2_.9, bf16[512,256]{1,0:T(8,128)(2,1)} %get-tuple-element.26.refs_3_, bf16[512,256]{1,0:T(8,128)(2,1)} %get-tuple-element.27.refs_4_, ...), custom_call_target="tpu_custom_call" | custom-call | flops 67108864 | bytes 4194304 | tf_op jit(solution)/shard_map/pallas_call | solution.py:509
  32.8 5.0 %all-to-all-start.1 = ((bf16[64,2,128,128]{3,2,1,0:T(8,128)(2,1)}), bf16[64,2,128,128]{3,2,1,0:T(8,128)(2,1)}, u32[]{:S(2)}, u32[]{:S(2)}) async-start(bf16[64,2,128,128]{3,2,1,0:T(8,128)(2,1)} %shard_map.112), calls=%async_computation.1 | async-start | bytes 8388608 | tf_op jit(solution)/shard_map/all_to_all | solution.py:524
  37.9 2.4 %collective-permute-start.7 = (bf16[4,272,256]{2,1,0:T(8,128)(2,1)}, bf16[4,272,256]{2,1,0:T(8,128)(2,1)S(1)}, u32[]{:S(2)}, u32[]{:S(2)}) collective-permute-start(bf16[4,272,256]{2,1,0:T(8,128)(2,1)} %all-to-all-done.refs_7_), channel_id=1, source_target_pairs={{0,8},{4,12},{8,0},{12,4},{1,9},{5,13},{9,1},{13,5},{2,10},{6,14},... | collective-permute-start | bytes 1671176 | tf_op jit(solution)/shard_map/ppermute | solution.py:344
  41.8 2.4 %collective-permute-start.17 = (bf16[512,256]{1,0:T(8,128)(2,1)S(1)}, bf16[512,256]{1,0:T(8,128)(2,1)S(1)}, u32[]{:S(2)}, u32[]{:S(2)}) collective-permute-start(bf16[512,256]{1,0:T(8,128)(2,1)S(1)} %copy-done.10), channel_id=1, source_target_pairs={{0,2},{2,3},{3,1},{1,0},{4,6},{6,7},{7,5},{5,4},{8,10},{10,11},{11... | collective-permute-start | bytes 786440 | tf_op jit(solution)/shard_map/ppermute | solution.py:493
  44.2 10.0 %collective-permute-done.12.refs_15_ = bf16[256,1024]{1,0:T(8,128)(2,1)S(1)} collective-permute-done((bf16[256,1024]{1,0:T(8,128)(2,1)}, bf16[256,1024]{1,0:T(8,128)(2,1)S(1)}, u32[]{:S(2)}, u32[]{:S(2)}) %collective-permute-start.12) | collective-permute-done | bytes 524320 | tf_op jit(solution)/shard_map/ppermute | solution.py:499
  54.2 44.1 %collective-permute-done.7.refs_9_ = bf16[4,272,256]{2,1,0:T(8,128)(2,1)S(1)} collective-permute-done((bf16[4,272,256]{2,1,0:T(8,128)(2,1)}, bf16[4,272,256]{2,1,0:T(8,128)(2,1)S(1)}, u32[]{:S(2)}, u32[]{:S(2)}) %collective-permute-start.7) | collective-permute-done | bytes 557088 | tf_op jit(solution)/shard_map/ppermute | solution.py:344
  98.3 2.5 %collective-permute-start.3 = (bf16[512,256]{1,0:T(8,128)(2,1)S(1)}, bf16[512,256]{1,0:T(8,128)(2,1)S(1)}, u32[]{:S(2)}, u32[]{:S(2)}) collective-permute-start(bf16[512,256]{1,0:T(8,128)(2,1)S(1)} %get-tuple-element.16.refs_3_), channel_id=1, source_target_pairs={{0,2},{2,3},{3,1},{1,0},{4,6},{6,7},{7,5},{5,4},{8,10},{10,11},{11... | collective-permute-start | bytes 786440 | tf_op jit(solution)/shard_map/ppermute | solution.py:493
  102.6 4.9 %collective-permute-done.3.refs_4_ = bf16[512,256]{1,0:T(8,128)(2,1)S(1)} collective-permute-done((bf16[512,256]{1,0:T(8,128)(2,1)S(1)}, bf16[512,256]{1,0:T(8,128)(2,1)S(1)}, u32[]{:S(2)}, u32[]{:S(2)}) %collective-permute-start.3) | collective-permute-done | bytes 262176 | tf_op jit(solution)/shard_map/ppermute | solution.py:493
  107.5 3.4 %collective-permute-start.4 = (bf16[512,256]{1,0:T(8,128)(2,1)S(1)}, bf16[512,256]{1,0:T(8,128)(2,1)S(1)}, u32[]{:S(2)}, u32[]{:S(2)}) collective-permute-start(bf16[512,256]{1,0:T(8,128)(2,1)S(1)} %collective-permute-done.3.refs_4_), channel_id=1, source_target_pairs={{0,2},{2,3},{3,1},{1,0},{4,6},{6,7},{7,5},{5,4},{8,10},{10,11},{11... | collective-permute-start | bytes 786440 | tf_op jit(solution)/shard_map/ppermute | solution.py:493
  110.9 2.2 %collective-permute-done.18.refs_5_ = bf16[512,256]{1,0:T(8,128)(2,1)S(1)} collective-permute-done((bf16[512,256]{1,0:T(8,128)(2,1)S(1)}, bf16[512,256]{1,0:T(8,128)(2,1)S(1)}, u32[]{:S(2)}, u32[]{:S(2)}) %collective-permute-start.18) | collective-permute-done | bytes 262176 | tf_op jit(solution)/shard_map/ppermute | solution.py:493
  113.1 3.4 %collective-permute-start.19 = (bf16[512,256]{1,0:T(8,128)(2,1)S(1)}, bf16[512,256]{1,0:T(8,128)(2,1)S(1)}, u32[]{:S(2)}, u32[]{:S(2)}) collective-permute-start(bf16[512,256]{1,0:T(8,128)(2,1)S(1)} %collective-permute-done.18.refs_5_), channel_id=1, source_target_pairs={{0,2},{2,3},{3,1},{1,0},{4,6},{6,7},{7,5},{5,4},{8,10},{10,11},{11... | collective-permute-start | bytes 786440 | tf_op jit(solution)/shard_map/ppermute | solution.py:493
  118.8 3.4 %collective-permute-start.5 = (bf16[512,256]{1,0:T(8,128)(2,1)S(1)}, bf16[512,256]{1,0:T(8,128)(2,1)S(1)}, u32[]{:S(2)}, u32[]{:S(2)}) collective-permute-start(bf16[512,256]{1,0:T(8,128)(2,1)S(1)} %collective-permute-done.4.refs_5_), channel_id=1, source_target_pairs={{0,2},{2,3},{3,1},{1,0},{4,6},{6,7},{7,5},{5,4},{8,10},{10,11},{11... | collective-permute-start | bytes 786440 | tf_op jit(solution)/shard_map/ppermute | solution.py:493
  125.9 8.6 %shard_map.109 = (f32[512,256]{1,0:T(8,128)}, bf16[512,256]{1,0:T(8,128)(2,1)}, bf16[512,256]{1,0:T(8,128)(2,1)}, bf16[512,256]{1,0:T(8,128)(2,1)}) custom-call(s32[7]{0:T(128)S(1)} %pad_add_fusion.refs_0_, f32[4,1024]{1,0:T(4,128)S(1)} %pad_maximum_fusion.1.refs_1_.refs_0_, bf16[1024,1024]{1,0:T(8,128)(2,1)S(1)} %copy-done, bf16[512,256]{1,0:T(8,128)(2,1)} %copy-done.9, ...), custom_call_target="tpu_custom_call" | custom-call | flops 3221225472 | bytes 4194304 | tf_op jit(solution)/shard_map/pallas_call | solution.py:528
  134.5 3.4 %collective-permute-start.20 = (bf16[512,256]{1,0:T(8,128)(2,1)}, bf16[512,256]{1,0:T(8,128)(2,1)S(1)}, u32[]{:S(2)}, u32[]{:S(2)}) collective-permute-start(bf16[512,256]{1,0:T(8,128)(2,1)} %get-tuple-element.23), channel_id=1, source_target_pairs={{0,2},{2,3},{3,1},{1,0},{4,6},{6,7},{7,5},{5,4},{8,10},{10,11},{11... | collective-permute-start | bytes 786440 | tf_op jit(solution)/shard_map/ppermute | solution.py:565
  138.7 8.6 %shard_map.105 = (f32[512,256]{1,0:T(8,128)}, bf16[512,256]{1,0:T(8,128)(2,1)}, bf16[512,256]{1,0:T(8,128)(2,1)}, bf16[512,256]{1,0:T(8,128)(2,1)}) custom-call(s32[7]{0:T(128)S(1)} %pad_add_fusion.refs_0_, f32[4,1024]{1,0:T(4,128)S(1)} %pad_maximum_fusion.1.refs_1_.refs_0_, bf16[1024,1024]{1,0:T(8,128)(2,1)S(1)} %copy-done, bf16[512,256]{1,0:T(8,128)(2,1)} %copy-done.8, ...), custom_call_target="tpu_custom_call" | custom-call | flops 3221225472 | bytes 4194304 | tf_op jit(solution)/shard_map/pallas_call | solution.py:528
  152.3 4.4 %collective-permute-done.14.a_ref = bf16[512,256]{1,0:T(8,128)(2,1)S(1)} collective-permute-done((bf16[512,256]{1,0:T(8,128)(2,1)}, bf16[512,256]{1,0:T(8,128)(2,1)S(1)}, u32[]{:S(2)}, u32[]{:S(2)}) %collective-permute-start.14) | collective-permute-done | bytes 262176 | tf_op jit(solution)/shard_map/ppermute | solution.py:565
  159.2 3.2 %collective-permute-done.21.a_ref = bf16[512,256]{1,0:T(8,128)(2,1)S(1)} collective-permute-done((bf16[512,256]{1,0:T(8,128)(2,1)S(1)}, bf16[512,256]{1,0:T(8,128)(2,1)S(1)}, u32[]{:S(2)}, u32[]{:S(2)}) %collective-permute-start.21) | collective-permute-done | bytes 262176 | tf_op jit(solution)/shard_map/ppermute | solution.py:565
  163.8 4.2 %collective-permute-done.15.a_ref = bf16[512,256]{1,0:T(8,128)(2,1)S(1)} collective-permute-done((bf16[512,256]{1,0:T(8,128)(2,1)S(1)}, bf16[512,256]{1,0:T(8,128)(2,1)S(1)}, u32[]{:S(2)}, u32[]{:S(2)}) %collective-permute-start.15) | collective-permute-done | bytes 262176 | tf_op jit(solution)/shard_map/ppermute | solution.py:565
  170.5 3.1 %collective-permute-done.22.refs_2_ = bf16[512,256]{1,0:T(8,128)(2,1)S(1)} collective-permute-done((bf16[512,256]{1,0:T(8,128)(2,1)S(1)}, bf16[512,256]{1,0:T(8,128)(2,1)S(1)}, u32[]{:S(2)}, u32[]{:S(2)}) %collective-permute-start.22) | collective-permute-done | bytes 262176 | tf_op jit(solution)/shard_map/ppermute | solution.py:565
  178.4 4.3 %unpack.1 = f32[32,2,128,128]{3,2,1,0:T(8,128)} custom-call(s32[32]{0:T(128)S(1)} %broadcast_add_fusion.src_ref, bf16[64,2,128,128]{3,2,1,0:T(8,128)(2,1)} %all-to-all-done.1.recv_ref), custom_call_target="tpu_custom_call" | custom-call | bytes 6291456 | tf_op jit(solution)/shard_map/unpack/pallas_call | solution.py:590
  (116 shorter events, 36.3 us)
Async XLA Ops:
  1.9 15.0 %collective-permute-start.1 = (bf16[1024,256]{1,0:T(8,128)(2,1)S(1)}, bf16[1024,256]{1,0:T(8,128)(2,1)S(1)}, u32[]{:S(2)}, u32[]{:S(2)}) collective-permute-start(bf16[1024,256]{1,0:T(8,128)(2,1)S(1)} %bitcast.18), channel_id=1, source_target_pairs={{0,8},{4,12},{8,0},{12,4},{1,9},{5,13},{9,1},{13,5},{2,10},{6,14},... | collective-permute-start | bytes 1572872 | tf_op jit(solution)/shard_map/ppermute | solution.py:344
  4.9 12.1 %collective-permute-start = (bf16[1024,256]{1,0:T(8,128)(2,1)S(1)}, bf16[1024,256]{1,0:T(8,128)(2,1)}, u32[]{:S(2)}, u32[]{:S(2)}) collective-permute-start(bf16[1024,256]{1,0:T(8,128)(2,1)S(1)} %bitcast.19), channel_id=1, source_target_pairs={{0,4},{4,0},{8,12},{12,8},{1,5},{5,1},{9,13},{13,9},{2,6},{6,2},{1... | collective-permute-start | bytes 1572872 | tf_op jit(solution)/shard_map/ppermute | solution.py:344
  7.4 25.4 %all-to-all-start = ((bf16[4,272,256]{2,1,0:T(8,128)(2,1)}), bf16[4,272,256]{2,1,0:T(8,128)(2,1)}, u32[]{:S(2)}, u32[]{:S(2)}) async-start(bf16[4,272,256]{2,1,0:T(8,128)(2,1)} %broadcast_in_dim.19), calls=%async_computation | async-start | bytes 1114112 | tf_op jit(solution)/shard_map/all_to_all | solution.py:429
  12.3 88.5 %collective-permute-start.9 = (bf16[2,256,1024]{2,1,0:T(8,128)(2,1)}, bf16[2,256,1024]{2,1,0:T(8,128)(2,1)}, u32[]{:S(2)}, u32[]{:S(2)}) collective-permute-start(bf16[2,256,1024]{2,1,0:T(8,128)(2,1)} %refs_11_.3), channel_id=1, source_target_pairs={{0,4},{4,0},{8,12},{12,8},{1,5},{5,1},{9,13},{13,9},{2,6},{6,2},{1... | collective-permute-start | bytes 3145736 | tf_op jit(solution)/shard_map/ppermute | solution.py:503
  14.4 25.8 %collective-permute-start.10 = (bf16[256,1024]{1,0:T(8,128)(2,1)}, bf16[256,1024]{1,0:T(8,128)(2,1)}, u32[]{:S(2)}, u32[]{:S(2)}) collective-permute-start(bf16[256,1024]{1,0:T(8,128)(2,1)} %dynamic-slice_bitcast_fusion), channel_id=1, source_target_pairs={{0,8},{4,12},{8,0},{12,4},{1,9},{5,13},{9,1},{13,5},{2,10},{6,14},... | collective-permute-start | bytes 1572872 | tf_op jit(solution)/shard_map/ppermute | solution.py:344
  32.8 145.6 %all-to-all-start.1 = ((bf16[64,2,128,128]{3,2,1,0:T(8,128)(2,1)}), bf16[64,2,128,128]{3,2,1,0:T(8,128)(2,1)}, u32[]{:S(2)}, u32[]{:S(2)}) async-start(bf16[64,2,128,128]{3,2,1,0:T(8,128)(2,1)} %shard_map.112), calls=%async_computation.1 | async-start | bytes 8388608 | tf_op jit(solution)/shard_map/all_to_all | solution.py:524
  37.9 60.4 %collective-permute-start.7 = (bf16[4,272,256]{2,1,0:T(8,128)(2,1)}, bf16[4,272,256]{2,1,0:T(8,128)(2,1)S(1)}, u32[]{:S(2)}, u32[]{:S(2)}) collective-permute-start(bf16[4,272,256]{2,1,0:T(8,128)(2,1)} %all-to-all-done.refs_7_), channel_id=1, source_target_pairs={{0,8},{4,12},{8,0},{12,4},{1,9},{5,13},{9,1},{13,5},{2,10},{6,14},... | collective-permute-start | bytes 1671176 | tf_op jit(solution)/shard_map/ppermute | solution.py:344
  40.2 13.9 %collective-permute-start.12 = (bf16[256,1024]{1,0:T(8,128)(2,1)}, bf16[256,1024]{1,0:T(8,128)(2,1)S(1)}, u32[]{:S(2)}, u32[]{:S(2)}) collective-permute-start(bf16[256,1024]{1,0:T(8,128)(2,1)} %collective-permute-done.10.refs_13_), channel_id=1, source_target_pairs={{0,16},{16,0},{1,17},{17,1},{2,18},{18,2},{3,19},{19,3},{4,20},{20... | collective-permute-start | bytes 1572872 | tf_op jit(solution)/shard_map/ppermute | solution.py:499
  41.8 56.5 %collective-permute-start.11 = (bf16[256,1024]{1,0:T(8,128)(2,1)}, bf16[256,1024]{1,0:T(8,128)(2,1)S(1)}, u32[]{:S(2)}, u32[]{:S(2)}) collective-permute-start(bf16[256,1024]{1,0:T(8,128)(2,1)} %collective-permute-done.10.refs_13_), channel_id=1, source_target_pairs={{0,4},{4,0},{8,12},{12,8},{1,5},{5,1},{9,13},{13,9},{2,6},{6,2},{1... | collective-permute-start | bytes 1572872 | tf_op jit(solution)/shard_map/ppermute | solution.py:503
  41.8 59.3 %collective-permute-start.17 = (bf16[512,256]{1,0:T(8,128)(2,1)S(1)}, bf16[512,256]{1,0:T(8,128)(2,1)S(1)}, u32[]{:S(2)}, u32[]{:S(2)}) collective-permute-start(bf16[512,256]{1,0:T(8,128)(2,1)S(1)} %copy-done.10), channel_id=1, source_target_pairs={{0,2},{2,3},{3,1},{1,0},{4,6},{6,7},{7,5},{5,4},{8,10},{10,11},{11... | collective-permute-start | bytes 786440 | tf_op jit(solution)/shard_map/ppermute | solution.py:493
  54.2 68.0 %collective-permute-start.6 = (bf16[4,272,256]{2,1,0:T(8,128)(2,1)}, bf16[4,272,256]{2,1,0:T(8,128)(2,1)S(1)}, u32[]{:S(2)}, u32[]{:S(2)}) collective-permute-start(bf16[4,272,256]{2,1,0:T(8,128)(2,1)} %all-to-all-done.refs_7_), channel_id=1, source_target_pairs={{0,4},{4,0},{8,12},{12,8},{1,5},{5,1},{9,13},{13,9},{2,6},{6,2},{1... | collective-permute-start | bytes 1671176 | tf_op jit(solution)/shard_map/ppermute | solution.py:344
  98.3 26.1 %collective-permute-start.8 = (bf16[4,272,256]{2,1,0:T(8,128)(2,1)S(1)}, bf16[4,272,256]{2,1,0:T(8,128)(2,1)S(1)}, u32[]{:S(2)}, u32[]{:S(2)}) collective-permute-start(bf16[4,272,256]{2,1,0:T(8,128)(2,1)S(1)} %collective-permute-done.7.refs_9_), channel_id=1, source_target_pairs={{0,4},{4,0},{8,12},{12,8},{1,5},{5,1},{9,13},{13,9},{2,6},{6,2},{1... | collective-permute-start | bytes 1671176 | tf_op jit(solution)/shard_map/ppermute | solution.py:344
  98.3 9.2 %collective-permute-start.3 = (bf16[512,256]{1,0:T(8,128)(2,1)S(1)}, bf16[512,256]{1,0:T(8,128)(2,1)S(1)}, u32[]{:S(2)}, u32[]{:S(2)}) collective-permute-start(bf16[512,256]{1,0:T(8,128)(2,1)S(1)} %get-tuple-element.16.refs_3_), channel_id=1, source_target_pairs={{0,2},{2,3},{3,1},{1,0},{4,6},{6,7},{7,5},{5,4},{8,10},{10,11},{11... | collective-permute-start | bytes 786440 | tf_op jit(solution)/shard_map/ppermute | solution.py:493
  100.8 21.3 %collective-permute-start.13 = (bf16[256,1024]{1,0:T(8,128)(2,1)S(1)}, bf16[256,1024]{1,0:T(8,128)(2,1)S(1)}, u32[]{:S(2)}, u32[]{:S(2)}) collective-permute-start(bf16[256,1024]{1,0:T(8,128)(2,1)S(1)} %collective-permute-done.12.refs_15_), channel_id=1, source_target_pairs={{0,4},{4,0},{8,12},{12,8},{1,5},{5,1},{9,13},{13,9},{2,6},{6,2},{1... | collective-permute-start | bytes 1572872 | tf_op jit(solution)/shard_map/ppermute | solution.py:503
  101.0 12.1 %collective-permute-start.18 = (bf16[512,256]{1,0:T(8,128)(2,1)S(1)}, bf16[512,256]{1,0:T(8,128)(2,1)S(1)}, u32[]{:S(2)}, u32[]{:S(2)}) collective-permute-start(bf16[512,256]{1,0:T(8,128)(2,1)S(1)} %collective-permute-done.17.refs_4_), channel_id=1, source_target_pairs={{0,2},{2,3},{3,1},{1,0},{4,6},{6,7},{7,5},{5,4},{8,10},{10,11},{11... | collective-permute-start | bytes 786440 | tf_op jit(solution)/shard_map/ppermute | solution.py:493
  107.5 11.2 %collective-permute-start.4 = (bf16[512,256]{1,0:T(8,128)(2,1)S(1)}, bf16[512,256]{1,0:T(8,128)(2,1)S(1)}, u32[]{:S(2)}, u32[]{:S(2)}) collective-permute-start(bf16[512,256]{1,0:T(8,128)(2,1)S(1)} %collective-permute-done.3.refs_4_), channel_id=1, source_target_pairs={{0,2},{2,3},{3,1},{1,0},{4,6},{6,7},{7,5},{5,4},{8,10},{10,11},{11... | collective-permute-start | bytes 786440 | tf_op jit(solution)/shard_map/ppermute | solution.py:493
  113.1 11.2 %collective-permute-start.19 = (bf16[512,256]{1,0:T(8,128)(2,1)S(1)}, bf16[512,256]{1,0:T(8,128)(2,1)S(1)}, u32[]{:S(2)}, u32[]{:S(2)}) collective-permute-start(bf16[512,256]{1,0:T(8,128)(2,1)S(1)} %collective-permute-done.18.refs_5_), channel_id=1, source_target_pairs={{0,2},{2,3},{3,1},{1,0},{4,6},{6,7},{7,5},{5,4},{8,10},{10,11},{11... | collective-permute-start | bytes 786440 | tf_op jit(solution)/shard_map/ppermute | solution.py:493
  118.8 19.2 %collective-permute-start.5 = (bf16[512,256]{1,0:T(8,128)(2,1)S(1)}, bf16[512,256]{1,0:T(8,128)(2,1)S(1)}, u32[]{:S(2)}, u32[]{:S(2)}) collective-permute-start(bf16[512,256]{1,0:T(8,128)(2,1)S(1)} %collective-permute-done.4.refs_5_), channel_id=1, source_target_pairs={{0,2},{2,3},{3,1},{1,0},{4,6},{6,7},{7,5},{5,4},{8,10},{10,11},{11... | collective-permute-start | bytes 786440 | tf_op jit(solution)/shard_map/ppermute | solution.py:493
  134.5 16.4 %collective-permute-start.20 = (bf16[512,256]{1,0:T(8,128)(2,1)}, bf16[512,256]{1,0:T(8,128)(2,1)S(1)}, u32[]{:S(2)}, u32[]{:S(2)}) collective-permute-start(bf16[512,256]{1,0:T(8,128)(2,1)} %get-tuple-element.23), channel_id=1, source_target_pairs={{0,2},{2,3},{3,1},{1,0},{4,6},{6,7},{7,5},{5,4},{8,10},{10,11},{11... | collective-permute-start | bytes 786440 | tf_op jit(solution)/shard_map/ppermute | solution.py:565
  147.3 9.4 %collective-permute-start.14 = (bf16[512,256]{1,0:T(8,128)(2,1)}, bf16[512,256]{1,0:T(8,128)(2,1)S(1)}, u32[]{:S(2)}, u32[]{:S(2)}) collective-permute-start(bf16[512,256]{1,0:T(8,128)(2,1)} %get-tuple-element.18), channel_id=1, source_target_pairs={{0,2},{2,3},{3,1},{1,0},{4,6},{6,7},{7,5},{5,4},{8,10},{10,11},{11... | collective-permute-start | bytes 786440 | tf_op jit(solution)/shard_map/ppermute | solution.py:565
  151.0 11.4 %collective-permute-start.21 = (bf16[512,256]{1,0:T(8,128)(2,1)S(1)}, bf16[512,256]{1,0:T(8,128)(2,1)S(1)}, u32[]{:S(2)}, u32[]{:S(2)}) collective-permute-start(bf16[512,256]{1,0:T(8,128)(2,1)S(1)} %shard_map.110), channel_id=1, source_target_pairs={{0,2},{2,3},{3,1},{1,0},{4,6},{6,7},{7,5},{5,4},{8,10},{10,11},{11... | collective-permute-start | bytes 786440 | tf_op jit(solution)/shard_map/ppermute | solution.py:565
  157.8 10.2 %collective-permute-start.15 = (bf16[512,256]{1,0:T(8,128)(2,1)S(1)}, bf16[512,256]{1,0:T(8,128)(2,1)S(1)}, u32[]{:S(2)}, u32[]{:S(2)}) collective-permute-start(bf16[512,256]{1,0:T(8,128)(2,1)S(1)} %shard_map.106), channel_id=1, source_target_pairs={{0,2},{2,3},{3,1},{1,0},{4,6},{6,7},{7,5},{5,4},{8,10},{10,11},{11... | collective-permute-start | bytes 786440 | tf_op jit(solution)/shard_map/ppermute | solution.py:565
  162.4 11.2 %collective-permute-start.22 = (bf16[512,256]{1,0:T(8,128)(2,1)S(1)}, bf16[512,256]{1,0:T(8,128)(2,1)S(1)}, u32[]{:S(2)}, u32[]{:S(2)}) collective-permute-start(bf16[512,256]{1,0:T(8,128)(2,1)S(1)} %shard_map.111), channel_id=1, source_target_pairs={{0,2},{2,3},{3,1},{1,0},{4,6},{6,7},{7,5},{5,4},{8,10},{10,11},{11... | collective-permute-start | bytes 786440 | tf_op jit(solution)/shard_map/ppermute | solution.py:565
  169.0 8.1 %collective-permute-start.16 = (bf16[512,256]{1,0:T(8,128)(2,1)S(1)}, bf16[512,256]{1,0:T(8,128)(2,1)S(1)}, u32[]{:S(2)}, u32[]{:S(2)}) collective-permute-start(bf16[512,256]{1,0:T(8,128)(2,1)S(1)} %shard_map.107), channel_id=1, source_target_pairs={{0,2},{2,3},{3,1},{1,0},{4,6},{6,7},{7,5},{5,4},{8,10},{10,11},{11... | collective-permute-start | bytes 786440 | tf_op jit(solution)/shard_map/ppermute | solution.py:565
  (26 other events, 477.5 us)

commit v4 on v3

--- a/solution.py
+++ b/solution.py
@@ -266,13 +266,14 @@
         down_copies.append(ffn_copy(near[k - 2], 1, k))
     gated_copies = [
         pltpu.make_async_copy(source, gated.at[k], gated_sems.at[k])
-        for k, source in enumerate(gated_hbm)
+        for k, source in enumerate(gated_hbm[:-1])
     ]
     done_copies = [pltpu.make_async_copy(own_ref, own_hbm, done_sems.at[0])]
     for k in range(1, n_tensor):
         done_copies.append(
             pltpu.make_async_copy(part_ref.at[k - 1], part_hbm[k - 1], done_sems.at[k])
         )
+    here = [gated.at[k] for k in range(n_tensor - 1)] + [gated_hbm[-1]]
     for copy in out_copies + gated_copies:
         copy.start()
     for copy in up_copies[:2] + rest:
@@ -283,9 +284,9 @@
         copy.start()
     for r in range(0, rows, block):
         span = slice(r, r + block)
-        attended = dot_nt(gated[0, span], wo_ref[ids_ref[2]])
+        attended = dot_nt(here[0][span], wo_ref[ids_ref[2]])
         for k in range(1, n_tensor):
-            attended += dot_nt(gated[k, span], wo_ref[ids_ref[2 + k]])
+            attended += dot_nt(here[k][span], wo_ref[ids_ref[2 + k]])
         residual = tok_ref[base + r : base + r + block].astype(jnp.float32) + attended
         res_ref[span] = residual
         hid_ref[span] = rms_scale(residual, small_ref[1:2, :])
@@ -420,26 +421,28 @@
     target_dev = new_slot // sessions_here
     session_ids = jnp.arange(sessions_here, dtype=jnp.int32)
     proj_rows = attn_weights.shape[1]
-    proj_pieces = xor_gather(attn_weights[:4].reshape(-1, cols_here), "dp")
     notes = jnp.stack([jnp.where(survive, target_dev, -1), new_slot % sessions_here])
-    note_rows = 16
-    notes = jnp.pad(
-        notes.astype(bf16), ((0, note_rows - 2), (0, cols_here - sessions_here))
-    )
+    notes = jnp.pad(notes.astype(bf16), ((0, 6), (0, cols_here - sessions_here)))
+    proj_own = jnp.concatenate([attn_weights[:4].reshape(4 * proj_rows, cols_here), notes])
+    proj_pieces = xor_gather(proj_own, "dp")
     out_own = lax.all_to_all(
-        jnp.broadcast_to(
-            jnp.concatenate([attn_weights[4], notes])[None],
-            (n_tensor, proj_rows + note_rows, cols_here),
-        ),
+        jnp.broadcast_to(attn_weights[4:], (n_tensor, proj_rows, cols_here)),
         "tensor",
         split_axis=0,
         concat_axis=0,
         tiled=True,
     )
-    half_own = lax.dynamic_index_in_dim(ffn_weights, lax.axis_index("group"), 0, keepdims=False)
+    half_own = lax.dynamic_index_in_dim(
+        ffn_weights, lax.axis_index("group"), 0, keepdims=False
+    )
     sources = jnp.array(ring_sources(n_tensor), jnp.int32)[tensor_at]
     places = jnp.stack([dp_at, tensor_at]).astype(jnp.int32)
-    ids = jnp.concatenate([places, sources, lax.axis_index("group").astype(jnp.int32)[None]])
+    group_at = lax.axis_index("group").astype(jnp.int32)
+    ids = jnp.concatenate([places, sources, group_at[None]])
+    head_decay = lax.dynamic_slice_in_dim(head_rates, tensor_at * heads_here, heads_here)
+    small = jnp.concatenate(
+        [norm_gains, jnp.broadcast_to(head_decay[:, None], (heads_here, width))]
+    )
     out_pieces = xor_gather(out_own, "dp")
 
     earlier = (
@@ -449,7 +452,7 @@
     )
     pair_rank = jnp.sum(earlier.astype(jnp.int32), axis=1)
     send_pos = jnp.where(survive, target_dev * pair_cap + pair_rank, -1)
-    meta = jnp.stack([piece[0, proj_rows:, :sessions_here] for piece in out_pieces])
+    meta = jnp.stack([piece[4 * proj_rows :, :sessions_here] for piece in proj_pieces])
     meta = meta.astype(jnp.int32)
     from_dev = jnp.bitwise_xor(dp_at, jnp.arange(n_dp, dtype=jnp.int32))
     coming = meta[:, 0] == dp_at
@@ -461,10 +464,6 @@
 
     rows_shape = shape_of((chunk_rows, cols_here), bf16)
     decay_shape = pltpu.VMEM((heads_here, block, block), f32)
-    head_decay = lax.dynamic_slice_in_dim(head_rates, tensor_at * heads_here, heads_here)
-    small = jnp.concatenate(
-        [norm_gains, jnp.broadcast_to(head_decay[:, None], (heads_here, width))]
-    )
     chunk_sessions = chunk_rows // event_count
     split = (width // n_dp) % 128 == 0
     gated, keys, values = [], [], []
@@ -484,6 +483,7 @@
                 pltpu.SemaphoreType.DMA((3,)),
             ],
             2 * chunk_rows * width * cols_here * 4,
+            limit_mib=12,
         )(ids, small, tokens, *in_hbm([past_states]), *proj_pieces)
         gated.append([g])
         keys.append(k)
@@ -527,7 +527,11 @@
     for c in range(CHUNKS):
         own, *part = kernel_call(
             functools.partial(feed_kernel, n_dp, n_tensor, block, c * chunk_rows),
-            [smem_spec()] + [vmem_spec()] * 2 + [hbm_spec()] * (n_tensor + n_dp + 2 * n_dp - 2),
+            [smem_spec()]
+            + [vmem_spec()] * 2
+            + [hbm_spec()] * (n_tensor - 1)
+            + [vmem_spec()]
+            + [hbm_spec()] * (3 * n_dp - 2),
             [hbm_spec()] * n_tensor,
             [pltpu.HBM((chunk_rows, share), f32)]
             + [pltpu.HBM((chunk_rows, share), bf16)] * (n_tensor - 1),
@@ -535,7 +539,7 @@
                 pltpu.VMEM((n_tensor, width, cols_here), bf16),
                 pltpu.VMEM((2, width, units_here), bf16),
                 pltpu.VMEM((chunk_rows, width), f32),
-                pltpu.VMEM((n_tensor, chunk_rows, cols_here), bf16),
+                pltpu.VMEM((n_tensor - 1, chunk_rows, cols_here), bf16),
                 pltpu.VMEM((chunk_rows, share), f32),
                 pltpu.VMEM((n_tensor - 1, chunk_rows, share), bf16),
                 pltpu.VMEM((chunk_rows, width), bf16),
@@ -545,7 +549,14 @@
                 pltpu.SemaphoreType.DMA((n_tensor,)),
             ],
             2 * chunk_rows * width * (width + 2 * units_here),
-        )(ids, small, tokens, *in_hbm(gated[c] + out_pieces + ffn_pieces))
+        )(
+            ids,
+            small,
+            tokens,
+            *in_hbm(gated[c][:-1]),
+            gated[c][-1],
+            *in_hbm(out_pieces + ffn_pieces),
+        )
         owns.append(own)
         parts.append(part)
         sums.append(None)

time: 184 us -> 182 us (0.989)
  local copies, waits for them, and re-layouts: 12.6 us -> 9 us
    ppermute x7, waiting for transfers between devices: 46.7 us -> 58.9 us  [xor_gather(): arrived.append(lax.ppermute(piece, axis, pairs))]
    ppermute x1, waiting for transfers between devices: 9.97 us -> 0.01 us  [per_device(): far.append(lax.ppermute(piece, 'group', swap))]
    slice x5 -> x1, local copies, waits for them, and re-layouts: 3.95 us -> 1.23 us  [per_device(): attn_weights[:4].reshape(4 * proj_rows, cols_here)]
    unnamed x51 -> x47, local copies, waits for them, and re-layouts: 4.15 us -> 2 us
  transfers between devices with their start and end apart: 25 -> 25, of which waited for: 13 -> 11; matrix products, arithmetic and copies ran while one was open for 5% -> 4% of each run, Pallas kernels for 19% -> 19%
where the time goes in v4:
time: 182 us; the launch traced here: 181 us
  waiting for transfers between devices  87.1 us (48%)
  starting transfers between devices  43.4 us (24%)
  Pallas kernels  38.6 us (21%)
  local copies, waits for them, and re-layouts  9 us (5%)
    ppermute x7, waiting for transfers between devices, xor_gather(): arrived.append(lax.ppermute(piece, axis, pairs))  58.9 us
    ppermute x6, waiting for transfers between devices, per_device(): sums[c] = lax.ppermute(mine, 'tensor', ring)  18.4 us
    pallas_call x2, Pallas kernels, per_device(): kernel_call(functools.partial(feed_kernel, n_dp, n_tensor, block, c * chu...  17.2 us
    ppermute x6, starting transfers between devices, per_device(): gated[c].append(lax.ppermute(gated[c][-1], 'tensor', ring))  15.2 us
    ppermute x6, starting transfers between devices, per_device(): sums[c] = lax.ppermute(mine, 'tensor', ring)  10.3 us
    ppermute x6, waiting for transfers between devices, per_device(): gated[c].append(lax.ppermute(gated[c][-1], 'tensor', ring))  9.85 us
    pallas_call x2, Pallas kernels, per_device(): kernel_call(functools.partial(project_kernel, n_dp, heads_here, event_cou...  9.51 us
    ppermute x7, starting transfers between devices, xor_gather(): arrived.append(lax.ppermute(piece, axis, pairs))  5.45 us
  transfers between devices with their start and end apart: 25, of which 11 were waited for; matrix products, arithmetic and copies ran while one was open for 4% of the time, Pallas kernels for 19%

profile of v4, /device:TPU:0, one launch (start us, length us, event | category | flops | bytes accessed | tf_op | source)
XLA Modules:
  0.0 180.9 jit_solution(2373182629452044372)
XLA Ops:
  2.7 3.0 %collective-permute-start.1 = (bf16[1032,256]{1,0:T(8,128)(2,1)S(1)}, bf16[1032,256]{1,0:T(8,128)(2,1)S(1)}, u32[]{:S(2)}, u32[]{:S(2)}) collective-permute-start(bf16[1032,256]{1,0:T(8,128)(2,1)S(1)} %pad_maximum_fusion.refs_4_), channel_id=1, source_target_pairs={{0,8},{4,12},{8,0},{12,4},{1,9},{5,13},{9,1},{13,5},{2,10},{6,14},... | collective-permute-start | bytes 1585160 | tf_op jit(solution)/shard_map/ppermute | solution.py:345
  7.4 4.9 %all-to-all-start = ((bf16[4,256,256]{2,1,0:T(8,128)(2,1)}), bf16[4,256,256]{2,1,0:T(8,128)(2,1)}, u32[]{:S(2)}, u32[]{:S(2)}) async-start(bf16[4,256,256]{2,1,0:T(8,128)(2,1)} %broadcast_in_dim.22), calls=%async_computation | async-start | bytes 1048576 | tf_op jit(solution)/shard_map/all_to_all | solution.py:428
  18.3 10.8 %collective-permute-done.10.refs_13_ = bf16[256,1024]{1,0:T(8,128)(2,1)} collective-permute-done((bf16[256,1024]{1,0:T(8,128)(2,1)}, bf16[256,1024]{1,0:T(8,128)(2,1)}, u32[]{:S(2)}, u32[]{:S(2)}) %collective-permute-start.10) | collective-permute-done | bytes 524320 | tf_op jit(solution)/shard_map/ppermute | solution.py:345
  30.8 4.8 %shard_map.108 = (bf16[512,256]{1,0:T(8,128)(2,1)S(1)}, bf16[512,256]{1,0:T(8,128)(2,1)}, bf16[512,256]{1,0:T(8,128)(2,1)}) custom-call(s32[7]{0:T(128)S(1)} %pad_add_fusion.refs_0_, f32[4,1024]{1,0:T(4,128)S(1)} %pad_maximum_fusion.1.refs_1_.refs_0_, bf16[1024,1024]{1,0:T(8,128)(2,1)S(1)} %copy-done, f32[32,2,128,128]{3,2,1,0:T(8,128)} %refs_2_.9, ...), custom_call_target="tpu_custom_call" | custom-call | flops 1073741824 | bytes 4194304 | tf_op jit(solution)/shard_map/pallas_call | solution.py:471
  35.7 4.7 %shard_map.104 = (bf16[512,256]{1,0:T(8,128)(2,1)S(1)}, bf16[512,256]{1,0:T(8,128)(2,1)}, bf16[512,256]{1,0:T(8,128)(2,1)}) custom-call(s32[7]{0:T(128)S(1)} %pad_add_fusion.refs_0_, f32[4,1024]{1,0:T(4,128)S(1)} %pad_maximum_fusion.1.refs_1_.refs_0_, bf16[1024,1024]{1,0:T(8,128)(2,1)S(1)} %copy-done, f32[32,2,128,128]{3,2,1,0:T(8,128)} %refs_2_.9, ...), custom_call_target="tpu_custom_call" | custom-call | flops 1073741824 | bytes 4194304 | tf_op jit(solution)/shard_map/pallas_call | solution.py:471
  40.4 4.7 %shard_map.112 = bf16[64,2,128,128]{3,2,1,0:T(8,128)(2,1)} custom-call(f32[4,1024]{1,0:T(4,128)S(1)} %pad_maximum_fusion.1.refs_1_.refs_0_, s32[32]{0:T(128)S(1)} %add_select_fusion.refs_1_, f32[32,2,128,128]{3,2,1,0:T(8,128)} %refs_2_.9, bf16[512,256]{1,0:T(8,128)(2,1)} %get-tuple-element.26.refs_3_, bf16[512,256]{1,0:T(8,128)(2,1)} %get-tuple-element.27.refs_4_, ...), custom_call_target="tpu_custom_call" | custom-call | flops 67108864 | bytes 4194304 | tf_op jit(solution)/shard_map/pallas_call | solution.py:509
  45.2 5.0 %all-to-all-start.1 = ((bf16[64,2,128,128]{3,2,1,0:T(8,128)(2,1)}), bf16[64,2,128,128]{3,2,1,0:T(8,128)(2,1)}, u32[]{:S(2)}, u32[]{:S(2)}) async-start(bf16[64,2,128,128]{3,2,1,0:T(8,128)(2,1)} %shard_map.112), calls=%async_computation.1 | async-start | bytes 8388608 | tf_op jit(solution)/shard_map/all_to_all | solution.py:524
  50.2 2.6 %collective-permute-start.17 = (bf16[512,256]{1,0:T(8,128)(2,1)S(1)}, bf16[512,256]{1,0:T(8,128)(2,1)S(1)}, u32[]{:S(2)}, u32[]{:S(2)}) collective-permute-start(bf16[512,256]{1,0:T(8,128)(2,1)S(1)} %copy-done.11), channel_id=1, source_target_pairs={{0,2},{2,3},{3,1},{1,0},{4,6},{6,7},{7,5},{5,4},{8,10},{10,11},{11... | collective-permute-start | bytes 786440 | tf_op jit(solution)/shard_map/ppermute | solution.py:493
  56.3 3.2 %collective-permute-done.17.refs_4_ = bf16[512,256]{1,0:T(8,128)(2,1)S(1)} collective-permute-done((bf16[512,256]{1,0:T(8,128)(2,1)S(1)}, bf16[512,256]{1,0:T(8,128)(2,1)S(1)}, u32[]{:S(2)}, u32[]{:S(2)}) %collective-permute-start.17) | collective-permute-done | bytes 262176 | tf_op jit(solution)/shard_map/ppermute | solution.py:493
  59.5 3.4 %collective-permute-start.18 = (bf16[512,256]{1,0:T(8,128)(2,1)S(1)}, bf16[512,256]{1,0:T(8,128)(2,1)S(1)}, u32[]{:S(2)}, u32[]{:S(2)}) collective-permute-start(bf16[512,256]{1,0:T(8,128)(2,1)S(1)} %collective-permute-done.17.refs_4_), channel_id=1, source_target_pairs={{0,2},{2,3},{3,1},{1,0},{4,6},{6,7},{7,5},{5,4},{8,10},{10,11},{11... | collective-permute-start | bytes 786440 | tf_op jit(solution)/shard_map/ppermute | solution.py:493
  63.5 46.0 %collective-permute-done.7.refs_9_ = bf16[4,256,256]{2,1,0:T(8,128)(2,1)S(1)} collective-permute-done((bf16[4,256,256]{2,1,0:T(8,128)(2,1)}, bf16[4,256,256]{2,1,0:T(8,128)(2,1)S(1)}, u32[]{:S(2)}, u32[]{:S(2)}) %collective-permute-start.7) | collective-permute-done | bytes 524320 | tf_op jit(solution)/shard_map/ppermute | solution.py:345
  109.5 2.6 %collective-permute-start.4 = (bf16[512,256]{1,0:T(8,128)(2,1)S(1)}, bf16[512,256]{1,0:T(8,128)(2,1)S(1)}, u32[]{:S(2)}, u32[]{:S(2)}) collective-permute-start(bf16[512,256]{1,0:T(8,128)(2,1)S(1)} %collective-permute-done.3.refs_4_), channel_id=1, source_target_pairs={{0,2},{2,3},{3,1},{1,0},{4,6},{6,7},{7,5},{5,4},{8,10},{10,11},{11... | collective-permute-start | bytes 786440 | tf_op jit(solution)/shard_map/ppermute | solution.py:493
  114.4 4.5 %collective-permute-done.4.refs_5_ = bf16[512,256]{1,0:T(8,128)(2,1)S(1)} collective-permute-done((bf16[512,256]{1,0:T(8,128)(2,1)S(1)}, bf16[512,256]{1,0:T(8,128)(2,1)S(1)}, u32[]{:S(2)}, u32[]{:S(2)}) %collective-permute-start.4) | collective-permute-done | bytes 262176 | tf_op jit(solution)/shard_map/ppermute | solution.py:493
  118.9 3.4 %collective-permute-start.5 = (bf16[512,256]{1,0:T(8,128)(2,1)S(1)}, bf16[512,256]{1,0:T(8,128)(2,1)S(1)}, u32[]{:S(2)}, u32[]{:S(2)}) collective-permute-start(bf16[512,256]{1,0:T(8,128)(2,1)S(1)} %collective-permute-done.4.refs_5_), channel_id=1, source_target_pairs={{0,2},{2,3},{3,1},{1,0},{4,6},{6,7},{7,5},{5,4},{8,10},{10,11},{11... | collective-permute-start | bytes 786440 | tf_op jit(solution)/shard_map/ppermute | solution.py:493
  122.3 2.2 %collective-permute-done.19.refs_6_ = bf16[512,256]{1,0:T(8,128)(2,1)S(1)} collective-permute-done((bf16[512,256]{1,0:T(8,128)(2,1)S(1)}, bf16[512,256]{1,0:T(8,128)(2,1)S(1)}, u32[]{:S(2)}, u32[]{:S(2)}) %collective-permute-start.19) | collective-permute-done | bytes 262176 | tf_op jit(solution)/shard_map/ppermute | solution.py:493
  124.5 8.6 %shard_map.109 = (f32[512,256]{1,0:T(8,128)}, bf16[512,256]{1,0:T(8,128)(2,1)}, bf16[512,256]{1,0:T(8,128)(2,1)}, bf16[512,256]{1,0:T(8,128)(2,1)}) custom-call(s32[7]{0:T(128)S(1)} %pad_add_fusion.refs_0_, f32[4,1024]{1,0:T(4,128)S(1)} %pad_maximum_fusion.1.refs_1_.refs_0_, bf16[1024,1024]{1,0:T(8,128)(2,1)S(1)} %copy-done, bf16[512,256]{1,0:T(8,128)(2,1)} %copy-done.10, ...), custom_call_target="tpu_custom_call" | custom-call | flops 3221225472 | bytes 4194304 | tf_op jit(solution)/shard_map/pallas_call | solution.py:528
  133.2 3.4 %collective-permute-start.20 = (bf16[512,256]{1,0:T(8,128)(2,1)}, bf16[512,256]{1,0:T(8,128)(2,1)S(1)}, u32[]{:S(2)}, u32[]{:S(2)}) collective-permute-start(bf16[512,256]{1,0:T(8,128)(2,1)} %get-tuple-element.23), channel_id=1, source_target_pairs={{0,2},{2,3},{3,1},{1,0},{4,6},{6,7},{7,5},{5,4},{8,10},{10,11},{11... | collective-permute-start | bytes 786440 | tf_op jit(solution)/shard_map/ppermute | solution.py:576
  136.6 8.6 %shard_map.105 = (f32[512,256]{1,0:T(8,128)}, bf16[512,256]{1,0:T(8,128)(2,1)}, bf16[512,256]{1,0:T(8,128)(2,1)}, bf16[512,256]{1,0:T(8,128)(2,1)}) custom-call(s32[7]{0:T(128)S(1)} %pad_add_fusion.refs_0_, f32[4,1024]{1,0:T(4,128)S(1)} %pad_maximum_fusion.1.refs_1_.refs_0_, bf16[1024,1024]{1,0:T(8,128)(2,1)S(1)} %copy-done, bf16[512,256]{1,0:T(8,128)(2,1)} %copy-done.9, ...), custom_call_target="tpu_custom_call" | custom-call | flops 3221225472 | bytes 4194304 | tf_op jit(solution)/shard_map/pallas_call | solution.py:528
  148.2 6.5 %collective-permute-done.14.a_ref = bf16[512,256]{1,0:T(8,128)(2,1)S(1)} collective-permute-done((bf16[512,256]{1,0:T(8,128)(2,1)}, bf16[512,256]{1,0:T(8,128)(2,1)S(1)}, u32[]{:S(2)}, u32[]{:S(2)}) %collective-permute-start.14) | collective-permute-done | bytes 262176 | tf_op jit(solution)/shard_map/ppermute | solution.py:576
  157.4 2.9 %collective-permute-done.21.a_ref = bf16[512,256]{1,0:T(8,128)(2,1)S(1)} collective-permute-done((bf16[512,256]{1,0:T(8,128)(2,1)S(1)}, bf16[512,256]{1,0:T(8,128)(2,1)S(1)}, u32[]{:S(2)}, u32[]{:S(2)}) %collective-permute-start.21) | collective-permute-done | bytes 262176 | tf_op jit(solution)/shard_map/ppermute | solution.py:576
  161.9 3.9 %collective-permute-done.15.a_ref = bf16[512,256]{1,0:T(8,128)(2,1)S(1)} collective-permute-done((bf16[512,256]{1,0:T(8,128)(2,1)S(1)}, bf16[512,256]{1,0:T(8,128)(2,1)S(1)}, u32[]{:S(2)}, u32[]{:S(2)}) %collective-permute-start.15) | collective-permute-done | bytes 262176 | tf_op jit(solution)/shard_map/ppermute | solution.py:576
  168.6 2.9 %collective-permute-done.22.refs_2_ = bf16[512,256]{1,0:T(8,128)(2,1)S(1)} collective-permute-done((bf16[512,256]{1,0:T(8,128)(2,1)S(1)}, bf16[512,256]{1,0:T(8,128)(2,1)S(1)}, u32[]{:S(2)}, u32[]{:S(2)}) %collective-permute-start.22) | collective-permute-done | bytes 262176 | tf_op jit(solution)/shard_map/ppermute | solution.py:576
  172.8 2.2 %collective-permute-done.16.refs_2_ = bf16[512,256]{1,0:T(8,128)(2,1)S(1)} collective-permute-done((bf16[512,256]{1,0:T(8,128)(2,1)S(1)}, bf16[512,256]{1,0:T(8,128)(2,1)S(1)}, u32[]{:S(2)}, u32[]{:S(2)}) %collective-permute-start.16) | collective-permute-done | bytes 262176 | tf_op jit(solution)/shard_map/ppermute | solution.py:576
  176.4 4.3 %unpack.1 = f32[32,2,128,128]{3,2,1,0:T(8,128)} custom-call(s32[32]{0:T(128)S(1)} %broadcast_add_fusion.src_ref, bf16[64,2,128,128]{3,2,1,0:T(8,128)(2,1)} %all-to-all-done.1.recv_ref), custom_call_target="tpu_custom_call" | custom-call | bytes 6291456 | tf_op jit(solution)/shard_map/unpack/pallas_call | solution.py:601
  (112 shorter events, 30.6 us)
Async XLA Ops:
  2.7 15.4 %collective-permute-start.1 = (bf16[1032,256]{1,0:T(8,128)(2,1)S(1)}, bf16[1032,256]{1,0:T(8,128)(2,1)S(1)}, u32[]{:S(2)}, u32[]{:S(2)}) collective-permute-start(bf16[1032,256]{1,0:T(8,128)(2,1)S(1)} %pad_maximum_fusion.refs_4_), channel_id=1, source_target_pairs={{0,8},{4,12},{8,0},{12,4},{1,9},{5,13},{9,1},{13,5},{2,10},{6,14},... | collective-permute-start | bytes 1585160 | tf_op jit(solution)/shard_map/ppermute | solution.py:345
  5.7 25.1 %collective-permute-start = (bf16[1032,256]{1,0:T(8,128)(2,1)S(1)}, bf16[1032,256]{1,0:T(8,128)(2,1)}, u32[]{:S(2)}, u32[]{:S(2)}) collective-permute-start(bf16[1032,256]{1,0:T(8,128)(2,1)S(1)} %pad_maximum_fusion.refs_4_), channel_id=1, source_target_pairs={{0,4},{4,0},{8,12},{12,8},{1,5},{5,1},{9,13},{13,9},{2,6},{6,2},{1... | collective-permute-start | bytes 1585160 | tf_op jit(solution)/shard_map/ppermute | solution.py:345
  7.4 37.7 %all-to-all-start = ((bf16[4,256,256]{2,1,0:T(8,128)(2,1)}), bf16[4,256,256]{2,1,0:T(8,128)(2,1)}, u32[]{:S(2)}, u32[]{:S(2)}) async-start(bf16[4,256,256]{2,1,0:T(8,128)(2,1)} %broadcast_in_dim.22), calls=%async_computation | async-start | bytes 1048576 | tf_op jit(solution)/shard_map/all_to_all | solution.py:428
  12.3 50.7 %collective-permute-start.9 = (bf16[2,256,1024]{2,1,0:T(8,128)(2,1)}, bf16[2,256,1024]{2,1,0:T(8,128)(2,1)}, u32[]{:S(2)}, u32[]{:S(2)}) collective-permute-start(bf16[2,256,1024]{2,1,0:T(8,128)(2,1)} %refs_11_.3), channel_id=1, source_target_pairs={{0,4},{4,0},{8,12},{12,8},{1,5},{5,1},{9,13},{13,9},{2,6},{6,2},{1... | collective-permute-start | bytes 3145736 | tf_op jit(solution)/shard_map/ppermute | solution.py:503
  14.4 14.6 %collective-permute-start.10 = (bf16[256,1024]{1,0:T(8,128)(2,1)}, bf16[256,1024]{1,0:T(8,128)(2,1)}, u32[]{:S(2)}, u32[]{:S(2)}) collective-permute-start(bf16[256,1024]{1,0:T(8,128)(2,1)} %dynamic-slice_bitcast_fusion), channel_id=1, source_target_pairs={{0,8},{4,12},{8,0},{12,4},{1,9},{5,13},{9,1},{13,5},{2,10},{6,14},... | collective-permute-start | bytes 1572872 | tf_op jit(solution)/shard_map/ppermute | solution.py:345
  18.1 12.7 %collective-permute-start.2 = (bf16[1032,256]{1,0:T(8,128)(2,1)S(1)}, bf16[1032,256]{1,0:T(8,128)(2,1)S(1)}, u32[]{:S(2)}, u32[]{:S(2)}) collective-permute-start(bf16[1032,256]{1,0:T(8,128)(2,1)S(1)} %collective-permute-done.1.refs_6_), channel_id=1, source_target_pairs={{0,4},{4,0},{8,12},{12,8},{1,5},{5,1},{9,13},{13,9},{2,6},{6,2},{1... | collective-permute-start | bytes 1585160 | tf_op jit(solution)/shard_map/ppermute | solution.py:345
  29.0 25.7 %collective-permute-start.12 = (bf16[256,1024]{1,0:T(8,128)(2,1)}, bf16[256,1024]{1,0:T(8,128)(2,1)}, u32[]{:S(2)}, u32[]{:S(2)}) collective-permute-start(bf16[256,1024]{1,0:T(8,128)(2,1)} %collective-permute-done.10.refs_13_), channel_id=1, source_target_pairs={{0,16},{16,0},{1,17},{17,1},{2,18},{18,2},{3,19},{19,3},{4,20},{20... | collective-permute-start | bytes 1572872 | tf_op jit(solution)/shard_map/ppermute | solution.py:499
  45.2 131.2 %all-to-all-start.1 = ((bf16[64,2,128,128]{3,2,1,0:T(8,128)(2,1)}), bf16[64,2,128,128]{3,2,1,0:T(8,128)(2,1)}, u32[]{:S(2)}, u32[]{:S(2)}) async-start(bf16[64,2,128,128]{3,2,1,0:T(8,128)(2,1)} %shard_map.112), calls=%async_computation.1 | async-start | bytes 8388608 | tf_op jit(solution)/shard_map/all_to_all | solution.py:524
  50.2 9.3 %collective-permute-start.17 = (bf16[512,256]{1,0:T(8,128)(2,1)S(1)}, bf16[512,256]{1,0:T(8,128)(2,1)S(1)}, u32[]{:S(2)}, u32[]{:S(2)}) collective-permute-start(bf16[512,256]{1,0:T(8,128)(2,1)S(1)} %copy-done.11), channel_id=1, source_target_pairs={{0,2},{2,3},{3,1},{1,0},{4,6},{6,7},{7,5},{5,4},{8,10},{10,11},{11... | collective-permute-start | bytes 786440 | tf_op jit(solution)/shard_map/ppermute | solution.py:493
  52.8 10.1 %collective-permute-start.11 = (bf16[256,1024]{1,0:T(8,128)(2,1)}, bf16[256,1024]{1,0:T(8,128)(2,1)S(1)}, u32[]{:S(2)}, u32[]{:S(2)}) collective-permute-start(bf16[256,1024]{1,0:T(8,128)(2,1)} %collective-permute-done.10.refs_13_), channel_id=1, source_target_pairs={{0,4},{4,0},{8,12},{12,8},{1,5},{5,1},{9,13},{13,9},{2,6},{6,2},{1... | collective-permute-start | bytes 1572872 | tf_op jit(solution)/shard_map/ppermute | solution.py:503
  52.9 56.6 %collective-permute-start.7 = (bf16[4,256,256]{2,1,0:T(8,128)(2,1)}, bf16[4,256,256]{2,1,0:T(8,128)(2,1)S(1)}, u32[]{:S(2)}, u32[]{:S(2)}) collective-permute-start(bf16[4,256,256]{2,1,0:T(8,128)(2,1)} %all-to-all-done.refs_7_), channel_id=1, source_target_pairs={{0,8},{4,12},{8,0},{12,4},{1,9},{5,13},{9,1},{13,5},{2,10},{6,14},... | collective-permute-start | bytes 1572872 | tf_op jit(solution)/shard_map/ppermute | solution.py:345
  54.7 54.8 %collective-permute-start.3 = (bf16[512,256]{1,0:T(8,128)(2,1)S(1)}, bf16[512,256]{1,0:T(8,128)(2,1)S(1)}, u32[]{:S(2)}, u32[]{:S(2)}) collective-permute-start(bf16[512,256]{1,0:T(8,128)(2,1)S(1)} %get-tuple-element.16.refs_3_), channel_id=1, source_target_pairs={{0,2},{2,3},{3,1},{1,0},{4,6},{6,7},{7,5},{5,4},{8,10},{10,11},{11... | collective-permute-start | bytes 786440 | tf_op jit(solution)/shard_map/ppermute | solution.py:493
  59.5 52.7 %collective-permute-start.18 = (bf16[512,256]{1,0:T(8,128)(2,1)S(1)}, bf16[512,256]{1,0:T(8,128)(2,1)S(1)}, u32[]{:S(2)}, u32[]{:S(2)}) collective-permute-start(bf16[512,256]{1,0:T(8,128)(2,1)S(1)} %collective-permute-done.17.refs_4_), channel_id=1, source_target_pairs={{0,2},{2,3},{3,1},{1,0},{4,6},{6,7},{7,5},{5,4},{8,10},{10,11},{11... | collective-permute-start | bytes 786440 | tf_op jit(solution)/shard_map/ppermute | solution.py:493
  62.9 59.3 %collective-permute-start.6 = (bf16[4,256,256]{2,1,0:T(8,128)(2,1)}, bf16[4,256,256]{2,1,0:T(8,128)(2,1)S(1)}, u32[]{:S(2)}, u32[]{:S(2)}) collective-permute-start(bf16[4,256,256]{2,1,0:T(8,128)(2,1)} %all-to-all-done.refs_7_), channel_id=1, source_target_pairs={{0,4},{4,0},{8,12},{12,8},{1,5},{5,1},{9,13},{13,9},{2,6},{6,2},{1... | collective-permute-start | bytes 1572872 | tf_op jit(solution)/shard_map/ppermute | solution.py:345
  63.0 59.2 %collective-permute-start.13 = (bf16[256,1024]{1,0:T(8,128)(2,1)}, bf16[256,1024]{1,0:T(8,128)(2,1)S(1)}, u32[]{:S(2)}, u32[]{:S(2)}) collective-permute-start(bf16[256,1024]{1,0:T(8,128)(2,1)} %collective-permute-done.12.refs_15_), channel_id=1, source_target_pairs={{0,4},{4,0},{8,12},{12,8},{1,5},{5,1},{9,13},{13,9},{2,6},{6,2},{1... | collective-permute-start | bytes 1572872 | tf_op jit(solution)/shard_map/ppermute | solution.py:503
  109.5 12.8 %collective-permute-start.8 = (bf16[4,256,256]{2,1,0:T(8,128)(2,1)S(1)}, bf16[4,256,256]{2,1,0:T(8,128)(2,1)S(1)}, u32[]{:S(2)}, u32[]{:S(2)}) collective-permute-start(bf16[4,256,256]{2,1,0:T(8,128)(2,1)S(1)} %collective-permute-done.7.refs_9_), channel_id=1, source_target_pairs={{0,4},{4,0},{8,12},{12,8},{1,5},{5,1},{9,13},{13,9},{2,6},{6,2},{1... | collective-permute-start | bytes 1572872 | tf_op jit(solution)/shard_map/ppermute | solution.py:345
  109.5 9.3 %collective-permute-start.4 = (bf16[512,256]{1,0:T(8,128)(2,1)S(1)}, bf16[512,256]{1,0:T(8,128)(2,1)S(1)}, u32[]{:S(2)}, u32[]{:S(2)}) collective-permute-start(bf16[512,256]{1,0:T(8,128)(2,1)S(1)} %collective-permute-done.3.refs_4_), channel_id=1, source_target_pairs={{0,2},{2,3},{3,1},{1,0},{4,6},{6,7},{7,5},{5,4},{8,10},{10,11},{11... | collective-permute-start | bytes 786440 | tf_op jit(solution)/shard_map/ppermute | solution.py:493
  112.2 12.3 %collective-permute-start.19 = (bf16[512,256]{1,0:T(8,128)(2,1)S(1)}, bf16[512,256]{1,0:T(8,128)(2,1)S(1)}, u32[]{:S(2)}, u32[]{:S(2)}) collective-permute-start(bf16[512,256]{1,0:T(8,128)(2,1)S(1)} %collective-permute-done.18.refs_5_), channel_id=1, source_target_pairs={{0,2},{2,3},{3,1},{1,0},{4,6},{6,7},{7,5},{5,4},{8,10},{10,11},{11... | collective-permute-start | bytes 786440 | tf_op jit(solution)/shard_map/ppermute | solution.py:493
  118.9 17.7 %collective-permute-start.5 = (bf16[512,256]{1,0:T(8,128)(2,1)S(1)}, bf16[512,256]{1,0:T(8,128)(2,1)S(1)}, u32[]{:S(2)}, u32[]{:S(2)}) collective-permute-start(bf16[512,256]{1,0:T(8,128)(2,1)S(1)} %collective-permute-done.4.refs_5_), channel_id=1, source_target_pairs={{0,2},{2,3},{3,1},{1,0},{4,6},{6,7},{7,5},{5,4},{8,10},{10,11},{11... | collective-permute-start | bytes 786440 | tf_op jit(solution)/shard_map/ppermute | solution.py:493
  133.2 13.6 %collective-permute-start.20 = (bf16[512,256]{1,0:T(8,128)(2,1)}, bf16[512,256]{1,0:T(8,128)(2,1)S(1)}, u32[]{:S(2)}, u32[]{:S(2)}) collective-permute-start(bf16[512,256]{1,0:T(8,128)(2,1)} %get-tuple-element.23), channel_id=1, source_target_pairs={{0,2},{2,3},{3,1},{1,0},{4,6},{6,7},{7,5},{5,4},{8,10},{10,11},{11... | collective-permute-start | bytes 786440 | tf_op jit(solution)/shard_map/ppermute | solution.py:576
  145.2 9.4 %collective-permute-start.14 = (bf16[512,256]{1,0:T(8,128)(2,1)}, bf16[512,256]{1,0:T(8,128)(2,1)S(1)}, u32[]{:S(2)}, u32[]{:S(2)}) collective-permute-start(bf16[512,256]{1,0:T(8,128)(2,1)} %get-tuple-element.18), channel_id=1, source_target_pairs={{0,2},{2,3},{3,1},{1,0},{4,6},{6,7},{7,5},{5,4},{8,10},{10,11},{11... | collective-permute-start | bytes 786440 | tf_op jit(solution)/shard_map/ppermute | solution.py:576
  146.9 13.4 %collective-permute-start.21 = (bf16[512,256]{1,0:T(8,128)(2,1)S(1)}, bf16[512,256]{1,0:T(8,128)(2,1)S(1)}, u32[]{:S(2)}, u32[]{:S(2)}) collective-permute-start(bf16[512,256]{1,0:T(8,128)(2,1)S(1)} %shard_map.110), channel_id=1, source_target_pairs={{0,2},{2,3},{3,1},{1,0},{4,6},{6,7},{7,5},{5,4},{8,10},{10,11},{11... | collective-permute-start | bytes 786440 | tf_op jit(solution)/shard_map/ppermute | solution.py:576
  155.7 10.2 %collective-permute-start.15 = (bf16[512,256]{1,0:T(8,128)(2,1)S(1)}, bf16[512,256]{1,0:T(8,128)(2,1)S(1)}, u32[]{:S(2)}, u32[]{:S(2)}) collective-permute-start(bf16[512,256]{1,0:T(8,128)(2,1)S(1)} %shard_map.106), channel_id=1, source_target_pairs={{0,2},{2,3},{3,1},{1,0},{4,6},{6,7},{7,5},{5,4},{8,10},{10,11},{11... | collective-permute-start | bytes 786440 | tf_op jit(solution)/shard_map/ppermute | solution.py:576
  160.3 11.2 %collective-permute-start.22 = (bf16[512,256]{1,0:T(8,128)(2,1)S(1)}, bf16[512,256]{1,0:T(8,128)(2,1)S(1)}, u32[]{:S(2)}, u32[]{:S(2)}) collective-permute-start(bf16[512,256]{1,0:T(8,128)(2,1)S(1)} %shard_map.111), channel_id=1, source_target_pairs={{0,2},{2,3},{3,1},{1,0},{4,6},{6,7},{7,5},{5,4},{8,10},{10,11},{11... | collective-permute-start | bytes 786440 | tf_op jit(solution)/shard_map/ppermute | solution.py:576
  (24 other events, 430.5 us)

commit v5 on v4

--- a/solution.py
+++ b/solution.py
@@ -260,10 +260,11 @@
     down_copies = [ffn_copy(pairs[k].at[1], 1, k) for k in range(2)]
     rest = []
     for k in range(2, n_dp):
-        rest.append(ffn_copy(near[k - 2], group, k))
-        rest.append(ffn_copy(far[k - 2], 1 - group, k))
-        up_copies.append(ffn_copy(near[k - 2], 0, k))
-        down_copies.append(ffn_copy(near[k - 2], 1, k))
+        near_rows = near[k - 2].at[pl.ds(0, depth)]
+        rest.append(ffn_copy(near_rows, group, k))
+        rest.append(ffn_copy(far[k - 2].at[pl.ds(0, depth)], 1 - group, k))
+        up_copies.append(ffn_copy(near_rows, 0, k))
+        down_copies.append(ffn_copy(near_rows, 1, k))
     gated_copies = [
         pltpu.make_async_copy(source, gated.at[k], gated_sems.at[k])
         for k, source in enumerate(gated_hbm[:-1])
@@ -421,19 +422,23 @@
     target_dev = new_slot // sessions_here
     session_ids = jnp.arange(sessions_here, dtype=jnp.int32)
     proj_rows = attn_weights.shape[1]
+    proj_own = attn_weights[:4].reshape(4 * proj_rows, cols_here)
+    proj_pieces = xor_gather(proj_own, "dp")
+    note_rows = 16
     notes = jnp.stack([jnp.where(survive, target_dev, -1), new_slot % sessions_here])
-    notes = jnp.pad(notes.astype(bf16), ((0, 6), (0, cols_here - sessions_here)))
-    proj_own = jnp.concatenate([attn_weights[:4].reshape(4 * proj_rows, cols_here), notes])
-    proj_pieces = xor_gather(proj_own, "dp")
+    notes = jnp.pad(
+        notes.astype(bf16), ((0, note_rows - 2), (0, units_here - sessions_here))
+    )
+    half_own = lax.dynamic_index_in_dim(
+        ffn_weights, lax.axis_index("group"), 0, keepdims=False
+    )
+    half_own = jnp.concatenate([half_own, notes])
     out_own = lax.all_to_all(
         jnp.broadcast_to(attn_weights[4:], (n_tensor, proj_rows, cols_here)),
         "tensor",
         split_axis=0,
         concat_axis=0,
         tiled=True,
-    )
-    half_own = lax.dynamic_index_in_dim(
-        ffn_weights, lax.axis_index("group"), 0, keepdims=False
     )
     sources = jnp.array(ring_sources(n_tensor), jnp.int32)[tensor_at]
     places = jnp.stack([dp_at, tensor_at]).astype(jnp.int32)
@@ -445,6 +450,26 @@
     )
     out_pieces = xor_gather(out_own, "dp")
 
+    near = xor_gather(half_own, "dp", last_bit=2)[1:]
+    swap = [(0, 1), (1, 0)]
+    far = []
+    for k, piece in enumerate(near):
+        far.append(lax.ppermute(piece, "group", swap))
+    beside = [(i, i ^ 1) for i in range(n_dp)]
+
+    def to_beside(value):
+        return lax.ppermute(value, "dp", beside)
+
+    ffn_pieces = [ffn_weights, to_beside(ffn_weights)]
+    noted = [notes[:2, :sessions_here], to_beside(notes[:, :128])[:2, :sessions_here]]
+    for name, side in (("near", near), ("far", far)):
+        for k, piece in enumerate(side):
+            ffn_pieces += [piece, to_beside(piece)]
+            if name == "near":
+                noted += [
+                    side_piece[proj_rows : proj_rows + 2, :sessions_here]
+                    for side_piece in ffn_pieces[-2:]
+                ]
     earlier = (
         (target_dev[None, :] == target_dev[:, None])
         & survive[None, :]
@@ -452,7 +477,7 @@
     )
     pair_rank = jnp.sum(earlier.astype(jnp.int32), axis=1)
     send_pos = jnp.where(survive, target_dev * pair_cap + pair_rank, -1)
-    meta = jnp.stack([piece[4 * proj_rows :, :sessions_here] for piece in proj_pieces])
+    meta = jnp.stack(noted)
     meta = meta.astype(jnp.int32)
     from_dev = jnp.bitwise_xor(dp_at, jnp.arange(n_dp, dtype=jnp.int32))
     coming = meta[:, 0] == dp_at
@@ -492,20 +517,6 @@
         for c in range(CHUNKS):
             gated[c].append(lax.ppermute(gated[c][-1], "tensor", ring))
 
-    near = xor_gather(half_own, "dp", last_bit=2)[1:]
-    swap = [(0, 1), (1, 0)]
-    far = []
-    for k, piece in enumerate(near):
-        far.append(lax.ppermute(piece, "group", swap))
-    beside = [(i, i ^ 1) for i in range(n_dp)]
-
-    def to_beside(value):
-        return lax.ppermute(value, "dp", beside)
-
-    ffn_pieces = [ffn_weights, to_beside(ffn_weights)]
-    for side in (near, far):
-        for k, piece in enumerate(side):
-            ffn_pieces += [piece, to_beside(piece)]
     packed = kernel_call(
         functools.partial(state_kernel, CHUNKS, heads_here, event_count),
         [vmem_spec(), smem_spec()] + [hbm_spec()] * (1 + 2 * CHUNKS),

time: 182 us -> 171 us (0.940)
  waiting for transfers between devices: 87.1 us -> 74.8 us
  other arithmetic: 1.46 us -> 3.58 us
    ppermute x7, waiting for transfers between devices: 58.9 us -> 43.2 us  [xor_gather(): arrived.append(lax.ppermute(piece, axis, pairs))]
    ppermute x6, waiting for transfers between devices: 9.85 us -> 11.7 us  [per_device(): gated[c].append(lax.ppermute(gated[c][-1], 'tensor', ring))]
  transfers between devices with their start and end apart: 25 -> 26, of which waited for: 11 -> 11; matrix products, arithmetic and copies ran while one was open for 4% -> 5% of each run, Pallas kernels for 19% -> 20%
where the time goes in v5:
time: 171 us; the launch traced here: 170 us
  waiting for transfers between devices  74.8 us (44%)
  starting transfers between devices  44.6 us (26%)
  Pallas kernels  38.6 us (23%)
  local copies, waits for them, and re-layouts  7.55 us (4%)
  other arithmetic  3.58 us (2%)
    ppermute x7, waiting for transfers between devices, xor_gather(): arrived.append(lax.ppermute(piece, axis, pairs))  43.2 us
    ppermute x6, waiting for transfers between devices, per_device(): sums[c] = lax.ppermute(mine, 'tensor', ring)  18.9 us
    pallas_call x2, Pallas kernels, per_device(): kernel_call(functools.partial(feed_kernel, n_dp, n_tensor, block, c * chu...  17 us
    ppermute x6, starting transfers between devices, per_device(): gated[c].append(lax.ppermute(gated[c][-1], 'tensor', ring))  15.2 us
    ppermute x6, waiting for transfers between devices, per_device(): gated[c].append(lax.ppermute(gated[c][-1], 'tensor', ring))  11.7 us
    ppermute x6, starting transfers between devices, per_device(): sums[c] = lax.ppermute(mine, 'tensor', ring)  10.3 us
    pallas_call x2, Pallas kernels, per_device(): kernel_call(functools.partial(project_kernel, n_dp, heads_here, event_cou...  9.62 us
    ppermute x7, starting transfers between devices, xor_gather(): arrived.append(lax.ppermute(piece, axis, pairs))  6.65 us
  transfers between devices with their start and end apart: 26, of which 11 were waited for; matrix products, arithmetic and copies ran while one was open for 5% of the time, Pallas kernels for 20%

profile of v5, /device:TPU:0, one launch (start us, length us, event | category | flops | bytes accessed | tf_op | source)
XLA Modules:
  0.0 170.3 jit_solution(10780544053473813586)
XLA Ops:
  1.9 3.0 %collective-permute-start.1 = (bf16[1024,256]{1,0:T(8,128)(2,1)S(1)}, bf16[1024,256]{1,0:T(8,128)(2,1)S(1)}, u32[]{:S(2)}, u32[]{:S(2)}) collective-permute-start(bf16[1024,256]{1,0:T(8,128)(2,1)S(1)} %bitcast.28), channel_id=1, source_target_pairs={{0,8},{4,12},{8,0},{12,4},{1,9},{5,13},{9,1},{13,5},{2,10},{6,14},... | collective-permute-start | bytes 1572872 | tf_op jit(solution)/shard_map/ppermute | solution.py:346
  6.7 4.9 %all-to-all-start = ((bf16[4,256,256]{2,1,0:T(8,128)(2,1)}), bf16[4,256,256]{2,1,0:T(8,128)(2,1)}, u32[]{:S(2)}, u32[]{:S(2)}) async-start(bf16[4,256,256]{2,1,0:T(8,128)(2,1)} %broadcast_in_dim.22), calls=%async_computation | async-start | bytes 1048576 | tf_op jit(solution)/shard_map/all_to_all | solution.py:436
  20.4 4.8 %shard_map.108 = (bf16[512,256]{1,0:T(8,128)(2,1)S(1)}, bf16[512,256]{1,0:T(8,128)(2,1)}, bf16[512,256]{1,0:T(8,128)(2,1)}) custom-call(s32[7]{0:T(128)S(1)} %pad_add_fusion.refs_0_, f32[4,1024]{1,0:T(4,128)S(1)} %pad_maximum_fusion.1.refs_1_.refs_0_, bf16[1024,1024]{1,0:T(8,128)(2,1)S(1)} %copy-done, f32[32,2,128,128]{3,2,1,0:T(8,128)} %refs_2_.9, ...), custom_call_target="tpu_custom_call" | custom-call | flops 1073741824 | bytes 4194304 | tf_op jit(solution)/shard_map/pallas_call | solution.py:496
  25.2 4.9 %shard_map.104 = (bf16[512,256]{1,0:T(8,128)(2,1)S(1)}, bf16[512,256]{1,0:T(8,128)(2,1)}, bf16[512,256]{1,0:T(8,128)(2,1)}) custom-call(s32[7]{0:T(128)S(1)} %pad_add_fusion.refs_0_, f32[4,1024]{1,0:T(4,128)S(1)} %pad_maximum_fusion.1.refs_1_.refs_0_, bf16[1024,1024]{1,0:T(8,128)(2,1)S(1)} %copy-done, f32[32,2,128,128]{3,2,1,0:T(8,128)} %refs_2_.9, ...), custom_call_target="tpu_custom_call" | custom-call | flops 1073741824 | bytes 4194304 | tf_op jit(solution)/shard_map/pallas_call | solution.py:496
  30.1 4.7 %shard_map.112 = bf16[64,2,128,128]{3,2,1,0:T(8,128)(2,1)} custom-call(f32[4,1024]{1,0:T(4,128)S(1)} %pad_maximum_fusion.1.refs_1_.refs_0_, s32[32]{0:T(128)S(1)} %get-tuple-element.33.refs_1_, f32[32,2,128,128]{3,2,1,0:T(8,128)} %refs_2_.9, bf16[512,256]{1,0:T(8,128)(2,1)} %get-tuple-element.26.refs_3_, bf16[512,256]{1,0:T(8,128)(2,1)} %get-tuple-element.27.refs_4_, ...), custom_call_target="tpu_custom_call" | custom-call | flops 67108864 | bytes 4194304 | tf_op jit(solution)/shard_map/pallas_call | solution.py:520
  34.9 5.0 %all-to-all-start.1 = ((bf16[64,2,128,128]{3,2,1,0:T(8,128)(2,1)}), bf16[64,2,128,128]{3,2,1,0:T(8,128)(2,1)}, u32[]{:S(2)}, u32[]{:S(2)}) async-start(bf16[64,2,128,128]{3,2,1,0:T(8,128)(2,1)} %shard_map.112), calls=%async_computation.1 | async-start | bytes 8388608 | tf_op jit(solution)/shard_map/all_to_all | solution.py:535
  41.6 1.8 %collective-permute-start.7 = (bf16[4,256,256]{2,1,0:T(8,128)(2,1)}, bf16[4,256,256]{2,1,0:T(8,128)(2,1)S(1)}, u32[]{:S(2)}, u32[]{:S(2)}) collective-permute-start(bf16[4,256,256]{2,1,0:T(8,128)(2,1)} %all-to-all-done.refs_7_), channel_id=1, source_target_pairs={{0,8},{4,12},{8,0},{12,4},{1,9},{5,13},{9,1},{13,5},{2,10},{6,14},... | collective-permute-start | bytes 1572872 | tf_op jit(solution)/shard_map/ppermute | solution.py:346
  44.5 2.6 %collective-permute-start.17 = (bf16[512,256]{1,0:T(8,128)(2,1)S(1)}, bf16[512,256]{1,0:T(8,128)(2,1)S(1)}, u32[]{:S(2)}, u32[]{:S(2)}) collective-permute-start(bf16[512,256]{1,0:T(8,128)(2,1)S(1)} %copy-done.10), channel_id=1, source_target_pairs={{0,2},{2,3},{3,1},{1,0},{4,6},{6,7},{7,5},{5,4},{8,10},{10,11},{11... | collective-permute-start | bytes 786440 | tf_op jit(solution)/shard_map/ppermute | solution.py:518
  48.8 5.0 %collective-permute-done.17.refs_4_ = bf16[512,256]{1,0:T(8,128)(2,1)S(1)} collective-permute-done((bf16[512,256]{1,0:T(8,128)(2,1)S(1)}, bf16[512,256]{1,0:T(8,128)(2,1)S(1)}, u32[]{:S(2)}, u32[]{:S(2)}) %collective-permute-start.17) | collective-permute-done | bytes 262176 | tf_op jit(solution)/shard_map/ppermute | solution.py:518
  53.8 3.4 %collective-permute-start.18 = (bf16[512,256]{1,0:T(8,128)(2,1)S(1)}, bf16[512,256]{1,0:T(8,128)(2,1)S(1)}, u32[]{:S(2)}, u32[]{:S(2)}) collective-permute-start(bf16[512,256]{1,0:T(8,128)(2,1)S(1)} %collective-permute-done.17.refs_4_), channel_id=1, source_target_pairs={{0,2},{2,3},{3,1},{1,0},{4,6},{6,7},{7,5},{5,4},{8,10},{10,11},{11... | collective-permute-start | bytes 786440 | tf_op jit(solution)/shard_map/ppermute | solution.py:518
  57.8 41.4 %collective-permute-done.7.refs_9_ = bf16[4,256,256]{2,1,0:T(8,128)(2,1)S(1)} collective-permute-done((bf16[4,256,256]{2,1,0:T(8,128)(2,1)}, bf16[4,256,256]{2,1,0:T(8,128)(2,1)S(1)}, u32[]{:S(2)}, u32[]{:S(2)}) %collective-permute-start.7) | collective-permute-done | bytes 524320 | tf_op jit(solution)/shard_map/ppermute | solution.py:346
  99.2 2.6 %collective-permute-start.4 = (bf16[512,256]{1,0:T(8,128)(2,1)S(1)}, bf16[512,256]{1,0:T(8,128)(2,1)S(1)}, u32[]{:S(2)}, u32[]{:S(2)}) collective-permute-start(bf16[512,256]{1,0:T(8,128)(2,1)S(1)} %collective-permute-done.3.refs_4_), channel_id=1, source_target_pairs={{0,2},{2,3},{3,1},{1,0},{4,6},{6,7},{7,5},{5,4},{8,10},{10,11},{11... | collective-permute-start | bytes 786440 | tf_op jit(solution)/shard_map/ppermute | solution.py:518
  104.1 4.4 %collective-permute-done.4.refs_5_ = bf16[512,256]{1,0:T(8,128)(2,1)S(1)} collective-permute-done((bf16[512,256]{1,0:T(8,128)(2,1)S(1)}, bf16[512,256]{1,0:T(8,128)(2,1)S(1)}, u32[]{:S(2)}, u32[]{:S(2)}) %collective-permute-start.4) | collective-permute-done | bytes 262176 | tf_op jit(solution)/shard_map/ppermute | solution.py:518
  108.6 3.4 %collective-permute-start.5 = (bf16[512,256]{1,0:T(8,128)(2,1)S(1)}, bf16[512,256]{1,0:T(8,128)(2,1)S(1)}, u32[]{:S(2)}, u32[]{:S(2)}) collective-permute-start(bf16[512,256]{1,0:T(8,128)(2,1)S(1)} %collective-permute-done.4.refs_5_), channel_id=1, source_target_pairs={{0,2},{2,3},{3,1},{1,0},{4,6},{6,7},{7,5},{5,4},{8,10},{10,11},{11... | collective-permute-start | bytes 786440 | tf_op jit(solution)/shard_map/ppermute | solution.py:518
  112.0 2.2 %collective-permute-done.19.refs_6_ = bf16[512,256]{1,0:T(8,128)(2,1)S(1)} collective-permute-done((bf16[512,256]{1,0:T(8,128)(2,1)S(1)}, bf16[512,256]{1,0:T(8,128)(2,1)S(1)}, u32[]{:S(2)}, u32[]{:S(2)}) %collective-permute-start.19) | collective-permute-done | bytes 262176 | tf_op jit(solution)/shard_map/ppermute | solution.py:518
  114.2 8.5 %shard_map.109 = (f32[512,256]{1,0:T(8,128)}, bf16[512,256]{1,0:T(8,128)(2,1)}, bf16[512,256]{1,0:T(8,128)(2,1)}, bf16[512,256]{1,0:T(8,128)(2,1)}) custom-call(s32[7]{0:T(128)S(1)} %pad_add_fusion.refs_0_, f32[4,1024]{1,0:T(4,128)S(1)} %pad_maximum_fusion.1.refs_1_.refs_0_, bf16[1024,1024]{1,0:T(8,128)(2,1)S(1)} %copy-done, bf16[512,256]{1,0:T(8,128)(2,1)} %copy-done.9, ...), custom_call_target="tpu_custom_call" | custom-call | flops 3221225472 | bytes 4194304 | tf_op jit(solution)/shard_map/pallas_call | solution.py:539
  122.8 3.4 %collective-permute-start.20 = (bf16[512,256]{1,0:T(8,128)(2,1)}, bf16[512,256]{1,0:T(8,128)(2,1)S(1)}, u32[]{:S(2)}, u32[]{:S(2)}) collective-permute-start(bf16[512,256]{1,0:T(8,128)(2,1)} %get-tuple-element.23), channel_id=1, source_target_pairs={{0,2},{2,3},{3,1},{1,0},{4,6},{6,7},{7,5},{5,4},{8,10},{10,11},{11... | collective-permute-start | bytes 786440 | tf_op jit(solution)/shard_map/ppermute | solution.py:587
  126.2 8.5 %shard_map.105 = (f32[512,256]{1,0:T(8,128)}, bf16[512,256]{1,0:T(8,128)(2,1)}, bf16[512,256]{1,0:T(8,128)(2,1)}, bf16[512,256]{1,0:T(8,128)(2,1)}) custom-call(s32[7]{0:T(128)S(1)} %pad_add_fusion.refs_0_, f32[4,1024]{1,0:T(4,128)S(1)} %pad_maximum_fusion.1.refs_1_.refs_0_, bf16[1024,1024]{1,0:T(8,128)(2,1)S(1)} %copy-done, bf16[512,256]{1,0:T(8,128)(2,1)} %copy-done.8, ...), custom_call_target="tpu_custom_call" | custom-call | flops 3221225472 | bytes 4194304 | tf_op jit(solution)/shard_map/pallas_call | solution.py:539
  136.9 7.3 %collective-permute-done.14.a_ref = bf16[512,256]{1,0:T(8,128)(2,1)S(1)} collective-permute-done((bf16[512,256]{1,0:T(8,128)(2,1)}, bf16[512,256]{1,0:T(8,128)(2,1)S(1)}, u32[]{:S(2)}, u32[]{:S(2)}) %collective-permute-start.14) | collective-permute-done | bytes 262176 | tf_op jit(solution)/shard_map/ppermute | solution.py:587
  147.1 2.7 %collective-permute-done.21.a_ref = bf16[512,256]{1,0:T(8,128)(2,1)S(1)} collective-permute-done((bf16[512,256]{1,0:T(8,128)(2,1)S(1)}, bf16[512,256]{1,0:T(8,128)(2,1)S(1)}, u32[]{:S(2)}, u32[]{:S(2)}) %collective-permute-start.21) | collective-permute-done | bytes 262176 | tf_op jit(solution)/shard_map/ppermute | solution.py:587
  151.5 3.9 %collective-permute-done.15.a_ref = bf16[512,256]{1,0:T(8,128)(2,1)S(1)} collective-permute-done((bf16[512,256]{1,0:T(8,128)(2,1)S(1)}, bf16[512,256]{1,0:T(8,128)(2,1)S(1)}, u32[]{:S(2)}, u32[]{:S(2)}) %collective-permute-start.15) | collective-permute-done | bytes 262176 | tf_op jit(solution)/shard_map/ppermute | solution.py:587
  158.2 2.9 %collective-permute-done.22.refs_2_ = bf16[512,256]{1,0:T(8,128)(2,1)S(1)} collective-permute-done((bf16[512,256]{1,0:T(8,128)(2,1)S(1)}, bf16[512,256]{1,0:T(8,128)(2,1)S(1)}, u32[]{:S(2)}, u32[]{:S(2)}) %collective-permute-start.22) | collective-permute-done | bytes 262176 | tf_op jit(solution)/shard_map/ppermute | solution.py:587
  162.4 2.1 %collective-permute-done.16.refs_2_ = bf16[512,256]{1,0:T(8,128)(2,1)S(1)} collective-permute-done((bf16[512,256]{1,0:T(8,128)(2,1)S(1)}, bf16[512,256]{1,0:T(8,128)(2,1)S(1)}, u32[]{:S(2)}, u32[]{:S(2)}) %collective-permute-start.16) | collective-permute-done | bytes 262176 | tf_op jit(solution)/shard_map/ppermute | solution.py:587
  165.8 4.3 %unpack.1 = f32[32,2,128,128]{3,2,1,0:T(8,128)} custom-call(s32[32]{0:T(128)S(1)} %broadcast_add_fusion.src_ref, bf16[64,2,128,128]{3,2,1,0:T(8,128)(2,1)} %all-to-all-done.1.recv_ref), custom_call_target="tpu_custom_call" | custom-call | bytes 6291456 | tf_op jit(solution)/shard_map/unpack/pallas_call | solution.py:612
  (116 shorter events, 31.3 us)
Async XLA Ops:
  1.9 15.0 %collective-permute-start.1 = (bf16[1024,256]{1,0:T(8,128)(2,1)S(1)}, bf16[1024,256]{1,0:T(8,128)(2,1)S(1)}, u32[]{:S(2)}, u32[]{:S(2)}) collective-permute-start(bf16[1024,256]{1,0:T(8,128)(2,1)S(1)} %bitcast.28), channel_id=1, source_target_pairs={{0,8},{4,12},{8,0},{12,4},{1,9},{5,13},{9,1},{13,5},{2,10},{6,14},... | collective-permute-start | bytes 1572872 | tf_op jit(solution)/shard_map/ppermute | solution.py:346
  4.9 15.5 %collective-permute-start = (bf16[1024,256]{1,0:T(8,128)(2,1)S(1)}, bf16[1024,256]{1,0:T(8,128)(2,1)}, u32[]{:S(2)}, u32[]{:S(2)}) collective-permute-start(bf16[1024,256]{1,0:T(8,128)(2,1)S(1)} %bitcast.29), channel_id=1, source_target_pairs={{0,4},{4,0},{8,12},{12,8},{1,5},{5,1},{9,13},{13,9},{2,6},{6,2},{1... | collective-permute-start | bytes 1572872 | tf_op jit(solution)/shard_map/ppermute | solution.py:346
  6.7 28.2 %all-to-all-start = ((bf16[4,256,256]{2,1,0:T(8,128)(2,1)}), bf16[4,256,256]{2,1,0:T(8,128)(2,1)}, u32[]{:S(2)}, u32[]{:S(2)}) async-start(bf16[4,256,256]{2,1,0:T(8,128)(2,1)} %broadcast_in_dim.22), calls=%async_computation | async-start | bytes 1048576 | tf_op jit(solution)/shard_map/all_to_all | solution.py:436
  11.5 35.6 %collective-permute-start.9 = (bf16[2,256,1024]{2,1,0:T(8,128)(2,1)}, bf16[2,256,1024]{2,1,0:T(8,128)(2,1)}, u32[]{:S(2)}, u32[]{:S(2)}) collective-permute-start(bf16[2,256,1024]{2,1,0:T(8,128)(2,1)} %refs_11_.3), channel_id=1, source_target_pairs={{0,4},{4,0},{8,12},{12,8},{1,5},{5,1},{9,13},{13,9},{2,6},{6,2},{1... | collective-permute-start | bytes 3145736 | tf_op jit(solution)/shard_map/ppermute | solution.py:461
  17.7 22.2 %collective-permute-start.10 = (bf16[272,1024]{1,0:T(8,128)(2,1)}, bf16[272,1024]{1,0:T(8,128)(2,1)}, u32[]{:S(2)}, u32[]{:S(2)}) collective-permute-start(bf16[272,1024]{1,0:T(8,128)(2,1)} %pad_maximum_fusion), channel_id=1, source_target_pairs={{0,8},{4,12},{8,0},{12,4},{1,9},{5,13},{9,1},{13,5},{2,10},{6,14},... | collective-permute-start | bytes 1671176 | tf_op jit(solution)/shard_map/ppermute | solution.py:346
  34.9 131.0 %all-to-all-start.1 = ((bf16[64,2,128,128]{3,2,1,0:T(8,128)(2,1)}), bf16[64,2,128,128]{3,2,1,0:T(8,128)(2,1)}, u32[]{:S(2)}, u32[]{:S(2)}) async-start(bf16[64,2,128,128]{3,2,1,0:T(8,128)(2,1)} %shard_map.112), calls=%async_computation.1 | async-start | bytes 8388608 | tf_op jit(solution)/shard_map/all_to_all | solution.py:535
  39.9 17.3 %collective-permute-start.12 = (bf16[272,1024]{1,0:T(8,128)(2,1)}, bf16[272,1024]{1,0:T(8,128)(2,1)S(1)}, u32[]{:S(2)}, u32[]{:S(2)}) collective-permute-start(bf16[272,1024]{1,0:T(8,128)(2,1)} %collective-permute-done.10.refs_13_), channel_id=1, source_target_pairs={{0,16},{16,0},{1,17},{17,1},{2,18},{18,2},{3,19},{19,3},{4,20},{20... | collective-permute-start | bytes 1671176 | tf_op jit(solution)/shard_map/ppermute | solution.py:457
  41.5 15.8 %collective-permute-start.11 = (bf16[272,1024]{1,0:T(8,128)(2,1)}, bf16[272,1024]{1,0:T(8,128)(2,1)S(1)}, u32[]{:S(2)}, u32[]{:S(2)}) collective-permute-start(bf16[272,1024]{1,0:T(8,128)(2,1)} %collective-permute-done.10.refs_13_), channel_id=1, source_target_pairs={{0,4},{4,0},{8,12},{12,8},{1,5},{5,1},{9,13},{13,9},{2,6},{6,2},{1... | collective-permute-start | bytes 1671176 | tf_op jit(solution)/shard_map/ppermute | solution.py:461
  41.6 57.6 %collective-permute-start.7 = (bf16[4,256,256]{2,1,0:T(8,128)(2,1)}, bf16[4,256,256]{2,1,0:T(8,128)(2,1)S(1)}, u32[]{:S(2)}, u32[]{:S(2)}) collective-permute-start(bf16[4,256,256]{2,1,0:T(8,128)(2,1)} %all-to-all-done.refs_7_), channel_id=1, source_target_pairs={{0,8},{4,12},{8,0},{12,4},{1,9},{5,13},{9,1},{13,5},{2,10},{6,14},... | collective-permute-start | bytes 1572872 | tf_op jit(solution)/shard_map/ppermute | solution.py:346
  44.5 9.3 %collective-permute-start.17 = (bf16[512,256]{1,0:T(8,128)(2,1)S(1)}, bf16[512,256]{1,0:T(8,128)(2,1)S(1)}, u32[]{:S(2)}, u32[]{:S(2)}) collective-permute-start(bf16[512,256]{1,0:T(8,128)(2,1)S(1)} %copy-done.10), channel_id=1, source_target_pairs={{0,2},{2,3},{3,1},{1,0},{4,6},{6,7},{7,5},{5,4},{8,10},{10,11},{11... | collective-permute-start | bytes 786440 | tf_op jit(solution)/shard_map/ppermute | solution.py:518
  47.2 52.1 %collective-permute-start.3 = (bf16[512,256]{1,0:T(8,128)(2,1)S(1)}, bf16[512,256]{1,0:T(8,128)(2,1)S(1)}, u32[]{:S(2)}, u32[]{:S(2)}) collective-permute-start(bf16[512,256]{1,0:T(8,128)(2,1)S(1)} %get-tuple-element.16.refs_3_), channel_id=1, source_target_pairs={{0,2},{2,3},{3,1},{1,0},{4,6},{6,7},{7,5},{5,4},{8,10},{10,11},{11... | collective-permute-start | bytes 786440 | tf_op jit(solution)/shard_map/ppermute | solution.py:518
  53.8 48.0 %collective-permute-start.18 = (bf16[512,256]{1,0:T(8,128)(2,1)S(1)}, bf16[512,256]{1,0:T(8,128)(2,1)S(1)}, u32[]{:S(2)}, u32[]{:S(2)}) collective-permute-start(bf16[512,256]{1,0:T(8,128)(2,1)S(1)} %collective-permute-done.17.refs_4_), channel_id=1, source_target_pairs={{0,2},{2,3},{3,1},{1,0},{4,6},{6,7},{7,5},{5,4},{8,10},{10,11},{11... | collective-permute-start | bytes 786440 | tf_op jit(solution)/shard_map/ppermute | solution.py:518
  57.2 54.7 %collective-permute-start.6 = (bf16[4,256,256]{2,1,0:T(8,128)(2,1)}, bf16[4,256,256]{2,1,0:T(8,128)(2,1)S(1)}, u32[]{:S(2)}, u32[]{:S(2)}) collective-permute-start(bf16[4,256,256]{2,1,0:T(8,128)(2,1)} %all-to-all-done.refs_7_), channel_id=1, source_target_pairs={{0,4},{4,0},{8,12},{12,8},{1,5},{5,1},{9,13},{13,9},{2,6},{6,2},{1... | collective-permute-start | bytes 1572872 | tf_op jit(solution)/shard_map/ppermute | solution.py:346
  57.3 54.6 %collective-permute-start.13 = (bf16[272,1024]{1,0:T(8,128)(2,1)S(1)}, bf16[272,1024]{1,0:T(8,128)(2,1)S(1)}, u32[]{:S(2)}, u32[]{:S(2)}) collective-permute-start(bf16[272,1024]{1,0:T(8,128)(2,1)S(1)} %collective-permute-done.12.refs_15_), channel_id=1, source_target_pairs={{0,4},{4,0},{8,12},{12,8},{1,5},{5,1},{9,13},{13,9},{2,6},{6,2},{1... | collective-permute-start | bytes 1671176 | tf_op jit(solution)/shard_map/ppermute | solution.py:461
  99.2 12.8 %collective-permute-start.8 = (bf16[4,256,256]{2,1,0:T(8,128)(2,1)S(1)}, bf16[4,256,256]{2,1,0:T(8,128)(2,1)S(1)}, u32[]{:S(2)}, u32[]{:S(2)}) collective-permute-start(bf16[4,256,256]{2,1,0:T(8,128)(2,1)S(1)} %collective-permute-done.7.refs_9_), channel_id=1, source_target_pairs={{0,4},{4,0},{8,12},{12,8},{1,5},{5,1},{9,13},{13,9},{2,6},{6,2},{1... | collective-permute-start | bytes 1572872 | tf_op jit(solution)/shard_map/ppermute | solution.py:346
  99.2 9.3 %collective-permute-start.4 = (bf16[512,256]{1,0:T(8,128)(2,1)S(1)}, bf16[512,256]{1,0:T(8,128)(2,1)S(1)}, u32[]{:S(2)}, u32[]{:S(2)}) collective-permute-start(bf16[512,256]{1,0:T(8,128)(2,1)S(1)} %collective-permute-done.3.refs_4_), channel_id=1, source_target_pairs={{0,2},{2,3},{3,1},{1,0},{4,6},{6,7},{7,5},{5,4},{8,10},{10,11},{11... | collective-permute-start | bytes 786440 | tf_op jit(solution)/shard_map/ppermute | solution.py:518
  101.9 12.3 %collective-permute-start.19 = (bf16[512,256]{1,0:T(8,128)(2,1)S(1)}, bf16[512,256]{1,0:T(8,128)(2,1)S(1)}, u32[]{:S(2)}, u32[]{:S(2)}) collective-permute-start(bf16[512,256]{1,0:T(8,128)(2,1)S(1)} %collective-permute-done.18.refs_5_), channel_id=1, source_target_pairs={{0,2},{2,3},{3,1},{1,0},{4,6},{6,7},{7,5},{5,4},{8,10},{10,11},{11... | collective-permute-start | bytes 786440 | tf_op jit(solution)/shard_map/ppermute | solution.py:518
  108.6 17.7 %collective-permute-start.5 = (bf16[512,256]{1,0:T(8,128)(2,1)S(1)}, bf16[512,256]{1,0:T(8,128)(2,1)S(1)}, u32[]{:S(2)}, u32[]{:S(2)}) collective-permute-start(bf16[512,256]{1,0:T(8,128)(2,1)S(1)} %collective-permute-done.4.refs_5_), channel_id=1, source_target_pairs={{0,2},{2,3},{3,1},{1,0},{4,6},{6,7},{7,5},{5,4},{8,10},{10,11},{11... | collective-permute-start | bytes 786440 | tf_op jit(solution)/shard_map/ppermute | solution.py:518
  122.8 12.7 %collective-permute-start.20 = (bf16[512,256]{1,0:T(8,128)(2,1)}, bf16[512,256]{1,0:T(8,128)(2,1)S(1)}, u32[]{:S(2)}, u32[]{:S(2)}) collective-permute-start(bf16[512,256]{1,0:T(8,128)(2,1)} %get-tuple-element.23), channel_id=1, source_target_pairs={{0,2},{2,3},{3,1},{1,0},{4,6},{6,7},{7,5},{5,4},{8,10},{10,11},{11... | collective-permute-start | bytes 786440 | tf_op jit(solution)/shard_map/ppermute | solution.py:587
  134.8 9.4 %collective-permute-start.14 = (bf16[512,256]{1,0:T(8,128)(2,1)}, bf16[512,256]{1,0:T(8,128)(2,1)S(1)}, u32[]{:S(2)}, u32[]{:S(2)}) collective-permute-start(bf16[512,256]{1,0:T(8,128)(2,1)} %get-tuple-element.18), channel_id=1, source_target_pairs={{0,2},{2,3},{3,1},{1,0},{4,6},{6,7},{7,5},{5,4},{8,10},{10,11},{11... | collective-permute-start | bytes 786440 | tf_op jit(solution)/shard_map/ppermute | solution.py:587
  135.6 14.2 %collective-permute-start.21 = (bf16[512,256]{1,0:T(8,128)(2,1)S(1)}, bf16[512,256]{1,0:T(8,128)(2,1)S(1)}, u32[]{:S(2)}, u32[]{:S(2)}) collective-permute-start(bf16[512,256]{1,0:T(8,128)(2,1)S(1)} %shard_map.110), channel_id=1, source_target_pairs={{0,2},{2,3},{3,1},{1,0},{4,6},{6,7},{7,5},{5,4},{8,10},{10,11},{11... | collective-permute-start | bytes 786440 | tf_op jit(solution)/shard_map/ppermute | solution.py:587
  145.2 10.2 %collective-permute-start.15 = (bf16[512,256]{1,0:T(8,128)(2,1)S(1)}, bf16[512,256]{1,0:T(8,128)(2,1)S(1)}, u32[]{:S(2)}, u32[]{:S(2)}) collective-permute-start(bf16[512,256]{1,0:T(8,128)(2,1)S(1)} %shard_map.106), channel_id=1, source_target_pairs={{0,2},{2,3},{3,1},{1,0},{4,6},{6,7},{7,5},{5,4},{8,10},{10,11},{11... | collective-permute-start | bytes 786440 | tf_op jit(solution)/shard_map/ppermute | solution.py:587
  149.9 11.2 %collective-permute-start.22 = (bf16[512,256]{1,0:T(8,128)(2,1)S(1)}, bf16[512,256]{1,0:T(8,128)(2,1)S(1)}, u32[]{:S(2)}, u32[]{:S(2)}) collective-permute-start(bf16[512,256]{1,0:T(8,128)(2,1)S(1)} %shard_map.111), channel_id=1, source_target_pairs={{0,2},{2,3},{3,1},{1,0},{4,6},{6,7},{7,5},{5,4},{8,10},{10,11},{11... | collective-permute-start | bytes 786440 | tf_op jit(solution)/shard_map/ppermute | solution.py:587
  156.4 8.0 %collective-permute-start.16 = (bf16[512,256]{1,0:T(8,128)(2,1)S(1)}, bf16[512,256]{1,0:T(8,128)(2,1)S(1)}, u32[]{:S(2)}, u32[]{:S(2)}) collective-permute-start(bf16[512,256]{1,0:T(8,128)(2,1)S(1)} %shard_map.107), channel_id=1, source_target_pairs={{0,2},{2,3},{3,1},{1,0},{4,6},{6,7},{7,5},{5,4},{8,10},{10,11},{11... | collective-permute-start | bytes 786440 | tf_op jit(solution)/shard_map/ppermute | solution.py:587
  (25 other events, 495.6 us)

commit v6 on v5

--- a/solution.py
+++ b/solution.py
@@ -38,10 +38,14 @@
 
 
 def project_kernel(n_dp, heads, event_count, block, base, *refs):
-    ids_ref, small_ref, tok_ref, past_hbm = refs[:4]
+    rates_ref, gains_hbm, tok_ref, past_hbm = refs[:4]
     pieces = refs[4 : 4 + n_dp]
     gated_ref, key_hbm, value_hbm = refs[4 + n_dp : 7 + n_dp]
-    normed_ref, past_ref, decay_ref, key_ref, value_ref, w_ref, sems = refs[7 + n_dp :]
+    normed_ref, past_ref, decay_ref, key_ref, value_ref, w_ref, gain_ref, sems = refs[7 + n_dp :]
+    gain_copy = pltpu.make_async_copy(gains_hbm, gain_ref, sems.at[3])
+    gain_copy.start()
+    me = lax.axis_index("dp")
+    first_head = lax.axis_index("tensor") * heads
     past_copy = pltpu.make_async_copy(
         past_hbm.at[pl.ds(base // event_count, past_ref.shape[0])], past_ref, sems.at[0]
     )
@@ -55,7 +59,7 @@
     sessions = block // event_count
     key_scale = head_dim ** (-0.5)
     depth = tok_ref.shape[1] // n_dp
-    starts = [pl.multiple_of(jnp.bitwise_xor(ids_ref[0], k) * depth, depth) for k in range(n_dp)]
+    starts = [pl.multiple_of(jnp.bitwise_xor(me, k) * depth, depth) for k in range(n_dp)]
     split = depth % 128 == 0
     if not split:
         for m in range(4):
@@ -69,9 +73,10 @@
     since = (place + 1).astype(jnp.float32)
     factors = []
     for h in range(heads):
-        rate = small_ref[2 + h : 3 + h, :]
-        decay_ref[h] = jnp.where(allowed, jnp.exp(-rate[:, :block] * distance), 0.0) * key_scale
-        factors.append(jnp.exp(-rate[:, :head_dim] * since))
+        rate = rates_ref[first_head + h]
+        decay_ref[h] = jnp.where(allowed, jnp.exp(-rate * distance), 0.0) * key_scale
+        factors.append(jnp.exp(-rate * since))
+    gain_copy.wait()
 
     def product(span, m):
         if not split:
@@ -87,7 +92,7 @@
     for r in range(0, rows, block):
         span = slice(r, r + block)
         normed_ref[span] = rms_scale(
-            tok_ref[base + r : base + r + block].astype(jnp.float32), small_ref[0:1, :]
+            tok_ref[base + r : base + r + block].astype(jnp.float32), gain_ref[0:1, :]
         )
         query = product(span, 0).astype(jnp.bfloat16)
         keys = product(span, 1).astype(jnp.bfloat16)
@@ -124,7 +129,8 @@
 
 
 def state_kernel(chunks, heads, event_count, *refs):
-    small_ref, pos_ref, past_hbm = refs[:3]
+    rates_ref, pos_ref, past_hbm = refs[:3]
+    first_head = lax.axis_index("tensor") * heads
     sources = refs[3 : 3 + 2 * chunks]
     out_ref, buf_ref, past_ref, kv_ref, sems, past_sems, kv_sems = refs[3 + 2 * chunks :]
     kv_copies = [
@@ -158,9 +164,9 @@
     left = (event_count - 1 - place).astype(jnp.float32)
     factors, carries = [], []
     for h in range(heads):
-        rate = small_ref[2 + h : 3 + h, :head_dim]
+        rate = rates_ref[first_head + h]
         factors.append(jnp.exp(-rate * left) * key_scale)
-        carries.append(jnp.exp(-rate * event_count))
+        carries.append(jnp.exp(jnp.full((1, head_dim), -rate * event_count, jnp.float32)))
     for c in range(chunks):
         kv_copies[c].wait()
         kv_copies[chunks + c].wait()
@@ -229,9 +235,9 @@
 
 
 def feed_kernel(n_dp, n_tensor, block, base, *refs):
-    ids_ref, small_ref, tok_ref = refs[:3]
-    gated_hbm = refs[3 : 3 + n_tensor]
-    at = 3 + n_tensor
+    gains_hbm, tok_ref = refs[:2]
+    gated_hbm = refs[2 : 2 + n_tensor]
+    at = 2 + n_tensor
     out_pieces = refs[at : at + n_dp]
     at += n_dp
     pairs = refs[at : at + 2]
@@ -239,12 +245,19 @@
     far = refs[at + n_dp : at + 2 * n_dp - 2]
     at += 2 * n_dp - 2
     own_hbm, *part_hbm = refs[at : at + n_tensor]
-    wo_ref, ffn_ref, res_ref, gated, own_ref, part_ref, hid_ref, act_ref = refs[
+    wo_ref, ffn_ref, res_ref, gated, own_ref, part_ref, hid_ref, act_ref, gain_ref = refs[
         at + n_tensor : -3
     ]
     sems, gated_sems, done_sems = refs[-3:]
     rows, width = own_ref.shape
-    me, group = ids_ref[0], ids_ref[2 + n_tensor]
+    me, group, here_at = (lax.axis_index(name) for name in ("dp", "group", "tensor"))
+    table = ring_sources(n_tensor)
+    sources = []
+    for k in range(n_tensor):
+        source = table[0][k]
+        for at_k in range(1, n_tensor):
+            source = jnp.where(here_at == at_k, table[at_k][k], source)
+        sources.append(source)
     out_copies = piece_copies(
         out_pieces, wo_ref, sems.at[0], me, lambda piece: piece.at[:, pl.ds(0, wo_ref.shape[1] // n_dp)]
     )
@@ -269,6 +282,7 @@
         pltpu.make_async_copy(source, gated.at[k], gated_sems.at[k])
         for k, source in enumerate(gated_hbm[:-1])
     ]
+    gated_copies.append(pltpu.make_async_copy(gains_hbm, gain_ref, gated_sems.at[n_tensor - 1]))
     done_copies = [pltpu.make_async_copy(own_ref, own_hbm, done_sems.at[0])]
     for k in range(1, n_tensor):
         done_copies.append(
@@ -285,12 +299,12 @@
         copy.start()
     for r in range(0, rows, block):
         span = slice(r, r + block)
-        attended = dot_nt(here[0][span], wo_ref[ids_ref[2]])
+        attended = dot_nt(here[0][span], wo_ref[sources[0]])
         for k in range(1, n_tensor):
-            attended += dot_nt(here[k][span], wo_ref[ids_ref[2 + k]])
+            attended += dot_nt(here[k][span], wo_ref[sources[k]])
         residual = tok_ref[base + r : base + r + block].astype(jnp.float32) + attended
         res_ref[span] = residual
-        hid_ref[span] = rms_scale(residual, small_ref[1:2, :])
+        hid_ref[span] = rms_scale(residual, gain_ref[1:2, :])
     for copy in up_copies:
         copy.wait()
     for r in range(0, rows, block):
@@ -301,10 +315,10 @@
         copy.wait()
 
     def term(k):
-        start = pl.multiple_of(ids_ref[2 + k] * width, width)
+        start = pl.multiple_of(sources[k] * width, width)
         return dot_nt(act_ref[...], ffn_ref[1, pl.ds(start, width), :])
 
-    mine = pl.ds(pl.multiple_of(ids_ref[1] * width, width), width)
+    mine = pl.ds(pl.multiple_of(here_at * width, width), width)
     own_ref[...] = res_ref[:, mine] + term(0)
     done_copies[0].start()
     for k in list(range(2, n_tensor)) + [1]:
@@ -408,7 +422,7 @@
     cols_here = heads_here * head_dim
     units_here = ffn_weights.shape[2]
     n_dp, n_tensor = lax.axis_size("dp"), lax.axis_size("tensor")
-    dp_at, tensor_at = lax.axis_index("dp"), lax.axis_index("tensor")
+    dp_at = lax.axis_index("dp")
     share = width // n_tensor
     pair_cap = max(2, 2 * sessions_here // n_dp)
     slot_count = n_dp * pair_cap
@@ -439,14 +453,6 @@
         split_axis=0,
         concat_axis=0,
         tiled=True,
-    )
-    sources = jnp.array(ring_sources(n_tensor), jnp.int32)[tensor_at]
-    places = jnp.stack([dp_at, tensor_at]).astype(jnp.int32)
-    group_at = lax.axis_index("group").astype(jnp.int32)
-    ids = jnp.concatenate([places, sources, group_at[None]])
-    head_decay = lax.dynamic_slice_in_dim(head_rates, tensor_at * heads_here, heads_here)
-    small = jnp.concatenate(
-        [norm_gains, jnp.broadcast_to(head_decay[:, None], (heads_here, width))]
     )
     out_pieces = xor_gather(out_own, "dp")
 
@@ -495,7 +501,7 @@
     for c in range(CHUNKS):
         g, k, v = kernel_call(
             functools.partial(project_kernel, n_dp, heads_here, event_count, block, c * chunk_rows),
-            [smem_spec()] + [vmem_spec()] * 2 + [hbm_spec()] + [vmem_spec()] * n_dp,
+            [smem_spec(), hbm_spec(), vmem_spec(), hbm_spec()] + [vmem_spec()] * n_dp,
             [vmem_spec()] + [hbm_spec()] * 2,
             [rows_shape] + [pltpu.HBM((chunk_rows, cols_here), bf16)] * 2,
             [
@@ -505,11 +511,17 @@
                 pltpu.VMEM((chunk_rows, cols_here), bf16),
                 pltpu.VMEM((chunk_rows, cols_here), bf16),
                 pltpu.VMEM((4, 16 if split else width, cols_here), bf16),
-                pltpu.SemaphoreType.DMA((3,)),
+                pltpu.VMEM(norm_gains.shape, f32),
+                pltpu.SemaphoreType.DMA((4,)),
             ],
             2 * chunk_rows * width * cols_here * 4,
             limit_mib=12,
-        )(ids, small, tokens, *in_hbm([past_states]), *proj_pieces)
+        )(
+            *in_hbm([head_rates, norm_gains]),
+            tokens,
+            *in_hbm([past_states]),
+            *proj_pieces,
+        )
         gated.append([g])
         keys.append(k)
         values.append(v)
@@ -519,7 +531,7 @@
 
     packed = kernel_call(
         functools.partial(state_kernel, CHUNKS, heads_here, event_count),
-        [vmem_spec(), smem_spec()] + [hbm_spec()] * (1 + 2 * CHUNKS),
+        [smem_spec()] * 2 + [hbm_spec()] * (1 + 2 * CHUNKS),
         hbm_spec(),
         pltpu.HBM((slot_count, heads_here, head_dim, head_dim), bf16),
         [
@@ -531,15 +543,14 @@
             pltpu.SemaphoreType.DMA((2 * CHUNKS,)),
         ],
         2 * row_count * head_dim * cols_here,
-    )(small, send_pos, *in_hbm([past_states, *keys, *values]))
+    )(*in_hbm([head_rates]), send_pos, *in_hbm([past_states, *keys, *values]))
     received = lax.all_to_all(packed, "dp", split_axis=0, concat_axis=0, tiled=True)
 
     owns, parts, sums = [], [], []
     for c in range(CHUNKS):
         own, *part = kernel_call(
             functools.partial(feed_kernel, n_dp, n_tensor, block, c * chunk_rows),
-            [smem_spec()]
-            + [vmem_spec()] * 2
+            [hbm_spec(), vmem_spec()]
             + [hbm_spec()] * (n_tensor - 1)
             + [vmem_spec()]
             + [hbm_spec()] * (3 * n_dp - 2),
@@ -555,14 +566,14 @@
                 pltpu.VMEM((n_tensor - 1, chunk_rows, share), bf16),
                 pltpu.VMEM((chunk_rows, width), bf16),
                 pltpu.VMEM((chunk_rows, units_here), bf16),
+                pltpu.VMEM(norm_gains.shape, f32),
                 pltpu.SemaphoreType.DMA((3, n_dp)),
                 pltpu.SemaphoreType.DMA((n_tensor,)),
                 pltpu.SemaphoreType.DMA((n_tensor,)),
             ],
             2 * chunk_rows * width * (width + 2 * units_here),
         )(
-            ids,
-            small,
+            *in_hbm([norm_gains]),
             tokens,
             *in_hbm(gated[c][:-1]),
             gated[c][-1],

time: 171 us -> 170 us (level)
  transfers between devices with their start and end apart: 26 -> 26, of which waited for: 11 -> 11; matrix products, arithmetic and copies ran while one was open for 5% -> 4% of each run, Pallas kernels for 20% -> 20%
where the time goes in v6:
time: 170 us
  waiting for transfers between devices  75.1 us (44%)
  starting transfers between devices  44.9 us (26%)
  Pallas kernels  37.8 us (22%)
  local copies, waits for them, and re-layouts  7.38 us (4%)
  other arithmetic  3.44 us (2%)
    ppermute x7, waiting for transfers between devices, xor_gather(): arrived.append(lax.ppermute(piece, axis, pairs))  44.3 us
    ppermute x6, waiting for transfers between devices, per_device(): sums[c] = lax.ppermute(mine, 'tensor', ring)  18.8 us
    pallas_call x2, Pallas kernels, per_device(): kernel_call(functools.partial(feed_kernel, n_dp, n_tensor, block, c * chu...  15.9 us
    ppermute x6, starting transfers between devices, per_device(): gated[c].append(lax.ppermute(gated[c][-1], 'tensor', ring))  15.3 us
    ppermute x6, waiting for transfers between devices, per_device(): gated[c].append(lax.ppermute(gated[c][-1], 'tensor', ring))  11 us
    ppermute x6, starting transfers between devices, per_device(): sums[c] = lax.ppermute(mine, 'tensor', ring)  10.4 us
    pallas_call x2, Pallas kernels, per_device(): kernel_call(functools.partial(project_kernel, n_dp, heads_here, event_cou...  9.82 us
    ppermute x7, starting transfers between devices, xor_gather(): arrived.append(lax.ppermute(piece, axis, pairs))  6.65 us
  transfers between devices with their start and end apart: 26, of which 11 were waited for; matrix products, arithmetic and copies ran while one was open for 4% of the time, Pallas kernels for 20%

profile of v6, /device:TPU:0, one launch (start us, length us, event | category | flops | bytes accessed | tf_op | source)
XLA Modules:
  0.0 169.7 jit_solution(6770713313349455003)
XLA Ops:
  1.9 3.0 %collective-permute-start.1 = (bf16[1024,256]{1,0:T(8,128)(2,1)S(1)}, bf16[1024,256]{1,0:T(8,128)(2,1)S(1)}, u32[]{:S(2)}, u32[]{:S(2)}) collective-permute-start(bf16[1024,256]{1,0:T(8,128)(2,1)S(1)} %bitcast.23), channel_id=1, source_target_pairs={{0,8},{4,12},{8,0},{12,4},{1,9},{5,13},{9,1},{13,5},{2,10},{6,14},... | collective-permute-start | bytes 1572872 | tf_op jit(solution)/shard_map/ppermute | solution.py:360
  6.6 4.9 %all-to-all-start = ((bf16[4,256,256]{2,1,0:T(8,128)(2,1)}), bf16[4,256,256]{2,1,0:T(8,128)(2,1)}, u32[]{:S(2)}, u32[]{:S(2)}) async-start(bf16[4,256,256]{2,1,0:T(8,128)(2,1)} %broadcast_in_dim.16), calls=%async_computation | async-start | bytes 1048576 | tf_op jit(solution)/shard_map/all_to_all | solution.py:450
  13.9 2.9 %collective-permute-done.1.refs_6_ = bf16[1024,256]{1,0:T(8,128)(2,1)S(1)} collective-permute-done((bf16[1024,256]{1,0:T(8,128)(2,1)S(1)}, bf16[1024,256]{1,0:T(8,128)(2,1)S(1)}, u32[]{:S(2)}, u32[]{:S(2)}) %collective-permute-start.1) | collective-permute-done | bytes 524320 | tf_op jit(solution)/shard_map/ppermute | solution.py:360
  20.6 4.9 %shard_map.99 = (bf16[512,256]{1,0:T(8,128)(2,1)S(1)}, bf16[512,256]{1,0:T(8,128)(2,1)}, bf16[512,256]{1,0:T(8,128)(2,1)}) custom-call(f32[8]{0:T(128)} %refs_0_.13, f32[2,1024]{1,0:T(2,128)} %refs_0_.10, bf16[1024,1024]{1,0:T(8,128)(2,1)S(1)} %copy-done, f32[32,2,128,128]{3,2,1,0:T(8,128)} %refs_2_.5, bf16[1024,256]{1,0:T(8,128)(2,1)S(1)} %bitcast.25, ...), custom_call_target="tpu_custom_call" | custom-call | flops 1073741824 | bytes 4194304 | tf_op jit(solution)/shard_map/pallas_call | solution.py:502
  25.4 5.0 %shard_map.95 = (bf16[512,256]{1,0:T(8,128)(2,1)S(1)}, bf16[512,256]{1,0:T(8,128)(2,1)}, bf16[512,256]{1,0:T(8,128)(2,1)}) custom-call(f32[8]{0:T(128)} %refs_0_.13, f32[2,1024]{1,0:T(2,128)} %refs_0_.10, bf16[1024,1024]{1,0:T(8,128)(2,1)S(1)} %copy-done, f32[32,2,128,128]{3,2,1,0:T(8,128)} %refs_2_.5, bf16[1024,256]{1,0:T(8,128)(2,1)S(1)} %bitcast.26, ...), custom_call_target="tpu_custom_call" | custom-call | flops 1073741824 | bytes 4194304 | tf_op jit(solution)/shard_map/pallas_call | solution.py:502
  30.4 4.9 %shard_map.103 = bf16[64,2,128,128]{3,2,1,0:T(8,128)(2,1)} custom-call(f32[8]{0:T(128)} %refs_0_.13, s32[32]{0:T(128)S(1)} %get-tuple-element.33.refs_1_, f32[32,2,128,128]{3,2,1,0:T(8,128)} %refs_2_.5, bf16[512,256]{1,0:T(8,128)(2,1)} %get-tuple-element.26.refs_3_, bf16[512,256]{1,0:T(8,128)(2,1)} %get-tuple-element.27.refs_4_, ...), custom_call_target="tpu_custom_call" | custom-call | flops 67108864 | bytes 4194304 | tf_op jit(solution)/shard_map/pallas_call | solution.py:532
  35.3 5.0 %all-to-all-start.1 = ((bf16[64,2,128,128]{3,2,1,0:T(8,128)(2,1)}), bf16[64,2,128,128]{3,2,1,0:T(8,128)(2,1)}, u32[]{:S(2)}, u32[]{:S(2)}) async-start(bf16[64,2,128,128]{3,2,1,0:T(8,128)(2,1)} %shard_map.103), calls=%async_computation.1 | async-start | bytes 8388608 | tf_op jit(solution)/shard_map/all_to_all | solution.py:547
  45.0 2.6 %collective-permute-start.17 = (bf16[512,256]{1,0:T(8,128)(2,1)S(1)}, bf16[512,256]{1,0:T(8,128)(2,1)}, u32[]{:S(2)}, u32[]{:S(2)}) collective-permute-start(bf16[512,256]{1,0:T(8,128)(2,1)S(1)} %copy-done.10), channel_id=1, source_target_pairs={{0,2},{2,3},{3,1},{1,0},{4,6},{6,7},{7,5},{5,4},{8,10},{10,11},{11... | collective-permute-start | bytes 786440 | tf_op jit(solution)/shard_map/ppermute | solution.py:530
  49.2 5.0 %collective-permute-done.17.refs_3_ = bf16[512,256]{1,0:T(8,128)(2,1)} collective-permute-done((bf16[512,256]{1,0:T(8,128)(2,1)S(1)}, bf16[512,256]{1,0:T(8,128)(2,1)}, u32[]{:S(2)}, u32[]{:S(2)}) %collective-permute-start.17) | collective-permute-done | bytes 262176 | tf_op jit(solution)/shard_map/ppermute | solution.py:530
  54.3 3.5 %collective-permute-start.18 = (bf16[512,256]{1,0:T(8,128)(2,1)}, bf16[512,256]{1,0:T(8,128)(2,1)S(1)}, u32[]{:S(2)}, u32[]{:S(2)}) collective-permute-start(bf16[512,256]{1,0:T(8,128)(2,1)} %collective-permute-done.17.refs_3_), channel_id=1, source_target_pairs={{0,2},{2,3},{3,1},{1,0},{4,6},{6,7},{7,5},{5,4},{8,10},{10,11},{11... | collective-permute-start | bytes 786440 | tf_op jit(solution)/shard_map/ppermute | solution.py:530
  58.3 41.4 %collective-permute-done.7.refs_8_ = bf16[4,256,256]{2,1,0:T(8,128)(2,1)} collective-permute-done((bf16[4,256,256]{2,1,0:T(8,128)(2,1)}, bf16[4,256,256]{2,1,0:T(8,128)(2,1)}, u32[]{:S(2)}, u32[]{:S(2)}) %collective-permute-start.7) | collective-permute-done | bytes 524320 | tf_op jit(solution)/shard_map/ppermute | solution.py:360
  99.8 2.6 %collective-permute-start.4 = (bf16[512,256]{1,0:T(8,128)(2,1)S(1)}, bf16[512,256]{1,0:T(8,128)(2,1)S(1)}, u32[]{:S(2)}, u32[]{:S(2)}) collective-permute-start(bf16[512,256]{1,0:T(8,128)(2,1)S(1)} %collective-permute-done.3.refs_3_), channel_id=1, source_target_pairs={{0,2},{2,3},{3,1},{1,0},{4,6},{6,7},{7,5},{5,4},{8,10},{10,11},{11... | collective-permute-start | bytes 786440 | tf_op jit(solution)/shard_map/ppermute | solution.py:530
  105.3 3.8 %collective-permute-done.4.refs_4_ = bf16[512,256]{1,0:T(8,128)(2,1)S(1)} collective-permute-done((bf16[512,256]{1,0:T(8,128)(2,1)S(1)}, bf16[512,256]{1,0:T(8,128)(2,1)S(1)}, u32[]{:S(2)}, u32[]{:S(2)}) %collective-permute-start.4) | collective-permute-done | bytes 262176 | tf_op jit(solution)/shard_map/ppermute | solution.py:530
  109.1 3.4 %collective-permute-start.5 = (bf16[512,256]{1,0:T(8,128)(2,1)S(1)}, bf16[512,256]{1,0:T(8,128)(2,1)S(1)}, u32[]{:S(2)}, u32[]{:S(2)}) collective-permute-start(bf16[512,256]{1,0:T(8,128)(2,1)S(1)} %collective-permute-done.4.refs_4_), channel_id=1, source_target_pairs={{0,2},{2,3},{3,1},{1,0},{4,6},{6,7},{7,5},{5,4},{8,10},{10,11},{11... | collective-permute-start | bytes 786440 | tf_op jit(solution)/shard_map/ppermute | solution.py:530
  112.5 2.2 %collective-permute-done.19.refs_5_ = bf16[512,256]{1,0:T(8,128)(2,1)S(1)} collective-permute-done((bf16[512,256]{1,0:T(8,128)(2,1)S(1)}, bf16[512,256]{1,0:T(8,128)(2,1)S(1)}, u32[]{:S(2)}, u32[]{:S(2)}) %collective-permute-start.19) | collective-permute-done | bytes 262176 | tf_op jit(solution)/shard_map/ppermute | solution.py:530
  114.7 8.0 %shard_map.100 = (f32[512,256]{1,0:T(8,128)}, bf16[512,256]{1,0:T(8,128)(2,1)}, bf16[512,256]{1,0:T(8,128)(2,1)}, bf16[512,256]{1,0:T(8,128)(2,1)}) custom-call(f32[2,1024]{1,0:T(2,128)} %refs_0_.10, bf16[1024,1024]{1,0:T(8,128)(2,1)S(1)} %copy-done, bf16[512,256]{1,0:T(8,128)(2,1)} %copy-done.9, bf16[512,256]{1,0:T(8,128)(2,1)} %collective-permute-done.17.refs_3_, ...), custom_call_target="tpu_custom_call" | custom-call | flops 3221225472 | bytes 4194304 | tf_op jit(solution)/shard_map/pallas_call | solution.py:551
  122.8 3.4 %collective-permute-start.20 = (bf16[512,256]{1,0:T(8,128)(2,1)}, bf16[512,256]{1,0:T(8,128)(2,1)S(1)}, u32[]{:S(2)}, u32[]{:S(2)}) collective-permute-start(bf16[512,256]{1,0:T(8,128)(2,1)} %get-tuple-element.23), channel_id=1, source_target_pairs={{0,2},{2,3},{3,1},{1,0},{4,6},{6,7},{7,5},{5,4},{8,10},{10,11},{11... | collective-permute-start | bytes 786440 | tf_op jit(solution)/shard_map/ppermute | solution.py:598
  126.2 7.9 %shard_map.96 = (f32[512,256]{1,0:T(8,128)}, bf16[512,256]{1,0:T(8,128)(2,1)}, bf16[512,256]{1,0:T(8,128)(2,1)}, bf16[512,256]{1,0:T(8,128)(2,1)}) custom-call(f32[2,1024]{1,0:T(2,128)} %refs_0_.10, bf16[1024,1024]{1,0:T(8,128)(2,1)S(1)} %copy-done, bf16[512,256]{1,0:T(8,128)(2,1)} %copy-done.8, bf16[512,256]{1,0:T(8,128)(2,1)} %copy-done.15, ...), custom_call_target="tpu_custom_call" | custom-call | flops 3221225472 | bytes 4194304 | tf_op jit(solution)/shard_map/pallas_call | solution.py:551
  136.3 7.3 %collective-permute-done.14.a_ref = bf16[512,256]{1,0:T(8,128)(2,1)S(1)} collective-permute-done((bf16[512,256]{1,0:T(8,128)(2,1)}, bf16[512,256]{1,0:T(8,128)(2,1)S(1)}, u32[]{:S(2)}, u32[]{:S(2)}) %collective-permute-start.14) | collective-permute-done | bytes 262176 | tf_op jit(solution)/shard_map/ppermute | solution.py:598
  146.5 2.7 %collective-permute-done.21.a_ref = bf16[512,256]{1,0:T(8,128)(2,1)S(1)} collective-permute-done((bf16[512,256]{1,0:T(8,128)(2,1)S(1)}, bf16[512,256]{1,0:T(8,128)(2,1)S(1)}, u32[]{:S(2)}, u32[]{:S(2)}) %collective-permute-start.21) | collective-permute-done | bytes 262176 | tf_op jit(solution)/shard_map/ppermute | solution.py:598
  150.9 3.9 %collective-permute-done.15.a_ref = bf16[512,256]{1,0:T(8,128)(2,1)S(1)} collective-permute-done((bf16[512,256]{1,0:T(8,128)(2,1)S(1)}, bf16[512,256]{1,0:T(8,128)(2,1)S(1)}, u32[]{:S(2)}, u32[]{:S(2)}) %collective-permute-start.15) | collective-permute-done | bytes 262176 | tf_op jit(solution)/shard_map/ppermute | solution.py:598
  157.6 2.8 %collective-permute-done.22.refs_2_ = bf16[512,256]{1,0:T(8,128)(2,1)S(1)} collective-permute-done((bf16[512,256]{1,0:T(8,128)(2,1)S(1)}, bf16[512,256]{1,0:T(8,128)(2,1)S(1)}, u32[]{:S(2)}, u32[]{:S(2)}) %collective-permute-start.22) | collective-permute-done | bytes 262176 | tf_op jit(solution)/shard_map/ppermute | solution.py:598
  161.8 2.1 %collective-permute-done.16.refs_2_ = bf16[512,256]{1,0:T(8,128)(2,1)S(1)} collective-permute-done((bf16[512,256]{1,0:T(8,128)(2,1)S(1)}, bf16[512,256]{1,0:T(8,128)(2,1)S(1)}, u32[]{:S(2)}, u32[]{:S(2)}) %collective-permute-start.16) | collective-permute-done | bytes 262176 | tf_op jit(solution)/shard_map/ppermute | solution.py:598
  165.2 4.3 %unpack.1 = f32[32,2,128,128]{3,2,1,0:T(8,128)} custom-call(s32[32]{0:T(128)S(1)} %broadcast_add_fusion.src_ref, bf16[64,2,128,128]{3,2,1,0:T(8,128)(2,1)} %all-to-all-done.1.recv_ref), custom_call_target="tpu_custom_call" | custom-call | bytes 6291456 | tf_op jit(solution)/shard_map/unpack/pallas_call | solution.py:623
  (101 shorter events, 31.1 us)
Async XLA Ops:
  1.9 15.0 %collective-permute-start.1 = (bf16[1024,256]{1,0:T(8,128)(2,1)S(1)}, bf16[1024,256]{1,0:T(8,128)(2,1)S(1)}, u32[]{:S(2)}, u32[]{:S(2)}) collective-permute-start(bf16[1024,256]{1,0:T(8,128)(2,1)S(1)} %bitcast.23), channel_id=1, source_target_pairs={{0,8},{4,12},{8,0},{12,4},{1,9},{5,13},{9,1},{13,5},{2,10},{6,14},... | collective-permute-start | bytes 1572872 | tf_op jit(solution)/shard_map/ppermute | solution.py:360
  4.9 15.6 %collective-permute-start = (bf16[1024,256]{1,0:T(8,128)(2,1)S(1)}, bf16[1024,256]{1,0:T(8,128)(2,1)}, u32[]{:S(2)}, u32[]{:S(2)}) collective-permute-start(bf16[1024,256]{1,0:T(8,128)(2,1)S(1)} %bitcast.24), channel_id=1, source_target_pairs={{0,4},{4,0},{8,12},{12,8},{1,5},{5,1},{9,13},{13,9},{2,6},{6,2},{1... | collective-permute-start | bytes 1572872 | tf_op jit(solution)/shard_map/ppermute | solution.py:360
  6.6 28.6 %all-to-all-start = ((bf16[4,256,256]{2,1,0:T(8,128)(2,1)}), bf16[4,256,256]{2,1,0:T(8,128)(2,1)}, u32[]{:S(2)}, u32[]{:S(2)}) async-start(bf16[4,256,256]{2,1,0:T(8,128)(2,1)} %broadcast_in_dim.16), calls=%async_computation | async-start | bytes 1048576 | tf_op jit(solution)/shard_map/all_to_all | solution.py:450
  11.5 36.0 %collective-permute-start.9 = (bf16[2,256,1024]{2,1,0:T(8,128)(2,1)}, bf16[2,256,1024]{2,1,0:T(8,128)(2,1)}, u32[]{:S(2)}, u32[]{:S(2)}) collective-permute-start(bf16[2,256,1024]{2,1,0:T(8,128)(2,1)} %refs_10_.3), channel_id=1, source_target_pairs={{0,4},{4,0},{8,12},{12,8},{1,5},{5,1},{9,13},{13,9},{2,6},{6,2},{1... | collective-permute-start | bytes 3145736 | tf_op jit(solution)/shard_map/ppermute | solution.py:467
  18.8 21.5 %collective-permute-start.10 = (bf16[272,1024]{1,0:T(8,128)(2,1)}, bf16[272,1024]{1,0:T(8,128)(2,1)}, u32[]{:S(2)}, u32[]{:S(2)}) collective-permute-start(bf16[272,1024]{1,0:T(8,128)(2,1)} %pad_maximum_fusion), channel_id=1, source_target_pairs={{0,8},{4,12},{8,0},{12,4},{1,9},{5,13},{9,1},{13,5},{2,10},{6,14},... | collective-permute-start | bytes 1671176 | tf_op jit(solution)/shard_map/ppermute | solution.py:360
  35.3 129.9 %all-to-all-start.1 = ((bf16[64,2,128,128]{3,2,1,0:T(8,128)(2,1)}), bf16[64,2,128,128]{3,2,1,0:T(8,128)(2,1)}, u32[]{:S(2)}, u32[]{:S(2)}) async-start(bf16[64,2,128,128]{3,2,1,0:T(8,128)(2,1)} %shard_map.103), calls=%async_computation.1 | async-start | bytes 8388608 | tf_op jit(solution)/shard_map/all_to_all | solution.py:547
  40.3 17.4 %collective-permute-start.12 = (bf16[272,1024]{1,0:T(8,128)(2,1)}, bf16[272,1024]{1,0:T(8,128)(2,1)S(1)}, u32[]{:S(2)}, u32[]{:S(2)}) collective-permute-start(bf16[272,1024]{1,0:T(8,128)(2,1)} %collective-permute-done.10.refs_12_), channel_id=1, source_target_pairs={{0,16},{16,0},{1,17},{17,1},{2,18},{18,2},{3,19},{19,3},{4,20},{20... | collective-permute-start | bytes 1671176 | tf_op jit(solution)/shard_map/ppermute | solution.py:463
  41.9 15.9 %collective-permute-start.11 = (bf16[272,1024]{1,0:T(8,128)(2,1)}, bf16[272,1024]{1,0:T(8,128)(2,1)}, u32[]{:S(2)}, u32[]{:S(2)}) collective-permute-start(bf16[272,1024]{1,0:T(8,128)(2,1)} %collective-permute-done.10.refs_12_), channel_id=1, source_target_pairs={{0,4},{4,0},{8,12},{12,8},{1,5},{5,1},{9,13},{13,9},{2,6},{6,2},{1... | collective-permute-start | bytes 1671176 | tf_op jit(solution)/shard_map/ppermute | solution.py:467
  42.0 57.7 %collective-permute-start.7 = (bf16[4,256,256]{2,1,0:T(8,128)(2,1)}, bf16[4,256,256]{2,1,0:T(8,128)(2,1)}, u32[]{:S(2)}, u32[]{:S(2)}) collective-permute-start(bf16[4,256,256]{2,1,0:T(8,128)(2,1)} %all-to-all-done.refs_6_), channel_id=1, source_target_pairs={{0,8},{4,12},{8,0},{12,4},{1,9},{5,13},{9,1},{13,5},{2,10},{6,14},... | collective-permute-start | bytes 1572872 | tf_op jit(solution)/shard_map/ppermute | solution.py:360
  45.0 9.3 %collective-permute-start.17 = (bf16[512,256]{1,0:T(8,128)(2,1)S(1)}, bf16[512,256]{1,0:T(8,128)(2,1)}, u32[]{:S(2)}, u32[]{:S(2)}) collective-permute-start(bf16[512,256]{1,0:T(8,128)(2,1)S(1)} %copy-done.10), channel_id=1, source_target_pairs={{0,2},{2,3},{3,1},{1,0},{4,6},{6,7},{7,5},{5,4},{8,10},{10,11},{11... | collective-permute-start | bytes 786440 | tf_op jit(solution)/shard_map/ppermute | solution.py:530
  47.6 52.2 %collective-permute-start.3 = (bf16[512,256]{1,0:T(8,128)(2,1)S(1)}, bf16[512,256]{1,0:T(8,128)(2,1)S(1)}, u32[]{:S(2)}, u32[]{:S(2)}) collective-permute-start(bf16[512,256]{1,0:T(8,128)(2,1)S(1)} %get-tuple-element.16.refs_2_), channel_id=1, source_target_pairs={{0,2},{2,3},{3,1},{1,0},{4,6},{6,7},{7,5},{5,4},{8,10},{10,11},{11... | collective-permute-start | bytes 786440 | tf_op jit(solution)/shard_map/ppermute | solution.py:530
  54.3 48.2 %collective-permute-start.18 = (bf16[512,256]{1,0:T(8,128)(2,1)}, bf16[512,256]{1,0:T(8,128)(2,1)S(1)}, u32[]{:S(2)}, u32[]{:S(2)}) collective-permute-start(bf16[512,256]{1,0:T(8,128)(2,1)} %collective-permute-done.17.refs_3_), channel_id=1, source_target_pairs={{0,2},{2,3},{3,1},{1,0},{4,6},{6,7},{7,5},{5,4},{8,10},{10,11},{11... | collective-permute-start | bytes 786440 | tf_op jit(solution)/shard_map/ppermute | solution.py:530
  57.8 54.7 %collective-permute-start.6 = (bf16[4,256,256]{2,1,0:T(8,128)(2,1)}, bf16[4,256,256]{2,1,0:T(8,128)(2,1)S(1)}, u32[]{:S(2)}, u32[]{:S(2)}) collective-permute-start(bf16[4,256,256]{2,1,0:T(8,128)(2,1)} %all-to-all-done.refs_6_), channel_id=1, source_target_pairs={{0,4},{4,0},{8,12},{12,8},{1,5},{5,1},{9,13},{13,9},{2,6},{6,2},{1... | collective-permute-start | bytes 1572872 | tf_op jit(solution)/shard_map/ppermute | solution.py:360
  57.8 54.7 %collective-permute-start.13 = (bf16[272,1024]{1,0:T(8,128)(2,1)S(1)}, bf16[272,1024]{1,0:T(8,128)(2,1)S(1)}, u32[]{:S(2)}, u32[]{:S(2)}) collective-permute-start(bf16[272,1024]{1,0:T(8,128)(2,1)S(1)} %collective-permute-done.12.refs_14_), channel_id=1, source_target_pairs={{0,4},{4,0},{8,12},{12,8},{1,5},{5,1},{9,13},{13,9},{2,6},{6,2},{1... | collective-permute-start | bytes 1671176 | tf_op jit(solution)/shard_map/ppermute | solution.py:467
  99.7 12.8 %collective-permute-start.8 = (bf16[4,256,256]{2,1,0:T(8,128)(2,1)}, bf16[4,256,256]{2,1,0:T(8,128)(2,1)S(1)}, u32[]{:S(2)}, u32[]{:S(2)}) collective-permute-start(bf16[4,256,256]{2,1,0:T(8,128)(2,1)} %collective-permute-done.7.refs_8_), channel_id=1, source_target_pairs={{0,4},{4,0},{8,12},{12,8},{1,5},{5,1},{9,13},{13,9},{2,6},{6,2},{1... | collective-permute-start | bytes 1572872 | tf_op jit(solution)/shard_map/ppermute | solution.py:360
  99.8 9.3 %collective-permute-start.4 = (bf16[512,256]{1,0:T(8,128)(2,1)S(1)}, bf16[512,256]{1,0:T(8,128)(2,1)S(1)}, u32[]{:S(2)}, u32[]{:S(2)}) collective-permute-start(bf16[512,256]{1,0:T(8,128)(2,1)S(1)} %collective-permute-done.3.refs_3_), channel_id=1, source_target_pairs={{0,2},{2,3},{3,1},{1,0},{4,6},{6,7},{7,5},{5,4},{8,10},{10,11},{11... | collective-permute-start | bytes 786440 | tf_op jit(solution)/shard_map/ppermute | solution.py:530
  102.4 12.3 %collective-permute-start.19 = (bf16[512,256]{1,0:T(8,128)(2,1)S(1)}, bf16[512,256]{1,0:T(8,128)(2,1)S(1)}, u32[]{:S(2)}, u32[]{:S(2)}) collective-permute-start(bf16[512,256]{1,0:T(8,128)(2,1)S(1)} %collective-permute-done.18.refs_4_), channel_id=1, source_target_pairs={{0,2},{2,3},{3,1},{1,0},{4,6},{6,7},{7,5},{5,4},{8,10},{10,11},{11... | collective-permute-start | bytes 786440 | tf_op jit(solution)/shard_map/ppermute | solution.py:530
  109.1 17.1 %collective-permute-start.5 = (bf16[512,256]{1,0:T(8,128)(2,1)S(1)}, bf16[512,256]{1,0:T(8,128)(2,1)S(1)}, u32[]{:S(2)}, u32[]{:S(2)}) collective-permute-start(bf16[512,256]{1,0:T(8,128)(2,1)S(1)} %collective-permute-done.4.refs_4_), channel_id=1, source_target_pairs={{0,2},{2,3},{3,1},{1,0},{4,6},{6,7},{7,5},{5,4},{8,10},{10,11},{11... | collective-permute-start | bytes 786440 | tf_op jit(solution)/shard_map/ppermute | solution.py:530
  122.8 12.1 %collective-permute-start.20 = (bf16[512,256]{1,0:T(8,128)(2,1)}, bf16[512,256]{1,0:T(8,128)(2,1)S(1)}, u32[]{:S(2)}, u32[]{:S(2)}) collective-permute-start(bf16[512,256]{1,0:T(8,128)(2,1)} %get-tuple-element.23), channel_id=1, source_target_pairs={{0,2},{2,3},{3,1},{1,0},{4,6},{6,7},{7,5},{5,4},{8,10},{10,11},{11... | collective-permute-start | bytes 786440 | tf_op jit(solution)/shard_map/ppermute | solution.py:598
  134.1 9.4 %collective-permute-start.14 = (bf16[512,256]{1,0:T(8,128)(2,1)}, bf16[512,256]{1,0:T(8,128)(2,1)S(1)}, u32[]{:S(2)}, u32[]{:S(2)}) collective-permute-start(bf16[512,256]{1,0:T(8,128)(2,1)} %get-tuple-element.18), channel_id=1, source_target_pairs={{0,2},{2,3},{3,1},{1,0},{4,6},{6,7},{7,5},{5,4},{8,10},{10,11},{11... | collective-permute-start | bytes 786440 | tf_op jit(solution)/shard_map/ppermute | solution.py:598
  135.0 14.2 %collective-permute-start.21 = (bf16[512,256]{1,0:T(8,128)(2,1)S(1)}, bf16[512,256]{1,0:T(8,128)(2,1)S(1)}, u32[]{:S(2)}, u32[]{:S(2)}) collective-permute-start(bf16[512,256]{1,0:T(8,128)(2,1)S(1)} %shard_map.101), channel_id=1, source_target_pairs={{0,2},{2,3},{3,1},{1,0},{4,6},{6,7},{7,5},{5,4},{8,10},{10,11},{11... | collective-permute-start | bytes 786440 | tf_op jit(solution)/shard_map/ppermute | solution.py:598
  144.6 10.2 %collective-permute-start.15 = (bf16[512,256]{1,0:T(8,128)(2,1)S(1)}, bf16[512,256]{1,0:T(8,128)(2,1)S(1)}, u32[]{:S(2)}, u32[]{:S(2)}) collective-permute-start(bf16[512,256]{1,0:T(8,128)(2,1)S(1)} %shard_map.97), channel_id=1, source_target_pairs={{0,2},{2,3},{3,1},{1,0},{4,6},{6,7},{7,5},{5,4},{8,10},{10,11},{11... | collective-permute-start | bytes 786440 | tf_op jit(solution)/shard_map/ppermute | solution.py:598
  149.3 11.2 %collective-permute-start.22 = (bf16[512,256]{1,0:T(8,128)(2,1)S(1)}, bf16[512,256]{1,0:T(8,128)(2,1)S(1)}, u32[]{:S(2)}, u32[]{:S(2)}) collective-permute-start(bf16[512,256]{1,0:T(8,128)(2,1)S(1)} %shard_map.102), channel_id=1, source_target_pairs={{0,2},{2,3},{3,1},{1,0},{4,6},{6,7},{7,5},{5,4},{8,10},{10,11},{11... | collective-permute-start | bytes 786440 | tf_op jit(solution)/shard_map/ppermute | solution.py:598
  155.8 8.0 %collective-permute-start.16 = (bf16[512,256]{1,0:T(8,128)(2,1)S(1)}, bf16[512,256]{1,0:T(8,128)(2,1)S(1)}, u32[]{:S(2)}, u32[]{:S(2)}) collective-permute-start(bf16[512,256]{1,0:T(8,128)(2,1)S(1)} %shard_map.98), channel_id=1, source_target_pairs={{0,2},{2,3},{3,1},{1,0},{4,6},{6,7},{7,5},{5,4},{8,10},{10,11},{11... | collective-permute-start | bytes 786440 | tf_op jit(solution)/shard_map/ppermute | solution.py:598
  (20 other events, 321.8 us)

commit v7 on v6

--- a/solution.py
+++ b/solution.py
@@ -204,34 +204,37 @@
             copy_of(session).wait()
 
 
-def unpack_kernel(src_ref, recv_ref, out_ref, buf_ref, sems):
-    per_step = out_ref.shape[0]
-    step = pl.program_id(0)
-
-    def copy_of(slot):
+def unpack_kernel(src_ref, recv_hbm, out_hbm, in_ref, out_ref, in_sems, out_sems):
+    slots = in_ref.shape[0]
+
+    def in_copy(slot):
         return pltpu.make_async_copy(
-            recv_ref.at[jnp.maximum(src_ref[slot], 0)], buf_ref.at[slot], sems.at[slot]
-        )
-
-    @pl.when(step == 0)
-    def _():
-        for slot in range(buf_ref.shape[0]):
-
-            @pl.when(src_ref[slot] >= 0)
-            def _():
-                copy_of(slot).start()
-
-    for i in range(per_step):
-        slot = step * per_step + i
+            recv_hbm.at[jnp.maximum(src_ref[slot], 0)], in_ref.at[slot], in_sems.at[slot]
+        )
+
+    def out_copy(slot):
+        return pltpu.make_async_copy(out_ref.at[slot], out_hbm.at[slot], out_sems.at[slot])
+
+    for slot in range(slots):
 
         @pl.when(src_ref[slot] >= 0)
         def _():
-            copy_of(slot).wait()
-            out_ref[i] = buf_ref[slot].astype(jnp.float32)
+            in_copy(slot).start()
+
+    for slot in range(slots):
+
+        @pl.when(src_ref[slot] >= 0)
+        def _():
+            in_copy(slot).wait()
+            out_ref[slot] = in_ref[slot].astype(jnp.float32)
 
         @pl.when(src_ref[slot] < 0)
         def _():
-            out_ref[i] = jnp.zeros(out_ref.shape[1:], jnp.float32)
+            out_ref[slot] = jnp.zeros(out_ref.shape[1:], jnp.float32)
+
+        out_copy(slot).start()
+    for slot in range(slots):
+        out_copy(slot).wait()
 
 
 def feed_kernel(n_dp, n_tensor, block, base, *refs):
@@ -376,10 +379,6 @@
 def ring_sources(size):
     order = ring_order(size)
     return [[order[(order.index(at) - k) % size] for k in range(size)] for at in range(size)]
-
-
-def any_spec():
-    return pl.BlockSpec(memory_space=pl.ANY)
 
 
 def smem_spec():
@@ -619,23 +618,21 @@
         ]
     (next_tokens,) = so_far
 
-    per_step = min(8, sessions_here)
-    moved_states = pl.pallas_call(
+    state_shape = (sessions_here, heads_here, head_dim, head_dim)
+    moved_states = kernel_call(
         unpack_kernel,
-        grid=(sessions_here // per_step,),
-        in_specs=[smem_spec(), any_spec()],
-        out_specs=pl.BlockSpec((per_step, heads_here, head_dim, head_dim), lambda i: (i, 0, 0, 0)),
-        out_shape=shape_of(past_states.shape, f32),
-        scratch_shapes=[
-            pltpu.VMEM((sessions_here, heads_here, head_dim, head_dim), bf16),
+        [smem_spec(), hbm_spec()],
+        hbm_spec(),
+        shape_of(state_shape, f32),
+        [
+            pltpu.VMEM(state_shape, bf16),
+            pltpu.VMEM(state_shape, f32),
+            pltpu.SemaphoreType.DMA((sessions_here,)),
             pltpu.SemaphoreType.DMA((sessions_here,)),
         ],
-        compiler_params=pltpu.CompilerParams(vmem_limit_bytes=16 * 1024 * 1024),
-        cost_estimate=pl.CostEstimate(
-            flops=0, bytes_accessed=past_states.size * 6, transcendentals=0
-        ),
-        name="unpack",
-    )(recv_src, received)
+        0,
+        limit_mib=16,
+    )(recv_src, *in_hbm([received]))
     return (next_tokens, moved_states)
 
 

time: 170 us -> 170 us (level)
  transfers between devices with their start and end apart: 26 -> 26, of which waited for: 11 -> 11; matrix products, arithmetic and copies ran while one was open for 4% -> 5% of each run, Pallas kernels for 20% -> 20%
where the time goes in v7:
time: 170 us; the launch traced here: 169 us
  waiting for transfers between devices  75.1 us (44%)
  starting transfers between devices  44.9 us (26%)
  Pallas kernels  37.3 us (22%)
  local copies, waits for them, and re-layouts  7.38 us (4%)
  other arithmetic  3.44 us (2%)
    ppermute x7, waiting for transfers between devices, xor_gather(): arrived.append(lax.ppermute(piece, axis, pairs))  44.3 us
    ppermute x6, waiting for transfers between devices, per_device(): sums[c] = lax.ppermute(mine, 'tensor', ring)  18.8 us
    pallas_call x2, Pallas kernels, per_device(): kernel_call(functools.partial(feed_kernel, n_dp, n_tensor, block, c * chu...  15.9 us
    ppermute x6, starting transfers between devices, per_device(): gated[c].append(lax.ppermute(gated[c][-1], 'tensor', ring))  15.3 us
    ppermute x6, waiting for transfers between devices, per_device(): gated[c].append(lax.ppermute(gated[c][-1], 'tensor', ring))  11 us
    ppermute x6, starting transfers between devices, per_device(): sums[c] = lax.ppermute(mine, 'tensor', ring)  10.4 us
    pallas_call x2, Pallas kernels, per_device(): kernel_call(functools.partial(project_kernel, n_dp, heads_here, event_cou...  9.82 us
    ppermute x7, starting transfers between devices, xor_gather(): arrived.append(lax.ppermute(piece, axis, pairs))  6.65 us
  transfers between devices with their start and end apart: 26, of which 11 were waited for; matrix products, arithmetic and copies ran while one was open for 5% of the time, Pallas kernels for 20%

profile of v7, /device:TPU:0, one launch (start us, length us, event | category | flops | bytes accessed | tf_op | source)
XLA Modules:
  0.0 169.2 jit_solution(9354065151563485807)
XLA Ops:
  1.9 3.0 %collective-permute-start.1 = (bf16[1024,256]{1,0:T(8,128)(2,1)S(1)}, bf16[1024,256]{1,0:T(8,128)(2,1)S(1)}, u32[]{:S(2)}, u32[]{:S(2)}) collective-permute-start(bf16[1024,256]{1,0:T(8,128)(2,1)S(1)} %bitcast.23), channel_id=1, source_target_pairs={{0,8},{4,12},{8,0},{12,4},{1,9},{5,13},{9,1},{13,5},{2,10},{6,14},... | collective-permute-start | bytes 1572872 | tf_op jit(solution)/shard_map/ppermute | solution.py:363
  6.6 4.9 %all-to-all-start = ((bf16[4,256,256]{2,1,0:T(8,128)(2,1)}), bf16[4,256,256]{2,1,0:T(8,128)(2,1)}, u32[]{:S(2)}, u32[]{:S(2)}) async-start(bf16[4,256,256]{2,1,0:T(8,128)(2,1)} %broadcast_in_dim.16), calls=%async_computation | async-start | bytes 1048576 | tf_op jit(solution)/shard_map/all_to_all | solution.py:449
  13.9 2.9 %collective-permute-done.1.refs_6_ = bf16[1024,256]{1,0:T(8,128)(2,1)S(1)} collective-permute-done((bf16[1024,256]{1,0:T(8,128)(2,1)S(1)}, bf16[1024,256]{1,0:T(8,128)(2,1)S(1)}, u32[]{:S(2)}, u32[]{:S(2)}) %collective-permute-start.1) | collective-permute-done | bytes 524320 | tf_op jit(solution)/shard_map/ppermute | solution.py:363
  20.6 4.9 %shard_map.99 = (bf16[512,256]{1,0:T(8,128)(2,1)S(1)}, bf16[512,256]{1,0:T(8,128)(2,1)}, bf16[512,256]{1,0:T(8,128)(2,1)}) custom-call(f32[8]{0:T(128)} %refs_0_.13, f32[2,1024]{1,0:T(2,128)} %refs_0_.10, bf16[1024,1024]{1,0:T(8,128)(2,1)S(1)} %copy-done, f32[32,2,128,128]{3,2,1,0:T(8,128)} %refs_2_.5, bf16[1024,256]{1,0:T(8,128)(2,1)S(1)} %bitcast.25, ...), custom_call_target="tpu_custom_call" | custom-call | flops 1073741824 | bytes 4194304 | tf_op jit(solution)/shard_map/pallas_call | solution.py:501
  25.4 5.0 %shard_map.95 = (bf16[512,256]{1,0:T(8,128)(2,1)S(1)}, bf16[512,256]{1,0:T(8,128)(2,1)}, bf16[512,256]{1,0:T(8,128)(2,1)}) custom-call(f32[8]{0:T(128)} %refs_0_.13, f32[2,1024]{1,0:T(2,128)} %refs_0_.10, bf16[1024,1024]{1,0:T(8,128)(2,1)S(1)} %copy-done, f32[32,2,128,128]{3,2,1,0:T(8,128)} %refs_2_.5, bf16[1024,256]{1,0:T(8,128)(2,1)S(1)} %bitcast.26, ...), custom_call_target="tpu_custom_call" | custom-call | flops 1073741824 | bytes 4194304 | tf_op jit(solution)/shard_map/pallas_call | solution.py:501
  30.4 4.9 %shard_map.103 = bf16[64,2,128,128]{3,2,1,0:T(8,128)(2,1)} custom-call(f32[8]{0:T(128)} %refs_0_.13, s32[32]{0:T(128)S(1)} %get-tuple-element.33.refs_1_, f32[32,2,128,128]{3,2,1,0:T(8,128)} %refs_2_.5, bf16[512,256]{1,0:T(8,128)(2,1)} %get-tuple-element.26.refs_3_, bf16[512,256]{1,0:T(8,128)(2,1)} %get-tuple-element.27.refs_4_, ...), custom_call_target="tpu_custom_call" | custom-call | flops 67108864 | bytes 4194304 | tf_op jit(solution)/shard_map/pallas_call | solution.py:531
  35.3 5.0 %all-to-all-start.1 = ((bf16[64,2,128,128]{3,2,1,0:T(8,128)(2,1)}), bf16[64,2,128,128]{3,2,1,0:T(8,128)(2,1)}, u32[]{:S(2)}, u32[]{:S(2)}) async-start(bf16[64,2,128,128]{3,2,1,0:T(8,128)(2,1)} %shard_map.103), calls=%async_computation.1 | async-start | bytes 8388608 | tf_op jit(solution)/shard_map/all_to_all | solution.py:546
  45.0 2.6 %collective-permute-start.17 = (bf16[512,256]{1,0:T(8,128)(2,1)S(1)}, bf16[512,256]{1,0:T(8,128)(2,1)}, u32[]{:S(2)}, u32[]{:S(2)}) collective-permute-start(bf16[512,256]{1,0:T(8,128)(2,1)S(1)} %copy-done.10), channel_id=1, source_target_pairs={{0,2},{2,3},{3,1},{1,0},{4,6},{6,7},{7,5},{5,4},{8,10},{10,11},{11... | collective-permute-start | bytes 786440 | tf_op jit(solution)/shard_map/ppermute | solution.py:529
  49.2 5.0 %collective-permute-done.17.refs_3_ = bf16[512,256]{1,0:T(8,128)(2,1)} collective-permute-done((bf16[512,256]{1,0:T(8,128)(2,1)S(1)}, bf16[512,256]{1,0:T(8,128)(2,1)}, u32[]{:S(2)}, u32[]{:S(2)}) %collective-permute-start.17) | collective-permute-done | bytes 262176 | tf_op jit(solution)/shard_map/ppermute | solution.py:529
  54.3 3.5 %collective-permute-start.18 = (bf16[512,256]{1,0:T(8,128)(2,1)}, bf16[512,256]{1,0:T(8,128)(2,1)S(1)}, u32[]{:S(2)}, u32[]{:S(2)}) collective-permute-start(bf16[512,256]{1,0:T(8,128)(2,1)} %collective-permute-done.17.refs_3_), channel_id=1, source_target_pairs={{0,2},{2,3},{3,1},{1,0},{4,6},{6,7},{7,5},{5,4},{8,10},{10,11},{11... | collective-permute-start | bytes 786440 | tf_op jit(solution)/shard_map/ppermute | solution.py:529
  58.3 41.4 %collective-permute-done.7.refs_8_ = bf16[4,256,256]{2,1,0:T(8,128)(2,1)} collective-permute-done((bf16[4,256,256]{2,1,0:T(8,128)(2,1)}, bf16[4,256,256]{2,1,0:T(8,128)(2,1)}, u32[]{:S(2)}, u32[]{:S(2)}) %collective-permute-start.7) | collective-permute-done | bytes 524320 | tf_op jit(solution)/shard_map/ppermute | solution.py:363
  99.8 2.6 %collective-permute-start.4 = (bf16[512,256]{1,0:T(8,128)(2,1)S(1)}, bf16[512,256]{1,0:T(8,128)(2,1)S(1)}, u32[]{:S(2)}, u32[]{:S(2)}) collective-permute-start(bf16[512,256]{1,0:T(8,128)(2,1)S(1)} %collective-permute-done.3.refs_3_), channel_id=1, source_target_pairs={{0,2},{2,3},{3,1},{1,0},{4,6},{6,7},{7,5},{5,4},{8,10},{10,11},{11... | collective-permute-start | bytes 786440 | tf_op jit(solution)/shard_map/ppermute | solution.py:529
  105.3 3.8 %collective-permute-done.4.refs_4_ = bf16[512,256]{1,0:T(8,128)(2,1)S(1)} collective-permute-done((bf16[512,256]{1,0:T(8,128)(2,1)S(1)}, bf16[512,256]{1,0:T(8,128)(2,1)S(1)}, u32[]{:S(2)}, u32[]{:S(2)}) %collective-permute-start.4) | collective-permute-done | bytes 262176 | tf_op jit(solution)/shard_map/ppermute | solution.py:529
  109.1 3.4 %collective-permute-start.5 = (bf16[512,256]{1,0:T(8,128)(2,1)S(1)}, bf16[512,256]{1,0:T(8,128)(2,1)S(1)}, u32[]{:S(2)}, u32[]{:S(2)}) collective-permute-start(bf16[512,256]{1,0:T(8,128)(2,1)S(1)} %collective-permute-done.4.refs_4_), channel_id=1, source_target_pairs={{0,2},{2,3},{3,1},{1,0},{4,6},{6,7},{7,5},{5,4},{8,10},{10,11},{11... | collective-permute-start | bytes 786440 | tf_op jit(solution)/shard_map/ppermute | solution.py:529
  112.5 2.2 %collective-permute-done.19.refs_5_ = bf16[512,256]{1,0:T(8,128)(2,1)S(1)} collective-permute-done((bf16[512,256]{1,0:T(8,128)(2,1)S(1)}, bf16[512,256]{1,0:T(8,128)(2,1)S(1)}, u32[]{:S(2)}, u32[]{:S(2)}) %collective-permute-start.19) | collective-permute-done | bytes 262176 | tf_op jit(solution)/shard_map/ppermute | solution.py:529
  114.7 8.0 %shard_map.100 = (f32[512,256]{1,0:T(8,128)}, bf16[512,256]{1,0:T(8,128)(2,1)}, bf16[512,256]{1,0:T(8,128)(2,1)}, bf16[512,256]{1,0:T(8,128)(2,1)}) custom-call(f32[2,1024]{1,0:T(2,128)} %refs_0_.10, bf16[1024,1024]{1,0:T(8,128)(2,1)S(1)} %copy-done, bf16[512,256]{1,0:T(8,128)(2,1)} %copy-done.9, bf16[512,256]{1,0:T(8,128)(2,1)} %collective-permute-done.17.refs_3_, ...), custom_call_target="tpu_custom_call" | custom-call | flops 3221225472 | bytes 4194304 | tf_op jit(solution)/shard_map/pallas_call | solution.py:550
  122.8 3.4 %collective-permute-start.20 = (bf16[512,256]{1,0:T(8,128)(2,1)}, bf16[512,256]{1,0:T(8,128)(2,1)S(1)}, u32[]{:S(2)}, u32[]{:S(2)}) collective-permute-start(bf16[512,256]{1,0:T(8,128)(2,1)} %get-tuple-element.23), channel_id=1, source_target_pairs={{0,2},{2,3},{3,1},{1,0},{4,6},{6,7},{7,5},{5,4},{8,10},{10,11},{11... | collective-permute-start | bytes 786440 | tf_op jit(solution)/shard_map/ppermute | solution.py:597
  126.2 7.9 %shard_map.96 = (f32[512,256]{1,0:T(8,128)}, bf16[512,256]{1,0:T(8,128)(2,1)}, bf16[512,256]{1,0:T(8,128)(2,1)}, bf16[512,256]{1,0:T(8,128)(2,1)}) custom-call(f32[2,1024]{1,0:T(2,128)} %refs_0_.10, bf16[1024,1024]{1,0:T(8,128)(2,1)S(1)} %copy-done, bf16[512,256]{1,0:T(8,128)(2,1)} %copy-done.8, bf16[512,256]{1,0:T(8,128)(2,1)} %copy-done.15, ...), custom_call_target="tpu_custom_call" | custom-call | flops 3221225472 | bytes 4194304 | tf_op jit(solution)/shard_map/pallas_call | solution.py:550
  136.3 7.3 %collective-permute-done.14.a_ref = bf16[512,256]{1,0:T(8,128)(2,1)S(1)} collective-permute-done((bf16[512,256]{1,0:T(8,128)(2,1)}, bf16[512,256]{1,0:T(8,128)(2,1)S(1)}, u32[]{:S(2)}, u32[]{:S(2)}) %collective-permute-start.14) | collective-permute-done | bytes 262176 | tf_op jit(solution)/shard_map/ppermute | solution.py:597
  146.5 2.7 %collective-permute-done.21.a_ref = bf16[512,256]{1,0:T(8,128)(2,1)S(1)} collective-permute-done((bf16[512,256]{1,0:T(8,128)(2,1)S(1)}, bf16[512,256]{1,0:T(8,128)(2,1)S(1)}, u32[]{:S(2)}, u32[]{:S(2)}) %collective-permute-start.21) | collective-permute-done | bytes 262176 | tf_op jit(solution)/shard_map/ppermute | solution.py:597
  150.9 3.9 %collective-permute-done.15.a_ref = bf16[512,256]{1,0:T(8,128)(2,1)S(1)} collective-permute-done((bf16[512,256]{1,0:T(8,128)(2,1)S(1)}, bf16[512,256]{1,0:T(8,128)(2,1)S(1)}, u32[]{:S(2)}, u32[]{:S(2)}) %collective-permute-start.15) | collective-permute-done | bytes 262176 | tf_op jit(solution)/shard_map/ppermute | solution.py:597
  157.6 2.8 %collective-permute-done.22.refs_2_ = bf16[512,256]{1,0:T(8,128)(2,1)S(1)} collective-permute-done((bf16[512,256]{1,0:T(8,128)(2,1)S(1)}, bf16[512,256]{1,0:T(8,128)(2,1)S(1)}, u32[]{:S(2)}, u32[]{:S(2)}) %collective-permute-start.22) | collective-permute-done | bytes 262176 | tf_op jit(solution)/shard_map/ppermute | solution.py:597
  161.8 2.1 %collective-permute-done.16.refs_2_ = bf16[512,256]{1,0:T(8,128)(2,1)S(1)} collective-permute-done((bf16[512,256]{1,0:T(8,128)(2,1)S(1)}, bf16[512,256]{1,0:T(8,128)(2,1)S(1)}, u32[]{:S(2)}, u32[]{:S(2)}) %collective-permute-start.16) | collective-permute-done | bytes 262176 | tf_op jit(solution)/shard_map/ppermute | solution.py:597
  165.2 3.9 %shard_map.104 = f32[32,2,128,128]{3,2,1,0:T(8,128)} custom-call(s32[32]{0:T(128)S(1)} %broadcast_add_fusion.src_ref, bf16[64,2,128,128]{3,2,1,0:T(8,128)(2,1)} %all-to-all-done.1.recv_hbm), custom_call_target="tpu_custom_call" | custom-call | bytes 4194304 | tf_op jit(solution)/shard_map/pallas_call | solution.py:622
  (101 shorter events, 31.1 us)
Async XLA Ops:
  1.9 15.0 %collective-permute-start.1 = (bf16[1024,256]{1,0:T(8,128)(2,1)S(1)}, bf16[1024,256]{1,0:T(8,128)(2,1)S(1)}, u32[]{:S(2)}, u32[]{:S(2)}) collective-permute-start(bf16[1024,256]{1,0:T(8,128)(2,1)S(1)} %bitcast.23), channel_id=1, source_target_pairs={{0,8},{4,12},{8,0},{12,4},{1,9},{5,13},{9,1},{13,5},{2,10},{6,14},... | collective-permute-start | bytes 1572872 | tf_op jit(solution)/shard_map/ppermute | solution.py:363
  4.9 15.6 %collective-permute-start = (bf16[1024,256]{1,0:T(8,128)(2,1)S(1)}, bf16[1024,256]{1,0:T(8,128)(2,1)}, u32[]{:S(2)}, u32[]{:S(2)}) collective-permute-start(bf16[1024,256]{1,0:T(8,128)(2,1)S(1)} %bitcast.24), channel_id=1, source_target_pairs={{0,4},{4,0},{8,12},{12,8},{1,5},{5,1},{9,13},{13,9},{2,6},{6,2},{1... | collective-permute-start | bytes 1572872 | tf_op jit(solution)/shard_map/ppermute | solution.py:363
  6.6 28.6 %all-to-all-start = ((bf16[4,256,256]{2,1,0:T(8,128)(2,1)}), bf16[4,256,256]{2,1,0:T(8,128)(2,1)}, u32[]{:S(2)}, u32[]{:S(2)}) async-start(bf16[4,256,256]{2,1,0:T(8,128)(2,1)} %broadcast_in_dim.16), calls=%async_computation | async-start | bytes 1048576 | tf_op jit(solution)/shard_map/all_to_all | solution.py:449
  11.5 36.0 %collective-permute-start.9 = (bf16[2,256,1024]{2,1,0:T(8,128)(2,1)}, bf16[2,256,1024]{2,1,0:T(8,128)(2,1)}, u32[]{:S(2)}, u32[]{:S(2)}) collective-permute-start(bf16[2,256,1024]{2,1,0:T(8,128)(2,1)} %refs_10_.3), channel_id=1, source_target_pairs={{0,4},{4,0},{8,12},{12,8},{1,5},{5,1},{9,13},{13,9},{2,6},{6,2},{1... | collective-permute-start | bytes 3145736 | tf_op jit(solution)/shard_map/ppermute | solution.py:466
  18.8 21.5 %collective-permute-start.10 = (bf16[272,1024]{1,0:T(8,128)(2,1)}, bf16[272,1024]{1,0:T(8,128)(2,1)}, u32[]{:S(2)}, u32[]{:S(2)}) collective-permute-start(bf16[272,1024]{1,0:T(8,128)(2,1)} %pad_maximum_fusion), channel_id=1, source_target_pairs={{0,8},{4,12},{8,0},{12,4},{1,9},{5,13},{9,1},{13,5},{2,10},{6,14},... | collective-permute-start | bytes 1671176 | tf_op jit(solution)/shard_map/ppermute | solution.py:363
  35.3 129.9 %all-to-all-start.1 = ((bf16[64,2,128,128]{3,2,1,0:T(8,128)(2,1)}), bf16[64,2,128,128]{3,2,1,0:T(8,128)(2,1)}, u32[]{:S(2)}, u32[]{:S(2)}) async-start(bf16[64,2,128,128]{3,2,1,0:T(8,128)(2,1)} %shard_map.103), calls=%async_computation.1 | async-start | bytes 8388608 | tf_op jit(solution)/shard_map/all_to_all | solution.py:546
  40.3 17.4 %collective-permute-start.12 = (bf16[272,1024]{1,0:T(8,128)(2,1)}, bf16[272,1024]{1,0:T(8,128)(2,1)S(1)}, u32[]{:S(2)}, u32[]{:S(2)}) collective-permute-start(bf16[272,1024]{1,0:T(8,128)(2,1)} %collective-permute-done.10.refs_12_), channel_id=1, source_target_pairs={{0,16},{16,0},{1,17},{17,1},{2,18},{18,2},{3,19},{19,3},{4,20},{20... | collective-permute-start | bytes 1671176 | tf_op jit(solution)/shard_map/ppermute | solution.py:462
  41.9 15.9 %collective-permute-start.11 = (bf16[272,1024]{1,0:T(8,128)(2,1)}, bf16[272,1024]{1,0:T(8,128)(2,1)}, u32[]{:S(2)}, u32[]{:S(2)}) collective-permute-start(bf16[272,1024]{1,0:T(8,128)(2,1)} %collective-permute-done.10.refs_12_), channel_id=1, source_target_pairs={{0,4},{4,0},{8,12},{12,8},{1,5},{5,1},{9,13},{13,9},{2,6},{6,2},{1... | collective-permute-start | bytes 1671176 | tf_op jit(solution)/shard_map/ppermute | solution.py:466
  42.0 57.7 %collective-permute-start.7 = (bf16[4,256,256]{2,1,0:T(8,128)(2,1)}, bf16[4,256,256]{2,1,0:T(8,128)(2,1)}, u32[]{:S(2)}, u32[]{:S(2)}) collective-permute-start(bf16[4,256,256]{2,1,0:T(8,128)(2,1)} %all-to-all-done.refs_6_), channel_id=1, source_target_pairs={{0,8},{4,12},{8,0},{12,4},{1,9},{5,13},{9,1},{13,5},{2,10},{6,14},... | collective-permute-start | bytes 1572872 | tf_op jit(solution)/shard_map/ppermute | solution.py:363
  45.0 9.3 %collective-permute-start.17 = (bf16[512,256]{1,0:T(8,128)(2,1)S(1)}, bf16[512,256]{1,0:T(8,128)(2,1)}, u32[]{:S(2)}, u32[]{:S(2)}) collective-permute-start(bf16[512,256]{1,0:T(8,128)(2,1)S(1)} %copy-done.10), channel_id=1, source_target_pairs={{0,2},{2,3},{3,1},{1,0},{4,6},{6,7},{7,5},{5,4},{8,10},{10,11},{11... | collective-permute-start | bytes 786440 | tf_op jit(solution)/shard_map/ppermute | solution.py:529
  47.6 52.2 %collective-permute-start.3 = (bf16[512,256]{1,0:T(8,128)(2,1)S(1)}, bf16[512,256]{1,0:T(8,128)(2,1)S(1)}, u32[]{:S(2)}, u32[]{:S(2)}) collective-permute-start(bf16[512,256]{1,0:T(8,128)(2,1)S(1)} %get-tuple-element.16.refs_2_), channel_id=1, source_target_pairs={{0,2},{2,3},{3,1},{1,0},{4,6},{6,7},{7,5},{5,4},{8,10},{10,11},{11... | collective-permute-start | bytes 786440 | tf_op jit(solution)/shard_map/ppermute | solution.py:529
  54.3 48.2 %collective-permute-start.18 = (bf16[512,256]{1,0:T(8,128)(2,1)}, bf16[512,256]{1,0:T(8,128)(2,1)S(1)}, u32[]{:S(2)}, u32[]{:S(2)}) collective-permute-start(bf16[512,256]{1,0:T(8,128)(2,1)} %collective-permute-done.17.refs_3_), channel_id=1, source_target_pairs={{0,2},{2,3},{3,1},{1,0},{4,6},{6,7},{7,5},{5,4},{8,10},{10,11},{11... | collective-permute-start | bytes 786440 | tf_op jit(solution)/shard_map/ppermute | solution.py:529
  57.8 54.7 %collective-permute-start.6 = (bf16[4,256,256]{2,1,0:T(8,128)(2,1)}, bf16[4,256,256]{2,1,0:T(8,128)(2,1)S(1)}, u32[]{:S(2)}, u32[]{:S(2)}) collective-permute-start(bf16[4,256,256]{2,1,0:T(8,128)(2,1)} %all-to-all-done.refs_6_), channel_id=1, source_target_pairs={{0,4},{4,0},{8,12},{12,8},{1,5},{5,1},{9,13},{13,9},{2,6},{6,2},{1... | collective-permute-start | bytes 1572872 | tf_op jit(solution)/shard_map/ppermute | solution.py:363
  57.8 54.7 %collective-permute-start.13 = (bf16[272,1024]{1,0:T(8,128)(2,1)S(1)}, bf16[272,1024]{1,0:T(8,128)(2,1)S(1)}, u32[]{:S(2)}, u32[]{:S(2)}) collective-permute-start(bf16[272,1024]{1,0:T(8,128)(2,1)S(1)} %collective-permute-done.12.refs_14_), channel_id=1, source_target_pairs={{0,4},{4,0},{8,12},{12,8},{1,5},{5,1},{9,13},{13,9},{2,6},{6,2},{1... | collective-permute-start | bytes 1671176 | tf_op jit(solution)/shard_map/ppermute | solution.py:466
  99.7 12.8 %collective-permute-start.8 = (bf16[4,256,256]{2,1,0:T(8,128)(2,1)}, bf16[4,256,256]{2,1,0:T(8,128)(2,1)S(1)}, u32[]{:S(2)}, u32[]{:S(2)}) collective-permute-start(bf16[4,256,256]{2,1,0:T(8,128)(2,1)} %collective-permute-done.7.refs_8_), channel_id=1, source_target_pairs={{0,4},{4,0},{8,12},{12,8},{1,5},{5,1},{9,13},{13,9},{2,6},{6,2},{1... | collective-permute-start | bytes 1572872 | tf_op jit(solution)/shard_map/ppermute | solution.py:363
  99.8 9.3 %collective-permute-start.4 = (bf16[512,256]{1,0:T(8,128)(2,1)S(1)}, bf16[512,256]{1,0:T(8,128)(2,1)S(1)}, u32[]{:S(2)}, u32[]{:S(2)}) collective-permute-start(bf16[512,256]{1,0:T(8,128)(2,1)S(1)} %collective-permute-done.3.refs_3_), channel_id=1, source_target_pairs={{0,2},{2,3},{3,1},{1,0},{4,6},{6,7},{7,5},{5,4},{8,10},{10,11},{11... | collective-permute-start | bytes 786440 | tf_op jit(solution)/shard_map/ppermute | solution.py:529
  102.4 12.3 %collective-permute-start.19 = (bf16[512,256]{1,0:T(8,128)(2,1)S(1)}, bf16[512,256]{1,0:T(8,128)(2,1)S(1)}, u32[]{:S(2)}, u32[]{:S(2)}) collective-permute-start(bf16[512,256]{1,0:T(8,128)(2,1)S(1)} %collective-permute-done.18.refs_4_), channel_id=1, source_target_pairs={{0,2},{2,3},{3,1},{1,0},{4,6},{6,7},{7,5},{5,4},{8,10},{10,11},{11... | collective-permute-start | bytes 786440 | tf_op jit(solution)/shard_map/ppermute | solution.py:529
  109.1 17.1 %collective-permute-start.5 = (bf16[512,256]{1,0:T(8,128)(2,1)S(1)}, bf16[512,256]{1,0:T(8,128)(2,1)S(1)}, u32[]{:S(2)}, u32[]{:S(2)}) collective-permute-start(bf16[512,256]{1,0:T(8,128)(2,1)S(1)} %collective-permute-done.4.refs_4_), channel_id=1, source_target_pairs={{0,2},{2,3},{3,1},{1,0},{4,6},{6,7},{7,5},{5,4},{8,10},{10,11},{11... | collective-permute-start | bytes 786440 | tf_op jit(solution)/shard_map/ppermute | solution.py:529
  122.8 12.1 %collective-permute-start.20 = (bf16[512,256]{1,0:T(8,128)(2,1)}, bf16[512,256]{1,0:T(8,128)(2,1)S(1)}, u32[]{:S(2)}, u32[]{:S(2)}) collective-permute-start(bf16[512,256]{1,0:T(8,128)(2,1)} %get-tuple-element.23), channel_id=1, source_target_pairs={{0,2},{2,3},{3,1},{1,0},{4,6},{6,7},{7,5},{5,4},{8,10},{10,11},{11... | collective-permute-start | bytes 786440 | tf_op jit(solution)/shard_map/ppermute | solution.py:597
  134.1 9.4 %collective-permute-start.14 = (bf16[512,256]{1,0:T(8,128)(2,1)}, bf16[512,256]{1,0:T(8,128)(2,1)S(1)}, u32[]{:S(2)}, u32[]{:S(2)}) collective-permute-start(bf16[512,256]{1,0:T(8,128)(2,1)} %get-tuple-element.18), channel_id=1, source_target_pairs={{0,2},{2,3},{3,1},{1,0},{4,6},{6,7},{7,5},{5,4},{8,10},{10,11},{11... | collective-permute-start | bytes 786440 | tf_op jit(solution)/shard_map/ppermute | solution.py:597
  135.0 14.2 %collective-permute-start.21 = (bf16[512,256]{1,0:T(8,128)(2,1)S(1)}, bf16[512,256]{1,0:T(8,128)(2,1)S(1)}, u32[]{:S(2)}, u32[]{:S(2)}) collective-permute-start(bf16[512,256]{1,0:T(8,128)(2,1)S(1)} %shard_map.101), channel_id=1, source_target_pairs={{0,2},{2,3},{3,1},{1,0},{4,6},{6,7},{7,5},{5,4},{8,10},{10,11},{11... | collective-permute-start | bytes 786440 | tf_op jit(solution)/shard_map/ppermute | solution.py:597
  144.6 10.2 %collective-permute-start.15 = (bf16[512,256]{1,0:T(8,128)(2,1)S(1)}, bf16[512,256]{1,0:T(8,128)(2,1)S(1)}, u32[]{:S(2)}, u32[]{:S(2)}) collective-permute-start(bf16[512,256]{1,0:T(8,128)(2,1)S(1)} %shard_map.97), channel_id=1, source_target_pairs={{0,2},{2,3},{3,1},{1,0},{4,6},{6,7},{7,5},{5,4},{8,10},{10,11},{11... | collective-permute-start | bytes 786440 | tf_op jit(solution)/shard_map/ppermute | solution.py:597
  149.3 11.2 %collective-permute-start.22 = (bf16[512,256]{1,0:T(8,128)(2,1)S(1)}, bf16[512,256]{1,0:T(8,128)(2,1)S(1)}, u32[]{:S(2)}, u32[]{:S(2)}) collective-permute-start(bf16[512,256]{1,0:T(8,128)(2,1)S(1)} %shard_map.102), channel_id=1, source_target_pairs={{0,2},{2,3},{3,1},{1,0},{4,6},{6,7},{7,5},{5,4},{8,10},{10,11},{11... | collective-permute-start | bytes 786440 | tf_op jit(solution)/shard_map/ppermute | solution.py:597
  155.8 8.0 %collective-permute-start.16 = (bf16[512,256]{1,0:T(8,128)(2,1)S(1)}, bf16[512,256]{1,0:T(8,128)(2,1)S(1)}, u32[]{:S(2)}, u32[]{:S(2)}) collective-permute-start(bf16[512,256]{1,0:T(8,128)(2,1)S(1)} %shard_map.98), channel_id=1, source_target_pairs={{0,2},{2,3},{3,1},{1,0},{4,6},{6,7},{7,5},{5,4},{8,10},{10,11},{11... | collective-permute-start | bytes 786440 | tf_op jit(solution)/shard_map/ppermute | solution.py:597
  (20 other events, 321.8 us)

commit v8 on v7

--- a/solution.py
+++ b/solution.py
@@ -241,16 +241,21 @@
     gains_hbm, tok_ref = refs[:2]
     gated_hbm = refs[2 : 2 + n_tensor]
     at = 2 + n_tensor
-    out_pieces = refs[at : at + n_dp]
-    at += n_dp
-    pairs = refs[at : at + 2]
-    near = refs[at + 2 : at + n_dp]
-    far = refs[at + n_dp : at + 2 * n_dp - 2]
-    at += 2 * n_dp - 2
-    own_hbm, *part_hbm = refs[at : at + n_tensor]
-    wo_ref, ffn_ref, res_ref, gated, own_ref, part_ref, hid_ref, act_ref, gain_ref = refs[
-        at + n_tensor : -3
-    ]
+    if base == 0:
+        out_pieces = refs[at : at + n_dp]
+        at += n_dp
+        pairs = refs[at : at + 2]
+        near = refs[at + 2 : at + n_dp]
+        far = refs[at + n_dp : at + 2 * n_dp - 2]
+        at += 2 * n_dp - 2
+        own_hbm, *part_hbm = refs[at : at + n_tensor]
+        wo_ref, ffn_ref = refs[at + n_tensor : at + n_tensor + 2]
+        at += n_tensor + 2
+    else:
+        wo_ref, ffn_ref = refs[at : at + 2]
+        own_hbm, *part_hbm = refs[at + 2 : at + 2 + n_tensor]
+        at += n_tensor + 2
+    res_ref, gated, own_ref, part_ref, hid_ref, act_ref, gain_ref = refs[at:-3]
     sems, gated_sems, done_sems = refs[-3:]
     rows, width = own_ref.shape
     me, group, here_at = (lax.axis_index(name) for name in ("dp", "group", "tensor"))
@@ -261,9 +266,6 @@
         for at_k in range(1, n_tensor):
             source = jnp.where(here_at == at_k, table[at_k][k], source)
         sources.append(source)
-    out_copies = piece_copies(
-        out_pieces, wo_ref, sems.at[0], me, lambda piece: piece.at[:, pl.ds(0, wo_ref.shape[1] // n_dp)]
-    )
     depth = ffn_ref.shape[1] // n_dp
 
     def ffn_copy(source, half, k):
@@ -272,15 +274,19 @@
             source, ffn_ref.at[half, pl.ds(start, depth)], sems.at[1 + half, k]
         )
 
-    up_copies = [ffn_copy(pairs[k].at[0], 0, k) for k in range(2)]
-    down_copies = [ffn_copy(pairs[k].at[1], 1, k) for k in range(2)]
-    rest = []
-    for k in range(2, n_dp):
-        near_rows = near[k - 2].at[pl.ds(0, depth)]
-        rest.append(ffn_copy(near_rows, group, k))
-        rest.append(ffn_copy(far[k - 2].at[pl.ds(0, depth)], 1 - group, k))
-        up_copies.append(ffn_copy(near_rows, 0, k))
-        down_copies.append(ffn_copy(near_rows, 1, k))
+    out_copies, up_copies, down_copies, rest = [], [], [], []
+    if base == 0:
+        out_copies = piece_copies(
+            out_pieces, wo_ref, sems.at[0], me, lambda piece: piece.at[:, pl.ds(0, depth)]
+        )
+        up_copies = [ffn_copy(pairs[k].at[0], 0, k) for k in range(2)]
+        down_copies = [ffn_copy(pairs[k].at[1], 1, k) for k in range(2)]
+        for k in range(2, n_dp):
+            near_rows = near[k - 2].at[pl.ds(0, depth)]
+            rest.append(ffn_copy(near_rows, group, k))
+            rest.append(ffn_copy(far[k - 2].at[pl.ds(0, depth)], 1 - group, k))
+            up_copies.append(ffn_copy(near_rows, 0, k))
+            down_copies.append(ffn_copy(near_rows, 1, k))
     gated_copies = [
         pltpu.make_async_copy(source, gated.at[k], gated_sems.at[k])
         for k, source in enumerate(gated_hbm[:-1])
@@ -547,18 +553,22 @@
 
     owns, parts, sums = [], [], []
     for c in range(CHUNKS):
-        own, *part = kernel_call(
+        weight_shapes = [
+            pltpu.VMEM((n_tensor, width, cols_here), bf16),
+            pltpu.VMEM((2, width, units_here), bf16),
+        ]
+        first = c == 0
+        outs = kernel_call(
             functools.partial(feed_kernel, n_dp, n_tensor, block, c * chunk_rows),
             [hbm_spec(), vmem_spec()]
             + [hbm_spec()] * (n_tensor - 1)
             + [vmem_spec()]
-            + [hbm_spec()] * (3 * n_dp - 2),
-            [hbm_spec()] * n_tensor,
+            + ([hbm_spec()] * (3 * n_dp - 2) if first else [vmem_spec()] * 2),
+            [hbm_spec()] * n_tensor + ([vmem_spec()] * 2 if first else []),
             [pltpu.HBM((chunk_rows, share), f32)]
-            + [pltpu.HBM((chunk_rows, share), bf16)] * (n_tensor - 1),
+            + [pltpu.HBM((chunk_rows, share), bf16)] * (n_tensor - 1)
+            + (weight_shapes if first else []),
             [
-                pltpu.VMEM((n_tensor, width, cols_here), bf16),
-                pltpu.VMEM((2, width, units_here), bf16),
                 pltpu.VMEM((chunk_rows, width), f32),
                 pltpu.VMEM((n_tensor - 1, chunk_rows, cols_here), bf16),
                 pltpu.VMEM((chunk_rows, share), f32),
@@ -576,8 +586,11 @@
             tokens,
             *in_hbm(gated[c][:-1]),
             gated[c][-1],
-            *in_hbm(out_pieces + ffn_pieces),
-        )
+            *(in_hbm(out_pieces + ffn_pieces) if first else whole),
+        )
+        if first:
+            whole = outs[n_tensor:]
+        own, *part = outs[:n_tensor]
         owns.append(own)
         parts.append(part)
         sums.append(None)

time: 170 us -> 173 us (1.018)
  starting transfers between devices: 44.9 us -> 52.1 us
  waiting for transfers between devices: 75.1 us -> 72.6 us
  Pallas kernels: 37.3 us -> 35.4 us
    ppermute x6, starting transfers between devices: 10.4 us -> 17.8 us  [per_device(): sums[c] = lax.ppermute(mine, 'tensor', ring)]
    ppermute x6, waiting for transfers between devices: 18.8 us -> 16.2 us  [per_device(): sums[c] = lax.ppermute(mine, 'tensor', ring)]
    pallas_call x2, Pallas kernels: 15.9 us -> 13.9 us  [per_device(): kernel_call(functools.partial(feed_kernel, n_dp, n_tensor, block, c * chu...]
  transfers between devices with their start and end apart: 26 -> 26, of which waited for: 11 -> 11; matrix products, arithmetic and copies ran while one was open for 5% -> 4% of each run, Pallas kernels for 20% -> 18%
where the time goes in v8:
time: 173 us; the launch traced here: 172 us
  waiting for transfers between devices  72.6 us (42%)
  starting transfers between devices  52.1 us (30%)
  Pallas kernels  35.4 us (20%)
  local copies, waits for them, and re-layouts  7.38 us (4%)
  other arithmetic  3.43 us (2%)
    ppermute x7, waiting for transfers between devices, xor_gather(): arrived.append(lax.ppermute(piece, axis, pairs))  44.4 us
    ppermute x6, starting transfers between devices, per_device(): sums[c] = lax.ppermute(mine, 'tensor', ring)  17.8 us
    ppermute x6, waiting for transfers between devices, per_device(): sums[c] = lax.ppermute(mine, 'tensor', ring)  16.2 us
    ppermute x6, starting transfers between devices, per_device(): gated[c].append(lax.ppermute(gated[c][-1], 'tensor', ring))  15.2 us
    pallas_call x2, Pallas kernels, per_device(): kernel_call(functools.partial(feed_kernel, n_dp, n_tensor, block, c * chu...  13.9 us
    ppermute x6, waiting for transfers between devices, per_device(): gated[c].append(lax.ppermute(gated[c][-1], 'tensor', ring))  11 us
    pallas_call x2, Pallas kernels, per_device(): kernel_call(functools.partial(project_kernel, n_dp, heads_here, event_cou...  9.81 us
    ppermute x7, starting transfers between devices, xor_gather(): arrived.append(lax.ppermute(piece, axis, pairs))  6.65 us
  transfers between devices with their start and end apart: 26, of which 11 were waited for; matrix products, arithmetic and copies ran while one was open for 4% of the time, Pallas kernels for 18%

profile of v8, /device:TPU:0, one launch (start us, length us, event | category | flops | bytes accessed | tf_op | source)
XLA Modules:
  0.0 172.1 jit_solution(16467815851577343602)
XLA Ops:
  1.9 3.0 %collective-permute-start.1 = (bf16[1024,256]{1,0:T(8,128)(2,1)S(1)}, bf16[1024,256]{1,0:T(8,128)(2,1)S(1)}, u32[]{:S(2)}, u32[]{:S(2)}) collective-permute-start(bf16[1024,256]{1,0:T(8,128)(2,1)S(1)} %bitcast.23), channel_id=1, source_target_pairs={{0,8},{4,12},{8,0},{12,4},{1,9},{5,13},{9,1},{13,5},{2,10},{6,14},... | collective-permute-start | bytes 1572872 | tf_op jit(solution)/shard_map/ppermute | solution.py:369
  6.6 4.9 %all-to-all-start = ((bf16[4,256,256]{2,1,0:T(8,128)(2,1)}), bf16[4,256,256]{2,1,0:T(8,128)(2,1)}, u32[]{:S(2)}, u32[]{:S(2)}) async-start(bf16[4,256,256]{2,1,0:T(8,128)(2,1)} %broadcast_in_dim.16), calls=%async_computation | async-start | bytes 1048576 | tf_op jit(solution)/shard_map/all_to_all | solution.py:455
  13.9 2.9 %collective-permute-done.1.refs_6_ = bf16[1024,256]{1,0:T(8,128)(2,1)S(1)} collective-permute-done((bf16[1024,256]{1,0:T(8,128)(2,1)S(1)}, bf16[1024,256]{1,0:T(8,128)(2,1)S(1)}, u32[]{:S(2)}, u32[]{:S(2)}) %collective-permute-start.1) | collective-permute-done | bytes 524320 | tf_op jit(solution)/shard_map/ppermute | solution.py:369
  20.5 4.9 %shard_map.96 = (bf16[512,256]{1,0:T(8,128)(2,1)S(1)}, bf16[512,256]{1,0:T(8,128)(2,1)}, bf16[512,256]{1,0:T(8,128)(2,1)}) custom-call(f32[8]{0:T(128)} %refs_0_.13, f32[2,1024]{1,0:T(2,128)} %refs_0_.10, bf16[1024,1024]{1,0:T(8,128)(2,1)S(1)} %copy-done, f32[32,2,128,128]{3,2,1,0:T(8,128)} %refs_2_.5, bf16[1024,256]{1,0:T(8,128)(2,1)S(1)} %bitcast.25, ...), custom_call_target="tpu_custom_call" | custom-call | flops 1073741824 | bytes 4194304 | tf_op jit(solution)/shard_map/pallas_call | solution.py:507
  25.4 4.9 %shard_map.95 = (bf16[512,256]{1,0:T(8,128)(2,1)S(1)}, bf16[512,256]{1,0:T(8,128)(2,1)}, bf16[512,256]{1,0:T(8,128)(2,1)}) custom-call(f32[8]{0:T(128)} %refs_0_.13, f32[2,1024]{1,0:T(2,128)} %refs_0_.10, bf16[1024,1024]{1,0:T(8,128)(2,1)S(1)} %copy-done, f32[32,2,128,128]{3,2,1,0:T(8,128)} %refs_2_.5, bf16[1024,256]{1,0:T(8,128)(2,1)S(1)} %bitcast.26, ...), custom_call_target="tpu_custom_call" | custom-call | flops 1073741824 | bytes 4194304 | tf_op jit(solution)/shard_map/pallas_call | solution.py:507
  30.4 4.9 %shard_map.103 = bf16[64,2,128,128]{3,2,1,0:T(8,128)(2,1)} custom-call(f32[8]{0:T(128)} %refs_0_.13, s32[32]{0:T(128)S(1)} %get-tuple-element.37.refs_1_, f32[32,2,128,128]{3,2,1,0:T(8,128)} %refs_2_.5, bf16[512,256]{1,0:T(8,128)(2,1)} %get-tuple-element.30.refs_3_, bf16[512,256]{1,0:T(8,128)(2,1)} %get-tuple-element.31.refs_4_, ...), custom_call_target="tpu_custom_call" | custom-call | flops 67108864 | bytes 4194304 | tf_op jit(solution)/shard_map/pallas_call | solution.py:537
  35.3 5.0 %all-to-all-start.1 = ((bf16[64,2,128,128]{3,2,1,0:T(8,128)(2,1)}), bf16[64,2,128,128]{3,2,1,0:T(8,128)(2,1)}, u32[]{:S(2)}, u32[]{:S(2)}) async-start(bf16[64,2,128,128]{3,2,1,0:T(8,128)(2,1)} %shard_map.103), calls=%async_computation.1 | async-start | bytes 8388608 | tf_op jit(solution)/shard_map/all_to_all | solution.py:552
  45.0 2.6 %collective-permute-start.6 = (bf16[512,256]{1,0:T(8,128)(2,1)S(1)}, bf16[512,256]{1,0:T(8,128)(2,1)S(1)}, u32[]{:S(2)}, u32[]{:S(2)}) collective-permute-start(bf16[512,256]{1,0:T(8,128)(2,1)S(1)} %copy-done.10), channel_id=1, source_target_pairs={{0,2},{2,3},{3,1},{1,0},{4,6},{6,7},{7,5},{5,4},{8,10},{10,11},{11... | collective-permute-start | bytes 786440 | tf_op jit(solution)/shard_map/ppermute | solution.py:535
  49.2 5.0 %collective-permute-done.6.refs_3_ = bf16[512,256]{1,0:T(8,128)(2,1)S(1)} collective-permute-done((bf16[512,256]{1,0:T(8,128)(2,1)S(1)}, bf16[512,256]{1,0:T(8,128)(2,1)S(1)}, u32[]{:S(2)}, u32[]{:S(2)}) %collective-permute-start.6) | collective-permute-done | bytes 262176 | tf_op jit(solution)/shard_map/ppermute | solution.py:535
  54.3 3.4 %collective-permute-start.7 = (bf16[512,256]{1,0:T(8,128)(2,1)S(1)}, bf16[512,256]{1,0:T(8,128)(2,1)S(1)}, u32[]{:S(2)}, u32[]{:S(2)}) collective-permute-start(bf16[512,256]{1,0:T(8,128)(2,1)S(1)} %collective-permute-done.6.refs_3_), channel_id=1, source_target_pairs={{0,2},{2,3},{3,1},{1,0},{4,6},{6,7},{7,5},{5,4},{8,10},{10,11},{11... | collective-permute-start | bytes 786440 | tf_op jit(solution)/shard_map/ppermute | solution.py:535
  58.2 41.5 %collective-permute-done.10.refs_8_ = bf16[4,256,256]{2,1,0:T(8,128)(2,1)} collective-permute-done((bf16[4,256,256]{2,1,0:T(8,128)(2,1)}, bf16[4,256,256]{2,1,0:T(8,128)(2,1)}, u32[]{:S(2)}, u32[]{:S(2)}) %collective-permute-start.10) | collective-permute-done | bytes 524320 | tf_op jit(solution)/shard_map/ppermute | solution.py:369
  99.8 2.6 %collective-permute-start.4 = (bf16[512,256]{1,0:T(8,128)(2,1)S(1)}, bf16[512,256]{1,0:T(8,128)(2,1)S(1)}, u32[]{:S(2)}, u32[]{:S(2)}) collective-permute-start(bf16[512,256]{1,0:T(8,128)(2,1)S(1)} %collective-permute-done.3.refs_3_), channel_id=1, source_target_pairs={{0,2},{2,3},{3,1},{1,0},{4,6},{6,7},{7,5},{5,4},{8,10},{10,11},{11... | collective-permute-start | bytes 786440 | tf_op jit(solution)/shard_map/ppermute | solution.py:535
  105.3 3.8 %collective-permute-done.4.refs_4_ = bf16[512,256]{1,0:T(8,128)(2,1)S(1)} collective-permute-done((bf16[512,256]{1,0:T(8,128)(2,1)S(1)}, bf16[512,256]{1,0:T(8,128)(2,1)S(1)}, u32[]{:S(2)}, u32[]{:S(2)}) %collective-permute-start.4) | collective-permute-done | bytes 262176 | tf_op jit(solution)/shard_map/ppermute | solution.py:535
  109.1 3.4 %collective-permute-start.5 = (bf16[512,256]{1,0:T(8,128)(2,1)S(1)}, bf16[512,256]{1,0:T(8,128)(2,1)S(1)}, u32[]{:S(2)}, u32[]{:S(2)}) collective-permute-start(bf16[512,256]{1,0:T(8,128)(2,1)S(1)} %collective-permute-done.4.refs_4_), channel_id=1, source_target_pairs={{0,2},{2,3},{3,1},{1,0},{4,6},{6,7},{7,5},{5,4},{8,10},{10,11},{11... | collective-permute-start | bytes 786440 | tf_op jit(solution)/shard_map/ppermute | solution.py:535
  114.8 8.0 %shard_map.97 = (f32[512,256]{1,0:T(8,128)}, bf16[512,256]{1,0:T(8,128)(2,1)}, bf16[512,256]{1,0:T(8,128)(2,1)}, bf16[512,256]{1,0:T(8,128)(2,1)}, bf16[4,1024,2...) custom-call(f32[2,1024]{1,0:T(2,128)} %refs_0_.10, bf16[1024,1024]{1,0:T(8,128)(2,1)S(1)} %copy-done, ...), custom_call_target="tpu_custom_call" | custom-call | flops 3221225472 | bytes 4194304 | tf_op jit(solution)/shard_map/pallas_call | solution.py:561
  122.9 5.9 %shard_map.98 = (f32[512,256]{1,0:T(8,128)}, bf16[512,256]{1,0:T(8,128)(2,1)}, bf16[512,256]{1,0:T(8,128)(2,1)}, bf16[512,256]{1,0:T(8,128)(2,1)}) custom-call(f32[2,1024]{1,0:T(2,128)} %refs_0_.10, bf16[1024,1024]{1,0:T(8,128)(2,1)S(1)} %copy-done, bf16[512,256]{1,0:T(8,128)(2,1)} %copy-done.8, bf16[512,256]{1,0:T(8,128)(2,1)} %copy-done.16, ...), custom_call_target="tpu_custom_call" | custom-call | flops 3221225472 | bytes 4194304 | tf_op jit(solution)/shard_map/pallas_call | solution.py:561
  128.8 3.4 %collective-permute-start.17 = (bf16[512,256]{1,0:T(8,128)(2,1)}, bf16[512,256]{1,0:T(8,128)(2,1)S(1)}, u32[]{:S(2)}, u32[]{:S(2)}) collective-permute-start(bf16[512,256]{1,0:T(8,128)(2,1)} %get-tuple-element.23), channel_id=1, source_target_pairs={{0,2},{2,3},{3,1},{1,0},{4,6},{6,7},{7,5},{5,4},{8,10},{10,11},{11... | collective-permute-start | bytes 786440 | tf_op jit(solution)/shard_map/ppermute | solution.py:610
  133.0 6.3 %collective-permute-done.17.a_ref = bf16[512,256]{1,0:T(8,128)(2,1)S(1)} collective-permute-done((bf16[512,256]{1,0:T(8,128)(2,1)}, bf16[512,256]{1,0:T(8,128)(2,1)S(1)}, u32[]{:S(2)}, u32[]{:S(2)}) %collective-permute-start.17) | collective-permute-done | bytes 262176 | tf_op jit(solution)/shard_map/ppermute | solution.py:610
  140.3 3.3 %collective-permute-start.18 = (bf16[512,256]{1,0:T(8,128)(2,1)S(1)}, bf16[512,256]{1,0:T(8,128)(2,1)S(1)}, u32[]{:S(2)}, u32[]{:S(2)}) collective-permute-start(bf16[512,256]{1,0:T(8,128)(2,1)S(1)} %shard_map.99), channel_id=1, source_target_pairs={{0,2},{2,3},{3,1},{1,0},{4,6},{6,7},{7,5},{5,4},{8,10},{10,11},{11... | collective-permute-start | bytes 786440 | tf_op jit(solution)/shard_map/ppermute | solution.py:610
  144.8 3.4 %collective-permute-start.21 = (bf16[512,256]{1,0:T(8,128)(2,1)S(1)}, bf16[512,256]{1,0:T(8,128)(2,1)S(1)}, u32[]{:S(2)}, u32[]{:S(2)}) collective-permute-start(bf16[512,256]{1,0:T(8,128)(2,1)S(1)} %shard_map.101), channel_id=1, source_target_pairs={{0,2},{2,3},{3,1},{1,0},{4,6},{6,7},{7,5},{5,4},{8,10},{10,11},{11... | collective-permute-start | bytes 786440 | tf_op jit(solution)/shard_map/ppermute | solution.py:610
  151.4 3.4 %collective-permute-start.19 = (bf16[512,256]{1,0:T(8,128)(2,1)S(1)}, bf16[512,256]{1,0:T(8,128)(2,1)S(1)}, u32[]{:S(2)}, u32[]{:S(2)}) collective-permute-start(bf16[512,256]{1,0:T(8,128)(2,1)S(1)} %shard_map.100), channel_id=1, source_target_pairs={{0,2},{2,3},{3,1},{1,0},{4,6},{6,7},{7,5},{5,4},{8,10},{10,11},{11... | collective-permute-start | bytes 786440 | tf_op jit(solution)/shard_map/ppermute | solution.py:610
  156.1 3.4 %collective-permute-start.22 = (bf16[512,256]{1,0:T(8,128)(2,1)S(1)}, bf16[512,256]{1,0:T(8,128)(2,1)S(1)}, u32[]{:S(2)}, u32[]{:S(2)}) collective-permute-start(bf16[512,256]{1,0:T(8,128)(2,1)S(1)} %shard_map.102), channel_id=1, source_target_pairs={{0,2},{2,3},{3,1},{1,0},{4,6},{6,7},{7,5},{5,4},{8,10},{10,11},{11... | collective-permute-start | bytes 786440 | tf_op jit(solution)/shard_map/ppermute | solution.py:610
  159.6 5.7 %collective-permute-done.22.refs_2_ = bf16[512,256]{1,0:T(8,128)(2,1)S(1)} collective-permute-done((bf16[512,256]{1,0:T(8,128)(2,1)S(1)}, bf16[512,256]{1,0:T(8,128)(2,1)S(1)}, u32[]{:S(2)}, u32[]{:S(2)}) %collective-permute-start.22) | collective-permute-done | bytes 262176 | tf_op jit(solution)/shard_map/ppermute | solution.py:610
  168.0 3.9 %shard_map.104 = f32[32,2,128,128]{3,2,1,0:T(8,128)} custom-call(s32[32]{0:T(128)S(1)} %broadcast_add_fusion.src_ref, bf16[64,2,128,128]{3,2,1,0:T(8,128)(2,1)} %all-to-all-done.1.recv_hbm), custom_call_target="tpu_custom_call" | custom-call | bytes 4194304 | tf_op jit(solution)/shard_map/pallas_call | solution.py:635
  (105 shorter events, 31.2 us)
Async XLA Ops:
  1.9 15.0 %collective-permute-start.1 = (bf16[1024,256]{1,0:T(8,128)(2,1)S(1)}, bf16[1024,256]{1,0:T(8,128)(2,1)S(1)}, u32[]{:S(2)}, u32[]{:S(2)}) collective-permute-start(bf16[1024,256]{1,0:T(8,128)(2,1)S(1)} %bitcast.23), channel_id=1, source_target_pairs={{0,8},{4,12},{8,0},{12,4},{1,9},{5,13},{9,1},{13,5},{2,10},{6,14},... | collective-permute-start | bytes 1572872 | tf_op jit(solution)/shard_map/ppermute | solution.py:369
  4.9 15.6 %collective-permute-start = (bf16[1024,256]{1,0:T(8,128)(2,1)S(1)}, bf16[1024,256]{1,0:T(8,128)(2,1)}, u32[]{:S(2)}, u32[]{:S(2)}) collective-permute-start(bf16[1024,256]{1,0:T(8,128)(2,1)S(1)} %bitcast.24), channel_id=1, source_target_pairs={{0,4},{4,0},{8,12},{12,8},{1,5},{5,1},{9,13},{13,9},{2,6},{6,2},{1... | collective-permute-start | bytes 1572872 | tf_op jit(solution)/shard_map/ppermute | solution.py:369
  6.6 28.6 %all-to-all-start = ((bf16[4,256,256]{2,1,0:T(8,128)(2,1)}), bf16[4,256,256]{2,1,0:T(8,128)(2,1)}, u32[]{:S(2)}, u32[]{:S(2)}) async-start(bf16[4,256,256]{2,1,0:T(8,128)(2,1)} %broadcast_in_dim.16), calls=%async_computation | async-start | bytes 1048576 | tf_op jit(solution)/shard_map/all_to_all | solution.py:455
  11.5 36.1 %collective-permute-start.12 = (bf16[2,256,1024]{2,1,0:T(8,128)(2,1)}, bf16[2,256,1024]{2,1,0:T(8,128)(2,1)}, u32[]{:S(2)}, u32[]{:S(2)}) collective-permute-start(bf16[2,256,1024]{2,1,0:T(8,128)(2,1)} %refs_10_.1), channel_id=1, source_target_pairs={{0,4},{4,0},{8,12},{12,8},{1,5},{5,1},{9,13},{13,9},{2,6},{6,2},{1... | collective-permute-start | bytes 3145736 | tf_op jit(solution)/shard_map/ppermute | solution.py:472
  18.8 21.5 %collective-permute-start.13 = (bf16[272,1024]{1,0:T(8,128)(2,1)}, bf16[272,1024]{1,0:T(8,128)(2,1)}, u32[]{:S(2)}, u32[]{:S(2)}) collective-permute-start(bf16[272,1024]{1,0:T(8,128)(2,1)} %pad_maximum_fusion), channel_id=1, source_target_pairs={{0,8},{4,12},{8,0},{12,4},{1,9},{5,13},{9,1},{13,5},{2,10},{6,14},... | collective-permute-start | bytes 1671176 | tf_op jit(solution)/shard_map/ppermute | solution.py:369
  35.3 132.7 %all-to-all-start.1 = ((bf16[64,2,128,128]{3,2,1,0:T(8,128)(2,1)}), bf16[64,2,128,128]{3,2,1,0:T(8,128)(2,1)}, u32[]{:S(2)}, u32[]{:S(2)}) async-start(bf16[64,2,128,128]{3,2,1,0:T(8,128)(2,1)} %shard_map.103), calls=%async_computation.1 | async-start | bytes 8388608 | tf_op jit(solution)/shard_map/all_to_all | solution.py:552
  40.3 17.3 %collective-permute-start.15 = (bf16[272,1024]{1,0:T(8,128)(2,1)}, bf16[272,1024]{1,0:T(8,128)(2,1)S(1)}, u32[]{:S(2)}, u32[]{:S(2)}) collective-permute-start(bf16[272,1024]{1,0:T(8,128)(2,1)} %collective-permute-done.13.refs_12_), channel_id=1, source_target_pairs={{0,16},{16,0},{1,17},{17,1},{2,18},{18,2},{3,19},{19,3},{4,20},{20... | collective-permute-start | bytes 1671176 | tf_op jit(solution)/shard_map/ppermute | solution.py:468
  41.9 15.8 %collective-permute-start.14 = (bf16[272,1024]{1,0:T(8,128)(2,1)}, bf16[272,1024]{1,0:T(8,128)(2,1)}, u32[]{:S(2)}, u32[]{:S(2)}) collective-permute-start(bf16[272,1024]{1,0:T(8,128)(2,1)} %collective-permute-done.13.refs_12_), channel_id=1, source_target_pairs={{0,4},{4,0},{8,12},{12,8},{1,5},{5,1},{9,13},{13,9},{2,6},{6,2},{1... | collective-permute-start | bytes 1671176 | tf_op jit(solution)/shard_map/ppermute | solution.py:472
  42.0 57.8 %collective-permute-start.10 = (bf16[4,256,256]{2,1,0:T(8,128)(2,1)}, bf16[4,256,256]{2,1,0:T(8,128)(2,1)}, u32[]{:S(2)}, u32[]{:S(2)}) collective-permute-start(bf16[4,256,256]{2,1,0:T(8,128)(2,1)} %all-to-all-done.refs_6_), channel_id=1, source_target_pairs={{0,8},{4,12},{8,0},{12,4},{1,9},{5,13},{9,1},{13,5},{2,10},{6,14},... | collective-permute-start | bytes 1572872 | tf_op jit(solution)/shard_map/ppermute | solution.py:369
  45.0 9.3 %collective-permute-start.6 = (bf16[512,256]{1,0:T(8,128)(2,1)S(1)}, bf16[512,256]{1,0:T(8,128)(2,1)S(1)}, u32[]{:S(2)}, u32[]{:S(2)}) collective-permute-start(bf16[512,256]{1,0:T(8,128)(2,1)S(1)} %copy-done.10), channel_id=1, source_target_pairs={{0,2},{2,3},{3,1},{1,0},{4,6},{6,7},{7,5},{5,4},{8,10},{10,11},{11... | collective-permute-start | bytes 786440 | tf_op jit(solution)/shard_map/ppermute | solution.py:535
  47.6 52.2 %collective-permute-start.3 = (bf16[512,256]{1,0:T(8,128)(2,1)S(1)}, bf16[512,256]{1,0:T(8,128)(2,1)S(1)}, u32[]{:S(2)}, u32[]{:S(2)}) collective-permute-start(bf16[512,256]{1,0:T(8,128)(2,1)S(1)} %get-tuple-element.18.refs_2_), channel_id=1, source_target_pairs={{0,2},{2,3},{3,1},{1,0},{4,6},{6,7},{7,5},{5,4},{8,10},{10,11},{11... | collective-permute-start | bytes 786440 | tf_op jit(solution)/shard_map/ppermute | solution.py:535
  54.3 48.2 %collective-permute-start.7 = (bf16[512,256]{1,0:T(8,128)(2,1)S(1)}, bf16[512,256]{1,0:T(8,128)(2,1)S(1)}, u32[]{:S(2)}, u32[]{:S(2)}) collective-permute-start(bf16[512,256]{1,0:T(8,128)(2,1)S(1)} %collective-permute-done.6.refs_3_), channel_id=1, source_target_pairs={{0,2},{2,3},{3,1},{1,0},{4,6},{6,7},{7,5},{5,4},{8,10},{10,11},{11... | collective-permute-start | bytes 786440 | tf_op jit(solution)/shard_map/ppermute | solution.py:535
  57.7 54.8 %collective-permute-start.9 = (bf16[4,256,256]{2,1,0:T(8,128)(2,1)}, bf16[4,256,256]{2,1,0:T(8,128)(2,1)S(1)}, u32[]{:S(2)}, u32[]{:S(2)}) collective-permute-start(bf16[4,256,256]{2,1,0:T(8,128)(2,1)} %all-to-all-done.refs_6_), channel_id=1, source_target_pairs={{0,4},{4,0},{8,12},{12,8},{1,5},{5,1},{9,13},{13,9},{2,6},{6,2},{1... | collective-permute-start | bytes 1572872 | tf_op jit(solution)/shard_map/ppermute | solution.py:369
  57.7 54.8 %collective-permute-start.16 = (bf16[272,1024]{1,0:T(8,128)(2,1)S(1)}, bf16[272,1024]{1,0:T(8,128)(2,1)S(1)}, u32[]{:S(2)}, u32[]{:S(2)}) collective-permute-start(bf16[272,1024]{1,0:T(8,128)(2,1)S(1)} %collective-permute-done.15.refs_14_), channel_id=1, source_target_pairs={{0,4},{4,0},{8,12},{12,8},{1,5},{5,1},{9,13},{13,9},{2,6},{6,2},{1... | collective-permute-start | bytes 1671176 | tf_op jit(solution)/shard_map/ppermute | solution.py:472
  99.8 12.8 %collective-permute-start.11 = (bf16[4,256,256]{2,1,0:T(8,128)(2,1)}, bf16[4,256,256]{2,1,0:T(8,128)(2,1)S(1)}, u32[]{:S(2)}, u32[]{:S(2)}) collective-permute-start(bf16[4,256,256]{2,1,0:T(8,128)(2,1)} %collective-permute-done.10.refs_8_), channel_id=1, source_target_pairs={{0,4},{4,0},{8,12},{12,8},{1,5},{5,1},{9,13},{13,9},{2,6},{6,2},{1... | collective-permute-start | bytes 1572872 | tf_op jit(solution)/shard_map/ppermute | solution.py:369
  99.8 9.3 %collective-permute-start.4 = (bf16[512,256]{1,0:T(8,128)(2,1)S(1)}, bf16[512,256]{1,0:T(8,128)(2,1)S(1)}, u32[]{:S(2)}, u32[]{:S(2)}) collective-permute-start(bf16[512,256]{1,0:T(8,128)(2,1)S(1)} %collective-permute-done.3.refs_3_), channel_id=1, source_target_pairs={{0,2},{2,3},{3,1},{1,0},{4,6},{6,7},{7,5},{5,4},{8,10},{10,11},{11... | collective-permute-start | bytes 786440 | tf_op jit(solution)/shard_map/ppermute | solution.py:535
  102.4 12.3 %collective-permute-start.8 = (bf16[512,256]{1,0:T(8,128)(2,1)S(1)}, bf16[512,256]{1,0:T(8,128)(2,1)S(1)}, u32[]{:S(2)}, u32[]{:S(2)}) collective-permute-start(bf16[512,256]{1,0:T(8,128)(2,1)S(1)} %collective-permute-done.7.refs_4_), channel_id=1, source_target_pairs={{0,2},{2,3},{3,1},{1,0},{4,6},{6,7},{7,5},{5,4},{8,10},{10,11},{11... | collective-permute-start | bytes 786440 | tf_op jit(solution)/shard_map/ppermute | solution.py:535
  109.1 13.7 %collective-permute-start.5 = (bf16[512,256]{1,0:T(8,128)(2,1)S(1)}, bf16[512,256]{1,0:T(8,128)(2,1)S(1)}, u32[]{:S(2)}, u32[]{:S(2)}) collective-permute-start(bf16[512,256]{1,0:T(8,128)(2,1)S(1)} %collective-permute-done.4.refs_4_), channel_id=1, source_target_pairs={{0,2},{2,3},{3,1},{1,0},{4,6},{6,7},{7,5},{5,4},{8,10},{10,11},{11... | collective-permute-start | bytes 786440 | tf_op jit(solution)/shard_map/ppermute | solution.py:535
  128.8 10.4 %collective-permute-start.17 = (bf16[512,256]{1,0:T(8,128)(2,1)}, bf16[512,256]{1,0:T(8,128)(2,1)S(1)}, u32[]{:S(2)}, u32[]{:S(2)}) collective-permute-start(bf16[512,256]{1,0:T(8,128)(2,1)} %get-tuple-element.23), channel_id=1, source_target_pairs={{0,2},{2,3},{3,1},{1,0},{4,6},{6,7},{7,5},{5,4},{8,10},{10,11},{11... | collective-permute-start | bytes 786440 | tf_op jit(solution)/shard_map/ppermute | solution.py:610
  132.2 12.5 %collective-permute-start.20 = (bf16[512,256]{1,0:T(8,128)(2,1)S(1)}, bf16[512,256]{1,0:T(8,128)(2,1)S(1)}, u32[]{:S(2)}, u32[]{:S(2)}) collective-permute-start(bf16[512,256]{1,0:T(8,128)(2,1)S(1)} %copy-done.18), channel_id=1, source_target_pairs={{0,2},{2,3},{3,1},{1,0},{4,6},{6,7},{7,5},{5,4},{8,10},{10,11},{11... | collective-permute-start | bytes 786440 | tf_op jit(solution)/shard_map/ppermute | solution.py:610
  140.3 10.1 %collective-permute-start.18 = (bf16[512,256]{1,0:T(8,128)(2,1)S(1)}, bf16[512,256]{1,0:T(8,128)(2,1)S(1)}, u32[]{:S(2)}, u32[]{:S(2)}) collective-permute-start(bf16[512,256]{1,0:T(8,128)(2,1)S(1)} %shard_map.99), channel_id=1, source_target_pairs={{0,2},{2,3},{3,1},{1,0},{4,6},{6,7},{7,5},{5,4},{8,10},{10,11},{11... | collective-permute-start | bytes 786440 | tf_op jit(solution)/shard_map/ppermute | solution.py:610
  144.8 11.2 %collective-permute-start.21 = (bf16[512,256]{1,0:T(8,128)(2,1)S(1)}, bf16[512,256]{1,0:T(8,128)(2,1)S(1)}, u32[]{:S(2)}, u32[]{:S(2)}) collective-permute-start(bf16[512,256]{1,0:T(8,128)(2,1)S(1)} %shard_map.101), channel_id=1, source_target_pairs={{0,2},{2,3},{3,1},{1,0},{4,6},{6,7},{7,5},{5,4},{8,10},{10,11},{11... | collective-permute-start | bytes 786440 | tf_op jit(solution)/shard_map/ppermute | solution.py:610
  151.4 15.3 %collective-permute-start.19 = (bf16[512,256]{1,0:T(8,128)(2,1)S(1)}, bf16[512,256]{1,0:T(8,128)(2,1)S(1)}, u32[]{:S(2)}, u32[]{:S(2)}) collective-permute-start(bf16[512,256]{1,0:T(8,128)(2,1)S(1)} %shard_map.100), channel_id=1, source_target_pairs={{0,2},{2,3},{3,1},{1,0},{4,6},{6,7},{7,5},{5,4},{8,10},{10,11},{11... | collective-permute-start | bytes 786440 | tf_op jit(solution)/shard_map/ppermute | solution.py:610
  156.1 9.3 %collective-permute-start.22 = (bf16[512,256]{1,0:T(8,128)(2,1)S(1)}, bf16[512,256]{1,0:T(8,128)(2,1)S(1)}, u32[]{:S(2)}, u32[]{:S(2)}) collective-permute-start(bf16[512,256]{1,0:T(8,128)(2,1)S(1)} %shard_map.102), channel_id=1, source_target_pairs={{0,2},{2,3},{3,1},{1,0},{4,6},{6,7},{7,5},{5,4},{8,10},{10,11},{11... | collective-permute-start | bytes 786440 | tf_op jit(solution)/shard_map/ppermute | solution.py:610
  (22 other events, 419.2 us)

commit v9 on v7

--- a/solution.py
+++ b/solution.py
@@ -237,23 +237,46 @@
         out_copy(slot).wait()
 
 
-def feed_kernel(n_dp, n_tensor, block, base, *refs):
+def collect_kernel(n_dp, *refs):
+    out_pieces = refs[:n_dp]
+    pairs = refs[n_dp : n_dp + 2]
+    near = refs[n_dp + 2 : 2 * n_dp]
+    far = refs[2 * n_dp : 3 * n_dp - 2]
+    wo_ref, ffn_ref, sems = refs[3 * n_dp - 2 :]
+    me, group = lax.axis_index("dp"), lax.axis_index("group")
+    depth = ffn_ref.shape[1] // n_dp
+
+    def ffn_copy(source, half, k):
+        start = pl.multiple_of(jnp.bitwise_xor(me, k) * depth, depth)
+        return pltpu.make_async_copy(
+            source, ffn_ref.at[half, pl.ds(start, depth)], sems.at[1 + half, k]
+        )
+
+    copies = piece_copies(
+        out_pieces, wo_ref, sems.at[0], me, lambda piece: piece.at[:, pl.ds(0, depth)]
+    )
+    for k in range(2):
+        copies += [ffn_copy(pairs[k].at[half], half, k) for half in range(2)]
+    for k in range(2, n_dp):
+        copies.append(ffn_copy(near[k - 2].at[pl.ds(0, depth)], group, k))
+        copies.append(ffn_copy(far[k - 2].at[pl.ds(0, depth)], 1 - group, k))
+    for copy in copies:
+        copy.start()
+    for copy in copies:
+        copy.wait()
+
+
+def feed_kernel(n_tensor, block, base, *refs):
     gains_hbm, tok_ref = refs[:2]
     gated_hbm = refs[2 : 2 + n_tensor]
     at = 2 + n_tensor
-    out_pieces = refs[at : at + n_dp]
-    at += n_dp
-    pairs = refs[at : at + 2]
-    near = refs[at + 2 : at + n_dp]
-    far = refs[at + n_dp : at + 2 * n_dp - 2]
-    at += 2 * n_dp - 2
-    own_hbm, *part_hbm = refs[at : at + n_tensor]
-    wo_ref, ffn_ref, res_ref, gated, own_ref, part_ref, hid_ref, act_ref, gain_ref = refs[
-        at + n_tensor : -3
-    ]
-    sems, gated_sems, done_sems = refs[-3:]
+    wo_ref, ffn_ref = refs[at : at + 2]
+    own_hbm, *part_hbm = refs[at + 2 : at + 2 + n_tensor]
+    at += n_tensor + 2
+    res_ref, gated, own_ref, part_ref, hid_ref, act_ref, gain_ref = refs[at:-2]
+    gated_sems, done_sems = refs[-2:]
     rows, width = own_ref.shape
-    me, group, here_at = (lax.axis_index(name) for name in ("dp", "group", "tensor"))
+    here_at = lax.axis_index("tensor")
     table = ring_sources(n_tensor)
     sources = []
     for k in range(n_tensor):
@@ -261,26 +284,6 @@
         for at_k in range(1, n_tensor):
             source = jnp.where(here_at == at_k, table[at_k][k], source)
         sources.append(source)
-    out_copies = piece_copies(
-        out_pieces, wo_ref, sems.at[0], me, lambda piece: piece.at[:, pl.ds(0, wo_ref.shape[1] // n_dp)]
-    )
-    depth = ffn_ref.shape[1] // n_dp
-
-    def ffn_copy(source, half, k):
-        start = pl.multiple_of(jnp.bitwise_xor(me, k) * depth, depth)
-        return pltpu.make_async_copy(
-            source, ffn_ref.at[half, pl.ds(start, depth)], sems.at[1 + half, k]
-        )
-
-    up_copies = [ffn_copy(pairs[k].at[0], 0, k) for k in range(2)]
-    down_copies = [ffn_copy(pairs[k].at[1], 1, k) for k in range(2)]
-    rest = []
-    for k in range(2, n_dp):
-        near_rows = near[k - 2].at[pl.ds(0, depth)]
-        rest.append(ffn_copy(near_rows, group, k))
-        rest.append(ffn_copy(far[k - 2].at[pl.ds(0, depth)], 1 - group, k))
-        up_copies.append(ffn_copy(near_rows, 0, k))
-        down_copies.append(ffn_copy(near_rows, 1, k))
     gated_copies = [
         pltpu.make_async_copy(source, gated.at[k], gated_sems.at[k])
         for k, source in enumerate(gated_hbm[:-1])
@@ -292,14 +295,10 @@
             pltpu.make_async_copy(part_ref.at[k - 1], part_hbm[k - 1], done_sems.at[k])
         )
     here = [gated.at[k] for k in range(n_tensor - 1)] + [gated_hbm[-1]]
-    for copy in out_copies + gated_copies:
+    for copy in gated_copies:
         copy.start()
-    for copy in up_copies[:2] + rest:
-        copy.start()
-    for copy in out_copies + gated_copies:
+    for copy in gated_copies:
         copy.wait()
-    for copy in down_copies[:2]:
-        copy.start()
     for r in range(0, rows, block):
         span = slice(r, r + block)
         attended = dot_nt(here[0][span], wo_ref[sources[0]])
@@ -308,14 +307,10 @@
         residual = tok_ref[base + r : base + r + block].astype(jnp.float32) + attended
         res_ref[span] = residual
         hid_ref[span] = rms_scale(residual, gain_ref[1:2, :])
-    for copy in up_copies:
-        copy.wait()
     for r in range(0, rows, block):
         span = slice(r, r + block)
         activated = jax.nn.gelu(dot_nn(hid_ref[span], ffn_ref[0]), approximate=True)
         act_ref[span] = activated.astype(jnp.bfloat16)
-    for copy in down_copies:
-        copy.wait()
 
     def term(k):
         start = pl.multiple_of(sources[k] * width, width)
@@ -545,20 +540,26 @@
     )(*in_hbm([head_rates]), send_pos, *in_hbm([past_states, *keys, *values]))
     received = lax.all_to_all(packed, "dp", split_axis=0, concat_axis=0, tiled=True)
 
+    whole = kernel_call(
+        functools.partial(collect_kernel, n_dp),
+        [hbm_spec()] * (3 * n_dp - 2),
+        [vmem_spec()] * 2,
+        [pltpu.VMEM((n_tensor, width, cols_here), bf16), pltpu.VMEM((2, width, units_here), bf16)],
+        [pltpu.SemaphoreType.DMA((3, n_dp))],
+        0,
+        limit_mib=8,
+    )(*in_hbm(out_pieces + ffn_pieces))
     owns, parts, sums = [], [], []
     for c in range(CHUNKS):
-        own, *part = kernel_call(
-            functools.partial(feed_kernel, n_dp, n_tensor, block, c * chunk_rows),
+        outs = kernel_call(
+            functools.partial(feed_kernel, n_tensor, block, c * chunk_rows),
             [hbm_spec(), vmem_spec()]
             + [hbm_spec()] * (n_tensor - 1)
-            + [vmem_spec()]
-            + [hbm_spec()] * (3 * n_dp - 2),
+            + [vmem_spec()] * 3,
             [hbm_spec()] * n_tensor,
             [pltpu.HBM((chunk_rows, share), f32)]
             + [pltpu.HBM((chunk_rows, share), bf16)] * (n_tensor - 1),
             [
-                pltpu.VMEM((n_tensor, width, cols_here), bf16),
-                pltpu.VMEM((2, width, units_here), bf16),
                 pltpu.VMEM((chunk_rows, width), f32),
                 pltpu.VMEM((n_tensor - 1, chunk_rows, cols_here), bf16),
                 pltpu.VMEM((chunk_rows, share), f32),
@@ -566,7 +567,6 @@
                 pltpu.VMEM((chunk_rows, width), bf16),
                 pltpu.VMEM((chunk_rows, units_here), bf16),
                 pltpu.VMEM(norm_gains.shape, f32),
-                pltpu.SemaphoreType.DMA((3, n_dp)),
                 pltpu.SemaphoreType.DMA((n_tensor,)),
                 pltpu.SemaphoreType.DMA((n_tensor,)),
             ],
@@ -576,8 +576,9 @@
             tokens,
             *in_hbm(gated[c][:-1]),
             gated[c][-1],
-            *in_hbm(out_pieces + ffn_pieces),
-        )
+            *whole,
+        )
+        own, *part = outs[:n_tensor]
         owns.append(own)
         parts.append(part)
         sums.append(None)

time: 170 us -> 165 us (0.971)
  waiting for transfers between devices: 75.1 us -> 71.5 us
  local copies, waits for them, and re-layouts: 7.38 us -> 9.11 us
    ppermute x6, waiting for transfers between devices: 11 us -> 8.83 us  [per_device(): gated[c].append(lax.ppermute(gated[c][-1], 'tensor', ring))]
    unnamed x37 -> x39, local copies, waits for them, and re-layouts: 1.97 us -> 3.72 us
    pallas_call x2 -> x3, Pallas kernels: 15.9 us -> 14.3 us  [the longest x2 11.4 us: per_device(): kernel_call(functools.partial(feed_kernel, n_tensor, block, c * chunk_row...]
  transfers between devices with their start and end apart: 26 -> 26, of which waited for: 11 -> 10; matrix products, arithmetic and copies ran while one was open for 5% -> 5% of each run, Pallas kernels for 20% -> 19%
where the time goes in v9:
time: 165 us
  waiting for transfers between devices  71.5 us (43%)
  starting transfers between devices  43.9 us (27%)
  Pallas kernels  35.7 us (22%)
  local copies, waits for them, and re-layouts  9.11 us (6%)
  other arithmetic  3.43 us (2%)
    ppermute x7, waiting for transfers between devices, xor_gather(): arrived.append(lax.ppermute(piece, axis, pairs))  44.4 us
    ppermute x6, waiting for transfers between devices, per_device(): sums[c] = lax.ppermute(mine, 'tensor', ring)  17.3 us
    ppermute x6, starting transfers between devices, per_device(): gated[c].append(lax.ppermute(gated[c][-1], 'tensor', ring))  15.2 us
    pallas_call x2, Pallas kernels, per_device(): kernel_call(functools.partial(feed_kernel, n_tensor, block, c * chunk_row...  11.4 us
    pallas_call x2, Pallas kernels, per_device(): kernel_call(functools.partial(project_kernel, n_dp, heads_here, event_cou...  9.81 us
    ppermute x6, starting transfers between devices, per_device(): sums[c] = lax.ppermute(mine, 'tensor', ring)  9.5 us
    ppermute x6, waiting for transfers between devices, per_device(): gated[c].append(lax.ppermute(gated[c][-1], 'tensor', ring))  8.83 us
    ppermute x7, starting transfers between devices, xor_gather(): arrived.append(lax.ppermute(piece, axis, pairs))  6.65 us
  transfers between devices with their start and end apart: 26, of which 10 were waited for; matrix products, arithmetic and copies ran while one was open for 5% of the time, Pallas kernels for 19%

profile of v9, /device:TPU:0, one launch (start us, length us, event | category | flops | bytes accessed | tf_op | source)
XLA Modules:
  0.0 164.8 jit_solution(9596759491563382880)
XLA Ops:
  1.9 3.0 %collective-permute-start.1 = (bf16[1024,256]{1,0:T(8,128)(2,1)S(1)}, bf16[1024,256]{1,0:T(8,128)(2,1)S(1)}, u32[]{:S(2)}, u32[]{:S(2)}) collective-permute-start(bf16[1024,256]{1,0:T(8,128)(2,1)S(1)} %bitcast.23), channel_id=1, source_target_pairs={{0,8},{4,12},{8,0},{12,4},{1,9},{5,13},{9,1},{13,5},{2,10},{6,14},... | collective-permute-start | bytes 1572872 | tf_op jit(solution)/shard_map/ppermute | solution.py:358
  6.6 4.9 %all-to-all-start = ((bf16[4,256,256]{2,1,0:T(8,128)(2,1)}), bf16[4,256,256]{2,1,0:T(8,128)(2,1)}, u32[]{:S(2)}, u32[]{:S(2)}) async-start(bf16[4,256,256]{2,1,0:T(8,128)(2,1)} %broadcast_in_dim.16), calls=%async_computation | async-start | bytes 1048576 | tf_op jit(solution)/shard_map/all_to_all | solution.py:444
  13.9 2.9 %collective-permute-done.1.refs_6_ = bf16[1024,256]{1,0:T(8,128)(2,1)S(1)} collective-permute-done((bf16[1024,256]{1,0:T(8,128)(2,1)S(1)}, bf16[1024,256]{1,0:T(8,128)(2,1)S(1)}, u32[]{:S(2)}, u32[]{:S(2)}) %collective-permute-start.1) | collective-permute-done | bytes 524320 | tf_op jit(solution)/shard_map/ppermute | solution.py:358
  20.5 4.9 %shard_map.100 = (bf16[512,256]{1,0:T(8,128)(2,1)S(1)}, bf16[512,256]{1,0:T(8,128)(2,1)}, bf16[512,256]{1,0:T(8,128)(2,1)}) custom-call(f32[8]{0:T(128)} %refs_0_.13, f32[2,1024]{1,0:T(2,128)} %refs_0_.10, bf16[1024,1024]{1,0:T(8,128)(2,1)S(1)} %copy-done, f32[32,2,128,128]{3,2,1,0:T(8,128)} %refs_2_.5, bf16[1024,256]{1,0:T(8,128)(2,1)S(1)} %bitcast.25, ...), custom_call_target="tpu_custom_call" | custom-call | flops 1073741824 | bytes 4194304 | tf_op jit(solution)/shard_map/pallas_call | solution.py:496
  25.4 4.9 %shard_map.95 = (bf16[512,256]{1,0:T(8,128)(2,1)S(1)}, bf16[512,256]{1,0:T(8,128)(2,1)}, bf16[512,256]{1,0:T(8,128)(2,1)}) custom-call(f32[8]{0:T(128)} %refs_0_.13, f32[2,1024]{1,0:T(2,128)} %refs_0_.10, bf16[1024,1024]{1,0:T(8,128)(2,1)S(1)} %copy-done, f32[32,2,128,128]{3,2,1,0:T(8,128)} %refs_2_.5, bf16[1024,256]{1,0:T(8,128)(2,1)S(1)} %bitcast.26, ...), custom_call_target="tpu_custom_call" | custom-call | flops 1073741824 | bytes 4194304 | tf_op jit(solution)/shard_map/pallas_call | solution.py:496
  30.4 4.9 %shard_map.104 = bf16[64,2,128,128]{3,2,1,0:T(8,128)(2,1)} custom-call(f32[8]{0:T(128)} %refs_0_.13, s32[32]{0:T(128)S(1)} %get-tuple-element.37.refs_1_, f32[32,2,128,128]{3,2,1,0:T(8,128)} %refs_2_.5, bf16[512,256]{1,0:T(8,128)(2,1)} %get-tuple-element.30.refs_3_, bf16[512,256]{1,0:T(8,128)(2,1)} %get-tuple-element.31.refs_4_, ...), custom_call_target="tpu_custom_call" | custom-call | flops 67108864 | bytes 4194304 | tf_op jit(solution)/shard_map/pallas_call | solution.py:526
  35.3 5.0 %all-to-all-start.1 = ((bf16[64,2,128,128]{3,2,1,0:T(8,128)(2,1)}), bf16[64,2,128,128]{3,2,1,0:T(8,128)(2,1)}, u32[]{:S(2)}, u32[]{:S(2)}) async-start(bf16[64,2,128,128]{3,2,1,0:T(8,128)(2,1)} %shard_map.104), calls=%async_computation.1 | async-start | bytes 8388608 | tf_op jit(solution)/shard_map/all_to_all | solution.py:541
  45.0 2.6 %collective-permute-start.17 = (bf16[512,256]{1,0:T(8,128)(2,1)S(1)}, bf16[512,256]{1,0:T(8,128)(2,1)S(1)}, u32[]{:S(2)}, u32[]{:S(2)}) collective-permute-start(bf16[512,256]{1,0:T(8,128)(2,1)S(1)} %copy-done.10), channel_id=1, source_target_pairs={{0,2},{2,3},{3,1},{1,0},{4,6},{6,7},{7,5},{5,4},{8,10},{10,11},{11... | collective-permute-start | bytes 786440 | tf_op jit(solution)/shard_map/ppermute | solution.py:524
  49.2 5.0 %collective-permute-done.17.refs_3_ = bf16[512,256]{1,0:T(8,128)(2,1)S(1)} collective-permute-done((bf16[512,256]{1,0:T(8,128)(2,1)S(1)}, bf16[512,256]{1,0:T(8,128)(2,1)S(1)}, u32[]{:S(2)}, u32[]{:S(2)}) %collective-permute-start.17) | collective-permute-done | bytes 262176 | tf_op jit(solution)/shard_map/ppermute | solution.py:524
  54.3 3.4 %collective-permute-start.18 = (bf16[512,256]{1,0:T(8,128)(2,1)S(1)}, bf16[512,256]{1,0:T(8,128)(2,1)S(1)}, u32[]{:S(2)}, u32[]{:S(2)}) collective-permute-start(bf16[512,256]{1,0:T(8,128)(2,1)S(1)} %collective-permute-done.17.refs_3_), channel_id=1, source_target_pairs={{0,2},{2,3},{3,1},{1,0},{4,6},{6,7},{7,5},{5,4},{8,10},{10,11},{11... | collective-permute-start | bytes 786440 | tf_op jit(solution)/shard_map/ppermute | solution.py:524
  58.2 41.5 %collective-permute-done.7.refs_2_ = bf16[4,256,256]{2,1,0:T(8,128)(2,1)} collective-permute-done((bf16[4,256,256]{2,1,0:T(8,128)(2,1)}, bf16[4,256,256]{2,1,0:T(8,128)(2,1)}, u32[]{:S(2)}, u32[]{:S(2)}) %collective-permute-start.7) | collective-permute-done | bytes 524320 | tf_op jit(solution)/shard_map/ppermute | solution.py:358
  99.8 2.6 %collective-permute-start.4 = (bf16[512,256]{1,0:T(8,128)(2,1)S(1)}, bf16[512,256]{1,0:T(8,128)(2,1)S(1)}, u32[]{:S(2)}, u32[]{:S(2)}) collective-permute-start(bf16[512,256]{1,0:T(8,128)(2,1)S(1)} %collective-permute-done.3.refs_3_), channel_id=1, source_target_pairs={{0,2},{2,3},{3,1},{1,0},{4,6},{6,7},{7,5},{5,4},{8,10},{10,11},{11... | collective-permute-start | bytes 786440 | tf_op jit(solution)/shard_map/ppermute | solution.py:524
  105.3 3.8 %collective-permute-done.4.refs_4_ = bf16[512,256]{1,0:T(8,128)(2,1)S(1)} collective-permute-done((bf16[512,256]{1,0:T(8,128)(2,1)S(1)}, bf16[512,256]{1,0:T(8,128)(2,1)S(1)}, u32[]{:S(2)}, u32[]{:S(2)}) %collective-permute-start.4) | collective-permute-done | bytes 262176 | tf_op jit(solution)/shard_map/ppermute | solution.py:524
  109.1 3.4 %collective-permute-start.5 = (bf16[512,256]{1,0:T(8,128)(2,1)S(1)}, bf16[512,256]{1,0:T(8,128)(2,1)S(1)}, u32[]{:S(2)}, u32[]{:S(2)}) collective-permute-start(bf16[512,256]{1,0:T(8,128)(2,1)S(1)} %collective-permute-done.4.refs_4_), channel_id=1, source_target_pairs={{0,2},{2,3},{3,1},{1,0},{4,6},{6,7},{7,5},{5,4},{8,10},{10,11},{11... | collective-permute-start | bytes 786440 | tf_op jit(solution)/shard_map/ppermute | solution.py:524
  114.3 2.9 %shard_map.96 = (bf16[4,1024,256]{2,1,0:T(8,128)(2,1)S(1)}, bf16[2,1024,1024]{2,1,0:T(8,128)(2,1)S(1)}) custom-call(bf16[4,256,256]{2,1,0:T(8,128)(2,1)} %all-to-all-done.refs_0_, bf16[4,256,256]{2,1,0:T(8,128)(2,1)} %copy-done.13, bf16[4,256,256]{2,1,0:T(8,128)(2,1)} %collective-permute-done.7.refs_2_, bf16[4,256,256]{2,1,0:T(8,128)(2,1)} %copy-done.14, ...), custom_call_target="tpu_custom_call" | custom-call | bytes 4194304 | tf_op jit(solution)/shard_map/pallas_call | solution.py:543
  117.2 5.7 %shard_map.101 = (f32[512,256]{1,0:T(8,128)}, bf16[512,256]{1,0:T(8,128)(2,1)}, bf16[512,256]{1,0:T(8,128)(2,1)}, bf16[512,256]{1,0:T(8,128)(2,1)}) custom-call(f32[2,1024]{1,0:T(2,128)} %refs_0_.10, bf16[1024,1024]{1,0:T(8,128)(2,1)S(1)} %copy-done, bf16[512,256]{1,0:T(8,128)(2,1)} %copy-done.9, bf16[512,256]{1,0:T(8,128)(2,1)} %copy-done.15, ...), custom_call_target="tpu_custom_call" | custom-call | flops 3221225472 | bytes 4194304 | tf_op jit(solution)/shard_map/pallas_call | solution.py:554
  123.9 5.7 %shard_map.97 = (f32[512,256]{1,0:T(8,128)}, bf16[512,256]{1,0:T(8,128)(2,1)}, bf16[512,256]{1,0:T(8,128)(2,1)}, bf16[512,256]{1,0:T(8,128)(2,1)}) custom-call(f32[2,1024]{1,0:T(2,128)} %refs_0_.10, bf16[1024,1024]{1,0:T(8,128)(2,1)S(1)} %copy-done, bf16[512,256]{1,0:T(8,128)(2,1)} %copy-done.8, bf16[512,256]{1,0:T(8,128)(2,1)} %copy-done.16, ...), custom_call_target="tpu_custom_call" | custom-call | flops 3221225472 | bytes 4194304 | tf_op jit(solution)/shard_map/pallas_call | solution.py:554
  132.4 6.7 %collective-permute-done.14.a_ref = bf16[512,256]{1,0:T(8,128)(2,1)S(1)} collective-permute-done((bf16[512,256]{1,0:T(8,128)(2,1)}, bf16[512,256]{1,0:T(8,128)(2,1)S(1)}, u32[]{:S(2)}, u32[]{:S(2)}) %collective-permute-start.14) | collective-permute-done | bytes 262176 | tf_op jit(solution)/shard_map/ppermute | solution.py:598
  142.3 2.4 %collective-permute-done.21.a_ref = bf16[512,256]{1,0:T(8,128)(2,1)S(1)} collective-permute-done((bf16[512,256]{1,0:T(8,128)(2,1)S(1)}, bf16[512,256]{1,0:T(8,128)(2,1)S(1)}, u32[]{:S(2)}, u32[]{:S(2)}) %collective-permute-start.21) | collective-permute-done | bytes 262176 | tf_op jit(solution)/shard_map/ppermute | solution.py:598
  144.8 2.0 %collective-permute-start.22 = (bf16[512,256]{1,0:T(8,128)(2,1)S(1)}, bf16[512,256]{1,0:T(8,128)(2,1)S(1)}, u32[]{:S(2)}, u32[]{:S(2)}) collective-permute-start(bf16[512,256]{1,0:T(8,128)(2,1)S(1)} %shard_map.103), channel_id=1, source_target_pairs={{0,2},{2,3},{3,1},{1,0},{4,6},{6,7},{7,5},{5,4},{8,10},{10,11},{11... | collective-permute-start | bytes 786440 | tf_op jit(solution)/shard_map/ppermute | solution.py:598
  146.7 3.6 %collective-permute-done.15.a_ref = bf16[512,256]{1,0:T(8,128)(2,1)S(1)} collective-permute-done((bf16[512,256]{1,0:T(8,128)(2,1)S(1)}, bf16[512,256]{1,0:T(8,128)(2,1)S(1)}, u32[]{:S(2)}, u32[]{:S(2)}) %collective-permute-start.15) | collective-permute-done | bytes 262176 | tf_op jit(solution)/shard_map/ppermute | solution.py:598
  153.4 2.5 %collective-permute-done.22.refs_2_ = bf16[512,256]{1,0:T(8,128)(2,1)S(1)} collective-permute-done((bf16[512,256]{1,0:T(8,128)(2,1)S(1)}, bf16[512,256]{1,0:T(8,128)(2,1)S(1)}, u32[]{:S(2)}, u32[]{:S(2)}) %collective-permute-start.22) | collective-permute-done | bytes 262176 | tf_op jit(solution)/shard_map/ppermute | solution.py:598
  157.3 2.1 %collective-permute-done.16.refs_2_ = bf16[512,256]{1,0:T(8,128)(2,1)S(1)} collective-permute-done((bf16[512,256]{1,0:T(8,128)(2,1)S(1)}, bf16[512,256]{1,0:T(8,128)(2,1)S(1)}, u32[]{:S(2)}, u32[]{:S(2)}) %collective-permute-start.16) | collective-permute-done | bytes 262176 | tf_op jit(solution)/shard_map/ppermute | solution.py:598
  160.7 3.9 %shard_map.105 = f32[32,2,128,128]{3,2,1,0:T(8,128)} custom-call(s32[32]{0:T(128)S(1)} %broadcast_add_fusion.src_ref, bf16[64,2,128,128]{3,2,1,0:T(8,128)(2,1)} %all-to-all-done.1.recv_hbm), custom_call_target="tpu_custom_call" | custom-call | bytes 4194304 | tf_op jit(solution)/shard_map/pallas_call | solution.py:623
  (104 shorter events, 33.4 us)
Async XLA Ops:
  1.9 15.0 %collective-permute-start.1 = (bf16[1024,256]{1,0:T(8,128)(2,1)S(1)}, bf16[1024,256]{1,0:T(8,128)(2,1)S(1)}, u32[]{:S(2)}, u32[]{:S(2)}) collective-permute-start(bf16[1024,256]{1,0:T(8,128)(2,1)S(1)} %bitcast.23), channel_id=1, source_target_pairs={{0,8},{4,12},{8,0},{12,4},{1,9},{5,13},{9,1},{13,5},{2,10},{6,14},... | collective-permute-start | bytes 1572872 | tf_op jit(solution)/shard_map/ppermute | solution.py:358
  4.9 15.6 %collective-permute-start = (bf16[1024,256]{1,0:T(8,128)(2,1)S(1)}, bf16[1024,256]{1,0:T(8,128)(2,1)}, u32[]{:S(2)}, u32[]{:S(2)}) collective-permute-start(bf16[1024,256]{1,0:T(8,128)(2,1)S(1)} %bitcast.24), channel_id=1, source_target_pairs={{0,4},{4,0},{8,12},{12,8},{1,5},{5,1},{9,13},{13,9},{2,6},{6,2},{1... | collective-permute-start | bytes 1572872 | tf_op jit(solution)/shard_map/ppermute | solution.py:358
  6.6 28.6 %all-to-all-start = ((bf16[4,256,256]{2,1,0:T(8,128)(2,1)}), bf16[4,256,256]{2,1,0:T(8,128)(2,1)}, u32[]{:S(2)}, u32[]{:S(2)}) async-start(bf16[4,256,256]{2,1,0:T(8,128)(2,1)} %broadcast_in_dim.16), calls=%async_computation | async-start | bytes 1048576 | tf_op jit(solution)/shard_map/all_to_all | solution.py:444
  11.5 36.1 %collective-permute-start.9 = (bf16[2,256,1024]{2,1,0:T(8,128)(2,1)}, bf16[2,256,1024]{2,1,0:T(8,128)(2,1)}, u32[]{:S(2)}, u32[]{:S(2)}) collective-permute-start(bf16[2,256,1024]{2,1,0:T(8,128)(2,1)} %refs_4_.1), channel_id=1, source_target_pairs={{0,4},{4,0},{8,12},{12,8},{1,5},{5,1},{9,13},{13,9},{2,6},{6,2},{1... | collective-permute-start | bytes 3145736 | tf_op jit(solution)/shard_map/ppermute | solution.py:461
  18.8 21.5 %collective-permute-start.10 = (bf16[272,1024]{1,0:T(8,128)(2,1)}, bf16[272,1024]{1,0:T(8,128)(2,1)}, u32[]{:S(2)}, u32[]{:S(2)}) collective-permute-start(bf16[272,1024]{1,0:T(8,128)(2,1)} %pad_maximum_fusion), channel_id=1, source_target_pairs={{0,8},{4,12},{8,0},{12,4},{1,9},{5,13},{9,1},{13,5},{2,10},{6,14},... | collective-permute-start | bytes 1671176 | tf_op jit(solution)/shard_map/ppermute | solution.py:358
  35.3 125.4 %all-to-all-start.1 = ((bf16[64,2,128,128]{3,2,1,0:T(8,128)(2,1)}), bf16[64,2,128,128]{3,2,1,0:T(8,128)(2,1)}, u32[]{:S(2)}, u32[]{:S(2)}) async-start(bf16[64,2,128,128]{3,2,1,0:T(8,128)(2,1)} %shard_map.104), calls=%async_computation.1 | async-start | bytes 8388608 | tf_op jit(solution)/shard_map/all_to_all | solution.py:541
  40.3 17.3 %collective-permute-start.12 = (bf16[272,1024]{1,0:T(8,128)(2,1)}, bf16[272,1024]{1,0:T(8,128)(2,1)S(1)}, u32[]{:S(2)}, u32[]{:S(2)}) collective-permute-start(bf16[272,1024]{1,0:T(8,128)(2,1)} %collective-permute-done.10.refs_6_), channel_id=1, source_target_pairs={{0,16},{16,0},{1,17},{17,1},{2,18},{18,2},{3,19},{19,3},{4,20},{20... | collective-permute-start | bytes 1671176 | tf_op jit(solution)/shard_map/ppermute | solution.py:457
  41.9 15.8 %collective-permute-start.11 = (bf16[272,1024]{1,0:T(8,128)(2,1)}, bf16[272,1024]{1,0:T(8,128)(2,1)}, u32[]{:S(2)}, u32[]{:S(2)}) collective-permute-start(bf16[272,1024]{1,0:T(8,128)(2,1)} %collective-permute-done.10.refs_6_), channel_id=1, source_target_pairs={{0,4},{4,0},{8,12},{12,8},{1,5},{5,1},{9,13},{13,9},{2,6},{6,2},{1... | collective-permute-start | bytes 1671176 | tf_op jit(solution)/shard_map/ppermute | solution.py:461
  42.0 57.8 %collective-permute-start.7 = (bf16[4,256,256]{2,1,0:T(8,128)(2,1)}, bf16[4,256,256]{2,1,0:T(8,128)(2,1)}, u32[]{:S(2)}, u32[]{:S(2)}) collective-permute-start(bf16[4,256,256]{2,1,0:T(8,128)(2,1)} %all-to-all-done.refs_0_), channel_id=1, source_target_pairs={{0,8},{4,12},{8,0},{12,4},{1,9},{5,13},{9,1},{13,5},{2,10},{6,14},... | collective-permute-start | bytes 1572872 | tf_op jit(solution)/shard_map/ppermute | solution.py:358
  45.0 9.3 %collective-permute-start.17 = (bf16[512,256]{1,0:T(8,128)(2,1)S(1)}, bf16[512,256]{1,0:T(8,128)(2,1)S(1)}, u32[]{:S(2)}, u32[]{:S(2)}) collective-permute-start(bf16[512,256]{1,0:T(8,128)(2,1)S(1)} %copy-done.10), channel_id=1, source_target_pairs={{0,2},{2,3},{3,1},{1,0},{4,6},{6,7},{7,5},{5,4},{8,10},{10,11},{11... | collective-permute-start | bytes 786440 | tf_op jit(solution)/shard_map/ppermute | solution.py:524
  47.6 52.2 %collective-permute-start.3 = (bf16[512,256]{1,0:T(8,128)(2,1)S(1)}, bf16[512,256]{1,0:T(8,128)(2,1)S(1)}, u32[]{:S(2)}, u32[]{:S(2)}) collective-permute-start(bf16[512,256]{1,0:T(8,128)(2,1)S(1)} %get-tuple-element.18.refs_2_), channel_id=1, source_target_pairs={{0,2},{2,3},{3,1},{1,0},{4,6},{6,7},{7,5},{5,4},{8,10},{10,11},{11... | collective-permute-start | bytes 786440 | tf_op jit(solution)/shard_map/ppermute | solution.py:524
  54.3 48.2 %collective-permute-start.18 = (bf16[512,256]{1,0:T(8,128)(2,1)S(1)}, bf16[512,256]{1,0:T(8,128)(2,1)S(1)}, u32[]{:S(2)}, u32[]{:S(2)}) collective-permute-start(bf16[512,256]{1,0:T(8,128)(2,1)S(1)} %collective-permute-done.17.refs_3_), channel_id=1, source_target_pairs={{0,2},{2,3},{3,1},{1,0},{4,6},{6,7},{7,5},{5,4},{8,10},{10,11},{11... | collective-permute-start | bytes 786440 | tf_op jit(solution)/shard_map/ppermute | solution.py:524
  57.7 54.8 %collective-permute-start.6 = (bf16[4,256,256]{2,1,0:T(8,128)(2,1)}, bf16[4,256,256]{2,1,0:T(8,128)(2,1)S(1)}, u32[]{:S(2)}, u32[]{:S(2)}) collective-permute-start(bf16[4,256,256]{2,1,0:T(8,128)(2,1)} %all-to-all-done.refs_0_), channel_id=1, source_target_pairs={{0,4},{4,0},{8,12},{12,8},{1,5},{5,1},{9,13},{13,9},{2,6},{6,2},{1... | collective-permute-start | bytes 1572872 | tf_op jit(solution)/shard_map/ppermute | solution.py:358
  57.7 54.8 %collective-permute-start.13 = (bf16[272,1024]{1,0:T(8,128)(2,1)S(1)}, bf16[272,1024]{1,0:T(8,128)(2,1)S(1)}, u32[]{:S(2)}, u32[]{:S(2)}) collective-permute-start(bf16[272,1024]{1,0:T(8,128)(2,1)S(1)} %collective-permute-done.12.refs_8_), channel_id=1, source_target_pairs={{0,4},{4,0},{8,12},{12,8},{1,5},{5,1},{9,13},{13,9},{2,6},{6,2},{1... | collective-permute-start | bytes 1671176 | tf_op jit(solution)/shard_map/ppermute | solution.py:461
  99.8 12.8 %collective-permute-start.8 = (bf16[4,256,256]{2,1,0:T(8,128)(2,1)}, bf16[4,256,256]{2,1,0:T(8,128)(2,1)S(1)}, u32[]{:S(2)}, u32[]{:S(2)}) collective-permute-start(bf16[4,256,256]{2,1,0:T(8,128)(2,1)} %collective-permute-done.7.refs_2_), channel_id=1, source_target_pairs={{0,4},{4,0},{8,12},{12,8},{1,5},{5,1},{9,13},{13,9},{2,6},{6,2},{1... | collective-permute-start | bytes 1572872 | tf_op jit(solution)/shard_map/ppermute | solution.py:358
  99.8 9.3 %collective-permute-start.4 = (bf16[512,256]{1,0:T(8,128)(2,1)S(1)}, bf16[512,256]{1,0:T(8,128)(2,1)S(1)}, u32[]{:S(2)}, u32[]{:S(2)}) collective-permute-start(bf16[512,256]{1,0:T(8,128)(2,1)S(1)} %collective-permute-done.3.refs_3_), channel_id=1, source_target_pairs={{0,2},{2,3},{3,1},{1,0},{4,6},{6,7},{7,5},{5,4},{8,10},{10,11},{11... | collective-permute-start | bytes 786440 | tf_op jit(solution)/shard_map/ppermute | solution.py:524
  102.4 14.7 %collective-permute-start.19 = (bf16[512,256]{1,0:T(8,128)(2,1)S(1)}, bf16[512,256]{1,0:T(8,128)(2,1)S(1)}, u32[]{:S(2)}, u32[]{:S(2)}) collective-permute-start(bf16[512,256]{1,0:T(8,128)(2,1)S(1)} %collective-permute-done.18.refs_4_), channel_id=1, source_target_pairs={{0,2},{2,3},{3,1},{1,0},{4,6},{6,7},{7,5},{5,4},{8,10},{10,11},{11... | collective-permute-start | bytes 786440 | tf_op jit(solution)/shard_map/ppermute | solution.py:524
  109.1 14.8 %collective-permute-start.5 = (bf16[512,256]{1,0:T(8,128)(2,1)S(1)}, bf16[512,256]{1,0:T(8,128)(2,1)S(1)}, u32[]{:S(2)}, u32[]{:S(2)}) collective-permute-start(bf16[512,256]{1,0:T(8,128)(2,1)S(1)} %collective-permute-done.4.refs_4_), channel_id=1, source_target_pairs={{0,2},{2,3},{3,1},{1,0},{4,6},{6,7},{7,5},{5,4},{8,10},{10,11},{11... | collective-permute-start | bytes 786440 | tf_op jit(solution)/shard_map/ppermute | solution.py:524
  123.0 7.8 %collective-permute-start.20 = (bf16[512,256]{1,0:T(8,128)(2,1)}, bf16[512,256]{1,0:T(8,128)(2,1)S(1)}, u32[]{:S(2)}, u32[]{:S(2)}) collective-permute-start(bf16[512,256]{1,0:T(8,128)(2,1)} %get-tuple-element.27), channel_id=1, source_target_pairs={{0,2},{2,3},{3,1},{1,0},{4,6},{6,7},{7,5},{5,4},{8,10},{10,11},{11... | collective-permute-start | bytes 786440 | tf_op jit(solution)/shard_map/ppermute | solution.py:598
  129.6 9.4 %collective-permute-start.14 = (bf16[512,256]{1,0:T(8,128)(2,1)}, bf16[512,256]{1,0:T(8,128)(2,1)S(1)}, u32[]{:S(2)}, u32[]{:S(2)}) collective-permute-start(bf16[512,256]{1,0:T(8,128)(2,1)} %get-tuple-element.22), channel_id=1, source_target_pairs={{0,2},{2,3},{3,1},{1,0},{4,6},{6,7},{7,5},{5,4},{8,10},{10,11},{11... | collective-permute-start | bytes 786440 | tf_op jit(solution)/shard_map/ppermute | solution.py:598
  130.8 13.9 %collective-permute-start.21 = (bf16[512,256]{1,0:T(8,128)(2,1)S(1)}, bf16[512,256]{1,0:T(8,128)(2,1)S(1)}, u32[]{:S(2)}, u32[]{:S(2)}) collective-permute-start(bf16[512,256]{1,0:T(8,128)(2,1)S(1)} %shard_map.102), channel_id=1, source_target_pairs={{0,2},{2,3},{3,1},{1,0},{4,6},{6,7},{7,5},{5,4},{8,10},{10,11},{11... | collective-permute-start | bytes 786440 | tf_op jit(solution)/shard_map/ppermute | solution.py:598
  140.1 10.2 %collective-permute-start.15 = (bf16[512,256]{1,0:T(8,128)(2,1)S(1)}, bf16[512,256]{1,0:T(8,128)(2,1)S(1)}, u32[]{:S(2)}, u32[]{:S(2)}) collective-permute-start(bf16[512,256]{1,0:T(8,128)(2,1)S(1)} %shard_map.98), channel_id=1, source_target_pairs={{0,2},{2,3},{3,1},{1,0},{4,6},{6,7},{7,5},{5,4},{8,10},{10,11},{11... | collective-permute-start | bytes 786440 | tf_op jit(solution)/shard_map/ppermute | solution.py:598
  144.8 11.2 %collective-permute-start.22 = (bf16[512,256]{1,0:T(8,128)(2,1)S(1)}, bf16[512,256]{1,0:T(8,128)(2,1)S(1)}, u32[]{:S(2)}, u32[]{:S(2)}) collective-permute-start(bf16[512,256]{1,0:T(8,128)(2,1)S(1)} %shard_map.103), channel_id=1, source_target_pairs={{0,2},{2,3},{3,1},{1,0},{4,6},{6,7},{7,5},{5,4},{8,10},{10,11},{11... | collective-permute-start | bytes 786440 | tf_op jit(solution)/shard_map/ppermute | solution.py:598
  151.3 8.0 %collective-permute-start.16 = (bf16[512,256]{1,0:T(8,128)(2,1)S(1)}, bf16[512,256]{1,0:T(8,128)(2,1)S(1)}, u32[]{:S(2)}, u32[]{:S(2)}) collective-permute-start(bf16[512,256]{1,0:T(8,128)(2,1)S(1)} %shard_map.99), channel_id=1, source_target_pairs={{0,2},{2,3},{3,1},{1,0},{4,6},{6,7},{7,5},{5,4},{8,10},{10,11},{11... | collective-permute-start | bytes 786440 | tf_op jit(solution)/shard_map/ppermute | solution.py:598
  (21 other events, 358.0 us)
